TPU v7x, 32 devices: a whole 2x2x4 slice. The times are simulated.
32 devices in a mesh: dp: 2 (over x), ctx: 4 (over y, core), exp: 4 (over z).
Axes of the slice: x: 2, y: 2, z: 4, core: 2. Of those that a mesh axis runs over, the one named last changes fastest.
Arguments:
- inputs: bfloat16 [8, 2048, 768], P(('dp', 'exp'), 'ctx'), may hold values from -6 to 6
- lengths: int32 [8, 2], P(('dp', 'exp')), may hold values from 1 to 1536, 2048 in all within a row
- block_order: int32 [8, 8], P(('dp', 'exp')), may hold values from 0 to 7, each once within a row
- routes: int32 [8, 2048, 2], P(('dp', 'exp'), 'ctx'), may hold values from 0 to 11, all different within a row; in each aligned block of 512 rows (0 to 511, 512 to 1023, ..., all dimensions but the last counted through in order) at most 128 rows name the same one
- prev_logits: float32 [8, 2048, 12], P(('dp', 'exp'), 'ctx'), may hold values from -6 to 6
- norm1_gain: float32 [768], replicated, may hold values from 0.5 to 1.5
- norm2_gain: float32 [768], replicated, may hold values from 0.5 to 1.5
- w_qkv: bfloat16 [3, 768, 768], replicated, may hold values from -0.3125 to 0.3125
- w_out: bfloat16 [768, 768], replicated, may hold values from -1.25 to 1.25
- w_router: float32 [768, 12], replicated, may hold values from -0.109375 to 0.109375
- w_carry: float32 [12, 12], replicated, may hold values from -0.875 to 0.875
- const_logit_w: float32 [2, 768, 2], replicated, may hold values from -0.21875 to 0.21875
- const_vec: float32 [2, 768], replicated, may hold values from -6 to 6
- w_gate: bfloat16 [8, 768, 2048], P('exp'), may hold values from -0.21875 to 0.21875
- w_up: bfloat16 [8, 768, 2048], P('exp'), may hold values from -0.21875 to 0.21875
- w_down: bfloat16 [8, 2048, 768], P('exp'), may hold values from -2 to 2
- cotangent: bfloat16 [8, 2048, 768], P(('dp', 'exp'), 'ctx'), may hold values from -6 to 6
Outputs:
- output: bfloat16 [8, 2048, 768], P(('dp', 'exp'), 'ctx')
- input_grad: float32 [8, 2048, 768], P(('dp', 'exp'), 'ctx')
- norm1_gain_grad: float32 [768], replicated
- norm2_gain_grad: float32 [768], replicated
- qkv_grad: float32 [3, 768, 768], replicated
- out_grad: float32 [768, 768], replicated
- router_grad: float32 [768, 12], replicated
- carry_grad: float32 [12, 12], replicated
- const_logit_grad: float32 [2, 768, 2], replicated
- const_vec_grad: float32 [2, 768], replicated
- gate_grad: float32 [8, 768, 2048], P('exp', None, 'dp')
- up_grad: float32 [8, 768, 2048], P('exp', None, 'dp')
- down_grad: float32 [8, 2048, 768], P('exp', 'dp')
- clipped_qk: float32 [2, 768, 768], replicated
Inputs may be any that keep to these rules, and one draw needn't show every extreme that they name: Among the rows of one device no expert is named by more than 128 routes; a token's two experts differ. `lengths`: each row sums to 2048. `block_order`: each row is a permutation.
All inputs are finite; a program needn't handle non-finite values.
Results may differ from a plain program's by a relative error of at most 0.023.
Values may be sent and summed in bfloat16 or wider, within the bound.
A program may use at most 192 MiB of HBM per device.

v0:
```python
import math

import jax
import jax.numpy as jnp
from jax import lax
from jax.sharding import PartitionSpec as P

HEADS = 12
CAP = 128


norm_eps = 1e-05
clip_limit = 3.0
mask_fill = -1e30
highest = lax.Precision.HIGHEST


def norm_forward(values, gain):
    inverse = lax.rsqrt(jnp.mean(values * values, axis=-1, keepdims=True) + norm_eps)
    normed = values * inverse
    return (normed, inverse, normed * gain)


def norm_backward(grad_out, normed, inverse, gain):
    grad_gain = jnp.sum(grad_out * normed, axis=0)
    scaled = grad_out * gain
    grad_in = inverse * (scaled - normed * jnp.mean(scaled * normed, axis=-1, keepdims=True))
    return (grad_in, grad_gain)


def positions(order_row, length_row, deal_block):
    offsets = lax.broadcasted_iota(jnp.int32, (order_row.shape[0], deal_block), 1)
    position = (order_row[:, None] * deal_block + offsets).reshape(-1)
    ends = jnp.cumsum(length_row)
    document = jnp.sum((position[:, None] >= ends[None, :]).astype(jnp.int32), axis=1)
    return (position, document)


def block_scores(
    query_heads, key_block, query_position, query_document, key_position, key_document
):
    factor = query_heads.shape[2] ** (-0.5)
    raw = (
        jnp.einsum("qhd,khd->hqk", query_heads, key_block, preferred_element_type=jnp.float32)
        * factor
    )
    allowed = (key_position[None, :] <= query_position[:, None]) & (
        key_document[None, :] == query_document[:, None]
    )
    return (jnp.where(allowed[None], raw, mask_fill), allowed)


def key_blocks(key_rows, value_rows, key_position, key_document, head_count):
    row_count = key_rows.shape[0]
    span_rows = math.gcd(row_count, 512)
    head_width = key_rows.shape[1] // head_count
    block_shape = (row_count // span_rows, span_rows, head_count, head_width)
    return (
        key_rows.reshape(block_shape),
        value_rows.reshape(block_shape),
        key_position.reshape(row_count // span_rows, span_rows),
        key_document.reshape(row_count // span_rows, span_rows),
    )


def attend_keys(
    carried,
    key_rows,
    value_rows,
    query_heads,
    query_position,
    query_document,
    all_position,
    all_document,
):
    blocks = key_blocks(key_rows, value_rows, all_position, all_document, query_heads.shape[1])

    def advance(running, block_items):
        running_max, running_sum, weighted = running
        key_block, value_block, pos_block, doc_block = block_items
        masked, allowed = block_scores(
            query_heads, key_block, query_position, query_document, pos_block, doc_block
        )
        new_max = jnp.maximum(running_max, jnp.max(masked, axis=2))
        shrink = jnp.exp(running_max - new_max)
        weights = jnp.where(allowed[None], jnp.exp(masked - new_max[:, :, None]), 0.0)
        running_sum = running_sum * shrink + jnp.sum(weights, axis=2)
        update = jnp.einsum(
            "hqk,khd->qhd",
            weights.astype(jnp.bfloat16),
            value_block,
            preferred_element_type=jnp.float32,
        )
        weighted = weighted * jnp.transpose(shrink)[:, :, None] + update
        return ((new_max, running_sum, weighted), None)

    carried, _ = lax.scan(advance, carried, blocks)
    return carried


def attend_back(
    query_heads,
    key_rows,
    value_rows,
    grad_heads,
    grad_dot,
    log_total,
    query_position,
    query_document,
    all_position,
    all_document,
):
    blocks = key_blocks(key_rows, value_rows, all_position, all_document, query_heads.shape[1])
    factor = query_heads.shape[2] ** (-0.5)

    def advance(grad_query, block_items):
        key_block, value_block, pos_block, doc_block = block_items
        masked, allowed = block_scores(
            query_heads, key_block, query_position, query_document, pos_block, doc_block
        )
        probability = jnp.where(allowed[None], jnp.exp(masked - log_total[:, :, None]), 0.0)
        grad_value = jnp.einsum(
            "hqk,qhd->khd",
            probability.astype(jnp.bfloat16),
            grad_heads,
            preferred_element_type=jnp.float32,
        )
        grad_prob = jnp.einsum(
            "qhd,khd->hqk", grad_heads, value_block, preferred_element_type=jnp.float32
        )
        grad_score = (probability * (grad_prob - grad_dot[:, :, None]) * factor).astype(
            jnp.bfloat16
        )
        grad_query = grad_query + jnp.einsum(
            "hqk,khd->qhd", grad_score, key_block, preferred_element_type=jnp.float32
        )
        grad_key = jnp.einsum(
            "hqk,qhd->khd", grad_score, query_heads, preferred_element_type=jnp.float32
        )
        return (grad_query, (grad_key, grad_value))

    zero_grads = jnp.zeros(query_heads.shape, jnp.float32)
    grad_query, (grad_key, grad_value) = lax.scan(advance, zero_grads, blocks)
    row_count = key_rows.shape[0]
    return (grad_query, grad_key.reshape(row_count, -1), grad_value.reshape(row_count, -1))


def reduce_experts(expert_parts):
    shares = (
        lax.psum_scatter(
            expert_parts[0].astype(jnp.bfloat16), "dp", scatter_dimension=2, tiled=True
        ).astype(jnp.float32),
        lax.psum_scatter(
            expert_parts[1].astype(jnp.bfloat16), "dp", scatter_dimension=2, tiled=True
        ).astype(jnp.float32),
        lax.psum_scatter(
            expert_parts[2].astype(jnp.bfloat16), "dp", scatter_dimension=1, tiled=True
        ).astype(jnp.float32),
    )
    return (
        lax.psum(shares[0].astype(jnp.bfloat16), "ctx").astype(jnp.float32),
        lax.psum(shares[1].astype(jnp.bfloat16), "ctx").astype(jnp.float32),
        lax.psum(shares[2].astype(jnp.bfloat16), "ctx").astype(jnp.float32),
    )


def shards(
    inputs,
    lengths,
    block_order,
    routes,
    prev_logits,
    norm1_gain,
    norm2_gain,
    w_qkv,
    w_out,
    w_router,
    w_carry,
    const_logit_w,
    const_vec,
    w_gate,
    w_up,
    w_down,
    cotangent,
):
    local_rows = inputs.shape[1]
    model_width = inputs.shape[2]
    head_count = HEADS
    head_width = model_width // head_count
    group_rows = local_rows * lax.axis_size("ctx")
    deal_block = group_rows // block_order.shape[1]
    expert_count = w_gate.shape[0] * lax.axis_size("exp")
    slot_count = CAP
    all_position, all_document = positions(block_order[0], lengths[0], deal_block)
    first_row = lax.axis_index("ctx") * local_rows
    query_position = lax.dynamic_slice_in_dim(all_position, first_row, local_rows)
    query_document = lax.dynamic_slice_in_dim(all_document, first_row, local_rows)
    residual_in = inputs[0].astype(jnp.float32)
    first_normed, first_inverse, first_scaled = norm_forward(residual_in, norm1_gain)
    first_low = first_scaled.astype(jnp.bfloat16)
    query_rows = jnp.dot(first_low, w_qkv[0], preferred_element_type=jnp.float32).astype(
        jnp.bfloat16
    )
    key_rows = jnp.dot(first_low, w_qkv[1], preferred_element_type=jnp.float32).astype(jnp.bfloat16)
    value_rows = jnp.dot(first_low, w_qkv[2], preferred_element_type=jnp.float32).astype(
        jnp.bfloat16
    )
    query_heads = query_rows.reshape(local_rows, head_count, head_width)
    carried = (
        jnp.full((head_count, local_rows), mask_fill, jnp.float32),
        jnp.zeros((head_count, local_rows), jnp.float32),
        jnp.zeros((local_rows, head_count, head_width), jnp.float32),
    )
    carried = attend_keys(
        carried,
        lax.all_gather(key_rows, "ctx", axis=0, tiled=True),
        lax.all_gather(value_rows, "ctx", axis=0, tiled=True),
        query_heads,
        query_position,
        query_document,
        all_position,
        all_document,
    )
    running_max, running_sum, weighted = carried
    attended = weighted / jnp.transpose(running_sum)[:, :, None]
    log_total = running_max + jnp.log(running_sum)
    head_max = lax.pmax(jnp.max(running_max, axis=1), ("dp", "ctx", "exp"))
    attended_low = attended.reshape(local_rows, model_width).astype(jnp.bfloat16)
    after_attn = residual_in + jnp.dot(attended_low, w_out, preferred_element_type=jnp.float32)
    second_normed, second_inverse, second_scaled = norm_forward(after_attn, norm2_gain)
    second_low = second_scaled.astype(jnp.bfloat16)
    previous = prev_logits[0]
    logits = jnp.dot(second_scaled, w_router, precision=highest) + jnp.dot(
        previous, w_carry, precision=highest
    )
    probability = jax.nn.softmax(logits, axis=-1)
    route_ids = routes[0]
    all_ids = lax.broadcasted_iota(jnp.int32, (1, 1, probability.shape[1]), 2)
    picked = (route_ids[:, :, None] == all_ids).astype(jnp.float32)
    gate_values = jnp.sum(picked * probability[:, None, :], axis=2)
    route_flat = route_ids.reshape(-1)
    route_count = route_flat.shape[0]
    expert_iota = lax.broadcasted_iota(jnp.int32, (1, expert_count), 1)
    route_hits = (route_flat[:, None] == expert_iota).astype(jnp.int32)
    slot_ranks = jnp.cumsum(route_hits, axis=0) - 1
    routed_flag = jnp.sum(route_hits, axis=1)
    slot_target = jnp.sum(route_hits * (expert_iota * slot_count + slot_ranks), axis=1) + (
        1 - routed_flag
    ) * (expert_count * slot_count)
    slot_route = (
        jnp.full((expert_count * slot_count + 1,), route_count, jnp.int32)
        .at[slot_target]
        .set(lax.iota(jnp.int32, route_count))[: expert_count * slot_count]
    )
    slot_token = slot_route // 2
    padded = jnp.concatenate([second_low, jnp.zeros((1, model_width), jnp.bfloat16)], axis=0)
    outgoing = padded[slot_token].reshape(expert_count, slot_count, model_width)
    arrived = lax.all_to_all(outgoing, "exp", split_axis=0, concat_axis=1, tiled=True)
    gate_pre = jnp.einsum("erd,edf->erf", arrived, w_gate, preferred_element_type=jnp.float32)
    up_pre = jnp.einsum("erd,edf->erf", arrived, w_up, preferred_element_type=jnp.float32)
    hidden = (jax.nn.silu(gate_pre) * up_pre).astype(jnp.bfloat16)
    produced = jnp.einsum(
        "erf,efd->erd", hidden, w_down, preferred_element_type=jnp.float32
    ).astype(jnp.bfloat16)
    returned = lax.all_to_all(produced, "exp", split_axis=1, concat_axis=0, tiled=True)
    returned_pad = jnp.concatenate(
        [
            returned.reshape(expert_count * slot_count, model_width),
            jnp.zeros((1, model_width), jnp.bfloat16),
        ],
        axis=0,
    )
    routed = returned_pad[slot_target].astype(jnp.float32).reshape(local_rows, 2, model_width)
    is_copy = (route_ids == expert_count + 1).astype(jnp.float32)
    const_ids = expert_count + 2 + lax.broadcasted_iota(jnp.int32, (1, 1, const_vec.shape[0]), 2)
    is_const = (route_ids[:, :, None] == const_ids).astype(jnp.float32)
    mix_weight = jax.nn.softmax(
        jnp.einsum("td,cde->tce", second_scaled, const_logit_w, precision=highest), axis=-1
    )
    const_out = (
        mix_weight[:, :, 0:1] * second_scaled[:, None, :] + mix_weight[:, :, 1:2] * const_vec[None]
    )
    branch = (
        routed
        + is_copy[:, :, None] * second_scaled[:, None, :]
        + jnp.einsum("tkc,tcd->tkd", is_const, const_out, precision=highest)
    )
    result = after_attn + jnp.sum(gate_values[:, :, None] * branch, axis=1)
    grad_result = cotangent[0].astype(jnp.float32)
    grad_gates = jnp.sum(branch * grad_result[:, None, :], axis=2)
    grad_branch = gate_values[:, :, None] * grad_result[:, None, :]
    branch_pad = jnp.concatenate(
        [grad_branch.reshape(route_count, model_width), jnp.zeros((1, model_width), jnp.float32)],
        axis=0,
    )
    grad_slots = (
        branch_pad[slot_route].astype(jnp.bfloat16).reshape(expert_count, slot_count, model_width)
    )
    grad_produced = lax.all_to_all(grad_slots, "exp", split_axis=0, concat_axis=1, tiled=True)
    down_part = jnp.einsum(
        "erf,erd->efd", hidden, grad_produced, preferred_element_type=jnp.float32
    )
    grad_hidden = jnp.einsum(
        "erd,efd->erf", grad_produced, w_down, preferred_element_type=jnp.float32
    )
    sigmoid_gate = jax.nn.sigmoid(gate_pre)
    grad_gate_pre = (
        grad_hidden * up_pre * sigmoid_gate * (1.0 + gate_pre * (1.0 - sigmoid_gate))
    ).astype(jnp.bfloat16)
    grad_up_pre = (grad_hidden * gate_pre * sigmoid_gate).astype(jnp.bfloat16)
    gate_part = jnp.einsum(
        "erd,erf->edf", arrived, grad_gate_pre, preferred_element_type=jnp.float32
    )
    up_part = jnp.einsum("erd,erf->edf", arrived, grad_up_pre, preferred_element_type=jnp.float32)
    grad_arrived = jnp.einsum(
        "erf,edf->erd", grad_gate_pre, w_gate, preferred_element_type=jnp.float32
    )
    grad_arrived = (
        grad_arrived
        + jnp.einsum("erf,edf->erd", grad_up_pre, w_up, preferred_element_type=jnp.float32)
    ).astype(jnp.bfloat16)
    grad_returned = lax.all_to_all(grad_arrived, "exp", split_axis=1, concat_axis=0, tiled=True)
    grad_pad = jnp.concatenate(
        [
            grad_returned.reshape(expert_count * slot_count, model_width),
            jnp.zeros((1, model_width), jnp.bfloat16),
        ],
        axis=0,
    )
    grad_second = jnp.sum(
        grad_pad[slot_target].astype(jnp.float32).reshape(local_rows, 2, model_width), axis=1
    )
    grad_second = grad_second + jnp.sum(is_copy[:, :, None] * grad_branch, axis=1)
    grad_const = jnp.einsum("tkc,tkd->tcd", is_const, grad_branch, precision=highest)
    grad_mix = jnp.stack(
        [
            jnp.sum(grad_const * second_scaled[:, None, :], axis=2),
            jnp.sum(grad_const * const_vec[None], axis=2),
        ],
        axis=2,
    )
    grad_score = mix_weight * (grad_mix - jnp.sum(mix_weight * grad_mix, axis=2, keepdims=True))
    grad_second = grad_second + jnp.sum(mix_weight[:, :, 0:1] * grad_const, axis=1)
    grad_second = grad_second + jnp.einsum(
        "tce,cde->td", grad_score, const_logit_w, precision=highest
    )
    const_vec_grad = jnp.sum(mix_weight[:, :, 1:2] * grad_const, axis=0)
    const_logit_grad = jnp.einsum("td,tce->cde", second_scaled, grad_score, precision=highest)
    grad_probs = jnp.sum(picked * grad_gates[:, :, None], axis=1)
    grad_logits = probability * (
        grad_probs - jnp.sum(probability * grad_probs, axis=1, keepdims=True)
    )
    router_grad = jnp.einsum("td,te->de", second_scaled, grad_logits, precision=highest)
    carry_grad = jnp.einsum("tf,te->fe", previous, grad_logits, precision=highest)
    grad_second = grad_second + jnp.einsum("te,de->td", grad_logits, w_router, precision=highest)
    grad_after_norm, norm2_grad = norm_backward(
        grad_second, second_normed, second_inverse, norm2_gain
    )
    grad_after = grad_result + grad_after_norm
    grad_attn_out = grad_after.astype(jnp.bfloat16)
    out_grad = jnp.einsum(
        "td,te->de", attended_low, grad_attn_out, preferred_element_type=jnp.float32
    )
    grad_attended = jnp.einsum(
        "te,de->td", grad_attn_out, w_out, preferred_element_type=jnp.float32
    ).astype(jnp.bfloat16)
    grad_heads = grad_attended.reshape(local_rows, head_count, head_width)
    grad_dot = jnp.transpose(jnp.sum(grad_heads.astype(jnp.float32) * attended, axis=2))
    keys_back, values_back = (
        lax.all_gather(key_rows, "ctx", axis=0, tiled=True),
        lax.all_gather(value_rows, "ctx", axis=0, tiled=True),
    )
    grad_query, grad_key_all, grad_value_all = attend_back(
        query_heads,
        keys_back,
        values_back,
        grad_heads,
        grad_dot,
        log_total,
        query_position,
        query_document,
        all_position,
        all_document,
    )
    grad_key_own, grad_value_own = (
        lax.psum_scatter(
            grad_key_all.astype(jnp.bfloat16), "ctx", scatter_dimension=0, tiled=True
        ).astype(jnp.float32),
        lax.psum_scatter(
            grad_value_all.astype(jnp.bfloat16), "ctx", scatter_dimension=0, tiled=True
        ).astype(jnp.float32),
    )
    grad_query_low = grad_query.reshape(local_rows, model_width).astype(jnp.bfloat16)
    grad_key_low = grad_key_own.astype(jnp.bfloat16)
    grad_value_low = grad_value_own.astype(jnp.bfloat16)
    qkv_grad = jnp.stack(
        [
            jnp.einsum("td,te->de", first_low, grad_query_low, preferred_element_type=jnp.float32),
            jnp.einsum("td,te->de", first_low, grad_key_low, preferred_element_type=jnp.float32),
            jnp.einsum("td,te->de", first_low, grad_value_low, preferred_element_type=jnp.float32),
        ]
    )
    grad_first = jnp.einsum(
        "te,de->td", grad_query_low, w_qkv[0], preferred_element_type=jnp.float32
    )
    grad_first = grad_first + jnp.einsum(
        "te,de->td", grad_key_low, w_qkv[1], preferred_element_type=jnp.float32
    )
    grad_first = grad_first + jnp.einsum(
        "te,de->td", grad_value_low, w_qkv[2], preferred_element_type=jnp.float32
    )
    grad_in_norm, norm1_grad = norm_backward(grad_first, first_normed, first_inverse, norm1_gain)
    input_grad = grad_after + grad_in_norm
    dense_total = lax.psum(
        (
            qkv_grad,
            out_grad,
            norm1_grad,
            norm2_grad,
            router_grad,
            carry_grad,
            const_logit_grad,
            const_vec_grad,
        ),
        ("dp", "ctx", "exp"),
    )
    gate_grad, up_grad, down_grad = reduce_experts((gate_part, up_part, down_part))
    clip_ratio = jnp.sqrt(jnp.minimum(1.0, clip_limit / head_max))
    head_scale = jnp.repeat(clip_ratio, head_width)
    clipped = w_qkv[:2].astype(jnp.float32) * head_scale[None, None, :]
    return (
        result.astype(jnp.bfloat16)[None],
        input_grad[None],
        dense_total[2],
        dense_total[3],
        dense_total[0],
        dense_total[1],
        dense_total[4],
        dense_total[5],
        dense_total[6],
        dense_total[7],
        gate_grad,
        up_grad,
        down_grad,
        clipped,
    )


def solution(mesh):
    in_specs = (
        P(("dp", "exp"), "ctx", None),
        P(("dp", "exp"), None),
        P(("dp", "exp"), None),
        P(("dp", "exp"), "ctx", None),
        P(("dp", "exp"), "ctx", None),
        P(),
        P(),
        P(),
        P(),
        P(),
        P(),
        P(),
        P(),
        P("exp", None, None),
        P("exp", None, None),
        P("exp", None, None),
        P(("dp", "exp"), "ctx", None),
    )
    out_specs = (
        P(("dp", "exp"), "ctx", None),
        P(("dp", "exp"), "ctx", None),
        P(),
        P(),
        P(),
        P(),
        P(),
        P(),
        P(),
        P(),
        P("exp", None, "dp"),
        P("exp", None, "dp"),
        P("exp", "dp", None),
        P(),
    )
    return jax.shard_map(shards, mesh=mesh, in_specs=in_specs, out_specs=out_specs, check_vma=False)
```

profile of v0, /device:TPU:0, one launch (start us, length us, event | category | flops | bytes accessed | tf_op | source)
XLA Modules:
  0.0 1076.5 jit_solution(18001324185694065335)
XLA Ops:
  29.2 14.2 %all-gather.3.cloned.1.call-done = bf16[2048,768]{1,0:T(8,128)(2,1)} async-done(((bf16[512,768]{1,0:T(8,128)(2,1)}), bf16[2048,768]{1,0:T(8,128)(2,1)}) %all-gather.3.cloned.1.call-update) | async-done | bytes 3145744 | tf_op jit(solution)/shard_map/all_gather | solution.py:216
  48.1 6.2 reshape.426
  58.6 15.5 %all-gather.5.cloned.1.call-done = bf16[2048,768]{1,0:T(8,128)(2,1)} async-done(((bf16[512,768]{1,0:T(8,128)(2,1)}), bf16[2048,768]{1,0:T(8,128)(2,1)}) %all-gather.5.cloned.1.call-update) | async-done | bytes 3145744 | tf_op jit(solution)/shard_map/all_gather | solution.py:217
  78.8 6.1 reshape.428
  89.2 88.0 %while.30 = (s32[]{:T(128)}, f32[12,512]{1,0:T(8,128)S(1)}, f32[12,512]{1,0:T(8,128)S(1)}, f32[512,12,64]{0,2,1:T(8,128)}, s32[4,512]{1,0:T(4,128)S(1)}, /*index...) while((s32[]{:T(128)}, f32[12,512]{1,0:T(8,128)S(1)}, ...), condition=%wide.region_6.7_spmd.clone, body=%wide.region_3.6_spmd.clone.sunk | while | flops 848203776 | bytes 95043760 | solution.py:97
  89.5 7.7 fusion.210
  97.2 7.8 fusion.212
  111.3 7.7 fusion.210
  119.0 7.8 fusion.212
  127.3 5.7 bitcast_add_fusion.6
  133.4 7.7 fusion.210
  141.1 7.8 fusion.212
  149.4 5.7 bitcast_add_fusion.6
  155.4 7.7 fusion.210
  163.1 7.8 fusion.212
  171.4 5.7 bitcast_add_fusion.6
  213.6 15.6 %all-to-all-done = bf16[8,128,768]{2,1,0:T(8,128)(2,1)} async-done(((bf16[8,128,768]{2,1,0:T(8,128)(2,1)}), bf16[8,128,768]{2,1,0:T(8,128)(2,1)}, u32[]{:S(2)}, u32[]{:S(2)}) %all-to-all-start) | async-done | bytes 1572896 | tf_op jit(solution)/shard_map/all_to_all | solution.py:258
  234.3 9.0 fusion.138
  243.4 8.4 fusion.139
  251.8 17.5 %all-to-all-done.2 = bf16[8,128,768]{2,1,0:T(8,128)(2,1)S(1)} async-done(((bf16[8,128,768]{2,1,0:T(8,128)(2,1)}), bf16[8,128,768]{2,1,0:T(8,128)(2,1)S(1)}, u32[]{:S(2)}, u32[]{:S(2)}) %all-to-all-start.2) | async-done | bytes 1572896 | tf_op jit(solution)/shard_map/all_to_all | solution.py:299
  269.4 14.7 %multiply_convert_fusion = (bf16[2,512,2048]{2,1,0:T(8,128)(2,1)}, bf16[2,512,2048]{2,1,0:T(8,128)(2,1)}, bf16[2,512,2048]{2,1,0:T(8,128)(2,1)}) fusion(f32[2,512,2048]{2,1,0:T(8,128)} %fusion.138, f32[2,512,2048]{2,1,0:T(8,128)} %fusion.139, bf16[2,512,768]{2,1,0:T(8,128)(2,1)S(1)} %bitcast.357, bf16[2,2048,768]{2,1,0:T(8,128)(2,1)} %param.36), kind=kOutput, calls=%fused_computation.62 | convolution fusion | flops 3254779904 | bytes 37224448 | tf_op jit(solution)/shard_map/erd,efd->erf/dot_general | solution.py:303
  284.1 7.6 convolution_convert_fusion.2
  291.9 7.6 convolution_convert_fusion.1
  309.6 20.8 %multiply_reduce_fusion = (f32[2,768]{1,0:T(2,128)}, f32[512,2]{1,0:T(8,128)}, f32[512,2]{1,0:T(8,128)}, f32[512,768]{1,0:T(8,128)}) fusion(f32[512,2]{1,0:T(8,128)} %bitcast.363, f32[2,768]{1,0:T(2,128)} %param.33, f32[512,768]{1,0:T(8,128)S(1)} %copy-done.7, f32[512,2]{1,0:T(8,128)} %bitcast.365, f32[512,768]{1,0:T(8,128)} %copy-done.19, ...), kind=kOutput, calls=%fused_computation.75 | convolution fusion | flops 25557504 | bytes 4755464 | tf_op jit(solution)/shard_map/tkc,tkd->tcd/dot_general | solution.py:334
  330.4 6.2 convolution_convert_fusion.3
  352.9 7.3 fusion.140
  360.2 6.3 add_convert_fusion
  369.3 10.6 all-to-all-done.1
  384.3 8.8 convolution_convert_fusion
  393.5 5.6 gather_fusion.1
  404.2 31.0 %multiply_reduce_fusion.1 = (f32[512,2]{1,0:T(8,128)}, f32[512,768]{1,0:T(8,128)}, f32[512,768]{1,0:T(8,128)}) fusion(f32[512,768]{1,0:T(8,128)} %copy-done.19, f32[512,2]{1,0:T(8,128)} %copy-done.41, f32[512,2]{1,0:T(8,128)} %copy.177, f32[2,768]{1,0:T(2,128)} %param.33, f32[512,2]{1,0:T(8,128)} %bitcast.364, f32[512,2]{1,0:T(8,128)} %bitcast.366, ...), kind=kOutput, calls=%fused_computation.76 | convolution fusion | flops 28312576 | bytes 9467912 | tf_op jit(solution)/shard_map/tkc,tcd->tkd/dot_general | solution.py:286
  450.5 6.9 reduce_sum.234
  470.6 129.5 %while.31 = (s32[]{:T(128)}, f32[512,12,64]{0,2,1:T(8,128)S(1)}, bf16[4,512,12,64]{1,3,2,0:T(8,128)(2,1)}, bf16[4,512,12,64]{1,3,2,0:T(8,128)(2,1)}, bf16[4,512,...) while((s32[]{:T(128)}, f32[512,12,64]{0,2,1:T(8,128)S(1)}, ...), condition=%wide.region_31.32_spmd.clone, body=%wide.region_30.31_spmd.clone.sunk | while | flops 2055733248 | bytes 195133808 | solution.py:143
  478.6 7.7 fusion.225
  494.3 7.4 bitcast_dynamic-update-slice_fusion.5
  510.8 7.7 fusion.225
  526.3 7.6 bitcast_dynamic-update-slice_fusion.5
  543.0 7.7 fusion.225
  558.5 7.6 bitcast_dynamic-update-slice_fusion.5
  575.3 7.7 fusion.225
  590.8 7.6 bitcast_dynamic-update-slice_fusion.5
  620.9 24.7 %reduce-scatter.8.cloned.1.call-done = bf16[512,768]{0,1:T(8,128)(2,1)} async-done(((bf16[2048,768]{0,1:T(8,128)(2,1)}), bf16[512,768]{0,1:T(8,128)(2,1)}) %reduce-scatter.8.cloned.1.call-update) | async-done | bytes 786448 | tf_op jit(solution)/shard_map/reduce_scatter | solution.py:389
  649.1 37.6 %reduce-scatter.6.cloned.1.call-done = bf16[512,768]{0,1:T(8,128)(2,1)} async-done(((bf16[2048,768]{0,1:T(8,128)(2,1)}), bf16[512,768]{0,1:T(8,128)(2,1)}) %reduce-scatter.6.cloned.1.call-update) | async-done | bytes 786448 | tf_op jit(solution)/shard_map/reduce_scatter | solution.py:386
  694.7 40.7 %pmax.7 = f32[12]{0:T(128)S(1)} all-reduce(f32[12]{0:T(128)S(1)} %copy-done.81), channel_id=1, replica_groups=mesh['dp'=2,'ctx'=4,'exp'=4] {'dp','ctx','exp'}, use_global_device_ids=true, to_apply=%region_53.54 | all-reduce | flops 12 | bytes 96 | tf_op jit(solution)/shard_map/pmax | solution.py:227
  746.2 43.3 %all-reduce.4 = (f32[768]{0:T(1024)}, f32[768]{0:T(1024)}, f32[768,12]{0,1:T(8,128)}, f32[12,12]{0,1:T(8,128)S(1)}, f32[2,768,2]{1,2,0:T(2,128)}, /*index=5*/f32[2,768]{1,0:T(2,128)}) all-reduce(f32[768]{0:T(1024)S(1)} %get-tuple-element.437, f32[768]{0:T(1024)S(1)} %copy-done.76, ...), channel_id=1, replica_groups=mesh['dp'=2,'ctx'=4,'exp'=4] {'dp','ctx','exp'}, use_global_device_ids=true, to_apply=%region_36.37 | all-reduce | flops 15504 | bytes 124032 | tf_op jit(solution)/shard_map/psum | solution.py:414
  793.1 69.8 %all-reduce.12.cloned.1.call-done = (bf16[2,768,1024]{2,1,0:T(8,128)(2,1)}, bf16[2,768,1024]{2,1,0:T(8,128)(2,1)}, bf16[2,1024,768]{2,1,0:T(8,128)(2,1)}) async-done(((bf16[2,768,1024]{2,1,0:T(8,128)(2,1)}, bf16[2,768,1024]{2,1,0:T(8,128)(2,1)}, bf16[2,1024,768]{2,1,0:T(8,128)(2,1)}), (bf16[2,768,1024]{2,1,0:T(8,128)(2,1)}, bf16[2,768,1024]{2,1,0:T(8,128)(2,1)}, ...) | async-done | bytes 9437200 | tf_op jit(solution)/shard_map/psum | solution.py:161
  875.0 186.7 %all-reduce.10.cloned.1.call-done = (f32[3,768,768]{2,1,0:T(8,128)}, f32[768,768]{1,0:T(8,128)}) async-done(((f32[3,768,768]{2,1,0:T(8,128)}, f32[768,768]{1,0:T(8,128)}), (f32[3,768,768]{2,1,0:T(8,128)}, f32[768,768]{1,0:T(8,128)})) %all-reduce.10.cloned.1.call-update) | async-done | bytes 9437200 | tf_op jit(solution)/shard_map/psum | solution.py:414
  1061.7 6.6 copy.259
  (411 shorter events, 285.0 us)
Async XLA Ops:
  7.2 171.7 %copy-start = (bf16[768,768]{1,0:T(8,128)(2,1)S(1)}, bf16[768,768]{1,0:T(8,128)(2,1)}, u32[]{:S(2)}) copy-start(bf16[768,768]{1,0:T(8,128)(2,1)} %param.29) | copy-start | bytes 3538948
  7.2 36.2 %all-gather.3.cloned.1.call-start = ((), (), s32[]{:S(2)}) async-start(), calls=%async_computation.9 | async-start | bytes 3932160 | tf_op jit(solution)/shard_map/all_gather | solution.py:216
  8.8 7.6 copy-start.57
  12.0 62.1 %all-gather.5.cloned.1.call-start = ((), (), s32[]{:S(2)}) async-start(), calls=%async_computation.10 | async-start | bytes 3932160 | tf_op jit(solution)/shard_map/all_gather | solution.py:217
  23.7 24.4 %copy-start.77 = (s32[1024,1]{0,1:T(1,128)}, s32[1024,1]{0,1:T(1,128)S(1)}, u32[]{:S(2)}) copy-start(s32[1024,1]{0,1:T(1,128)S(1)} %compare_select_fusion) | copy-start | bytes 12292
  97.2 8.3 copy-start.2
  119.0 8.3 copy-start.2
  141.1 8.3 copy-start.2
  163.1 8.3 copy-start.2
  179.9 6.9 copy-start.70
  186.8 42.4 %all-to-all-start = ((bf16[8,128,768]{2,1,0:T(8,128)(2,1)}), bf16[8,128,768]{2,1,0:T(8,128)(2,1)}, u32[]{:S(2)}, u32[]{:S(2)}) async-start(bf16[8,128,768]{2,1,0:T(8,128)(2,1)} %bitcast.347), calls=%async_computation | async-start | bytes 3145728 | tf_op jit(solution)/shard_map/all_to_all | solution.py:258
  195.8 7.6 copy-start.79
  229.2 40.1 %all-to-all-start.2 = ((bf16[8,128,768]{2,1,0:T(8,128)(2,1)}), bf16[8,128,768]{2,1,0:T(8,128)(2,1)S(1)}, u32[]{:S(2)}, u32[]{:S(2)}) async-start(bf16[8,128,768]{2,1,0:T(8,128)(2,1)} %bitcast.348), calls=%async_computation.2 | async-start | bytes 3145728 | tf_op jit(solution)/shard_map/all_to_all | solution.py:299
  232.8 381.6 %reduce-scatter.10.cloned.1.call-start = ((), (), s32[]{:S(2)}) async-start(), calls=%async_computation.13 | async-start | bytes 9437184 | tf_op jit(solution)/shard_map/reduce_scatter | solution.py:150
  234.3 9.0 copy-start.38
  269.4 14.7 %copy-start.37 = (bf16[2,4,128,768]{3,2,1,0:T(8,128)(2,1)}, bf16[2,4,128,768]{3,2,1,0:T(8,128)(2,1)S(1)}, u32[]{:S(2)}) copy-start(bf16[2,4,128,768]{3,2,1,0:T(8,128)(2,1)S(1)} %copy.183) | copy-start | bytes 4718596
  269.4 14.7 %copy-start.39 = (bf16[2,4,128,768]{3,2,1,0:T(8,128)(2,1)S(1)}, bf16[2,4,128,768]{3,2,1,0:T(8,128)(2,1)}, u32[]{:S(2)}) copy-start(bf16[2,4,128,768]{3,2,1,0:T(8,128)(2,1)} %copy-done.38) | copy-start | bytes 4718596
  291.7 322.7 %reduce-scatter.12.cloned.1.call-start = ((), (), s32[]{:S(2)}) async-start(), calls=%async_computation.14 | async-start | bytes 9437184 | tf_op jit(solution)/shard_map/reduce_scatter | solution.py:153
  306.5 42.5 %copy-start.50 = (f32[512,2,2]{0,2,1:T(2,128)}, f32[512,2,2]{0,2,1:T(2,128)S(1)}, u32[]{:S(2)}) copy-start(f32[512,2,2]{0,2,1:T(2,128)S(1)} %broadcast_divide_fusion.1) | copy-start | bytes 24580
  309.6 20.8 %copy-start.85 = (bf16[2,512,2048]{2,1,0:T(8,128)(2,1)S(1)}, bf16[2,512,2048]{2,1,0:T(8,128)(2,1)}, u32[]{:S(2)}) copy-start(bf16[2,512,2048]{2,1,0:T(8,128)(2,1)} %get-tuple-element.515) | copy-start | bytes 12582916
  339.4 40.4 %all-to-all-start.1 = ((bf16[2,512,768]{2,0,1:T(2,128)(2,1)}), bf16[2,512,768]{2,0,1:T(2,128)(2,1)S(1)}, u32[]{:S(2)}, u32[]{:S(2)}) async-start(bf16[2,512,768]{2,0,1:T(2,128)(2,1)} %copy.175), calls=%async_computation.1 | async-start | bytes 3145728 | tf_op jit(solution)/shard_map/all_to_all | solution.py:265
  346.6 13.6 %copy-start.59 = (f32[512,2,1]{0,2,1:T(1,128)}, f32[512,2,1]{0,2,1:T(1,128)S(1)}, u32[]{:S(2)}) copy-start(f32[512,2,1]{0,2,1:T(1,128)S(1)} %copy.209) | copy-start | bytes 12292
  352.9 7.3 copy-start.86
  379.8 58.6 %all-to-all-start.3 = ((bf16[2,512,768]{2,0,1:T(2,128)(2,1)}), bf16[2,512,768]{2,0,1:T(2,128)(2,1)}, u32[]{:S(2)}, u32[]{:S(2)}) async-start(bf16[2,512,768]{2,0,1:T(2,128)(2,1)} %copy.184), calls=%async_computation.3 | async-start | bytes 3145728 | tf_op jit(solution)/shard_map/all_to_all | solution.py:322
  384.2 230.2 %reduce-scatter.14.cloned.1.call-start = ((), (), s32[]{:S(2)}) async-start(), calls=%async_computation.15 | async-start | bytes 9437184 | tf_op jit(solution)/shard_map/reduce_scatter | solution.py:156
  393.2 252.4 %reduce-scatter.8.cloned.1.call-start = ((), (), s32[]{:S(2)}) async-start(), calls=%async_computation.12 | async-start | bytes 3932160 | tf_op jit(solution)/shard_map/reduce_scatter | solution.py:389
  404.1 32.1 %copy-start.63 = (f32[512]{0:T(512)S(1)}, f32[512]{0:T(512)}, u32[]{:S(2)}) copy-start(f32[512]{0:T(512)} %copy-done.62) | copy-start | bytes 6148
  404.1 32.1 %copy-start.74 = (f32[512]{0:T(512)S(1)}, f32[512]{0:T(512)}, u32[]{:S(2)}) copy-start(f32[512]{0:T(512)} %copy-done.73) | copy-start | bytes 6148
  450.5 6.9 copy-start.14
  450.5 6.9 copy-start.66
  450.5 6.9 copy-start.71
  486.3 5.7 copy-start.22
  494.0 7.6 copy-start.23
  526.3 7.6 copy-start.23
  558.5 7.6 copy-start.23
  583.0 5.7 copy-start.22
  590.8 7.6 copy-start.23
  607.1 79.6 %reduce-scatter.6.cloned.1.call-start = ((), (), s32[]{:S(2)}) async-start(), calls=%async_computation.11 | async-start | bytes 3932160 | tf_op jit(solution)/shard_map/reduce_scatter | solution.py:386
  614.3 248.6 %all-reduce.12.cloned.1.call-start = ((), (), s32[]{:S(2)}) async-start(), calls=%async_computation.17 | async-start | bytes 18874368 | tf_op jit(solution)/shard_map/psum | solution.py:161
  615.1 446.6 %all-reduce.10.cloned.1.call-start = ((), (), s32[]{:S(2)}) async-start(), calls=%async_computation.16 | async-start | bytes 18874368 | tf_op jit(solution)/shard_map/psum | solution.py:414
  694.0 41.5 %copy-start.9 = (f32[512,768]{1,0:T(8,128)S(1)}, f32[512,768]{1,0:T(8,128)}, u32[]{:S(2)}) copy-start(f32[512,768]{1,0:T(8,128)} %get-tuple-element.506) | copy-start | bytes 4718596
  694.0 41.5 %copy-start.51 = (f32[512,2,2]{0,2,1:T(2,128)S(1)}, f32[512,2,2]{0,2,1:T(2,128)}, u32[]{:S(2)}) copy-start(f32[512,2,2]{0,2,1:T(2,128)} %copy-done.50) | copy-start | bytes 24580
  694.0 41.5 %copy-start.60 = (f32[512,2,1]{0,2,1:T(1,128)S(1)}, f32[512,2,1]{0,2,1:T(1,128)}, u32[]{:S(2)}) copy-start(f32[512,2,1]{0,2,1:T(1,128)} %copy-done.59) | copy-start | bytes 12292
  694.0 41.5 %copy-start.61 = (f32[512,2,1]{0,2,1:T(1,128)S(1)}, f32[512,2,1]{0,2,1:T(1,128)}, u32[]{:S(2)}) copy-start(f32[512,2,1]{0,2,1:T(1,128)} %copy.208) | copy-start | bytes 12292
  694.0 41.5 %copy-start.68 = (f32[512,2]{0,1:T(2,128)S(1)}, f32[512,2]{0,1:T(2,128)}, u32[]{:S(2)}) copy-start(f32[512,2]{0,1:T(2,128)} %copy-done.67) | copy-start | bytes 12292
  743.8 46.3 %copy-start.17 = (f32[512,768]{1,0:T(8,128)S(1)}, f32[512,768]{1,0:T(8,128)}, u32[]{:S(2)}) copy-start(f32[512,768]{1,0:T(8,128)} %copy-done.15) | copy-start | bytes 4718596
  1061.7 6.6 copy-start.35
  1061.7 8.0 copy-start.1
  (73 other events, 227.9 us)
Sparse Core Ops, SparseCore 0:
  12.2 31.2 all-gather.2
  45.6 28.5 all-gather.4
  291.8 75.1 reduce-scatter.9
  369.8 77.0 reduce-scatter.11
  449.7 77.0 reduce-scatter.13
  607.2 38.3 reduce-scatter.7
  648.7 37.9 reduce-scatter.5
  689.6 173.2 all-reduce.11
  870.4 191.2 all-reduce.9
where the time goes:
time: 1080 us
  waiting for transfers between devices  393 us (36%)
  matrix products  322 us (30%)
  local copies, waits for them, and re-layouts  158 us (15%)
  other arithmetic  86.4 us (8%)
  blocking collectives  83.9 us (8%)
  starting transfers between devices  17.6 us (2%)
  between operations  15.1 us (1%)
    psum x1, waiting for transfers between devices, shards(): lax.psum((qkv_grad, out_grad, norm1_grad, norm2_grad, router_grad, carry_...  187 us
    psum x1, waiting for transfers between devices, reduce_experts(): lax.psum(shares[0].astype(jnp.bfloat16), 'ctx').astype(jnp.float32)  69.8 us
    psum x1, blocking collectives, shards(): lax.psum((qkv_grad, out_grad, norm1_grad, norm2_grad, router_grad, carry_...  43.3 us
    dot_general x8, matrix products, block_scores(): jnp.einsum('qhd,khd->hqk', query_heads, key_block, preferred_element_type...  42.7 us
    pmax x1, blocking collectives, shards(): head_max = lax.pmax(jnp.max(running_max, axis=1), ('dp', 'ctx', 'exp'))  40.7 us
    reduce_scatter x1, waiting for transfers between devices, shards(): lax.psum_scatter(grad_key_all.astype(jnp.bfloat16), 'ctx', scatter_dimens...  37.6 us
    reduce_sum x4, other arithmetic, advance(): running_sum = running_sum * shrink + jnp.sum(weights, axis=2)  31 us
    dot_general x4, matrix products, advance(): jnp.einsum('qhd,khd->hqk', grad_heads, value_block, preferred_element_typ...  31 us
  transfers between devices with their start and end apart: 13, of which 9 were waited for; matrix products, arithmetic and copies ran while one was open for 36% of the time, Pallas kernels for 0%

commit v1 on v0

v1 whole, which is shorter than its diff:
```python
import functools

import jax
import jax.numpy as jnp
from jax import lax
from jax.experimental import pallas as pl
from jax.experimental.pallas import tpu as pltpu
from jax.sharding import PartitionSpec as P

HEADS = 12
CAP = 128

norm_eps = 1e-05
clip_limit = 3.0
low_start = -1e30
mask_fill = -3e38
highest = lax.Precision.HIGHEST
NN = (((1,), (0,)), ((), ()))
NT = (((1,), (1,)), ((), ()))
TN = (((0,), (0,)), ((), ()))
f32 = jnp.float32
bf16 = jnp.bfloat16


def mm(left, right, dims=NN):
    return lax.dot_general(left, right, dims, preferred_element_type=f32)


def mm_full(left, right, dims=NN):
    return lax.dot_general(left, right, dims, precision=highest, preferred_element_type=f32)


def shape_of(shape, dtype):
    return jax.ShapeDtypeStruct(shape, dtype)


def whole(array):
    rank = len(array.shape)
    return pl.BlockSpec(array.shape, lambda *_: (0,) * rank)


def cost(flops, moved, exps=0):
    return pl.CostEstimate(flops=int(flops), bytes_accessed=int(moved), transcendentals=int(exps))


def run(body, grid, inputs, outputs, scratch=(), meta=None, flops=0, moved=0, exps=0, aliases=None):
    prefetch = 0 if meta is None else 1
    args = ([] if meta is None else [meta]) + [a for a, _ in inputs]
    return pl.pallas_call(
        body,
        out_shape=[o for o, _ in outputs],
        grid_spec=pltpu.PrefetchScalarGridSpec(
            num_scalar_prefetch=prefetch,
            grid=grid,
            in_specs=[s for _, s in inputs],
            out_specs=[s for _, s in outputs],
            scratch_shapes=list(scratch),
        ),
        compiler_params=pltpu.CompilerParams(
            dimension_semantics=("arbitrary",) * len(grid), vmem_limit_bytes=60 * 1024 * 1024
        ),
        cost_estimate=cost(flops, moved, exps),
        input_output_aliases={} if aliases is None else aliases,
    )(*args)


def swap(value, axis, distance):
    count = lax.axis_size(axis)
    return lax.ppermute(value, axis, [(i, i ^ distance) for i in range(count)])


def gather_near(value, axis):
    count = lax.axis_size(axis)
    found = {0: value}
    bit = count // 2
    while bit:
        for have in list(found):
            found[have | bit] = swap(found[have], axis, bit)
        bit //= 2
    return [found[j] for j in range(count)]


def butterfly(value, combine):
    for axis in ("ctx", "dp", "exp"):
        bit = 1
        while bit < lax.axis_size(axis):
            value = combine(value, swap(value, axis, bit))
            bit *= 2
    return value


def pick(stacked, index):
    return lax.dynamic_index_in_dim(stacked, index, 0, keepdims=False)


def add_low(*terms):
    total = terms[0].astype(f32)
    for term in terms[1:]:
        total = total + term.astype(f32)
    return total.astype(bf16)


def project(turn, rows_low, gain, weights_t, meta, earlier, group_rows):
    row_count, width = rows_low.shape
    per_group = weights_t.shape[2]
    head_width = width // HEADS
    heads = per_group // head_width
    tile = min(256, row_count)
    steps = row_count // tile
    scale = head_width**-0.5

    def body(meta_ref, x_ref, gain_ref, w_ref, *refs):
        q_ref, k_ref, v_ref, kt_ref, vt_ref, h_ref = refs[-6:]
        x = x_ref[...].astype(f32)
        inverse = lax.rsqrt(jnp.mean(x * x, axis=1, keepdims=True) + norm_eps)
        low = (x * inverse * gain_ref[...]).astype(bf16)
        h_ref[...] = low
        q = mm(low, w_ref[0, 0], NT).astype(bf16) * jnp.asarray(scale, bf16)
        k = mm(low, w_ref[1, 0], NT).astype(bf16)
        v = mm(low, w_ref[2, 0], NT).astype(bf16)
        for h in range(heads):
            part = slice(h * head_width, (h + 1) * head_width)
            q_ref[h] = q[:, part]
            k_ref[h] = k[:, part]
            v_ref[h] = v[:, part]
        kt_ref[...] = mm(w_ref[1, 0], low, NT).astype(bf16)
        vt_ref[...] = mm(w_ref[2, 0], low, NT).astype(bf16)

    by_head = shape_of((heads, group_rows, head_width), bf16)
    by_column = shape_of((per_group, group_rows), bf16)
    hidden = shape_of((group_rows, width), bf16)
    head_spec = pl.BlockSpec((heads, tile, head_width), lambda i, m: (0, turn * steps + i, 0))
    column_spec = pl.BlockSpec((per_group, tile), lambda i, m: (0, turn * steps + i))
    hidden_spec = pl.BlockSpec((tile, width), lambda i, m: (turn * steps + i, 0))
    inputs = [
        (rows_low, pl.BlockSpec((tile, width), lambda i, m: (i, 0))),
        (gain, pl.BlockSpec((1, width), lambda i, m: (0, 0))),
        (weights_t, pl.BlockSpec((3, 1, per_group, width), lambda i, m: (0, m[0], 0, 0))),
    ]
    aliases = None
    if earlier is not None:
        inputs += [(a, pl.BlockSpec(memory_space=pl.ANY)) for a in earlier]
        aliases = {4 + n: n for n in range(6)}
    return run(
        body,
        (steps,),
        inputs,
        [(by_head, head_spec)] * 3 + [(by_column, column_spec)] * 2 + [(hidden, hidden_spec)],
        meta=meta,
        flops=2 * row_count * width * per_group * 5,
        moved=row_count * width * 8 + weights_t.size // 2,
        aliases=aliases,
    )


def block_place(meta_ref, block, per_member, layout):
    member = meta_ref[0] ^ (block // per_member)
    return meta_ref[layout["order"] + member * per_member + block % per_member]


def document_start(meta_ref, position, layout):
    start = jnp.zeros_like(position)
    end = jnp.int32(0)
    for s in range(layout["sequences"]):
        end = end + meta_ref[layout["lengths"] + s]
        start = jnp.where(position >= end, end, start)
    return start


def block_range(meta_ref, query_block, key_block, rows, per_member, layout):
    q_first = block_place(meta_ref, query_block, per_member, layout) * rows
    k_first = block_place(meta_ref, key_block, per_member, layout) * rows
    begin = document_start(meta_ref, q_first, layout)
    begin_last = document_start(meta_ref, q_first + rows - 1, layout)
    needed = (k_first <= q_first) & (k_first + rows - 1 >= begin)
    full = (k_first < q_first) & (k_first >= begin_last)
    return q_first, k_first, needed, full


def allowed_pairs(meta_ref, q_first, k_first, rows, layout):
    q_pos = q_first + lax.broadcasted_iota(jnp.int32, (1, rows), 1)
    k_pos = k_first + lax.broadcasted_iota(jnp.int32, (rows, 1), 0)
    return (k_pos <= q_pos) & (k_pos >= document_start(meta_ref, q_pos, layout))


def attend(meta, q, k, vt, rows, per_member, layout):
    heads, group_rows, head_width = q.shape
    blocks = group_rows // rows
    width = heads * head_width

    def body(meta_ref, q_ref, k_ref, vt_ref, o_ref, ot_ref, lse_ref, top_ref, m_ref, l_ref, a_ref):
        i = pl.program_id(0)
        m_ref[...] = jnp.full_like(m_ref, low_start)
        l_ref[...] = jnp.zeros_like(l_ref)
        a_ref[...] = jnp.zeros_like(a_ref)

        def one(j, _):
            q_first, k_first, needed, full = block_range(meta_ref, i, j, rows, per_member, layout)
            at = pl.multiple_of(j * rows, rows)

            def step(masked):
                if masked:
                    allowed = allowed_pairs(meta_ref, q_first, k_first, rows, layout)
                for h in range(heads):
                    part = slice(h * head_width, (h + 1) * head_width)
                    s = mm(k_ref[h, pl.ds(at, rows), :], q_ref[h], NT)
                    if masked:
                        s = jnp.where(allowed, s, mask_fill)
                    old = m_ref[h]
                    new = jnp.maximum(old, jnp.max(s, axis=0, keepdims=True))
                    shrink = jnp.exp(old - new)
                    p = jnp.exp(s - new)
                    m_ref[h] = new
                    l_ref[h] = l_ref[h] * shrink + jnp.sum(p, axis=0, keepdims=True)
                    a_ref[part, :] = a_ref[part, :] * shrink + mm(
                        vt_ref[part, pl.ds(at, rows)], p.astype(bf16)
                    )

            @pl.when(full)
            def _():
                step(False)

            @pl.when(needed & jnp.logical_not(full))
            def _():
                step(True)

            return 0

        lax.fori_loop(0, blocks, one, 0)
        for h in range(heads):
            part = slice(h * head_width, (h + 1) * head_width)
            ot_ref[part, :] = a_ref[part, :] / l_ref[h]
            lse_ref[pl.ds(h, 1), :] = m_ref[h] + jnp.log(l_ref[h])
            top_ref[pl.ds(h, 1), :] = m_ref[h]
        o_ref[...] = jnp.transpose(ot_ref[...]).astype(bf16)

    row = shape_of((heads, group_rows), f32)
    row_spec = pl.BlockSpec((heads, rows), lambda i, m: (0, i))
    return run(
        body,
        (blocks,),
        [
            (q, pl.BlockSpec((heads, rows, head_width), lambda i, m: (0, i, 0))),
            (k, whole(k)),
            (vt, whole(vt)),
        ],
        [
            (shape_of((group_rows, width), bf16), pl.BlockSpec((rows, width), lambda i, m: (i, 0))),
            (shape_of((width, group_rows), f32), pl.BlockSpec((width, rows), lambda i, m: (0, i))),
            (row, row_spec),
            (row, row_spec),
        ],
        scratch=[
            pltpu.VMEM((heads, 1, rows), f32),
            pltpu.VMEM((heads, 1, rows), f32),
            pltpu.VMEM((width, rows), f32),
        ],
        meta=meta,
        flops=2 * 2 * group_rows * group_rows * width,
        moved=group_rows * width * 14,
        exps=group_rows * group_rows * heads // 2,
    )


def attend_back(meta, q, k, v, kt, grad, ot, lse, rows, per_member, layout):
    heads, group_rows, head_width = q.shape
    blocks = group_rows // rows
    width = heads * head_width
    scale = head_width**-0.5
    members = len(grad)
    per = grad[0].shape[0] // rows

    def body(meta_ref, q_ref, k_ref, v_ref, kt_ref, *refs):
        grads = refs[:members]
        ot_ref, lse_ref, out_ref, dk_ref, dv_ref, dq_ref, g_ref, delta_ref = refs[members:]
        i = pl.program_id(0)

        @pl.when(i == 0)
        def _():
            dk_ref[...] = jnp.zeros_like(dk_ref)
            dv_ref[...] = jnp.zeros_like(dv_ref)

        for n in range(members):

            @pl.when(i // per == n)
            def _():
                g = grads[n][...]
                for h in range(heads):
                    g_ref[h] = g[:, h * head_width : (h + 1) * head_width]
                product = jnp.transpose(g.astype(f32)) * ot_ref[...]
                for h in range(heads):
                    part = slice(h * head_width, (h + 1) * head_width)
                    delta_ref[h] = jnp.sum(product[part, :], axis=0, keepdims=True)

        dq_ref[...] = jnp.zeros_like(dq_ref)

        def one(j, _):
            q_first, k_first, needed, full = block_range(meta_ref, i, j, rows, per_member, layout)
            at = pl.multiple_of(j * rows, rows)

            def step(masked):
                if masked:
                    allowed = allowed_pairs(meta_ref, q_first, k_first, rows, layout)
                for h in range(heads):
                    part = slice(h * head_width, (h + 1) * head_width)
                    s = mm(k_ref[h, pl.ds(at, rows), :], q_ref[h], NT)
                    if masked:
                        s = jnp.where(allowed, s, mask_fill)
                    p = jnp.exp(s - lse_ref[pl.ds(h, 1), :])
                    dp = mm(v_ref[h, pl.ds(at, rows), :], g_ref[h], NT)
                    ds = (p * (dp - delta_ref[h])).astype(bf16)
                    dv_ref[h, pl.ds(at, rows), :] += mm(p.astype(bf16), g_ref[h])
                    dk_ref[h, pl.ds(at, rows), :] += mm(ds, q_ref[h])
                    dq_ref[part, :] += mm(kt_ref[part, pl.ds(at, rows)], ds)

            @pl.when(full)
            def _():
                step(False)

            @pl.when(needed & jnp.logical_not(full))
            def _():
                step(True)

            return 0

        lax.fori_loop(0, blocks, one, 0)
        here = pl.multiple_of(i * rows, rows)
        out_ref[pl.ds(here, rows), 0:width] = (jnp.transpose(dq_ref[...]) * scale).astype(bf16)

        @pl.when(i == blocks - 1)
        def _():
            def store(b, _):
                spot = pl.multiple_of(b * rows, rows)
                out_ref[pl.ds(spot, rows), width : 3 * width] = jnp.concatenate(
                    [dk_ref[h, pl.ds(spot, rows), :] for h in range(heads)]
                    + [dv_ref[h, pl.ds(spot, rows), :] for h in range(heads)],
                    axis=1,
                ).astype(bf16)
                return 0

            lax.fori_loop(0, blocks, store, 0)

    grad_specs = [
        pl.BlockSpec((rows, width), lambda i, m, n=n: (jnp.clip(i - n * per, 0, per - 1), 0))
        for n in range(members)
    ]
    out = shape_of((group_rows, 3 * width), bf16)
    return run(
        body,
        (blocks,),
        [
            (q, pl.BlockSpec((heads, rows, head_width), lambda i, m: (0, i, 0))),
            (k, whole(k)),
            (v, whole(v)),
            (kt, whole(kt)),
        ]
        + list(zip(grad, grad_specs))
        + [
            (ot, pl.BlockSpec((width, rows), lambda i, m: (0, i))),
            (lse, pl.BlockSpec((heads, rows), lambda i, m: (0, i))),
        ],
        [(out, whole(out))],
        scratch=[
            pltpu.VMEM((heads, group_rows, head_width), f32),
            pltpu.VMEM((heads, group_rows, head_width), f32),
            pltpu.VMEM((width, rows), f32),
            pltpu.VMEM((heads, rows, head_width), bf16),
            pltpu.VMEM((heads, 1, rows), f32),
        ],
        meta=meta,
        flops=5 * 2 * group_rows * group_rows * width,
        moved=group_rows * width * 24,
        exps=group_rows * group_rows * heads // 2,
    )[0]


def slot_targets(route_ids, expert_count, local_experts, mine):
    rows = route_ids.shape[0]
    groups = expert_count // local_experts
    experts = jnp.arange(expert_count, dtype=jnp.int32)
    hits = route_ids[:, :, None] == experts[None, None, :]
    hit = jnp.any(hits, axis=1)
    order = lax.broadcasted_iota(jnp.int32, (rows, rows), 0)
    other = lax.broadcasted_iota(jnp.int32, (rows, rows), 1)
    ahead = mm((other < order).astype(bf16), hit.astype(bf16)).astype(jnp.int32)
    rank = jnp.sum(jnp.where(hits, ahead[:, None, :], 0), axis=2)
    near = (route_ids // local_experts) ^ mine
    slot = (route_ids % local_experts) * (groups * CAP) + near * CAP + rank
    return jnp.where(route_ids < expert_count, slot, -1)


def slot_choice(first, count, target_ref):
    rows = target_ref.shape[1]
    ids = first + lax.broadcasted_iota(jnp.int32, (count, rows), 0)
    match = (ids == target_ref[0:1, :]) | (ids == target_ref[1:2, :])
    return jnp.where(match, 1.0, 0.0).astype(bf16)


def dispatch(target_rows, source, slots, pieces):
    rows, width = source.shape
    tile = 2 * CAP
    per_piece = slots // pieces

    def body(target_ref, source_ref, *outs):
        for n in range(pieces):
            for t in range(per_piece // tile):
                choice = slot_choice(n * per_piece + t * tile, tile, target_ref)
                outs[n][t * tile : (t + 1) * tile, :] = mm(choice, source_ref[...]).astype(bf16)

    out = shape_of((per_piece, width), bf16)
    return run(
        body,
        (1,),
        [(target_rows, whole(target_rows)), (source, whole(source))],
        [(out, whole(out))] * pieces,
        flops=2 * rows * width * slots,
        moved=(rows + slots) * width * 2,
    )


def token_front(meta, x, o_near, w_out, gain, w_router, previous, w_carry, target_rows, local, groups):
    rows, width = x.shape
    members = len(o_near)
    head_columns = o_near[0].shape[1]
    expert_all = w_router.shape[1]
    tile = 128
    steps = rows // tile
    per_piece = groups * CAP

    def body(meta_ref, x_ref, *refs):
        o_refs = refs[:members]
        w_refs = refs[members : 2 * members]
        gain_ref, router_ref, prev_ref, carry_ref, target_ref = refs[2 * members : 2 * members + 5]
        x1_ref, h2_ref, prob_ref, gates_ref = refs[2 * members + 5 : 2 * members + 9]
        piece_refs = refs[2 * members + 9 : 2 * members + 9 + local]
        low_ref, split_ref = refs[2 * members + 9 + local :]
        i = pl.program_id(0)
        total = x_ref[...].astype(f32)
        for n in range(members):
            total = total + mm(o_refs[n][...], w_refs[n][0])
        x1_ref[...] = total
        inverse = lax.rsqrt(jnp.mean(total * total, axis=1, keepdims=True) + norm_eps)
        h2 = total * inverse * gain_ref[...]
        h2_ref[...] = h2
        logits = mm_full(h2, router_ref[...]) + mm_full(prev_ref[...], carry_ref[...])
        shifted = jnp.exp(logits - jnp.max(logits, axis=1, keepdims=True))
        prob = shifted / jnp.sum(shifted, axis=1, keepdims=True)
        prob_ref[...] = prob
        here = pl.multiple_of(i * tile, tile)
        low_ref[pl.ds(here, tile), :] = h2.astype(bf16)
        top = prob.astype(bf16)
        rest = prob - top.astype(f32)
        middle = rest.astype(bf16)
        last = (rest - middle.astype(f32)).astype(bf16)
        split_ref[0, pl.ds(here, tile), :] = top
        split_ref[1, pl.ds(here, tile), :] = middle
        split_ref[2, pl.ds(here, tile), :] = last

        @pl.when(i == steps - 1)
        def _():
            diagonal = lax.broadcasted_iota(jnp.int32, (CAP, CAP), 0) == lax.broadcasted_iota(
                jnp.int32, (CAP, CAP), 1
            )
            lanes = lax.broadcasted_iota(jnp.int32, (CAP, expert_all), 1)
            for n in range(local):
                for g in range(groups):
                    choice = slot_choice(n * per_piece + g * CAP, CAP, target_ref)
                    piece_refs[n][g * CAP : (g + 1) * CAP, :] = mm(choice, low_ref[...]).astype(
                        bf16
                    )
                    picked = (
                        mm(choice, split_ref[0]) + mm(choice, split_ref[1]) + mm(choice, split_ref[2])
                    )
                    expert = (meta_ref[1] ^ g) * local + n
                    column = jnp.sum(
                        jnp.where(lanes == expert, picked, 0.0), axis=1, keepdims=True
                    )
                    gates_ref[n * groups + g : n * groups + g + 1, :] = jnp.sum(
                        jnp.where(diagonal, column, 0.0), axis=0, keepdims=True
                    )

    row_spec = pl.BlockSpec((tile, width), lambda i, m: (i, 0))
    wide = shape_of((rows, width), f32)
    small = shape_of((rows, expert_all), f32)
    small_spec = pl.BlockSpec((tile, expert_all), lambda i, m: (i, 0))
    gates = shape_of((local * groups, CAP), f32)
    piece = shape_of((per_piece, width), bf16)
    return run(
        body,
        (steps,),
        [(x, row_spec)]
        + [(o, pl.BlockSpec((tile, head_columns), lambda i, m: (i, 0))) for o in o_near]
        + [
            (w_out, pl.BlockSpec((1, head_columns, width), lambda i, m, n=n: (m[0] ^ n, 0, 0)))
            for n in range(members)
        ]
        + [
            (gain, whole(gain)),
            (w_router, whole(w_router)),
            (previous, small_spec),
            (w_carry, whole(w_carry)),
            (target_rows, whole(target_rows)),
        ],
        [(wide, row_spec), (wide, row_spec), (small, small_spec), (gates, whole(gates))]
        + [(piece, whole(piece))] * local,
        scratch=[pltpu.VMEM((rows, width), bf16), pltpu.VMEM((3, rows, expert_all), bf16)],
        meta=meta,
        flops=2 * rows * width * width + 2 * rows * width * per_piece * local,
        moved=rows * width * 14,
    )


def token_zero(x1, h2, grad, prob, routes, logit_w, vectors, expert_count):
    rows, width = x1.shape
    tile = 128
    kinds = vectors.shape[0]
    expert_all = prob.shape[1]

    def body(x1_ref, h2_ref, dy_ref, prob_ref, route_ref, w_ref, vec_ref, *outs):
        base_ref, dh_ref, dgate_ref, gate_ref, sums_ref = outs
        i = pl.program_id(0)
        h2 = h2_ref[...]
        dy = dy_ref[...].astype(f32)
        prob_now = prob_ref[...]
        lanes = lax.broadcasted_iota(jnp.int32, (tile, expert_all), 1)
        ids = [route_ref[:, c : c + 1] for c in range(2)]
        gates = [
            jnp.sum(jnp.where(lanes == r, prob_now, 0.0), axis=1, keepdims=True) for r in ids
        ]
        for c in range(2):
            gate_ref[:, c : c + 1] = gates[c]
        along = jnp.sum(dy * h2, axis=1, keepdims=True)
        copies = [(r == expert_count + 1).astype(f32) for r in ids]
        keep = copies[0] * gates[0] + copies[1] * gates[1]
        dgates = [copies[c] * along for c in range(2)]
        scores = [
            jnp.sum(h2 * w_ref[n : n + 1, :], axis=1, keepdims=True) for n in range(2 * kinds)
        ]
        base = x1_ref[...]
        dh = jnp.zeros_like(h2)
        for j in range(kinds):
            top = jnp.maximum(scores[2 * j], scores[2 * j + 1])
            e0 = jnp.exp(scores[2 * j] - top)
            e1 = jnp.exp(scores[2 * j + 1] - top)
            a0 = e0 / (e0 + e1)
            a1 = e1 / (e0 + e1)
            vec = vec_ref[j : j + 1, :]
            along_vec = jnp.sum(dy * vec, axis=1, keepdims=True)
            here = [(r == expert_count + 2 + j).astype(f32) for r in ids]
            weight = here[0] * gates[0] + here[1] * gates[1]
            for c in range(2):
                dgates[c] = dgates[c] + here[c] * (a0 * along + a1 * along_vec)
            keep = keep + weight * a0
            base = base + (weight * a1) * vec
            d0 = weight * along
            d1 = weight * along_vec
            mean = a0 * d0 + a1 * d1
            z0 = a0 * (d0 - mean)
            z1 = a1 * (d1 - mean)
            dh = dh + z0 * w_ref[2 * j : 2 * j + 1, :] + z1 * w_ref[2 * j + 1 : 2 * j + 2, :]
            found = [
                jnp.sum((weight * a1) * dy, axis=0, keepdims=True),
                jnp.sum(z0 * h2, axis=0, keepdims=True),
                jnp.sum(z1 * h2, axis=0, keepdims=True),
            ]
            places = [j, kinds + 2 * j, kinds + 2 * j + 1]
            for place, row in zip(places, found):

                @pl.when(i == 0)
                def _():
                    sums_ref[place : place + 1, :] = row

                @pl.when(i > 0)
                def _():
                    sums_ref[place : place + 1, :] += row

        base_ref[...] = base + keep * h2
        dh_ref[...] = dh + keep * dy
        for c in range(2):
            dgate_ref[:, c : c + 1] = dgates[c]

    row_spec = pl.BlockSpec((tile, width), lambda i: (i, 0))
    pair_spec = pl.BlockSpec((tile, 2), lambda i: (i, 0))
    wide = shape_of((rows, width), f32)
    pair = shape_of((rows, 2), f32)
    sums = shape_of((3 * kinds, width), f32)
    return run(
        body,
        (rows // tile,),
        [
            (x1, row_spec),
            (h2, row_spec),
            (grad, row_spec),
            (prob, pl.BlockSpec((tile, expert_all), lambda i: (i, 0))),
            (routes, pair_spec),
            (logit_w, whole(logit_w)),
            (vectors, whole(vectors)),
        ],
        [(wide, row_spec), (wide, row_spec), (pair, pair_spec), (pair, pair_spec), (sums, whole(sums))],
        flops=rows * width * 40,
        moved=rows * width * 18,
    )


def expert_layer(which, meta, arrived, grads, gates, w_gate, w_up, w_down, parts):
    groups = len(arrived)
    rows = groups * CAP
    width = w_gate.shape[1]
    hidden = w_gate.shape[2]
    half = width // 2
    tile = 256
    steps = hidden // tile
    per_part = hidden // parts
    tile_part = max(1, per_part // tile)
    chunk = 128

    def body(meta_ref, *refs):
        x_refs = refs[:groups]
        dy_refs = refs[groups : 2 * groups]
        gates_ref, wg_ref, wu_ref, wd_ref = refs[2 * groups : 2 * groups + 4]
        y_ref, dx_ref, dg_ref = refs[2 * groups + 4 : 2 * groups + 7]
        gs_ref, gk_ref, us_ref, uk_ref, ds_ref, dk_ref = refs[2 * groups + 7 : 2 * groups + 13]
        x_all, xt_all, dy_all, gate_all, y_acc, dx_acc, dot_acc, hid_t, dgt, dut, scaled_t = refs[
            2 * groups + 13 :
        ]
        f = pl.program_id(0)
        core = meta_ref[2]
        diagonal = lax.broadcasted_iota(jnp.int32, (CAP, CAP), 0) == lax.broadcasted_iota(
            jnp.int32, (CAP, CAP), 1
        )

        @pl.when(f == 0)
        def _():
            for g in range(groups):
                span = slice(g * CAP, (g + 1) * CAP)
                x_all[span, :] = x_refs[g][...]
                xt_all[:, span] = jnp.transpose(x_refs[g][...])
                dy_all[span, :] = dy_refs[g][...]
                gate_all[span, :] = jnp.sum(
                    jnp.where(diagonal, gates_ref[g : g + 1, :], 0.0), axis=1, keepdims=True
                )
            y_acc[...] = jnp.zeros_like(y_acc)
            dx_acc[...] = jnp.zeros_like(dx_acc)
            dot_acc[...] = jnp.zeros_like(dot_acc)

        for r in range(rows // chunk):
            span = slice(r * chunk, (r + 1) * chunk)
            g_pre = mm(x_all[span, :], wg_ref[0])
            u_pre = mm(x_all[span, :], wu_ref[0])
            back = mm(dy_all[span, :], wd_ref[0], NT)
            gate = gate_all[span, :]
            sig = 1.0 / (1.0 + jnp.exp(-g_pre))
            act = g_pre * sig
            hid = act * u_pre
            hid_t[span, :] = hid.astype(bf16)
            scaled_t[span, :] = (gate * hid).astype(bf16)
            dot_acc[span, :] += hid * back
            dhid = gate * back
            dgt[span, :] = (dhid * u_pre * sig * (1.0 + g_pre * (1.0 - sig))).astype(bf16)
            dut[span, :] = (dhid * act).astype(bf16)
        y_acc[...] += mm(hid_t[...], wd_ref[0])
        dx_acc[...] += mm(dgt[...], wg_ref[0], NT) + mm(dut[...], wu_ref[0], NT)
        mine = pl.multiple_of(core * half, half)
        theirs = pl.multiple_of((1 - core) * half, half)
        gs_ref[0] = mm(xt_all[pl.ds(theirs, half), :], dgt[...]).astype(bf16)
        gk_ref[0] = mm(xt_all[pl.ds(mine, half), :], dgt[...]).astype(bf16)
        us_ref[0] = mm(xt_all[pl.ds(theirs, half), :], dut[...]).astype(bf16)
        uk_ref[0] = mm(xt_all[pl.ds(mine, half), :], dut[...]).astype(bf16)
        ds_ref[0] = mm(scaled_t[...], dy_all[:, pl.ds(theirs, half)], TN).astype(bf16)
        dk_ref[0] = mm(scaled_t[...], dy_all[:, pl.ds(mine, half)], TN).astype(bf16)

        @pl.when(f == steps - 1)
        def _():
            y_ref[...] = (gate_all[...] * y_acc[...]).astype(bf16)
            dx_ref[...] = dx_acc[...].astype(bf16)
            for g in range(groups):
                span = slice(g * CAP, (g + 1) * CAP)
                column = jnp.sum(dot_acc[span, :], axis=1, keepdims=True)
                dg_ref[g : g + 1, :] = jnp.sum(
                    jnp.where(diagonal, column, 0.0), axis=0, keepdims=True
                )

    first = pl.BlockSpec((CAP, width), lambda f, m: (0, 0))
    up_shape = shape_of((parts, half, per_part), bf16)
    up_spec = pl.BlockSpec((1, half, tile), lambda f, m: (f // tile_part, 0, f % tile_part))
    down_shape = shape_of((parts, per_part, half), bf16)
    down_spec = pl.BlockSpec((1, tile, half), lambda f, m: (f // tile_part, f % tile_part, 0))
    wide = shape_of((rows, width), bf16)
    dots = shape_of((groups, CAP), f32)
    return run(
        body,
        (steps,),
        [(a, first) for a in arrived]
        + [(g, first) for g in grads]
        + [
            (gates, whole(gates)),
            (w_gate, pl.BlockSpec((1, width, tile), lambda f, m: (which, 0, f))),
            (w_up, pl.BlockSpec((1, width, tile), lambda f, m: (which, 0, f))),
            (w_down, pl.BlockSpec((1, tile, width), lambda f, m: (which, f, 0))),
        ],
        [(wide, whole(wide)), (wide, whole(wide)), (dots, whole(dots))]
        + [(up_shape, up_spec)] * 4
        + [(down_shape, down_spec)] * 2,
        scratch=[
            pltpu.VMEM((rows, width), bf16),
            pltpu.VMEM((width, rows), bf16),
            pltpu.VMEM((rows, width), bf16),
            pltpu.VMEM((rows, 1), f32),
            pltpu.VMEM((rows, width), f32),
            pltpu.VMEM((rows, width), f32),
            pltpu.VMEM((rows, tile), f32),
            pltpu.VMEM((rows, tile), bf16),
            pltpu.VMEM((rows, tile), bf16),
            pltpu.VMEM((rows, tile), bf16),
            pltpu.VMEM((rows, tile), bf16),
        ],
        meta=meta,
        flops=9 * 2 * rows * width * hidden,
        moved=12 * width * hidden + rows * width * 8,
        exps=rows * hidden,
    )


def slot_sum(target_ref, pieces, first_row, tile):
    total = None
    t0 = target_ref[:, 0:1]
    t1 = target_ref[:, 1:2]
    for first, ref in pieces:
        ids = first + lax.broadcasted_iota(jnp.int32, (tile, CAP), 1)
        choice = jnp.where((ids == t0) | (ids == t1), 1.0, 0.0).astype(bf16)
        part = mm(choice, ref[...])
        total = part if total is None else total + part
    return total


def token_output(base, targets, pieces):
    rows, width = base.shape
    tile = 128
    count = len(pieces)

    def body(base_ref, target_ref, *refs):
        listed = [(n * CAP, refs[n]) for n in range(count)]
        total = base_ref[...] + slot_sum(target_ref, listed, 0, tile)
        refs[count][...] = total.astype(bf16)

    row_spec = pl.BlockSpec((tile, width), lambda i: (i, 0))
    first = pl.BlockSpec((CAP, width), lambda i: (0, 0))
    return run(
        body,
        (rows // tile,),
        [(base, row_spec), (targets, pl.BlockSpec((tile, 2), lambda i: (i, 0)))]
        + [(p, first) for p in pieces],
        [(shape_of((rows, width), bf16), row_spec)],
        flops=2 * rows * width * count * CAP,
        moved=rows * width * 10,
    )[0]


def token_back(
    meta, x1, h2, grad, prob, previous, routes, targets, pieces, dots, dgate_zero, dh_zero, gain, router_t, w_out
):
    rows, width = x1.shape
    tile = 128
    count = len(pieces)
    expert_all = prob.shape[1]
    members, head_columns = w_out.shape[0], w_out.shape[1]

    def body(meta_ref, *refs):
        (x1_ref, h2_ref, dy_ref, prob_ref, prev_ref, route_ref, target_ref) = refs[:7]
        piece_refs = refs[7 : 7 + count]
        dots_ref, dz_ref, dh_ref, gain_ref, router_ref = refs[7 + count : 12 + count]
        w_refs = refs[12 + count : 12 + count + members]
        dx1_ref, low_ref = refs[12 + count + members : 14 + count + members]
        out_refs = refs[14 + count + members : 14 + count + 2 * members]
        sums_ref, carry_ref = refs[14 + count + 2 * members :]
        i = pl.program_id(0)
        prob_now = prob_ref[...]
        lanes = lax.broadcasted_iota(jnp.int32, (tile, expert_all), 1)
        dprob = jnp.zeros_like(prob_now)
        for c in range(2):
            target = target_ref[:, c : c + 1]
            dgate = dz_ref[:, c : c + 1]
            for n in range(count):
                ids = n * CAP + lax.broadcasted_iota(jnp.int32, (tile, CAP), 1)
                dgate = dgate + jnp.sum(
                    jnp.where(ids == target, dots_ref[n : n + 1, :], 0.0), axis=1, keepdims=True
                )
            dprob = dprob + jnp.where(lanes == route_ref[:, c : c + 1], dgate, 0.0)
        dlogit = prob_now * (dprob - jnp.sum(prob_now * dprob, axis=1, keepdims=True))
        h2 = h2_ref[...]
        dh2 = (
            slot_sum(target_ref, [(n * CAP, piece_refs[n]) for n in range(count)], 0, tile)
            + dh_ref[...]
            + mm_full(dlogit, router_ref[...])
        )
        x1 = x1_ref[...]
        inverse = lax.rsqrt(jnp.mean(x1 * x1, axis=1, keepdims=True) + norm_eps)
        normed = x1 * inverse
        router_part = mm_full(dlogit, h2, TN)
        carry_part = mm_full(dlogit, prev_ref[...], TN)
        gain_part = jnp.sum(dh2 * normed, axis=0, keepdims=True)

        @pl.when(i == 0)
        def _():
            sums_ref[0:expert_all, :] = router_part
            sums_ref[expert_all : expert_all + 1, :] = gain_part
            carry_ref[...] = carry_part

        @pl.when(i > 0)
        def _():
            sums_ref[0:expert_all, :] += router_part
            sums_ref[expert_all : expert_all + 1, :] += gain_part
            carry_ref[...] += carry_part

        dn = dh2 * gain_ref[...]
        dx1 = dy_ref[...].astype(f32) + inverse * (
            dn - normed * jnp.mean(dn * normed, axis=1, keepdims=True)
        )
        dx1_ref[...] = dx1
        low = dx1.astype(bf16)
        low_ref[...] = low
        for n in range(members):
            out_refs[n][...] = mm(low, w_refs[n][0], NT).astype(bf16)

    row_spec = pl.BlockSpec((tile, width), lambda i, m: (i, 0))
    pair_spec = pl.BlockSpec((tile, 2), lambda i, m: (i, 0))
    small_spec = pl.BlockSpec((tile, expert_all), lambda i, m: (i, 0))
    first = pl.BlockSpec((CAP, width), lambda i, m: (0, 0))
    sums = shape_of((expert_all + 1, width), f32)
    carry = shape_of((expert_all, expert_all), f32)
    return run(
        body,
        (rows // tile,),
        [
            (x1, row_spec),
            (h2, row_spec),
            (grad, row_spec),
            (prob, small_spec),
            (previous, small_spec),
            (routes, pair_spec),
            (targets, pair_spec),
        ]
        + [(p, first) for p in pieces]
        + [
            (dots, whole(dots)),
            (dgate_zero, pair_spec),
            (dh_zero, row_spec),
            (gain, whole(gain)),
            (router_t, whole(router_t)),
        ]
        + [
            (w_out, pl.BlockSpec((1, head_columns, width), lambda i, m, n=n: (m[0] ^ n, 0, 0)))
            for n in range(members)
        ],
        [
            (shape_of((rows, width), f32), row_spec),
            (shape_of((rows, width), bf16), row_spec),
        ]
        + [
            (
                shape_of((rows, head_columns), bf16),
                pl.BlockSpec((tile, head_columns), lambda i, m: (i, 0)),
            )
        ]
        * members
        + [(sums, whole(sums)), (carry, whole(carry))],
        meta=meta,
        flops=2 * rows * width * (count * CAP + width),
        moved=rows * width * 24,
    )


def input_back(meta, x, gain, dqkv, weights_t, dx1):
    rows, width = x.shape
    tile = 128
    members = len(dqkv)
    per_group = weights_t.shape[2]

    def body(meta_ref, x_ref, gain_ref, dx1_ref, *refs):
        d_refs = refs[:members]
        w_refs = refs[members : 2 * members]
        out_ref, sum_ref = refs[2 * members :]
        i = pl.program_id(0)
        dh = None
        for n in range(members):
            for w in range(3):
                part = mm(
                    d_refs[n][:, w * per_group : (w + 1) * per_group], w_refs[n][w, 0]
                )
                dh = part if dh is None else dh + part
        x = x_ref[...].astype(f32)
        inverse = lax.rsqrt(jnp.mean(x * x, axis=1, keepdims=True) + norm_eps)
        normed = x * inverse
        gain_part = jnp.sum(dh * normed, axis=0, keepdims=True)

        @pl.when(i == 0)
        def _():
            sum_ref[...] = gain_part

        @pl.when(i > 0)
        def _():
            sum_ref[...] += gain_part

        dn = dh * gain_ref[...]
        out_ref[...] = dx1_ref[...] + inverse * (
            dn - normed * jnp.mean(dn * normed, axis=1, keepdims=True)
        )

    row_spec = pl.BlockSpec((tile, width), lambda i, m: (i, 0))
    sums = shape_of((1, width), f32)
    return run(
        body,
        (rows // tile,),
        [(x, row_spec), (gain, whole(gain)), (dx1, row_spec)]
        + [(d, pl.BlockSpec((tile, 3 * per_group), lambda i, m: (i, 0))) for d in dqkv]
        + [
            (weights_t, pl.BlockSpec((3, 1, per_group, width), lambda i, m, n=n: (0, m[0] ^ n, 0, 0)))
            for n in range(members)
        ],
        [(shape_of((rows, width), f32), row_spec), (sums, whole(sums))],
        meta=meta,
        flops=2 * rows * width * width * 3,
        moved=rows * width * 20 + weights_t.size * 2,
    )


def sum_over_dp(parts):
    count = lax.axis_size("dp")
    mine = lax.axis_index("dp")
    if count == 2:
        out = add_low(*[pick(p, 1 - mine) for p in parts])
        return add_low(*[pick(p, mine) for p in parts], swap(out, "dp", 1))
    return lax.psum_scatter(add_low(*parts), "dp", scatter_dimension=0, tiled=False)


def gather_dp(value):
    count = lax.axis_size("dp")
    mine = lax.axis_index("dp")
    if count == 2:
        other = swap(value, "dp", 1)
        return jnp.concatenate(
            [jnp.where(mine == 0, value, other), jnp.where(mine == 0, other, value)], axis=0
        )
    return lax.all_gather(value, "dp", axis=0, tiled=True)


def sum_over_exp(value):
    bit = 1
    while bit < lax.axis_size("exp"):
        value = add_low(value, swap(value, "exp", bit))
        bit *= 2
    return value


def expert_share(send, keep):
    mine = sum_over_dp([keep, swap(send, "ctx", 1)])
    across = lax.axis_index("ctx") // 2
    halves = mine.reshape((2, mine.shape[0] // 2) + mine.shape[1:])
    total = add_low(pick(halves, across), swap(pick(halves, 1 - across), "ctx", 2))
    return gather_near(total, "ctx")


def place(meta, pieces, out_shape, place_of):
    block = pieces[0][0].shape
    flat = [p for listed in pieces for p in listed]
    members = len(pieces[0])

    def body(meta_ref, *refs):
        spot = pl.program_id(0) * members + pl.program_id(1)
        for n in range(len(flat)):

            @pl.when(spot == n)
            def _():
                refs[-1][0] = refs[n][...].astype(f32)

    return run(
        body,
        (len(pieces), members),
        [(p, whole(p)) for p in flat],
        [
            (
                shape_of(out_shape, f32),
                pl.BlockSpec((1,) + block, lambda e, j, m: (e,) + place_of(m[0] ^ j)),
            )
        ],
        meta=meta,
        moved=sum(p.size for p in flat) * 6,
    )[0]


def place_columns(meta, pieces, per_group):
    members = len(pieces)
    width = pieces[0].shape[1]

    def body(meta_ref, *refs):
        out_ref, hold = refs[members:]
        for n in range(members):
            at = pl.multiple_of((meta_ref[0] ^ n) * per_group, per_group)
            hold[pl.ds(at, per_group), :] = refs[n][...].astype(f32)
        out_ref[0] = jnp.transpose(hold[...])

    out = shape_of((3, width, width), f32)
    return run(
        body,
        (3,),
        [(p, pl.BlockSpec((per_group, width), lambda w, m: (w, 0))) for p in pieces],
        [(out, pl.BlockSpec((1, width, width), lambda w, m: (w, 0, 0)))],
        scratch=[pltpu.VMEM((width, width), f32)],
        meta=meta,
        moved=3 * width * width * 6,
    )[0]


def shards(
    inputs,
    lengths,
    block_order,
    routes,
    prev_logits,
    norm1_gain,
    norm2_gain,
    w_qkv,
    w_out,
    w_router,
    w_carry,
    const_logit_w,
    const_vec,
    w_gate,
    w_up,
    w_down,
    cotangent,
):
    members = lax.axis_size("ctx")
    groups = lax.axis_size("exp")
    parts = lax.axis_size("dp")
    me = lax.axis_index("ctx")
    mine = lax.axis_index("exp")
    x, grad = inputs[0], cotangent[0]
    rows, width = x.shape
    group_rows = rows * members
    deal_block = group_rows // block_order.shape[1]
    per_member = rows // deal_block
    local = w_gate.shape[0]
    expert_count = local * groups
    slots = expert_count * CAP
    head_width = width // HEADS
    heads = HEADS // members
    per_group = heads * head_width
    blocks = block_order.shape[1]
    layout = {"order": 4, "lengths": 4 + blocks, "sequences": lengths.shape[1]}
    meta = jnp.concatenate(
        [
            jnp.stack([me, mine, me % 2, me // 2]).astype(jnp.int32),
            block_order[0],
            lengths[0],
        ]
    )
    gain1 = norm1_gain.reshape(1, width)
    gain2 = norm2_gain.reshape(1, width)
    weights_t = jnp.swapaxes(w_qkv, 1, 2).reshape(3, members, per_group, width)
    w_out_parts = w_out.reshape(members, per_group, width)
    route_ids = routes[0]
    previous = prev_logits[0]

    near = gather_near(x, "ctx")
    held = None
    for j in range(members):
        held = project(j, near[j], gain1, weights_t, meta, held, group_rows)
    q, k, v, kt, vt, h1 = held
    o, ot, lse, tops = attend(meta, q, k, vt, deal_block, per_member, layout)
    o_near = [
        swap(o[j * rows : (j + 1) * rows], "ctx", j) if j else o[:rows] for j in range(members)
    ]

    targets = slot_targets(route_ids, expert_count, local, mine)
    target_rows = jnp.transpose(targets)
    grad_slots = dispatch(target_rows, grad, slots, local)
    grad_near = [
        [
            swap(grad_slots[e][g * CAP : (g + 1) * CAP], "exp", g) if g else grad_slots[e]
            for g in range(groups)
        ]
        for e in range(local)
    ]

    front = token_front(
        meta, x, o_near, w_out_parts, gain2, w_router, previous, w_carry, target_rows, local, groups
    )
    x1, h2, prob, gate_slots = front[:4]
    token_slots = front[4:]
    gate_view = gate_slots.reshape(local, groups, CAP)
    gate_near = [gate_view[:, g] if g == 0 else swap(gate_view[:, g], "exp", g) for g in range(groups)]
    token_near = [
        [
            swap(token_slots[e][g * CAP : (g + 1) * CAP], "exp", g) if g else token_slots[e]
            for g in range(groups)
        ]
        for e in range(local)
    ]
    logit_rows = jnp.swapaxes(const_logit_w, 1, 2).reshape(-1, width)
    base, dh_zero, dgate_zero, gates, zero_sums = token_zero(
        x1, h2, grad, prob, route_ids, logit_rows, const_vec, expert_count
    )

    out_rows, in_rows, dot_rows = [], [], []
    gate_pieces, up_pieces, down_pieces = [], [], []
    for e in range(local):
        gate_rows = jnp.stack([gate_near[g][e] for g in range(groups)])
        y, dx, dots, gs, gk, us, uk, ds, dk = expert_layer(
            e, meta, token_near[e], grad_near[e], gate_rows, w_gate, w_up, w_down, parts
        )
        in_rows += [swap(dx[g * CAP : (g + 1) * CAP], "exp", g) if g else dx for g in range(groups)]
        dot_rows += [swap(dots[g : g + 1], "exp", g) if g else dots[:1] for g in range(groups)]
        out_rows += [swap(y[g * CAP : (g + 1) * CAP], "exp", g) if g else y for g in range(groups)]
        gate_pieces.append(expert_share(gs, gk))
        up_pieces.append(expert_share(us, uk))
        down_pieces.append(expert_share(ds, dk))

    back = token_back(
        meta,
        x1,
        h2,
        grad,
        prob,
        previous,
        route_ids,
        targets,
        in_rows,
        jnp.concatenate(dot_rows, axis=0),
        dgate_zero,
        dh_zero,
        gain2,
        jnp.transpose(w_router),
        w_out_parts,
    )
    dx1, da = back[:2]
    do_near = [back[2 + j] if j == 0 else swap(back[2 + j], "ctx", j) for j in range(members)]
    token_sums, carry_sum = back[2 + members :]
    result = token_output(base, targets, out_rows)

    out_parts = [
        mm(o_near[j], da, TN).astype(bf16) for j in range(members)
    ]
    bit = 1
    while bit < members:
        kept = [j for j in range(members) if j % (2 * bit) == 0]
        out_parts = {
            j: add_low(out_parts[j], swap(out_parts[j + bit], "ctx", bit)) for j in kept
        }
        bit *= 2
    out_sum = out_parts[0]

    dqkv = attend_back(meta, q, k, v, kt, do_near, ot, lse, deal_block, per_member, layout)
    dqkv_near = [
        swap(dqkv[j * rows : (j + 1) * rows], "ctx", j) if j else dqkv[:rows]
        for j in range(members)
    ]
    qkv_sum = mm(dqkv, h1, TN).astype(bf16)
    input_grad, norm1_sum = input_back(meta, x, gain1, dqkv_near, weights_t, dx1)

    def dense_total(value):
        share = sum_over_dp([value.reshape((parts, value.shape[0] // parts, width))])
        return gather_near(gather_dp(sum_over_exp(share)), "ctx")

    out_grad = place(
        meta, [dense_total(out_sum)], (1, width, width), lambda a: (a, 0)
    )[0]
    qkv_grad = place_columns(meta, dense_total(qkv_sum), per_group)

    expert_all = w_router.shape[1]
    small = jnp.concatenate(
        [token_sums, zero_sums, jnp.pad(carry_sum, ((0, 0), (0, width - expert_all)))], axis=0
    )
    small = butterfly(small, jnp.add)
    norm1_grad = butterfly(norm1_sum, jnp.add)
    kinds = const_vec.shape[0]
    router_grad = jnp.transpose(small[:expert_all])
    norm2_grad = small[expert_all]
    at = expert_all + 1
    vec_grad = small[at : at + kinds]
    logit_grad = jnp.swapaxes(small[at + kinds : at + 3 * kinds].reshape(kinds, 2, width), 1, 2)
    carry_grad = jnp.transpose(small[at + 3 * kinds :, :expert_all])

    local_tops = jnp.max(tops, axis=1)
    top_all = jnp.zeros((members, heads), f32).at[me].set(local_tops)
    top_all = jnp.where(jnp.arange(members)[:, None] == me, top_all, low_start)
    head_max = butterfly(top_all, jnp.maximum).reshape(HEADS)
    clip_ratio = jnp.sqrt(jnp.minimum(1.0, clip_limit / head_max))
    head_scale = jnp.repeat(clip_ratio, head_width)
    clipped = w_qkv[:2].astype(f32) * head_scale[None, None, :]

    half = width // 2
    hidden_part = w_gate.shape[2] // parts
    up_shape = (local, width, hidden_part)
    down_shape = (local, hidden_part, width)
    gate_grad = place(meta, gate_pieces, up_shape, lambda a: ((a % 2) * 2 + a // 2, 0))
    up_grad = place(meta, up_pieces, up_shape, lambda a: ((a % 2) * 2 + a // 2, 0))
    down_grad = place(meta, down_pieces, down_shape, lambda a: (a // 2, a % 2))
    return (
        result[None],
        input_grad[None],
        norm1_grad[0],
        norm2_grad,
        qkv_grad,
        out_grad,
        router_grad,
        carry_grad,
        logit_grad,
        vec_grad,
        gate_grad,
        up_grad,
        down_grad,
        clipped,
    )


def solution(mesh):
    tokens = P(("dp", "exp"), "ctx", None)
    packs = P(("dp", "exp"), None)
    experts = P("exp", None, None)
    in_specs = (
        tokens, packs, packs, tokens, tokens, P(), P(), P(), P(), P(), P(), P(), P(),
        experts, experts, experts, tokens,
    )
    out_specs = (
        tokens, tokens, P(), P(), P(), P(), P(), P(), P(), P(),
        P("exp", None, "dp"), P("exp", None, "dp"), P("exp", "dp", None), P(),
    )
    return jax.shard_map(shards, mesh=mesh, in_specs=in_specs, out_specs=out_specs, check_vma=False)
```

time: 1080 us -> 722 us (0.67)
  matrix products: 322 us -> 10.2 us
  Pallas kernels: 0 us -> 212 us
  local copies, waits for them, and re-layouts: 158 us -> 42.5 us
  starting transfers between devices: 17.6 us -> 112 us
  blocking collectives: 83.9 us -> 0 us
  waiting for transfers between devices: 393 us -> 314 us
  other arithmetic: 86.4 us -> 21.4 us
  between operations: 15.1 us -> 2.23 us
    ppermute x0 -> x113, waiting for transfers between devices: none -> 314 us  [swap(): return lax.ppermute(value, axis, [(i, i ^ distance) for i in range(count)])]
    dot_general x59 -> x6, matrix products: 322 us -> 10.2 us  [mm(): return lax.dot_general(left, right, dims, preferred_element_type=f32)]
    psum x2 -> x0, waiting for transfers between devices: 256 us -> none  [the longest x1 187 us: shards(): lax.psum((qkv_grad, out_grad, norm1_grad, norm2_grad, router_grad, carry_...]
    pallas_call x0 -> x19, Pallas kernels: none -> 212 us  [run(): pl.pallas_call(body, out_shape=[o for o, _ in outputs], grid_spec=pltpu.P...]
    ppermute x0 -> x113, starting transfers between devices: none -> 112 us  [swap(): return lax.ppermute(value, axis, [(i, i ^ distance) for i in range(count)])]
    reduce_scatter x5 -> x0, waiting for transfers between devices: 62.3 us -> none  [the longest x1 37.6 us: shards(): lax.psum_scatter(grad_key_all.astype(jnp.bfloat16), 'ctx', scatter_dimens...]
    all_to_all x4 -> x0, waiting for transfers between devices: 43.6 us -> none  [the longest x1 17.5 us: shards(): lax.all_to_all(grad_slots, 'exp', split_axis=0, concat_axis=1, tiled=True)]
    psum x1 -> x0, blocking collectives: 43.3 us -> none  [shards(): lax.psum((qkv_grad, out_grad, norm1_grad, norm2_grad, router_grad, carry_...]
  transfers between devices with their start and end apart: 13 -> 113, of which waited for: 9 -> 42; matrix products, arithmetic and copies ran while one was open for 36% -> 10% of each run, Pallas kernels for 0% -> 29%
where the time goes in v1:
time: 722 us; the launch traced here: 715 us
  waiting for transfers between devices  314 us (43%)
  Pallas kernels  212 us (29%)
  starting transfers between devices  112 us (16%)
  local copies, waits for them, and re-layouts  42.5 us (6%)
  other arithmetic  21.4 us (3%)
  matrix products  10.2 us (1%)
    ppermute x113, waiting for transfers between devices, swap(): return lax.ppermute(value, axis, [(i, i ^ distance) for i in range(count)])  314 us
    pallas_call x19, Pallas kernels, run(): pl.pallas_call(body, out_shape=[o for o, _ in outputs], grid_spec=pltpu.P...  212 us
    ppermute x113, starting transfers between devices, swap(): return lax.ppermute(value, axis, [(i, i ^ distance) for i in range(count)])  112 us
  transfers between devices with their start and end apart: 113, of which 42 were waited for; matrix products, arithmetic and copies ran while one was open for 10% of the time, Pallas kernels for 29%

profile of v1, /device:TPU:0, one launch (start us, length us, event | category | flops | bytes accessed | tf_op | source)
XLA Modules:
  0.0 714.8 jit_solution(17485037908737993667)
XLA Ops:
  9.5 12.0 %collective-permute-done.x_ref = bf16[512,768]{1,0:T(8,128)(2,1)} collective-permute-done((bf16[512,768]{1,0:T(8,128)(2,1)}, bf16[512,768]{1,0:T(8,128)(2,1)}, u32[]{:S(2)}, u32[]{:S(2)}) %collective-permute-start) | collective-permute-done | bytes 786464 | tf_op jit(solution)/shard_map/ppermute | solution.py:69
  34.1 4.7 shard_map.272
  39.6 4.6 shard_map.273
  44.2 4.6 shard_map.274
  48.9 4.6 shard_map.275
  53.5 29.9 %shard_map.276 = (bf16[2048,192]{1,0:T(8,128)(2,1)}, f32[192,2048]{1,0:T(8,128)}, f32[3,2048]{1,0:T(4,128)}, f32[3,2048]{1,0:T(4,128)}) custom-call(s32[14]{0:T(128)} %concatenate.19.meta_ref, bf16[3,2048,64]{2,1,0:T(8,128)(2,1)} %get-tuple-element.112.q_ref, bf16[3,2048,64]{2,1,0:T(8,128)(2,1)} %get-tuple-element.113.k_ref, ...), custom_call_target="tpu_custom_call" | custom-call | flops 3221225472 | bytes 5505024 | tf_op jit(solution)/shard_map/pallas_call | solution.py:49
  91.1 8.8 %collective-permute-done.109 = f32[4,3]{1,0:T(4,128)S(1)} collective-permute-done((f32[4,3]{1,0:T(4,128)S(1)}, f32[4,3]{1,0:T(4,128)S(1)}, u32[]{:S(2)}, u32[]{:S(2)}) %collective-permute-start.109) | collective-permute-done | bytes 80 | tf_op jit(solution)/shard_map/ppermute | solution.py:69
  103.1 10.7 %shard_map.277 = (f32[512,768]{1,0:T(8,128)}, f32[512,768]{1,0:T(8,128)}, f32[512,12]{1,0:T(8,128)}, f32[8,128]{1,0:T(8,128)}, bf16[512,768]{1,0:T(8,128)(2,1)}, /*index=5*/bf16[512,768]{1,0:T(8,128)(2,1)}) custom-call(s32[14]{0:T(128)} %concatenate.19.meta_ref, bf16[512,768]{1,0:T(8,128)(2,1)} %bitcast.161, bf16[512,192]{1,0:T(8,128)(2,1)} %get-tuple-element.239.refs_0_, ...), custom_call_target="tpu_custom_call" | custom-call | flops 1409286144 | bytes 5505024 | tf_op jit(solution)/shard_map/pallas_call | solution.py:49
  121.4 4.3 collective-permute-done.13
  137.3 10.7 %collective-permute-done.7.refs_2_ = bf16[128,768]{1,0:T(8,128)(2,1)S(1)} collective-permute-done((bf16[128,768]{1,0:T(8,128)(2,1)S(1)}, bf16[128,768]{1,0:T(8,128)(2,1)S(1)}, u32[]{:S(2)}, u32[]{:S(2)}) %collective-permute-start.7) | collective-permute-done | bytes 196640 | tf_op jit(solution)/shard_map/ppermute | solution.py:69
  148.0 8.0 %collective-permute-start.19 = (bf16[128,768]{1,0:T(8,128)(2,1)S(1)}, bf16[128,768]{1,0:T(8,128)(2,1)S(1)}, u32[]{:S(2)}, u32[]{:S(2)}) collective-permute-start(bf16[128,768]{1,0:T(8,128)(2,1)S(1)} %get-tuple-element.255), channel_id=1, source_target_pairs={{0,2},{1,3},{2,0},{3,1},{4,6},{5,7},{6,4},{7,5},{8,10},{9,11},{10,... | collective-permute-start | bytes 589832 | tf_op jit(solution)/shard_map/ppermute | solution.py:69
  156.0 24.9 %shard_map.280 = (bf16[512,768]{1,0:T(8,128)(2,1)}, bf16[512,768]{1,0:T(8,128)(2,1)}, f32[4,128]{1,0:T(4,128)}, bf16[2,384,1024]{2,1,0:T(8,128)(2,1)}, bf16[2,38...) custom-call(s32[14]{0:T(128)} %concatenate.19.meta_ref, ...), custom_call_target="tpu_custom_call" | custom-call | flops 14495514624 | bytes 22020096 | tf_op jit(solution)/shard_map/pallas_call | solution.py:49
  192.8 24.9 %shard_map.281 = (bf16[512,768]{1,0:T(8,128)(2,1)}, bf16[512,768]{1,0:T(8,128)(2,1)}, f32[4,128]{1,0:T(4,128)}, bf16[2,384,1024]{2,1,0:T(8,128)(2,1)}, bf16[2,38...) custom-call(s32[14]{0:T(128)} %concatenate.19.meta_ref, ...), custom_call_target="tpu_custom_call" | custom-call | flops 14495514624 | bytes 22020096 | tf_op jit(solution)/shard_map/pallas_call | solution.py:49
  230.9 7.9 %shard_map.278 = (f32[512,768]{1,0:T(8,128)}, f32[512,768]{1,0:T(8,128)}, f32[512,2]{1,0:T(8,128)}, f32[512,2]{1,0:T(8,128)}, f32[6,768]{1,0:T(8,128)}) custom-call(f32[512,768]{1,0:T(8,128)} %get-tuple-element.116.x1_ref.refs_0_, f32[512,768]{1,0:T(8,128)} %get-tuple-element.117.h2_ref.refs_1_, bf16[512,768]{1,0:T(8,128)(2,1)} %bitcast.165, ...), custom_call_target="tpu_custom_call" | custom-call | flops 15728640 | bytes 7077888 | tf_op jit(solution)/shard_map/pallas_call | solution.py:49
  239.4 5.1 collective-permute-done.28.refs_9_
  244.5 8.2 %collective-permute-done.31.refs_13_ = bf16[128,768]{1,0:T(8,128)(2,1)S(1)} collective-permute-done((bf16[128,768]{1,0:T(8,128)(2,1)S(1)}, bf16[128,768]{1,0:T(8,128)(2,1)S(1)}, u32[]{:S(2)}, u32[]{:S(2)}) %collective-permute-start.31) | collective-permute-done | bytes 196640 | tf_op jit(solution)/shard_map/ppermute | solution.py:69
  253.5 12.2 %shard_map.283 = (f32[512,768]{1,0:T(8,128)}, bf16[512,768]{1,0:T(8,128)(2,1)}, bf16[512,192]{1,0:T(8,128)(2,1)}, bf16[512,192]{1,0:T(8,128)(2,1)}, bf16[512,192...) custom-call(s32[14]{0:T(128)} %concatenate.19.meta_ref, ...), custom_call_target="tpu_custom_call" | custom-call | flops 1409286144 | bytes 9437184 | tf_op jit(solution)/shard_map/pallas_call | solution.py:49
  275.2 5.1 collective-permute-done.41.refs_3_
  281.0 35.5 %shard_map.284 = bf16[2048,576]{1,0:T(8,128)(2,1)} custom-call(s32[14]{0:T(128)} %concatenate.19.meta_ref, bf16[3,2048,64]{2,1,0:T(8,128)(2,1)} %get-tuple-element.112.q_ref, bf16[3,2048,64]{2,1,0:T(8,128)(2,1)} %get-tuple-element.113.k_ref, bf16[3,2048,64]{2,1,0:T(8,128)(2,1)} %get-tuple-element.134.v_ref, bf16[192,2048]{1,0:T(8,128)(2,1)} %get-tuple-element.135.kt_ref, ...), custom_call_target="tpu_custom_call" | custom-call | flops 8053063680 | bytes 9437184 | tf_op jit(solution)/shard_map/pallas_call | solution.py:49
  351.8 8.0 %collective-permute-done.44 = bf16[512,576]{0,1:T(8,128)(2,1)S(1)} collective-permute-done((bf16[512,576]{0,1:T(8,128)(2,1)}, bf16[512,576]{0,1:T(8,128)(2,1)S(1)}, u32[]{:S(2)}, u32[]{:S(2)}) %collective-permute-start.44) | collective-permute-done | bytes 589856 | tf_op jit(solution)/shard_map/ppermute | solution.py:69
  363.6 8.4 %shard_map.285 = (f32[512,768]{1,0:T(8,128)}, f32[1,768]{1,0:T(1,128)}) custom-call(s32[14]{0:T(128)} %concatenate.19.meta_ref, bf16[512,768]{1,0:T(8,128)(2,1)} %bitcast.162, f32[1,768]{1,0:T(1,128)} %reshape.185.gain_ref, f32[512,768]{1,0:T(8,128)} %get-tuple-element.133.dx1_ref, bf16[512,576]{1,0:T(8,128)(2,1)} %get-tuple-element.235.refs_0_, ...), custom_call_target="tpu_custom_call" | custom-call | flops 1811939328 | bytes 11403264 | tf_op jit(solution)/shard_map/pallas_call | solution.py:49
  380.5 4.5 collective-permute-done.52
  393.9 5.7 collective-permute-done.68
  405.1 17.7 %collective-permute-done.57 = bf16[288,768]{1,0:T(8,128)(2,1)S(1)} collective-permute-done((bf16[288,768]{1,0:T(8,128)(2,1)S(1)}, bf16[288,768]{1,0:T(8,128)(2,1)S(1)}, u32[]{:S(2)}, u32[]{:S(2)}) %collective-permute-start.57) | collective-permute-done | bytes 442400 | tf_op jit(solution)/shard_map/ppermute | solution.py:69
  429.0 7.1 collective-permute-done.58
  436.5 16.4 %collective-permute-done.73 = bf16[384,1024]{1,0:T(8,128)(2,1)S(1)} collective-permute-done((bf16[384,1024]{1,0:T(8,128)(2,1)S(1)}, bf16[384,1024]{1,0:T(8,128)(2,1)S(1)}, u32[]{:S(2)}, u32[]{:S(2)}) %collective-permute-start.73) | collective-permute-done | bytes 786464 | tf_op jit(solution)/shard_map/ppermute | solution.py:69
  454.8 15.0 %collective-permute-done.79 = bf16[384,1024]{1,0:T(8,128)(2,1)S(1)} collective-permute-done((bf16[384,1024]{1,0:T(8,128)(2,1)S(1)}, bf16[384,1024]{1,0:T(8,128)(2,1)S(1)}, u32[]{:S(2)}, u32[]{:S(2)}) %collective-permute-start.79) | collective-permute-done | bytes 786464 | tf_op jit(solution)/shard_map/ppermute | solution.py:69
  471.6 15.0 %collective-permute-done.85 = bf16[384,1024]{1,0:T(8,128)(2,1)S(1)} collective-permute-done((bf16[384,1024]{1,0:T(8,128)(2,1)S(1)}, bf16[384,1024]{1,0:T(8,128)(2,1)S(1)}, u32[]{:S(2)}, u32[]{:S(2)}) %collective-permute-start.85) | collective-permute-done | bytes 786464 | tf_op jit(solution)/shard_map/ppermute | solution.py:69
  487.4 16.1 %collective-permute-done.91 = bf16[384,1024]{1,0:T(8,128)(2,1)S(1)} collective-permute-done((bf16[384,1024]{1,0:T(8,128)(2,1)S(1)}, bf16[384,1024]{1,0:T(8,128)(2,1)S(1)}, u32[]{:S(2)}, u32[]{:S(2)}) %collective-permute-start.91) | collective-permute-done | bytes 786464 | tf_op jit(solution)/shard_map/ppermute | solution.py:69
  506.9 13.5 %collective-permute-done.97 = bf16[1024,384]{1,0:T(8,128)(2,1)S(1)} collective-permute-done((bf16[1024,384]{1,0:T(8,128)(2,1)S(1)}, bf16[1024,384]{1,0:T(8,128)(2,1)S(1)}, u32[]{:S(2)}, u32[]{:S(2)}) %collective-permute-start.97) | collective-permute-done | bytes 786464 | tf_op jit(solution)/shard_map/ppermute | solution.py:69
  522.5 13.3 %collective-permute-done.103 = bf16[1024,384]{1,0:T(8,128)(2,1)S(1)} collective-permute-done((bf16[1024,384]{1,0:T(8,128)(2,1)S(1)}, bf16[1024,384]{1,0:T(8,128)(2,1)S(1)}, u32[]{:S(2)}, u32[]{:S(2)}) %collective-permute-start.103) | collective-permute-done | bytes 786464 | tf_op jit(solution)/shard_map/ppermute | solution.py:69
  544.5 12.3 %collective-permute-done.25.refs_6_ = bf16[128,768]{1,0:T(8,128)(2,1)S(1)} collective-permute-done((bf16[128,768]{1,0:T(8,128)(2,1)S(1)}, bf16[128,768]{1,0:T(8,128)(2,1)S(1)}, u32[]{:S(2)}, u32[]{:S(2)}) %collective-permute-start.25) | collective-permute-done | bytes 196640 | tf_op jit(solution)/shard_map/ppermute | solution.py:69
  556.8 5.8 collective-permute-start.49
  570.0 25.2 %collective-permute-done.86 = bf16[192,1024]{1,0:T(8,128)(2,1)S(1)} collective-permute-done((bf16[192,1024]{1,0:T(8,128)(2,1)S(1)}, bf16[192,1024]{1,0:T(8,128)(2,1)S(1)}, u32[]{:S(2)}, u32[]{:S(2)}) %collective-permute-start.86) | collective-permute-done | bytes 393248 | tf_op jit(solution)/shard_map/ppermute | solution.py:69
  595.2 8.4 %collective-permute-done.92 = bf16[192,1024]{1,0:T(8,128)(2,1)S(1)} collective-permute-done((bf16[192,1024]{1,0:T(8,128)(2,1)S(1)}, bf16[192,1024]{1,0:T(8,128)(2,1)S(1)}, u32[]{:S(2)}, u32[]{:S(2)}) %collective-permute-start.92) | collective-permute-done | bytes 393248 | tf_op jit(solution)/shard_map/ppermute | solution.py:69
  606.0 6.0 collective-permute-done.98
  612.0 8.4 %collective-permute-done.104 = bf16[512,384]{1,0:T(8,128)(2,1)S(1)} collective-permute-done((bf16[512,384]{1,0:T(8,128)(2,1)S(1)}, bf16[512,384]{1,0:T(8,128)(2,1)S(1)}, u32[]{:S(2)}, u32[]{:S(2)}) %collective-permute-start.104) | collective-permute-done | bytes 393248 | tf_op jit(solution)/shard_map/ppermute | solution.py:69
  622.6 6.4 collective-permute-done.76.refs_2_
  632.1 5.2 collective-permute-done.82.refs_6_
  638.7 7.0 collective-permute-done.88.refs_2_
  648.1 6.2 collective-permute-done.94.refs_6_
  654.8 7.9 %collective-permute-done.100.refs_2_ = bf16[512,384]{1,0:T(8,128)(2,1)} collective-permute-done((bf16[512,384]{1,0:T(8,128)(2,1)}, bf16[512,384]{1,0:T(8,128)(2,1)}, u32[]{:S(2)}, u32[]{:S(2)}) %collective-permute-start.100) | collective-permute-done | bytes 393248 | tf_op jit(solution)/shard_map/ppermute | solution.py:69
  662.7 6.6 collective-permute-done.106.refs_6_
  672.4 5.3 shard_map.282
  686.0 6.6 shard_map.288
  692.6 6.6 shard_map.289
  700.9 6.6 shard_map.290
  707.6 7.1 shard_map.286
  (493 shorter events, 207.3 us)
Async XLA Ops:
  3.7 35.9 %collective-permute-start.2 = (bf16[512,768]{1,0:T(8,128)(2,1)}, bf16[512,768]{1,0:T(8,128)(2,1)}, u32[]{:S(2)}, u32[]{:S(2)}) collective-permute-start(bf16[512,768]{1,0:T(8,128)(2,1)} %bitcast.159), channel_id=1, source_target_pairs={{0,4},{4,0},{8,12},{12,8},{1,5},{5,1},{9,13},{13,9},{2,6},{6,2},{1... | collective-permute-start | bytes 2359304 | tf_op jit(solution)/shard_map/ppermute | solution.py:69
  21.5 27.3 %collective-permute-start.1 = (bf16[512,768]{1,0:T(8,128)(2,1)}, bf16[512,768]{1,0:T(8,128)(2,1)}, u32[]{:S(2)}, u32[]{:S(2)}) collective-permute-start(bf16[512,768]{1,0:T(8,128)(2,1)} %collective-permute-done.x_ref), channel_id=1, source_target_pairs={{0,4},{4,0},{8,12},{12,8},{1,5},{5,1},{9,13},{13,9},{2,6},{6,2},{1... | collective-permute-start | bytes 2359304 | tf_op jit(solution)/shard_map/ppermute | solution.py:69
  23.5 106.6 %collective-permute-start.9 = (bf16[128,768]{1,0:T(8,128)(2,1)}, bf16[128,768]{1,0:T(8,128)(2,1)}, u32[]{:S(2)}, u32[]{:S(2)}) collective-permute-start(bf16[128,768]{1,0:T(8,128)(2,1)} %get-tuple-element.262), channel_id=1, source_target_pairs={{0,1},{1,0},{2,3},{3,2},{4,5},{5,4},{6,7},{7,6},{8,9},{9,8},{10,11... | collective-permute-start | bytes 589832 | tf_op jit(solution)/shard_map/ppermute | solution.py:69
  99.8 33.0 %collective-permute-start.10 = (bf16[128,768]{1,0:T(8,128)(2,1)S(1)}, bf16[128,768]{1,0:T(8,128)(2,1)S(1)}, u32[]{:S(2)}, u32[]{:S(2)}) collective-permute-start(bf16[128,768]{1,0:T(8,128)(2,1)S(1)} %copy-done.53), channel_id=1, source_target_pairs={{0,2},{1,3},{2,0},{3,1},{4,6},{5,7},{6,4},{7,5},{8,10},{9,11},{10,... | collective-permute-start | bytes 589832 | tf_op jit(solution)/shard_map/ppermute | solution.py:69
  100.7 33.3 %collective-permute-start.11 = (bf16[128,768]{1,0:T(8,128)(2,1)S(1)}, bf16[128,768]{1,0:T(8,128)(2,1)S(1)}, u32[]{:S(2)}, u32[]{:S(2)}) collective-permute-start(bf16[128,768]{1,0:T(8,128)(2,1)S(1)} %copy-done.52), channel_id=1, source_target_pairs={{0,3},{1,2},{2,1},{3,0},{4,7},{5,6},{6,5},{7,4},{8,11},{9,10},{10,... | collective-permute-start | bytes 589832 | tf_op jit(solution)/shard_map/ppermute | solution.py:69
  132.9 49.2 %collective-permute-start.21 = (bf16[128,768]{1,0:T(8,128)(2,1)S(1)}, bf16[128,768]{1,0:T(8,128)(2,1)S(1)}, u32[]{:S(2)}, u32[]{:S(2)}) collective-permute-start(bf16[128,768]{1,0:T(8,128)(2,1)S(1)} %get-tuple-element.253), channel_id=1, source_target_pairs={{0,1},{1,0},{2,3},{3,2},{4,5},{5,4},{6,7},{7,6},{8,9},{9,8},{10,11... | collective-permute-start | bytes 589832 | tf_op jit(solution)/shard_map/ppermute | solution.py:69
  134.0 50.6 %collective-permute-start.22 = (bf16[128,768]{1,0:T(8,128)(2,1)S(1)}, bf16[128,768]{1,0:T(8,128)(2,1)S(1)}, u32[]{:S(2)}, u32[]{:S(2)}) collective-permute-start(bf16[128,768]{1,0:T(8,128)(2,1)S(1)} %get-tuple-element.252), channel_id=1, source_target_pairs={{0,2},{1,3},{2,0},{3,1},{4,6},{5,7},{6,4},{7,5},{8,10},{9,11},{10,... | collective-permute-start | bytes 589832 | tf_op jit(solution)/shard_map/ppermute | solution.py:69
  135.7 50.5 %collective-permute-start.23 = (bf16[128,768]{1,0:T(8,128)(2,1)S(1)}, bf16[128,768]{1,0:T(8,128)(2,1)S(1)}, u32[]{:S(2)}, u32[]{:S(2)}) collective-permute-start(bf16[128,768]{1,0:T(8,128)(2,1)S(1)} %get-tuple-element.251), channel_id=1, source_target_pairs={{0,3},{1,2},{2,1},{3,0},{4,7},{5,6},{6,5},{7,4},{8,11},{9,10},{10,... | collective-permute-start | bytes 589832 | tf_op jit(solution)/shard_map/ppermute | solution.py:69
  148.0 38.2 %collective-permute-start.18 = (bf16[128,768]{1,0:T(8,128)(2,1)S(1)}, bf16[128,768]{1,0:T(8,128)(2,1)S(1)}, u32[]{:S(2)}, u32[]{:S(2)}) collective-permute-start(bf16[128,768]{1,0:T(8,128)(2,1)S(1)} %get-tuple-element.256), channel_id=1, source_target_pairs={{0,1},{1,0},{2,3},{3,2},{4,5},{5,4},{6,7},{7,6},{8,9},{9,8},{10,11... | collective-permute-start | bytes 589832 | tf_op jit(solution)/shard_map/ppermute | solution.py:69
  148.0 40.2 %collective-permute-start.19 = (bf16[128,768]{1,0:T(8,128)(2,1)S(1)}, bf16[128,768]{1,0:T(8,128)(2,1)S(1)}, u32[]{:S(2)}, u32[]{:S(2)}) collective-permute-start(bf16[128,768]{1,0:T(8,128)(2,1)S(1)} %get-tuple-element.255), channel_id=1, source_target_pairs={{0,2},{1,3},{2,0},{3,1},{4,6},{5,7},{6,4},{7,5},{8,10},{9,11},{10,... | collective-permute-start | bytes 589832 | tf_op jit(solution)/shard_map/ppermute | solution.py:69
  184.6 34.0 %collective-permute-start.110 = (f32[4,3]{1,0:T(4,128)S(1)}, f32[4,3]{1,0:T(4,128)S(1)}, u32[]{:S(2)}, u32[]{:S(2)}) collective-permute-start(f32[4,3]{1,0:T(4,128)S(1)} %max.16), channel_id=1, source_target_pairs={{0,16},{16,0},{1,17},{17,1},{2,18},{18,2},{3,19},{19,3},{4,20},{20... | collective-permute-start | bytes 152 | tf_op jit(solution)/shard_map/ppermute | solution.py:69
  186.2 42.6 %collective-permute-start.27 = (bf16[128,768]{1,0:T(8,128)(2,1)S(1)}, bf16[128,768]{1,0:T(8,128)(2,1)S(1)}, u32[]{:S(2)}, u32[]{:S(2)}) collective-permute-start(bf16[128,768]{1,0:T(8,128)(2,1)S(1)} %get-tuple-element.247), channel_id=1, source_target_pairs={{0,1},{1,0},{2,3},{3,2},{4,5},{5,4},{6,7},{7,6},{8,9},{9,8},{10,11... | collective-permute-start | bytes 589832 | tf_op jit(solution)/shard_map/ppermute | solution.py:69
  186.2 32.5 %collective-permute-start.33 = (f32[1,128]{1,0:T(1,128)S(1)}, f32[1,128]{1,0:T(1,128)S(1)}, u32[]{:S(2)}, u32[]{:S(2)}) collective-permute-start(f32[1,128]{1,0:T(1,128)S(1)} %get-tuple-element.281), channel_id=1, source_target_pairs={{0,1},{1,0},{2,3},{3,2},{4,5},{5,4},{6,7},{7,6},{8,9},{9,8},{10,11... | collective-permute-start | bytes 1544 | tf_op jit(solution)/shard_map/ppermute | solution.py:69
  188.2 32.5 %collective-permute-start.34 = (f32[1,128]{1,0:T(1,128)S(1)}, f32[1,128]{1,0:T(1,128)S(1)}, u32[]{:S(2)}, u32[]{:S(2)}) collective-permute-start(f32[1,128]{1,0:T(1,128)S(1)} %get-tuple-element.280), channel_id=1, source_target_pairs={{0,2},{1,3},{2,0},{3,1},{4,6},{5,7},{6,4},{7,5},{8,10},{9,11},{10,... | collective-permute-start | bytes 1544 | tf_op jit(solution)/shard_map/ppermute | solution.py:69
  190.5 33.7 %collective-permute-start.35 = (f32[1,128]{1,0:T(1,128)S(1)}, f32[1,128]{1,0:T(1,128)S(1)}, u32[]{:S(2)}, u32[]{:S(2)}) collective-permute-start(f32[1,128]{1,0:T(1,128)S(1)} %get-tuple-element.279), channel_id=1, source_target_pairs={{0,3},{1,2},{2,1},{3,0},{4,7},{5,6},{6,5},{7,4},{8,11},{9,10},{10,... | collective-permute-start | bytes 1544 | tf_op jit(solution)/shard_map/ppermute | solution.py:69
  227.7 25.0 %collective-permute-start.31 = (bf16[128,768]{1,0:T(8,128)(2,1)S(1)}, bf16[128,768]{1,0:T(8,128)(2,1)S(1)}, u32[]{:S(2)}, u32[]{:S(2)}) collective-permute-start(bf16[128,768]{1,0:T(8,128)(2,1)S(1)} %get-tuple-element.243), channel_id=1, source_target_pairs={{0,2},{1,3},{2,0},{3,1},{4,6},{5,7},{6,4},{7,5},{8,10},{9,11},{10,... | collective-permute-start | bytes 589832 | tf_op jit(solution)/shard_map/ppermute | solution.py:69
  244.5 155.1 %collective-permute-start.72 = (bf16[2,384,1024]{2,1,0:T(8,128)(2,1)}, bf16[2,384,1024]{2,1,0:T(8,128)(2,1)}, u32[]{:S(2)}, u32[]{:S(2)}) collective-permute-start(bf16[2,384,1024]{2,1,0:T(8,128)(2,1)} %get-tuple-element.150), channel_id=1, source_target_pairs={{0,4},{4,0},{8,12},{12,8},{1,5},{5,1},{9,13},{13,9},{2,6},{6,2},{1... | collective-permute-start | bytes 4718600 | tf_op jit(solution)/shard_map/ppermute | solution.py:69
  272.2 51.9 %collective-permute-start.63 = (bf16[192,768]{1,0:T(8,128)(2,1)}, bf16[192,768]{1,0:T(8,128)(2,1)}, u32[]{:S(2)}, u32[]{:S(2)}) collective-permute-start(bf16[192,768]{1,0:T(8,128)(2,1)} %convolution_convert_fusion.1), channel_id=1, source_target_pairs={{0,4},{4,0},{8,12},{12,8},{1,5},{5,1},{9,13},{13,9},{2,6},{6,2},{1... | collective-permute-start | bytes 884744 | tf_op jit(solution)/shard_map/ppermute | solution.py:69
  272.6 58.8 %collective-permute-start.62 = (bf16[192,768]{1,0:T(8,128)(2,1)}, bf16[192,768]{1,0:T(8,128)(2,1)}, u32[]{:S(2)}, u32[]{:S(2)}) collective-permute-start(bf16[192,768]{1,0:T(8,128)(2,1)} %convolution_convert_fusion.3), channel_id=1, source_target_pairs={{0,4},{4,0},{8,12},{12,8},{1,5},{5,1},{9,13},{13,9},{2,6},{6,2},{1... | collective-permute-start | bytes 884744 | tf_op jit(solution)/shard_map/ppermute | solution.py:69
  335.1 24.7 %collective-permute-start.44 = (bf16[512,576]{0,1:T(8,128)(2,1)}, bf16[512,576]{0,1:T(8,128)(2,1)S(1)}, u32[]{:S(2)}, u32[]{:S(2)}) collective-permute-start(bf16[512,576]{0,1:T(8,128)(2,1)} %copy.122), channel_id=1, source_target_pairs={{0,12},{4,8},{8,4},{12,0},{1,13},{5,9},{9,5},{13,1},{2,14},{6,10},... | collective-permute-start | bytes 1769480 | tf_op jit(solution)/shard_map/ppermute | solution.py:69
  342.7 57.6 %collective-permute-start.78 = (bf16[2,384,1024]{2,1,0:T(8,128)(2,1)}, bf16[2,384,1024]{2,1,0:T(8,128)(2,1)}, u32[]{:S(2)}, u32[]{:S(2)}) collective-permute-start(bf16[2,384,1024]{2,1,0:T(8,128)(2,1)} %get-tuple-element.152), channel_id=1, source_target_pairs={{0,4},{4,0},{8,12},{12,8},{1,5},{5,1},{9,13},{13,9},{2,6},{6,2},{1... | collective-permute-start | bytes 4718600 | tf_op jit(solution)/shard_map/ppermute | solution.py:69
  344.2 27.9 %collective-permute-start.111 = (f32[4,3]{1,0:T(4,128)S(1)}, f32[4,3]{1,0:T(4,128)S(1)}, u32[]{:S(2)}, u32[]{:S(2)}) collective-permute-start(f32[4,3]{1,0:T(4,128)S(1)} %max.17), channel_id=1, source_target_pairs={{0,1},{1,0},{2,3},{3,2},{4,5},{5,4},{6,7},{7,6},{8,9},{9,8},{10,11... | collective-permute-start | bytes 152 | tf_op jit(solution)/shard_map/ppermute | solution.py:69
  349.2 27.6 %collective-permute-start.51 = (f32[31,768]{1,0:T(8,128)S(1)}, f32[31,768]{1,0:T(8,128)S(1)}, u32[]{:S(2)}, u32[]{:S(2)}) collective-permute-start(f32[31,768]{1,0:T(8,128)S(1)} %fusion.36), channel_id=1, source_target_pairs={{0,8},{4,12},{8,0},{12,4},{1,9},{5,13},{9,1},{13,5},{2,10},{6,14},... | collective-permute-start | bytes 285704 | tf_op jit(solution)/shard_map/ppermute | solution.py:69
  393.2 29.7 %collective-permute-start.84 = (bf16[2,384,1024]{2,1,0:T(8,128)(2,1)}, bf16[2,384,1024]{2,1,0:T(8,128)(2,1)S(1)}, u32[]{:S(2)}, u32[]{:S(2)}) collective-permute-start(bf16[2,384,1024]{2,1,0:T(8,128)(2,1)} %get-tuple-element.154), channel_id=1, source_target_pairs={{0,4},{4,0},{8,12},{12,8},{1,5},{5,1},{9,13},{13,9},{2,6},{6,2},{1... | collective-permute-start | bytes 4718600 | tf_op jit(solution)/shard_map/ppermute | solution.py:69
  393.2 30.4 %collective-permute-start.90 = (bf16[2,384,1024]{2,1,0:T(8,128)(2,1)}, bf16[2,384,1024]{2,1,0:T(8,128)(2,1)S(1)}, u32[]{:S(2)}, u32[]{:S(2)}) collective-permute-start(bf16[2,384,1024]{2,1,0:T(8,128)(2,1)} %get-tuple-element.156), channel_id=1, source_target_pairs={{0,4},{4,0},{8,12},{12,8},{1,5},{5,1},{9,13},{13,9},{2,6},{6,2},{1... | collective-permute-start | bytes 4718600 | tf_op jit(solution)/shard_map/ppermute | solution.py:69
  399.5 26.2 %collective-permute-start.96 = (bf16[2,1024,384]{2,1,0:T(8,128)(2,1)}, bf16[2,1024,384]{2,1,0:T(8,128)(2,1)S(1)}, u32[]{:S(2)}, u32[]{:S(2)}) collective-permute-start(bf16[2,1024,384]{2,1,0:T(8,128)(2,1)} %get-tuple-element.158), channel_id=1, source_target_pairs={{0,4},{4,0},{8,12},{12,8},{1,5},{5,1},{9,13},{13,9},{2,6},{6,2},{1... | collective-permute-start | bytes 4718600 | tf_op jit(solution)/shard_map/ppermute | solution.py:69
  399.6 28.9 %collective-permute-start.102 = (bf16[2,1024,384]{2,1,0:T(8,128)(2,1)}, bf16[2,1024,384]{2,1,0:T(8,128)(2,1)S(1)}, u32[]{:S(2)}, u32[]{:S(2)}) collective-permute-start(bf16[2,1024,384]{2,1,0:T(8,128)(2,1)} %get-tuple-element.160), channel_id=1, source_target_pairs={{0,4},{4,0},{8,12},{12,8},{1,5},{5,1},{9,13},{13,9},{2,6},{6,2},{1... | collective-permute-start | bytes 4718600 | tf_op jit(solution)/shard_map/ppermute | solution.py:69
  422.8 115.5 %collective-permute-start.112 = (f32[4,3]{1,0:T(4,128)S(1)}, f32[4,3]{1,0:T(4,128)S(1)}, u32[]{:S(2)}, u32[]{:S(2)}) collective-permute-start(f32[4,3]{1,0:T(4,128)S(1)} %max.18), channel_id=1, source_target_pairs={{0,2},{1,3},{2,0},{3,1},{4,6},{5,7},{6,4},{7,5},{8,10},{9,11},{10,... | collective-permute-start | bytes 152 | tf_op jit(solution)/shard_map/ppermute | solution.py:69
  423.6 29.3 %collective-permute-start.73 = (bf16[384,1024]{1,0:T(8,128)(2,1)S(1)}, bf16[384,1024]{1,0:T(8,128)(2,1)S(1)}, u32[]{:S(2)}, u32[]{:S(2)}) collective-permute-start(bf16[384,1024]{1,0:T(8,128)(2,1)S(1)} %fusion.16), channel_id=1, source_target_pairs={{0,16},{16,0},{1,17},{17,1},{2,18},{18,2},{3,19},{19,3},{4,20},{20... | collective-permute-start | bytes 2359304 | tf_op jit(solution)/shard_map/ppermute | solution.py:69
  425.8 113.9 %collective-permute-start.15 = (bf16[128,768]{1,0:T(8,128)(2,1)S(1)}, bf16[128,768]{1,0:T(8,128)(2,1)S(1)}, u32[]{:S(2)}, u32[]{:S(2)}) collective-permute-start(bf16[128,768]{1,0:T(8,128)(2,1)S(1)} %get-tuple-element.259), channel_id=1, source_target_pairs={{0,1},{1,0},{2,3},{3,2},{4,5},{5,4},{6,7},{7,6},{8,9},{9,8},{10,11... | collective-permute-start | bytes 589832 | tf_op jit(solution)/shard_map/ppermute | solution.py:69
  428.4 41.4 %collective-permute-start.79 = (bf16[384,1024]{1,0:T(8,128)(2,1)S(1)}, bf16[384,1024]{1,0:T(8,128)(2,1)S(1)}, u32[]{:S(2)}, u32[]{:S(2)}) collective-permute-start(bf16[384,1024]{1,0:T(8,128)(2,1)S(1)} %fusion.17), channel_id=1, source_target_pairs={{0,16},{16,0},{1,17},{17,1},{2,18},{18,2},{3,19},{19,3},{4,20},{20... | collective-permute-start | bytes 2359304 | tf_op jit(solution)/shard_map/ppermute | solution.py:69
  436.1 50.6 %collective-permute-start.85 = (bf16[384,1024]{1,0:T(8,128)(2,1)S(1)}, bf16[384,1024]{1,0:T(8,128)(2,1)S(1)}, u32[]{:S(2)}, u32[]{:S(2)}) collective-permute-start(bf16[384,1024]{1,0:T(8,128)(2,1)S(1)} %fusion.18), channel_id=1, source_target_pairs={{0,16},{16,0},{1,17},{17,1},{2,18},{18,2},{3,19},{19,3},{4,20},{20... | collective-permute-start | bytes 2359304 | tf_op jit(solution)/shard_map/ppermute | solution.py:69
  452.9 50.6 %collective-permute-start.91 = (bf16[384,1024]{1,0:T(8,128)(2,1)S(1)}, bf16[384,1024]{1,0:T(8,128)(2,1)S(1)}, u32[]{:S(2)}, u32[]{:S(2)}) collective-permute-start(bf16[384,1024]{1,0:T(8,128)(2,1)S(1)} %fusion.19), channel_id=1, source_target_pairs={{0,16},{16,0},{1,17},{17,1},{2,18},{18,2},{3,19},{19,3},{4,20},{20... | collective-permute-start | bytes 2359304 | tf_op jit(solution)/shard_map/ppermute | solution.py:69
  469.8 50.6 %collective-permute-start.97 = (bf16[1024,384]{1,0:T(8,128)(2,1)S(1)}, bf16[1024,384]{1,0:T(8,128)(2,1)S(1)}, u32[]{:S(2)}, u32[]{:S(2)}) collective-permute-start(bf16[1024,384]{1,0:T(8,128)(2,1)S(1)} %fusion.20), channel_id=1, source_target_pairs={{0,16},{16,0},{1,17},{17,1},{2,18},{18,2},{3,19},{19,3},{4,20},{20... | collective-permute-start | bytes 2359304 | tf_op jit(solution)/shard_map/ppermute | solution.py:69
  486.7 49.1 %collective-permute-start.103 = (bf16[1024,384]{1,0:T(8,128)(2,1)S(1)}, bf16[1024,384]{1,0:T(8,128)(2,1)S(1)}, u32[]{:S(2)}, u32[]{:S(2)}) collective-permute-start(bf16[1024,384]{1,0:T(8,128)(2,1)S(1)} %fusion.21), channel_id=1, source_target_pairs={{0,16},{16,0},{1,17},{17,1},{2,18},{18,2},{3,19},{19,3},{4,20},{20... | collective-permute-start | bytes 2359304 | tf_op jit(solution)/shard_map/ppermute | solution.py:69
  503.5 36.9 %collective-permute-start.16 = (bf16[128,768]{1,0:T(8,128)(2,1)S(1)}, bf16[128,768]{1,0:T(8,128)(2,1)S(1)}, u32[]{:S(2)}, u32[]{:S(2)}) collective-permute-start(bf16[128,768]{1,0:T(8,128)(2,1)S(1)} %get-tuple-element.258), channel_id=1, source_target_pairs={{0,2},{1,3},{2,0},{3,1},{4,6},{5,7},{6,4},{7,5},{8,10},{9,11},{10,... | collective-permute-start | bytes 589832 | tf_op jit(solution)/shard_map/ppermute | solution.py:69
  538.3 27.2 %collective-permute-start.74 = (bf16[192,1024]{1,0:T(8,128)(2,1)S(1)}, bf16[192,1024]{1,0:T(8,128)(2,1)S(1)}, u32[]{:S(2)}, u32[]{:S(2)}) collective-permute-start(bf16[192,1024]{1,0:T(8,128)(2,1)S(1)} %dynamic-slice_bitcast_fusion.6), channel_id=1, source_target_pairs={{0,8},{4,12},{8,0},{12,4},{1,9},{5,13},{9,1},{13,5},{2,10},{6,14},... | collective-permute-start | bytes 1179656 | tf_op jit(solution)/shard_map/ppermute | solution.py:69
  539.6 26.5 %collective-permute-start.80 = (bf16[192,1024]{1,0:T(8,128)(2,1)S(1)}, bf16[192,1024]{1,0:T(8,128)(2,1)S(1)}, u32[]{:S(2)}, u32[]{:S(2)}) collective-permute-start(bf16[192,1024]{1,0:T(8,128)(2,1)S(1)} %dynamic-slice_bitcast_fusion.5), channel_id=1, source_target_pairs={{0,8},{4,12},{8,0},{12,4},{1,9},{5,13},{9,1},{13,5},{2,10},{6,14},... | collective-permute-start | bytes 1179656 | tf_op jit(solution)/shard_map/ppermute | solution.py:69
  564.2 57.6 %collective-permute-start.60 = (bf16[576,768]{1,0:T(8,128)(2,1)S(1)}, bf16[576,768]{1,0:T(8,128)(2,1)S(1)}, u32[]{:S(2)}, u32[]{:S(2)}) collective-permute-start(bf16[576,768]{1,0:T(8,128)(2,1)S(1)} %pad_maximum_fusion.refs_0_), channel_id=1, source_target_pairs={{0,8},{4,12},{8,0},{12,4},{1,9},{5,13},{9,1},{13,5},{2,10},{6,14},... | collective-permute-start | bytes 2654216 | tf_op jit(solution)/shard_map/ppermute | solution.py:69
  565.5 29.7 %collective-permute-start.86 = (bf16[192,1024]{1,0:T(8,128)(2,1)S(1)}, bf16[192,1024]{1,0:T(8,128)(2,1)S(1)}, u32[]{:S(2)}, u32[]{:S(2)}) collective-permute-start(bf16[192,1024]{1,0:T(8,128)(2,1)S(1)} %dynamic-slice_bitcast_fusion.4), channel_id=1, source_target_pairs={{0,8},{4,12},{8,0},{12,4},{1,9},{5,13},{9,1},{13,5},{2,10},{6,14},... | collective-permute-start | bytes 1179656 | tf_op jit(solution)/shard_map/ppermute | solution.py:69
  566.2 37.4 %collective-permute-start.92 = (bf16[192,1024]{1,0:T(8,128)(2,1)S(1)}, bf16[192,1024]{1,0:T(8,128)(2,1)S(1)}, u32[]{:S(2)}, u32[]{:S(2)}) collective-permute-start(bf16[192,1024]{1,0:T(8,128)(2,1)S(1)} %dynamic-slice_bitcast_fusion.3), channel_id=1, source_target_pairs={{0,8},{4,12},{8,0},{12,4},{1,9},{5,13},{9,1},{13,5},{2,10},{6,14},... | collective-permute-start | bytes 1179656 | tf_op jit(solution)/shard_map/ppermute | solution.py:69
  567.9 44.2 %collective-permute-start.98 = (bf16[512,384]{1,0:T(8,128)(2,1)S(1)}, bf16[512,384]{1,0:T(8,128)(2,1)S(1)}, u32[]{:S(2)}, u32[]{:S(2)}) collective-permute-start(bf16[512,384]{1,0:T(8,128)(2,1)S(1)} %dynamic-slice_bitcast_fusion.2), channel_id=1, source_target_pairs={{0,8},{4,12},{8,0},{12,4},{1,9},{5,13},{9,1},{13,5},{2,10},{6,14},... | collective-permute-start | bytes 1179656 | tf_op jit(solution)/shard_map/ppermute | solution.py:69
  568.7 51.8 %collective-permute-start.104 = (bf16[512,384]{1,0:T(8,128)(2,1)S(1)}, bf16[512,384]{1,0:T(8,128)(2,1)S(1)}, u32[]{:S(2)}, u32[]{:S(2)}) collective-permute-start(bf16[512,384]{1,0:T(8,128)(2,1)S(1)} %dynamic-slice_bitcast_fusion.1), channel_id=1, source_target_pairs={{0,8},{4,12},{8,0},{12,4},{1,9},{5,13},{9,1},{13,5},{2,10},{6,14},... | collective-permute-start | bytes 1179656 | tf_op jit(solution)/shard_map/ppermute | solution.py:69
  595.2 26.6 %collective-permute-start.75 = (bf16[192,1024]{1,0:T(8,128)(2,1)S(1)}, bf16[192,1024]{1,0:T(8,128)(2,1)S(1)}, u32[]{:S(2)}, u32[]{:S(2)}) collective-permute-start(bf16[192,1024]{1,0:T(8,128)(2,1)S(1)} %fusion.27.refs_0_), channel_id=1, source_target_pairs={{0,4},{4,0},{8,12},{12,8},{1,5},{5,1},{9,13},{13,9},{2,6},{6,2},{1... | collective-permute-start | bytes 1179656 | tf_op jit(solution)/shard_map/ppermute | solution.py:69
  603.6 25.4 %collective-permute-start.76 = (bf16[192,1024]{1,0:T(8,128)(2,1)S(1)}, bf16[192,1024]{1,0:T(8,128)(2,1)}, u32[]{:S(2)}, u32[]{:S(2)}) collective-permute-start(bf16[192,1024]{1,0:T(8,128)(2,1)S(1)} %fusion.27.refs_0_), channel_id=1, source_target_pairs={{0,8},{4,12},{8,0},{12,4},{1,9},{5,13},{9,1},{13,5},{2,10},{6,14},... | collective-permute-start | bytes 1179656 | tf_op jit(solution)/shard_map/ppermute | solution.py:69
  637.3 25.4 %collective-permute-start.100 = (bf16[512,384]{1,0:T(8,128)(2,1)}, bf16[512,384]{1,0:T(8,128)(2,1)}, u32[]{:S(2)}, u32[]{:S(2)}) collective-permute-start(bf16[512,384]{1,0:T(8,128)(2,1)} %fusion.23.refs_0_), channel_id=1, source_target_pairs={{0,8},{4,12},{8,0},{12,4},{1,9},{5,13},{9,1},{13,5},{2,10},{6,14},... | collective-permute-start | bytes 1179656 | tf_op jit(solution)/shard_map/ppermute | solution.py:69
  654.3 53.3 %collective-permute-start.59 = (bf16[576,768]{1,0:T(8,128)(2,1)}, bf16[576,768]{1,0:T(8,128)(2,1)}, u32[]{:S(2)}, u32[]{:S(2)}) collective-permute-start(bf16[576,768]{1,0:T(8,128)(2,1)} %copy-done.6), channel_id=1, source_target_pairs={{0,4},{4,0},{8,12},{12,8},{1,5},{5,1},{9,13},{13,9},{2,6},{6,2},{1... | collective-permute-start | bytes 2654216 | tf_op jit(solution)/shard_map/ppermute | solution.py:69
  654.3 53.3 %collective-permute-start.61 = (bf16[576,768]{1,0:T(8,128)(2,1)}, bf16[576,768]{1,0:T(8,128)(2,1)}, u32[]{:S(2)}, u32[]{:S(2)}) collective-permute-start(bf16[576,768]{1,0:T(8,128)(2,1)} %copy-done.28), channel_id=1, source_target_pairs={{0,4},{4,0},{8,12},{12,8},{1,5},{5,1},{9,13},{13,9},{2,6},{6,2},{1... | collective-permute-start | bytes 2654216 | tf_op jit(solution)/shard_map/ppermute | solution.py:69
  (153 other events, 2511.8 us)

commit v2 on v1

--- a/solution.py
+++ b/solution.py
@@ -20,6 +20,7 @@
 TN = (((0,), (0,)), ((), ()))
 f32 = jnp.float32
 bf16 = jnp.bfloat16
+MESH = pl.DeviceIdType.MESH
 
 
 def mm(left, right, dims=NN):
@@ -43,7 +44,7 @@
     return pl.CostEstimate(flops=int(flops), bytes_accessed=int(moved), transcendentals=int(exps))
 
 
-def run(body, grid, inputs, outputs, scratch=(), meta=None, flops=0, moved=0, exps=0, aliases=None):
+def run(body, grid, inputs, outputs, scratch=(), meta=None, flops=0, moved=0, exps=0, aliases=None, talks=None):
     prefetch = 0 if meta is None else 1
     args = ([] if meta is None else [meta]) + [a for a, _ in inputs]
     return pl.pallas_call(
@@ -57,7 +58,10 @@
             scratch_shapes=list(scratch),
         ),
         compiler_params=pltpu.CompilerParams(
-            dimension_semantics=("arbitrary",) * len(grid), vmem_limit_bytes=60 * 1024 * 1024
+            dimension_semantics=("arbitrary",) * len(grid),
+            vmem_limit_bytes=60 * 1024 * 1024,
+            collective_id=talks,
+            has_side_effects=talks is not None,
         ),
         cost_estimate=cost(flops, moved, exps),
         input_output_aliases={} if aliases is None else aliases,
@@ -602,75 +606,109 @@
     )
 
 
-def expert_layer(which, meta, arrived, grads, gates, w_gate, w_up, w_down, parts):
+def expert_layer(which, arrived, grads, gates, w_gate, w_up, w_down, parts):
     groups = len(arrived)
     rows = groups * CAP
     width = w_gate.shape[1]
     hidden = w_gate.shape[2]
     half = width // 2
-    tile = 256
+    per_part = hidden // parts
+    tile = min(256, per_part)
     steps = hidden // tile
-    per_part = hidden // parts
-    tile_part = max(1, per_part // tile)
+    tile_part = per_part // tile
     chunk = 128
 
-    def body(meta_ref, *refs):
+    def body(*refs):
         x_refs = refs[:groups]
         dy_refs = refs[groups : 2 * groups]
         gates_ref, wg_ref, wu_ref, wd_ref = refs[2 * groups : 2 * groups + 4]
-        y_ref, dx_ref, dg_ref = refs[2 * groups + 4 : 2 * groups + 7]
-        gs_ref, gk_ref, us_ref, uk_ref, ds_ref, dk_ref = refs[2 * groups + 7 : 2 * groups + 13]
-        x_all, xt_all, dy_all, gate_all, y_acc, dx_acc, dot_acc, hid_t, dgt, dut, scaled_t = refs[
-            2 * groups + 13 :
+        y_ref, dx_ref, dg_ref, sum_ref = refs[2 * groups + 4 : 2 * groups + 8]
+        (x_all, xt_all, dy_all, dyt_all, gate_all, y_acc, dx_acc, dot_acc, hid_t, dgt, dut, scaled_t) = refs[
+            2 * groups + 8 : 2 * groups + 20
         ]
+        keep, send, taken, send_sem, take_sem = refs[2 * groups + 20 :]
         f = pl.program_id(0)
-        core = meta_ref[2]
+        place_now = lax.axis_index("ctx")
+        core = lax.rem(place_now, 2)
+        sibling = place_now + 1 - 2 * core
         diagonal = lax.broadcasted_iota(jnp.int32, (CAP, CAP), 0) == lax.broadcasted_iota(
             jnp.int32, (CAP, CAP), 1
         )
 
+        def copy(step, slot):
+            return pltpu.make_async_remote_copy(
+                src_ref=send.at[slot],
+                dst_ref=taken.at[step],
+                send_sem=send_sem.at[slot],
+                recv_sem=take_sem.at[step],
+                device_id={"ctx": sibling},
+                device_id_type=MESH,
+            )
+
         @pl.when(f == 0)
         def _():
+            barrier = pltpu.get_barrier_semaphore()
+            pl.semaphore_signal(barrier, inc=1, device_id={"ctx": sibling}, device_id_type=MESH)
             for g in range(groups):
                 span = slice(g * CAP, (g + 1) * CAP)
                 x_all[span, :] = x_refs[g][...]
                 xt_all[:, span] = jnp.transpose(x_refs[g][...])
                 dy_all[span, :] = dy_refs[g][...]
+                dyt_all[:, span] = jnp.transpose(dy_refs[g][...])
                 gate_all[span, :] = jnp.sum(
                     jnp.where(diagonal, gates_ref[g : g + 1, :], 0.0), axis=1, keepdims=True
                 )
             y_acc[...] = jnp.zeros_like(y_acc)
             dx_acc[...] = jnp.zeros_like(dx_acc)
             dot_acc[...] = jnp.zeros_like(dot_acc)
-
-        for r in range(rows // chunk):
-            span = slice(r * chunk, (r + 1) * chunk)
-            g_pre = mm(x_all[span, :], wg_ref[0])
-            u_pre = mm(x_all[span, :], wu_ref[0])
-            back = mm(dy_all[span, :], wd_ref[0], NT)
-            gate = gate_all[span, :]
-            sig = 1.0 / (1.0 + jnp.exp(-g_pre))
-            act = g_pre * sig
-            hid = act * u_pre
-            hid_t[span, :] = hid.astype(bf16)
-            scaled_t[span, :] = (gate * hid).astype(bf16)
-            dot_acc[span, :] += hid * back
-            dhid = gate * back
-            dgt[span, :] = (dhid * u_pre * sig * (1.0 + g_pre * (1.0 - sig))).astype(bf16)
-            dut[span, :] = (dhid * act).astype(bf16)
-        y_acc[...] += mm(hid_t[...], wd_ref[0])
-        dx_acc[...] += mm(dgt[...], wg_ref[0], NT) + mm(dut[...], wu_ref[0], NT)
-        mine = pl.multiple_of(core * half, half)
-        theirs = pl.multiple_of((1 - core) * half, half)
-        gs_ref[0] = mm(xt_all[pl.ds(theirs, half), :], dgt[...]).astype(bf16)
-        gk_ref[0] = mm(xt_all[pl.ds(mine, half), :], dgt[...]).astype(bf16)
-        us_ref[0] = mm(xt_all[pl.ds(theirs, half), :], dut[...]).astype(bf16)
-        uk_ref[0] = mm(xt_all[pl.ds(mine, half), :], dut[...]).astype(bf16)
-        ds_ref[0] = mm(scaled_t[...], dy_all[:, pl.ds(theirs, half)], TN).astype(bf16)
-        dk_ref[0] = mm(scaled_t[...], dy_all[:, pl.ds(mine, half)], TN).astype(bf16)
-
-        @pl.when(f == steps - 1)
+            pl.semaphore_wait(barrier, 1)
+
+        @pl.when(f < steps)
         def _():
+            slot = lax.rem(f, 2)
+            for r in range(rows // chunk):
+                span = slice(r * chunk, (r + 1) * chunk)
+                g_pre = mm(x_all[span, :], wg_ref[0])
+                u_pre = mm(x_all[span, :], wu_ref[0])
+                back = mm(dy_all[span, :], wd_ref[0], NT)
+                gate = gate_all[span, :]
+                sig = 1.0 / (1.0 + jnp.exp(-g_pre))
+                act = g_pre * sig
+                hid = act * u_pre
+                hid_t[span, :] = hid.astype(bf16)
+                scaled_t[span, :] = (gate * hid).astype(bf16)
+                dot_acc[span, :] += hid * back
+                dhid = gate * back
+                dgt[span, :] = (dhid * u_pre * sig * (1.0 + g_pre * (1.0 - sig))).astype(bf16)
+                dut[span, :] = (dhid * act).astype(bf16)
+
+            @pl.when(f >= 2)
+            def _():
+                copy(f - 2, slot).wait_send()
+
+            mine = pl.multiple_of(core * half, half)
+            theirs = pl.multiple_of((1 - core) * half, half)
+            send[slot, 0] = mm(xt_all[pl.ds(theirs, half), :], dgt[...]).astype(bf16)
+            send[slot, 1] = mm(xt_all[pl.ds(theirs, half), :], dut[...]).astype(bf16)
+            send[slot, 2] = mm(dyt_all[pl.ds(theirs, half), :], scaled_t[...]).astype(bf16)
+            keep[slot, 0] = mm(xt_all[pl.ds(mine, half), :], dgt[...]).astype(bf16)
+            copy(f, slot).start()
+            keep[slot, 1] = mm(xt_all[pl.ds(mine, half), :], dut[...]).astype(bf16)
+            keep[slot, 2] = mm(dyt_all[pl.ds(mine, half), :], scaled_t[...]).astype(bf16)
+            y_acc[...] += mm(hid_t[...], wd_ref[0])
+            dx_acc[...] += mm(dgt[...], wg_ref[0], NT) + mm(dut[...], wu_ref[0], NT)
+
+        @pl.when(f >= 1)
+        def _():
+            slot = lax.rem(f - 1, 2)
+            copy(f - 1, slot).wait_recv()
+            for n in range(3):
+                sum_ref[0, n] = keep[slot, n] + taken[f - 1, n]
+
+        @pl.when(f == steps)
+        def _():
+            for last in range(max(0, steps - 2), steps):
+                copy(last, last % 2).wait_send()
             y_ref[...] = (gate_all[...] * y_acc[...]).astype(bf16)
             dx_ref[...] = dx_acc[...].astype(bf16)
             for g in range(groups):
@@ -680,31 +718,36 @@
                     jnp.where(diagonal, column, 0.0), axis=0, keepdims=True
                 )
 
-    first = pl.BlockSpec((CAP, width), lambda f, m: (0, 0))
-    up_shape = shape_of((parts, half, per_part), bf16)
-    up_spec = pl.BlockSpec((1, half, tile), lambda f, m: (f // tile_part, 0, f % tile_part))
-    down_shape = shape_of((parts, per_part, half), bf16)
-    down_spec = pl.BlockSpec((1, tile, half), lambda f, m: (f // tile_part, f % tile_part, 0))
+    first = pl.BlockSpec((CAP, width), lambda f: (0, 0))
+    sums = shape_of((parts, 3, half, per_part), bf16)
+
+    def sum_place(f):
+        done = jnp.maximum(f - 1, 0)
+        return (done // tile_part, 0, 0, done % tile_part)
+
+    def now(f):
+        return jnp.minimum(f, steps - 1)
+
     wide = shape_of((rows, width), bf16)
     dots = shape_of((groups, CAP), f32)
     return run(
         body,
-        (steps,),
+        (steps + 1,),
         [(a, first) for a in arrived]
         + [(g, first) for g in grads]
         + [
             (gates, whole(gates)),
-            (w_gate, pl.BlockSpec((1, width, tile), lambda f, m: (which, 0, f))),
-            (w_up, pl.BlockSpec((1, width, tile), lambda f, m: (which, 0, f))),
-            (w_down, pl.BlockSpec((1, tile, width), lambda f, m: (which, f, 0))),
+            (w_gate, pl.BlockSpec((1, width, tile), lambda f: (which, 0, now(f)))),
+            (w_up, pl.BlockSpec((1, width, tile), lambda f: (which, 0, now(f)))),
+            (w_down, pl.BlockSpec((1, tile, width), lambda f: (which, now(f), 0))),
         ],
         [(wide, whole(wide)), (wide, whole(wide)), (dots, whole(dots))]
-        + [(up_shape, up_spec)] * 4
-        + [(down_shape, down_spec)] * 2,
+        + [(sums, pl.BlockSpec((1, 3, half, tile), sum_place))],
         scratch=[
             pltpu.VMEM((rows, width), bf16),
             pltpu.VMEM((width, rows), bf16),
             pltpu.VMEM((rows, width), bf16),
+            pltpu.VMEM((width, rows), bf16),
             pltpu.VMEM((rows, 1), f32),
             pltpu.VMEM((rows, width), f32),
             pltpu.VMEM((rows, width), f32),
@@ -713,11 +756,16 @@
             pltpu.VMEM((rows, tile), bf16),
             pltpu.VMEM((rows, tile), bf16),
             pltpu.VMEM((rows, tile), bf16),
+            pltpu.VMEM((2, 3, half, tile), bf16),
+            pltpu.VMEM((2, 3, half, tile), bf16),
+            pltpu.VMEM((steps, 3, half, tile), bf16),
+            pltpu.SemaphoreType.DMA((2,)),
+            pltpu.SemaphoreType.DMA((steps,)),
         ],
-        meta=meta,
         flops=9 * 2 * rows * width * hidden,
         moved=12 * width * hidden + rows * width * 8,
         exps=rows * hidden,
+        talks=1 + which,
     )
 
 
@@ -952,12 +1000,53 @@
     return value
 
 
-def expert_share(send, keep):
-    mine = sum_over_dp([keep, swap(send, "ctx", 1)])
+def expert_share(sums):
+    mine = sum_over_dp([sums])
     across = lax.axis_index("ctx") // 2
-    halves = mine.reshape((2, mine.shape[0] // 2) + mine.shape[1:])
-    total = add_low(pick(halves, across), swap(pick(halves, 1 - across), "ctx", 2))
+    halves = mine.reshape((3, 2, mine.shape[1] // 2, mine.shape[2]))
+    here = lax.dynamic_index_in_dim(halves, across, 1, keepdims=False)
+    there = lax.dynamic_index_in_dim(halves, 1 - across, 1, keepdims=False)
+    total = add_low(here, swap(there, "ctx", 2))
     return gather_near(total, "ctx")
+
+
+def place_experts(meta, pieces, which, turned):
+    local, members = len(pieces), len(pieces[0])
+    _, rows, columns = pieces[0][0].shape
+    flat = [p for listed in pieces for p in listed]
+
+    def body(meta_ref, *refs):
+        out_ref, hold = refs[-2:]
+        e = pl.program_id(0)
+        for n in range(local):
+
+            @pl.when(e == n)
+            def _():
+                for j in range(members):
+                    member = meta_ref[0] ^ j
+                    at = pl.multiple_of(
+                        (lax.rem(member, 2) * 2 + lax.div(member, 2)) * rows, rows
+                    )
+                    piece = refs[n * members + j][0].astype(f32)
+                    if turned:
+                        hold[pl.ds(at, rows), :] = piece
+                    else:
+                        out_ref[0, pl.ds(at, rows), :] = piece
+
+        if turned:
+            out_ref[0] = jnp.transpose(hold[...])
+
+    full = (columns, members * rows) if turned else (members * rows, columns)
+    spec = pl.BlockSpec((1, rows, columns), lambda e, m: (which, 0, 0))
+    return run(
+        body,
+        (local,),
+        [(p, spec) for p in flat],
+        [(shape_of((local,) + full, f32), pl.BlockSpec((1,) + full, lambda e, m: (e, 0, 0)))],
+        scratch=[pltpu.VMEM((members * rows, columns) if turned else (8, 128), f32)],
+        meta=meta,
+        moved=sum(p.size for p in flat) * 2,
+    )[0]
 
 
 def place(meta, pieces, out_shape, place_of):
@@ -1102,19 +1191,16 @@
         x1, h2, grad, prob, route_ids, logit_rows, const_vec, expert_count
     )
 
-    out_rows, in_rows, dot_rows = [], [], []
-    gate_pieces, up_pieces, down_pieces = [], [], []
+    out_rows, in_rows, dot_rows, shares = [], [], [], []
     for e in range(local):
         gate_rows = jnp.stack([gate_near[g][e] for g in range(groups)])
-        y, dx, dots, gs, gk, us, uk, ds, dk = expert_layer(
-            e, meta, token_near[e], grad_near[e], gate_rows, w_gate, w_up, w_down, parts
+        y, dx, dots, sums = expert_layer(
+            e, token_near[e], grad_near[e], gate_rows, w_gate, w_up, w_down, parts
         )
         in_rows += [swap(dx[g * CAP : (g + 1) * CAP], "exp", g) if g else dx for g in range(groups)]
         dot_rows += [swap(dots[g : g + 1], "exp", g) if g else dots[:1] for g in range(groups)]
         out_rows += [swap(y[g * CAP : (g + 1) * CAP], "exp", g) if g else y for g in range(groups)]
-        gate_pieces.append(expert_share(gs, gk))
-        up_pieces.append(expert_share(us, uk))
-        down_pieces.append(expert_share(ds, dk))
+        shares.append(expert_share(sums))
 
     back = token_back(
         meta,
@@ -1189,13 +1275,9 @@
     head_scale = jnp.repeat(clip_ratio, head_width)
     clipped = w_qkv[:2].astype(f32) * head_scale[None, None, :]
 
-    half = width // 2
-    hidden_part = w_gate.shape[2] // parts
-    up_shape = (local, width, hidden_part)
-    down_shape = (local, hidden_part, width)
-    gate_grad = place(meta, gate_pieces, up_shape, lambda a: ((a % 2) * 2 + a // 2, 0))
-    up_grad = place(meta, up_pieces, up_shape, lambda a: ((a % 2) * 2 + a // 2, 0))
-    down_grad = place(meta, down_pieces, down_shape, lambda a: (a // 2, a % 2))
+    gate_grad = place_experts(meta, shares, 0, False)
+    up_grad = place_experts(meta, shares, 1, False)
+    down_grad = place_experts(meta, shares, 2, True)
     return (
         result[None],
         input_grad[None],

time: 722 us -> 649 us (0.90)
  waiting for transfers between devices: 314 us -> 220 us
  local copies, waits for them, and re-layouts: 42.5 us -> 53.4 us
  Pallas kernels: 212 us -> 221 us
    ppermute x113 -> x87, waiting for transfers between devices: 314 us -> 220 us  [swap(): return lax.ppermute(value, axis, [(i, i ^ distance) for i in range(count)])]
    pallas_call x19, Pallas kernels: 212 us -> 221 us  [run(): pl.pallas_call(body, out_shape=[o for o, _ in outputs], grid_spec=pltpu.P...]
    ppermute x113 -> x87, starting transfers between devices: 112 us -> 110 us  [swap(): return lax.ppermute(value, axis, [(i, i ^ distance) for i in range(count)])]
  transfers between devices with their start and end apart: 113 -> 87, of which waited for: 42 -> 31; matrix products, arithmetic and copies ran while one was open for 10% -> 13% of each run, Pallas kernels for 29% -> 32%
where the time goes in v2:
time: 649 us; the launch traced here: 642 us
  Pallas kernels  221 us (34%)
  waiting for transfers between devices  220 us (34%)
  starting transfers between devices  110 us (17%)
  local copies, waits for them, and re-layouts  53.4 us (8%)
  other arithmetic  23.8 us (4%)
  matrix products  12.2 us (2%)
    pallas_call x19, Pallas kernels, run(): pl.pallas_call(body, out_shape=[o for o, _ in outputs], grid_spec=pltpu.P...  221 us
    ppermute x87, waiting for transfers between devices, swap(): return lax.ppermute(value, axis, [(i, i ^ distance) for i in range(count)])  220 us
    ppermute x87, starting transfers between devices, swap(): return lax.ppermute(value, axis, [(i, i ^ distance) for i in range(count)])  110 us
  transfers between devices with their start and end apart: 87, of which 31 were waited for; matrix products, arithmetic and copies ran while one was open for 13% of the time, Pallas kernels for 32%

profile of v2, /device:TPU:0, one launch (start us, length us, event | category | flops | bytes accessed | tf_op | source)
XLA Modules:
  0.0 641.5 jit_solution(17149983211441113304)
XLA Ops:
  8.1 3.0 shard_map.279
  11.2 10.4 %collective-permute-done.x_ref = bf16[512,768]{1,0:T(8,128)(2,1)} collective-permute-done((bf16[512,768]{1,0:T(8,128)(2,1)}, bf16[512,768]{1,0:T(8,128)(2,1)}, u32[]{:S(2)}, u32[]{:S(2)}) %collective-permute-start) | collective-permute-done | bytes 786464 | tf_op jit(solution)/shard_map/ppermute | solution.py:73
  25.8 3.7 copy.112
  35.4 4.6 shard_map.272
  40.8 4.6 shard_map.273
  45.4 4.6 shard_map.274
  50.0 4.6 shard_map.275
  54.7 29.9 %shard_map.276 = (bf16[2048,192]{1,0:T(8,128)(2,1)}, f32[192,2048]{1,0:T(8,128)}, f32[3,2048]{1,0:T(4,128)}, f32[3,2048]{1,0:T(4,128)}) custom-call(s32[14]{0:T(128)} %concatenate.19.meta_ref, bf16[3,2048,64]{2,1,0:T(8,128)(2,1)} %get-tuple-element.102.q_ref, bf16[3,2048,64]{2,1,0:T(8,128)(2,1)} %get-tuple-element.103.k_ref, ...), custom_call_target="tpu_custom_call" | custom-call | flops 3221225472 | bytes 5505024 | tf_op jit(solution)/shard_map/pallas_call | solution.py:50
  93.2 7.7 %collective-permute-done.83 = f32[4,3]{1,0:T(4,128)S(1)} collective-permute-done((f32[4,3]{1,0:T(4,128)S(1)}, f32[4,3]{1,0:T(4,128)S(1)}, u32[]{:S(2)}, u32[]{:S(2)}) %collective-permute-start.83) | collective-permute-done | bytes 80 | tf_op jit(solution)/shard_map/ppermute | solution.py:73
  100.9 3.6 collective-permute-done.84
  104.5 3.6 collective-permute-done.85
  112.3 10.5 %shard_map.277 = (f32[512,768]{1,0:T(8,128)}, f32[512,768]{1,0:T(8,128)}, f32[512,12]{1,0:T(8,128)}, f32[8,128]{1,0:T(8,128)}, bf16[512,768]{1,0:T(8,128)(2,1)}, /*index=5*/bf16[512,768]{1,0:T(8,128)(2,1)}) custom-call(s32[14]{0:T(128)} %concatenate.19.meta_ref, bf16[512,768]{1,0:T(8,128)(2,1)} %bitcast.119, bf16[512,192]{1,0:T(8,128)(2,1)} %get-tuple-element.219.refs_0_, ...), custom_call_target="tpu_custom_call" | custom-call | flops 1409286144 | bytes 5505024 | tf_op jit(solution)/shard_map/pallas_call | solution.py:50
  126.3 3.2 collective-permute-start.14
  130.6 7.5 %shard_map.278 = (f32[512,768]{1,0:T(8,128)}, f32[512,768]{1,0:T(8,128)}, f32[512,2]{1,0:T(8,128)}, f32[512,2]{1,0:T(8,128)}, f32[6,768]{1,0:T(8,128)}) custom-call(f32[512,768]{1,0:T(8,128)} %get-tuple-element.106.x1_ref.refs_0_, f32[512,768]{1,0:T(8,128)} %get-tuple-element.107.h2_ref.refs_1_, bf16[512,768]{1,0:T(8,128)(2,1)} %bitcast.123, ...), custom_call_target="tpu_custom_call" | custom-call | flops 15728640 | bytes 7077888 | tf_op jit(solution)/shard_map/pallas_call | solution.py:50
  138.7 4.0 collective-permute-done.13
  155.3 13.2 %collective-permute-done.7.refs_2_ = bf16[128,768]{1,0:T(8,128)(2,1)S(1)} collective-permute-done((bf16[128,768]{1,0:T(8,128)(2,1)S(1)}, bf16[128,768]{1,0:T(8,128)(2,1)S(1)}, u32[]{:S(2)}, u32[]{:S(2)}) %collective-permute-start.7) | collective-permute-done | bytes 196640 | tf_op jit(solution)/shard_map/ppermute | solution.py:73
  168.5 5.2 collective-permute-start.19
  173.7 30.6 %shard_map.280 = (bf16[512,768]{1,0:T(8,128)(2,1)}, bf16[512,768]{1,0:T(8,128)(2,1)}, f32[4,128]{1,0:T(4,128)}, bf16[2,3,384,1024]{3,2,1,0:T(8,128)(2,1)}) custom-call(bf16[512,768]{1,0:T(8,128)(2,1)} %get-tuple-element.110.refs_0_, bf16[128,768]{1,0:T(8,128)(2,1)} %copy-done.59, bf16[128,768]{1,0:T(8,128)(2,1)} %copy-done.65, bf16[128,768]{1,0:T(8,128)(2,1)} %copy-done.66, ...), custom_call_target="tpu_custom_call" | custom-call | flops 14495514624 | bytes 22020096 | tf_op jit(solution)/shard_map/pallas_call | solution.py:50
  215.8 30.7 %shard_map.281 = (bf16[512,768]{1,0:T(8,128)(2,1)}, bf16[512,768]{1,0:T(8,128)(2,1)}, f32[4,128]{1,0:T(4,128)}, bf16[2,3,384,1024]{3,2,1,0:T(8,128)(2,1)}) custom-call(bf16[512,768]{1,0:T(8,128)(2,1)} %get-tuple-element.114.refs_0_, bf16[128,768]{1,0:T(8,128)(2,1)} %copy-done.63, bf16[128,768]{1,0:T(8,128)(2,1)} %copy-done.64, bf16[128,768]{1,0:T(8,128)(2,1)} %copy-done.67, ...), custom_call_target="tpu_custom_call" | custom-call | flops 14495514624 | bytes 22020096 | tf_op jit(solution)/shard_map/pallas_call | solution.py:50
  261.5 3.4 dynamic-slice_bitcast_fusion.1
  267.1 4.3 collective-permute-done.28.refs_9_
  273.4 13.4 %collective-permute-done.31.refs_13_ = bf16[128,768]{1,0:T(8,128)(2,1)S(1)} collective-permute-done((bf16[128,768]{1,0:T(8,128)(2,1)S(1)}, bf16[128,768]{1,0:T(8,128)(2,1)S(1)}, u32[]{:S(2)}, u32[]{:S(2)}) %collective-permute-start.31) | collective-permute-done | bytes 196640 | tf_op jit(solution)/shard_map/ppermute | solution.py:73
  287.6 12.2 %shard_map.283 = (f32[512,768]{1,0:T(8,128)}, bf16[512,768]{1,0:T(8,128)(2,1)}, bf16[512,192]{1,0:T(8,128)(2,1)}, bf16[512,192]{1,0:T(8,128)(2,1)}, bf16[512,192...) custom-call(s32[14]{0:T(128)} %concatenate.19.meta_ref, ...), custom_call_target="tpu_custom_call" | custom-call | flops 1409286144 | bytes 9437184 | tf_op jit(solution)/shard_map/pallas_call | solution.py:50
  309.3 4.8 collective-permute-done.41.refs_3_
  314.7 36.0 %shard_map.284 = bf16[2048,576]{1,0:T(8,128)(2,1)} custom-call(s32[14]{0:T(128)} %concatenate.19.meta_ref, bf16[3,2048,64]{2,1,0:T(8,128)(2,1)} %get-tuple-element.102.q_ref, bf16[3,2048,64]{2,1,0:T(8,128)(2,1)} %get-tuple-element.103.k_ref, bf16[3,2048,64]{2,1,0:T(8,128)(2,1)} %get-tuple-element.124.v_ref, bf16[192,2048]{1,0:T(8,128)(2,1)} %get-tuple-element.125.kt_ref, ...), custom_call_target="tpu_custom_call" | custom-call | flops 8053063680 | bytes 9437184 | tf_op jit(solution)/shard_map/pallas_call | solution.py:50
  350.7 4.9 convolution_convert_fusion
  363.0 3.5 collective-permute-done.64
  373.1 12.3 %collective-permute-done.55 = bf16[288,768]{1,0:T(8,128)(2,1)} collective-permute-done((bf16[288,768]{1,0:T(8,128)(2,1)}, bf16[288,768]{1,0:T(8,128)(2,1)}, u32[]{:S(2)}, u32[]{:S(2)}) %collective-permute-start.55) | collective-permute-done | bytes 442400 | tf_op jit(solution)/shard_map/ppermute | solution.py:73
  391.6 10.2 %collective-permute-done.43 = bf16[512,576]{0,1:T(8,128)(2,1)} collective-permute-done((bf16[512,576]{0,1:T(8,128)(2,1)S(1)}, bf16[512,576]{0,1:T(8,128)(2,1)}, u32[]{:S(2)}, u32[]{:S(2)}) %collective-permute-start.43) | collective-permute-done | bytes 589856 | tf_op jit(solution)/shard_map/ppermute | solution.py:73
  405.7 4.4 collective-permute-done.44
  412.3 3.8 collective-permute-start.67
  416.0 8.4 %shard_map.285 = (f32[512,768]{1,0:T(8,128)}, f32[1,768]{1,0:T(1,128)}) custom-call(s32[14]{0:T(128)} %concatenate.19.meta_ref, bf16[512,768]{1,0:T(8,128)(2,1)} %bitcast.120, f32[1,768]{1,0:T(1,128)} %reshape.127.gain_ref, f32[512,768]{1,0:T(8,128)} %get-tuple-element.123.dx1_ref, bf16[512,576]{1,0:T(8,128)(2,1)} %get-tuple-element.215.refs_0_, ...), custom_call_target="tpu_custom_call" | custom-call | flops 1811939328 | bytes 11403264 | tf_op jit(solution)/shard_map/pallas_call | solution.py:50
  425.2 3.6 fusion.1
  430.6 3.6 fusion
  438.0 3.4 collective-permute-start.15
  441.5 15.4 %collective-permute-done.57 = bf16[288,768]{1,0:T(8,128)(2,1)S(1)} collective-permute-done((bf16[288,768]{1,0:T(8,128)(2,1)S(1)}, bf16[288,768]{1,0:T(8,128)(2,1)S(1)}, u32[]{:S(2)}, u32[]{:S(2)}) %collective-permute-start.57) | collective-permute-done | bytes 442400 | tf_op jit(solution)/shard_map/ppermute | solution.py:73
  459.8 22.3 %collective-permute-done.78 = bf16[3,192,1024]{2,1,0:T(8,128)(2,1)S(1)} collective-permute-done((bf16[3,192,1024]{2,1,0:T(8,128)(2,1)S(1)}, bf16[3,192,1024]{2,1,0:T(8,128)(2,1)S(1)}, u32[]{:S(2)}, u32[]{:S(2)}) %collective-permute-start.78) | collective-permute-done | bytes 1179680 | tf_op jit(solution)/shard_map/ppermute | solution.py:73
  496.0 10.9 %collective-permute-done.25.refs_6_ = bf16[128,768]{1,0:T(8,128)(2,1)S(1)} collective-permute-done((bf16[128,768]{1,0:T(8,128)(2,1)S(1)}, bf16[128,768]{1,0:T(8,128)(2,1)S(1)}, u32[]{:S(2)}, u32[]{:S(2)}) %collective-permute-start.25) | collective-permute-done | bytes 196640 | tf_op jit(solution)/shard_map/ppermute | solution.py:73
  508.9 32.7 %collective-permute-done.46 = f32[1,768]{1,0:T(1,128)S(1)} collective-permute-done((f32[1,768]{1,0:T(1,128)S(1)}, f32[1,768]{1,0:T(1,128)S(1)}, u32[]{:S(2)}, u32[]{:S(2)}) %collective-permute-start.46) | collective-permute-done | bytes 3104 | tf_op jit(solution)/shard_map/ppermute | solution.py:73
  545.2 7.9 %collective-permute-start.53 = (f32[31,768]{1,0:T(8,128)S(1)}, f32[31,768]{1,0:T(8,128)S(1)}, u32[]{:S(2)}, u32[]{:S(2)}) collective-permute-start(f32[31,768]{1,0:T(8,128)S(1)} %add.131), channel_id=1, source_target_pairs={{0,1},{1,0},{2,3},{3,2},{4,5},{5,4},{6,7},{7,6},{8,9},{9,8},{10,11... | collective-permute-start | bytes 285704 | tf_op jit(solution)/shard_map/ppermute | solution.py:73
  571.4 21.4 %collective-permute-done.70.refs_2_ = bf16[192,768]{1,0:T(8,128)(2,1)S(1)} collective-permute-done((bf16[192,768]{1,0:T(8,128)(2,1)S(1)}, bf16[192,768]{1,0:T(8,128)(2,1)S(1)}, u32[]{:S(2)}, u32[]{:S(2)}) %collective-permute-start.70) | collective-permute-done | bytes 294944 | tf_op jit(solution)/shard_map/ppermute | solution.py:73
  596.3 4.2 convert_multiply_fusion
  600.5 5.3 shard_map.282
  613.2 3.8 shard_map.287
  617.0 7.1 %shard_map.286 = f32[3,768,768]{2,1,0:T(8,128)} custom-call(s32[14]{0:T(128)} %concatenate.19.meta_ref, bf16[576,768]{1,0:T(8,128)(2,1)} %pad_maximum_fusion.refs_0_, bf16[576,768]{1,0:T(8,128)(2,1)} %copy-done.18, bf16[576,768]{1,0:T(8,128)(2,1)} %collective-permute-done.60.refs_2_, bf16[576,768]{1,0:T(8,128)(2,1)} %collective-permute-done.61.refs_3_), custom_call_target="tpu_custom_call" | custom-call | bytes 10616832 | tf_op jit(solution)/shard_map/pallas_call | solution.py:50
  624.1 5.4 shard_map.288
  629.5 5.4 shard_map.289
  635.0 6.4 shard_map.290
  (385 shorter events, 174.2 us)
Async XLA Ops:
  3.7 37.1 %collective-permute-start.2 = (bf16[512,768]{1,0:T(8,128)(2,1)}, bf16[512,768]{1,0:T(8,128)(2,1)}, u32[]{:S(2)}, u32[]{:S(2)}) collective-permute-start(bf16[512,768]{1,0:T(8,128)(2,1)} %bitcast.117), channel_id=1, source_target_pairs={{0,4},{4,0},{8,12},{12,8},{1,5},{5,1},{9,13},{13,9},{2,6},{6,2},{1... | collective-permute-start | bytes 2359304 | tf_op jit(solution)/shard_map/ppermute | solution.py:73
  21.5 28.5 %collective-permute-start.1 = (bf16[512,768]{1,0:T(8,128)(2,1)}, bf16[512,768]{1,0:T(8,128)(2,1)}, u32[]{:S(2)}, u32[]{:S(2)}) collective-permute-start(bf16[512,768]{1,0:T(8,128)(2,1)} %collective-permute-done.x_ref), channel_id=1, source_target_pairs={{0,4},{4,0},{8,12},{12,8},{1,5},{5,1},{9,13},{13,9},{2,6},{6,2},{1... | collective-permute-start | bytes 2359304 | tf_op jit(solution)/shard_map/ppermute | solution.py:73
  23.5 123.4 %collective-permute-start.9 = (bf16[128,768]{1,0:T(8,128)(2,1)}, bf16[128,768]{1,0:T(8,128)(2,1)}, u32[]{:S(2)}, u32[]{:S(2)}) collective-permute-start(bf16[128,768]{1,0:T(8,128)(2,1)} %get-tuple-element.242), channel_id=1, source_target_pairs={{0,1},{1,0},{2,3},{3,2},{4,5},{5,4},{6,7},{7,6},{8,9},{9,8},{10,11... | collective-permute-start | bytes 589832 | tf_op jit(solution)/shard_map/ppermute | solution.py:73
  86.5 24.9 %collective-permute-start.3 = (bf16[512,192]{1,0:T(8,128)(2,1)S(1)}, bf16[512,192]{1,0:T(8,128)(2,1)S(1)}, u32[]{:S(2)}, u32[]{:S(2)}) collective-permute-start(bf16[512,192]{1,0:T(8,128)(2,1)S(1)} %get-tuple-element.218), channel_id=1, source_target_pairs={{0,4},{4,0},{8,12},{12,8},{1,5},{5,1},{9,13},{13,9},{2,6},{6,2},{1... | collective-permute-start | bytes 589832 | tf_op jit(solution)/shard_map/ppermute | solution.py:73
  86.7 24.8 %collective-permute-start.4 = (bf16[512,192]{1,0:T(8,128)(2,1)S(1)}, bf16[512,192]{1,0:T(8,128)(2,1)S(1)}, u32[]{:S(2)}, u32[]{:S(2)}) collective-permute-start(bf16[512,192]{1,0:T(8,128)(2,1)S(1)} %get-tuple-element.217), channel_id=1, source_target_pairs={{0,8},{4,12},{8,0},{12,4},{1,9},{5,13},{9,1},{13,5},{2,10},{6,14},... | collective-permute-start | bytes 589832 | tf_op jit(solution)/shard_map/ppermute | solution.py:73
  88.3 23.2 %collective-permute-start.5 = (bf16[512,192]{1,0:T(8,128)(2,1)S(1)}, bf16[512,192]{1,0:T(8,128)(2,1)S(1)}, u32[]{:S(2)}, u32[]{:S(2)}) collective-permute-start(bf16[512,192]{1,0:T(8,128)(2,1)S(1)} %get-tuple-element.216), channel_id=1, source_target_pairs={{0,12},{4,8},{8,4},{12,0},{1,13},{5,9},{9,5},{13,1},{2,14},{6,10},... | collective-permute-start | bytes 589832 | tf_op jit(solution)/shard_map/ppermute | solution.py:73
  108.1 42.8 %collective-permute-start.10 = (bf16[128,768]{1,0:T(8,128)(2,1)S(1)}, bf16[128,768]{1,0:T(8,128)(2,1)S(1)}, u32[]{:S(2)}, u32[]{:S(2)}) collective-permute-start(bf16[128,768]{1,0:T(8,128)(2,1)S(1)} %copy-done.33), channel_id=1, source_target_pairs={{0,2},{1,3},{2,0},{3,1},{4,6},{5,7},{6,4},{7,5},{8,10},{9,11},{10,... | collective-permute-start | bytes 589832 | tf_op jit(solution)/shard_map/ppermute | solution.py:73
  111.5 39.6 %collective-permute-start.11 = (bf16[128,768]{1,0:T(8,128)(2,1)S(1)}, bf16[128,768]{1,0:T(8,128)(2,1)S(1)}, u32[]{:S(2)}, u32[]{:S(2)}) collective-permute-start(bf16[128,768]{1,0:T(8,128)(2,1)S(1)} %copy-done.32), channel_id=1, source_target_pairs={{0,3},{1,2},{2,1},{3,0},{4,7},{5,6},{6,5},{7,4},{8,11},{9,10},{10,... | collective-permute-start | bytes 589832 | tf_op jit(solution)/shard_map/ppermute | solution.py:73
  125.5 26.9 %collective-permute-start.6 = (bf16[128,768]{1,0:T(8,128)(2,1)S(1)}, bf16[128,768]{1,0:T(8,128)(2,1)S(1)}, u32[]{:S(2)}, u32[]{:S(2)}) collective-permute-start(bf16[128,768]{1,0:T(8,128)(2,1)S(1)} %get-tuple-element.245), channel_id=1, source_target_pairs={{0,1},{1,0},{2,3},{3,2},{4,5},{5,4},{6,7},{7,6},{8,9},{9,8},{10,11... | collective-permute-start | bytes 589832 | tf_op jit(solution)/shard_map/ppermute | solution.py:73
  150.9 54.6 %collective-permute-start.21 = (bf16[128,768]{1,0:T(8,128)(2,1)S(1)}, bf16[128,768]{1,0:T(8,128)(2,1)S(1)}, u32[]{:S(2)}, u32[]{:S(2)}) collective-permute-start(bf16[128,768]{1,0:T(8,128)(2,1)S(1)} %get-tuple-element.233), channel_id=1, source_target_pairs={{0,1},{1,0},{2,3},{3,2},{4,5},{5,4},{6,7},{7,6},{8,9},{9,8},{10,11... | collective-permute-start | bytes 589832 | tf_op jit(solution)/shard_map/ppermute | solution.py:73
  151.1 57.7 %collective-permute-start.22 = (bf16[128,768]{1,0:T(8,128)(2,1)S(1)}, bf16[128,768]{1,0:T(8,128)(2,1)S(1)}, u32[]{:S(2)}, u32[]{:S(2)}) collective-permute-start(bf16[128,768]{1,0:T(8,128)(2,1)S(1)} %get-tuple-element.232), channel_id=1, source_target_pairs={{0,2},{1,3},{2,0},{3,1},{4,6},{5,7},{6,4},{7,5},{8,10},{9,11},{10,... | collective-permute-start | bytes 589832 | tf_op jit(solution)/shard_map/ppermute | solution.py:73
  152.4 56.5 %collective-permute-start.23 = (bf16[128,768]{1,0:T(8,128)(2,1)S(1)}, bf16[128,768]{1,0:T(8,128)(2,1)S(1)}, u32[]{:S(2)}, u32[]{:S(2)}) collective-permute-start(bf16[128,768]{1,0:T(8,128)(2,1)S(1)} %get-tuple-element.231), channel_id=1, source_target_pairs={{0,3},{1,2},{2,1},{3,0},{4,7},{5,6},{6,5},{7,4},{8,11},{9,10},{10,... | collective-permute-start | bytes 589832 | tf_op jit(solution)/shard_map/ppermute | solution.py:73
  168.5 42.4 %collective-permute-start.18 = (bf16[128,768]{1,0:T(8,128)(2,1)S(1)}, bf16[128,768]{1,0:T(8,128)(2,1)S(1)}, u32[]{:S(2)}, u32[]{:S(2)}) collective-permute-start(bf16[128,768]{1,0:T(8,128)(2,1)S(1)} %get-tuple-element.236), channel_id=1, source_target_pairs={{0,1},{1,0},{2,3},{3,2},{4,5},{5,4},{6,7},{7,6},{8,9},{9,8},{10,11... | collective-permute-start | bytes 589832 | tf_op jit(solution)/shard_map/ppermute | solution.py:73
  168.5 42.4 %collective-permute-start.19 = (bf16[128,768]{1,0:T(8,128)(2,1)S(1)}, bf16[128,768]{1,0:T(8,128)(2,1)S(1)}, u32[]{:S(2)}, u32[]{:S(2)}) collective-permute-start(bf16[128,768]{1,0:T(8,128)(2,1)S(1)} %get-tuple-element.235), channel_id=1, source_target_pairs={{0,2},{1,3},{2,0},{3,1},{4,6},{5,7},{6,4},{7,5},{8,10},{9,11},{10,... | collective-permute-start | bytes 589832 | tf_op jit(solution)/shard_map/ppermute | solution.py:73
  208.8 50.2 %collective-permute-start.27 = (bf16[128,768]{1,0:T(8,128)(2,1)S(1)}, bf16[128,768]{1,0:T(8,128)(2,1)S(1)}, u32[]{:S(2)}, u32[]{:S(2)}) collective-permute-start(bf16[128,768]{1,0:T(8,128)(2,1)S(1)} %get-tuple-element.227), channel_id=1, source_target_pairs={{0,1},{1,0},{2,3},{3,2},{4,5},{5,4},{6,7},{7,6},{8,9},{9,8},{10,11... | collective-permute-start | bytes 589832 | tf_op jit(solution)/shard_map/ppermute | solution.py:73
  208.9 41.0 %collective-permute-start.33 = (f32[1,128]{1,0:T(1,128)S(1)}, f32[1,128]{1,0:T(1,128)S(1)}, u32[]{:S(2)}, u32[]{:S(2)}) collective-permute-start(f32[1,128]{1,0:T(1,128)S(1)} %get-tuple-element.261), channel_id=1, source_target_pairs={{0,1},{1,0},{2,3},{3,2},{4,5},{5,4},{6,7},{7,6},{8,9},{9,8},{10,11... | collective-permute-start | bytes 1544 | tf_op jit(solution)/shard_map/ppermute | solution.py:73
  210.9 39.5 %collective-permute-start.34 = (f32[1,128]{1,0:T(1,128)S(1)}, f32[1,128]{1,0:T(1,128)S(1)}, u32[]{:S(2)}, u32[]{:S(2)}) collective-permute-start(f32[1,128]{1,0:T(1,128)S(1)} %get-tuple-element.260), channel_id=1, source_target_pairs={{0,2},{1,3},{2,0},{3,1},{4,6},{5,7},{6,4},{7,5},{8,10},{9,11},{10,... | collective-permute-start | bytes 1544 | tf_op jit(solution)/shard_map/ppermute | solution.py:73
  211.0 42.6 %collective-permute-start.35 = (f32[1,128]{1,0:T(1,128)S(1)}, f32[1,128]{1,0:T(1,128)S(1)}, u32[]{:S(2)}, u32[]{:S(2)}) collective-permute-start(f32[1,128]{1,0:T(1,128)S(1)} %get-tuple-element.259), channel_id=1, source_target_pairs={{0,3},{1,2},{2,1},{3,0},{4,7},{5,6},{6,5},{7,4},{8,11},{9,10},{10,... | collective-permute-start | bytes 1544 | tf_op jit(solution)/shard_map/ppermute | solution.py:73
  257.1 29.7 %collective-permute-start.31 = (bf16[128,768]{1,0:T(8,128)(2,1)S(1)}, bf16[128,768]{1,0:T(8,128)(2,1)S(1)}, u32[]{:S(2)}, u32[]{:S(2)}) collective-permute-start(bf16[128,768]{1,0:T(8,128)(2,1)S(1)} %get-tuple-element.223), channel_id=1, source_target_pairs={{0,2},{1,3},{2,0},{3,1},{4,6},{5,7},{6,4},{7,5},{8,10},{9,11},{10,... | collective-permute-start | bytes 589832 | tf_op jit(solution)/shard_map/ppermute | solution.py:73
  259.0 27.8 %collective-permute-start.32 = (bf16[128,768]{1,0:T(8,128)(2,1)S(1)}, bf16[128,768]{1,0:T(8,128)(2,1)S(1)}, u32[]{:S(2)}, u32[]{:S(2)}) collective-permute-start(bf16[128,768]{1,0:T(8,128)(2,1)S(1)} %get-tuple-element.222), channel_id=1, source_target_pairs={{0,3},{1,2},{2,1},{3,0},{4,7},{5,6},{6,5},{7,4},{8,11},{9,10},{10,... | collective-permute-start | bytes 589832 | tf_op jit(solution)/shard_map/ppermute | solution.py:73
  271.4 153.3 %collective-permute-start.72 = (bf16[3,384,1024]{2,1,0:T(8,128)(2,1)}, bf16[3,384,1024]{2,1,0:T(8,128)(2,1)}, u32[]{:S(2)}, u32[]{:S(2)}) collective-permute-start(bf16[3,384,1024]{2,1,0:T(8,128)(2,1)} %dynamic-slice_bitcast_fusion.1), channel_id=1, source_target_pairs={{0,16},{16,0},{1,17},{17,1},{2,18},{18,2},{3,19},{19,3},{4,20},{20... | collective-permute-start | bytes 7077896 | tf_op jit(solution)/shard_map/ppermute | solution.py:73
  271.7 157.2 %collective-permute-start.77 = (bf16[3,384,1024]{2,1,0:T(8,128)(2,1)}, bf16[3,384,1024]{2,1,0:T(8,128)(2,1)}, u32[]{:S(2)}, u32[]{:S(2)}) collective-permute-start(bf16[3,384,1024]{2,1,0:T(8,128)(2,1)} %dynamic-slice_bitcast_fusion), channel_id=1, source_target_pairs={{0,16},{16,0},{1,17},{17,1},{2,18},{18,2},{3,19},{19,3},{4,20},{20... | collective-permute-start | bytes 7077896 | tf_op jit(solution)/shard_map/ppermute | solution.py:73
  307.7 61.0 %collective-permute-start.50 = (f32[31,768]{1,0:T(8,128)}, f32[31,768]{1,0:T(8,128)S(1)}, u32[]{:S(2)}, u32[]{:S(2)}) collective-permute-start(f32[31,768]{1,0:T(8,128)} %select_maximum_fusion), channel_id=1, source_target_pairs={{0,4},{4,0},{8,12},{12,8},{1,5},{5,1},{9,13},{13,9},{2,6},{6,2},{1... | collective-permute-start | bytes 285704 | tf_op jit(solution)/shard_map/ppermute | solution.py:73
  309.3 46.3 %collective-permute-start.63 = (bf16[192,768]{1,0:T(8,128)(2,1)}, bf16[192,768]{1,0:T(8,128)(2,1)}, u32[]{:S(2)}, u32[]{:S(2)}) collective-permute-start(bf16[192,768]{1,0:T(8,128)(2,1)} %convolution_convert_fusion.1), channel_id=1, source_target_pairs={{0,4},{4,0},{8,12},{12,8},{1,5},{5,1},{9,13},{13,9},{2,6},{6,2},{1... | collective-permute-start | bytes 884744 | tf_op jit(solution)/shard_map/ppermute | solution.py:73
  314.0 48.6 %collective-permute-start.62 = (bf16[192,768]{1,0:T(8,128)(2,1)}, bf16[192,768]{1,0:T(8,128)(2,1)}, u32[]{:S(2)}, u32[]{:S(2)}) collective-permute-start(bf16[192,768]{1,0:T(8,128)(2,1)} %convolution_convert_fusion.3), channel_id=1, source_target_pairs={{0,4},{4,0},{8,12},{12,8},{1,5},{5,1},{9,13},{13,9},{2,6},{6,2},{1... | collective-permute-start | bytes 884744 | tf_op jit(solution)/shard_map/ppermute | solution.py:73
  362.6 25.6 %collective-permute-start.42 = (bf16[512,576]{0,1:T(8,128)(2,1)}, bf16[512,576]{0,1:T(8,128)(2,1)}, u32[]{:S(2)}, u32[]{:S(2)}) collective-permute-start(bf16[512,576]{0,1:T(8,128)(2,1)} %copy.126), channel_id=1, source_target_pairs={{0,4},{4,0},{8,12},{12,8},{1,5},{5,1},{9,13},{13,9},{2,6},{6,2},{1... | collective-permute-start | bytes 1769480 | tf_op jit(solution)/shard_map/ppermute | solution.py:73
  387.2 22.9 %collective-permute-start.44 = (bf16[512,576]{0,1:T(8,128)(2,1)S(1)}, bf16[512,576]{0,1:T(8,128)(2,1)}, u32[]{:S(2)}, u32[]{:S(2)}) collective-permute-start(bf16[512,576]{0,1:T(8,128)(2,1)S(1)} %copy.128), channel_id=1, source_target_pairs={{0,12},{4,8},{8,4},{12,0},{1,13},{5,9},{9,5},{13,1},{2,14},{6,10},... | collective-permute-start | bytes 1769480 | tf_op jit(solution)/shard_map/ppermute | solution.py:73
  388.2 24.0 %collective-permute-start.66 = (bf16[96,768]{1,0:T(8,128)(2,1)S(1)}, bf16[96,768]{1,0:T(8,128)(2,1)S(1)}, u32[]{:S(2)}, u32[]{:S(2)}) collective-permute-start(bf16[96,768]{1,0:T(8,128)(2,1)S(1)} %fusion.14), channel_id=1, source_target_pairs={{0,1},{1,0},{2,3},{3,2},{4,5},{5,4},{6,7},{7,6},{8,9},{9,8},{10,11... | collective-permute-start | bytes 442376 | tf_op jit(solution)/shard_map/ppermute | solution.py:73
  401.8 33.1 %collective-permute-start.51 = (f32[31,768]{1,0:T(8,128)S(1)}, f32[31,768]{1,0:T(8,128)S(1)}, u32[]{:S(2)}, u32[]{:S(2)}) collective-permute-start(f32[31,768]{1,0:T(8,128)S(1)} %fusion.22), channel_id=1, source_target_pairs={{0,8},{4,12},{8,0},{12,4},{1,9},{5,13},{9,1},{13,5},{2,10},{6,14},... | collective-permute-start | bytes 285704 | tf_op jit(solution)/shard_map/ppermute | solution.py:73
  410.1 24.2 %collective-permute-start.56 = (bf16[288,768]{1,0:T(8,128)(2,1)S(1)}, bf16[288,768]{1,0:T(8,128)(2,1)S(1)}, u32[]{:S(2)}, u32[]{:S(2)}) collective-permute-start(bf16[288,768]{1,0:T(8,128)(2,1)S(1)} %fusion.13), channel_id=1, source_target_pairs={{0,1},{1,0},{2,3},{3,2},{4,5},{5,4},{6,7},{7,6},{8,9},{9,8},{10,11... | collective-permute-start | bytes 1327112 | tf_op jit(solution)/shard_map/ppermute | solution.py:73
  428.9 28.9 %collective-permute-start.73 = (bf16[3,192,1024]{2,1,0:T(8,128)(2,1)S(1)}, bf16[3,192,1024]{2,1,0:T(8,128)(2,1)S(1)}, u32[]{:S(2)}, u32[]{:S(2)}) collective-permute-start(bf16[3,192,1024]{2,1,0:T(8,128)(2,1)S(1)} %dynamic-slice_bitcast_fusion.3), channel_id=1, source_target_pairs={{0,8},{4,12},{8,0},{12,4},{1,9},{5,13},{9,1},{13,5},{2,10},{6,14},... | collective-permute-start | bytes 3538952 | tf_op jit(solution)/shard_map/ppermute | solution.py:73
  434.3 47.8 %collective-permute-start.78 = (bf16[3,192,1024]{2,1,0:T(8,128)(2,1)S(1)}, bf16[3,192,1024]{2,1,0:T(8,128)(2,1)S(1)}, u32[]{:S(2)}, u32[]{:S(2)}) collective-permute-start(bf16[3,192,1024]{2,1,0:T(8,128)(2,1)S(1)} %dynamic-slice_bitcast_fusion.2), channel_id=1, source_target_pairs={{0,8},{4,12},{8,0},{12,4},{1,9},{5,13},{9,1},{13,5},{2,10},{6,14},... | collective-permute-start | bytes 3538952 | tf_op jit(solution)/shard_map/ppermute | solution.py:73
  434.9 22.1 %collective-permute-start.57 = (bf16[288,768]{1,0:T(8,128)(2,1)S(1)}, bf16[288,768]{1,0:T(8,128)(2,1)S(1)}, u32[]{:S(2)}, u32[]{:S(2)}) collective-permute-start(bf16[288,768]{1,0:T(8,128)(2,1)S(1)} %add_convert_fusion.1), channel_id=1, source_target_pairs={{0,2},{1,3},{2,0},{3,1},{4,6},{5,7},{6,4},{7,5},{8,10},{9,11},{10,... | collective-permute-start | bytes 1327112 | tf_op jit(solution)/shard_map/ppermute | solution.py:73
  437.4 47.5 %collective-permute-start.86 = (f32[4,3]{1,0:T(4,128)S(1)}, f32[4,3]{1,0:T(4,128)S(1)}, u32[]{:S(2)}, u32[]{:S(2)}) collective-permute-start(f32[4,3]{1,0:T(4,128)S(1)} %copy-done.48), channel_id=1, source_target_pairs={{0,2},{1,3},{2,0},{3,1},{4,6},{5,7},{6,4},{7,5},{8,10},{9,11},{10,... | collective-permute-start | bytes 152 | tf_op jit(solution)/shard_map/ppermute | solution.py:73
  438.0 48.0 %collective-permute-start.15 = (bf16[128,768]{1,0:T(8,128)(2,1)S(1)}, bf16[128,768]{1,0:T(8,128)(2,1)S(1)}, u32[]{:S(2)}, u32[]{:S(2)}) collective-permute-start(bf16[128,768]{1,0:T(8,128)(2,1)S(1)} %copy-done.35), channel_id=1, source_target_pairs={{0,1},{1,0},{2,3},{3,2},{4,5},{5,4},{6,7},{7,6},{8,9},{9,8},{10,11... | collective-permute-start | bytes 589832 | tf_op jit(solution)/shard_map/ppermute | solution.py:73
  456.9 30.7 %collective-permute-start.16 = (bf16[128,768]{1,0:T(8,128)(2,1)S(1)}, bf16[128,768]{1,0:T(8,128)(2,1)S(1)}, u32[]{:S(2)}, u32[]{:S(2)}) collective-permute-start(bf16[128,768]{1,0:T(8,128)(2,1)S(1)} %copy-done.34), channel_id=1, source_target_pairs={{0,2},{1,3},{2,0},{3,1},{4,6},{5,7},{6,4},{7,5},{8,10},{9,11},{10,... | collective-permute-start | bytes 589832 | tf_op jit(solution)/shard_map/ppermute | solution.py:73
  457.7 35.2 %collective-permute-start.58 = (bf16[288,768]{1,0:T(8,128)(2,1)S(1)}, bf16[288,768]{1,0:T(8,128)(2,1)S(1)}, u32[]{:S(2)}, u32[]{:S(2)}) collective-permute-start(bf16[288,768]{1,0:T(8,128)(2,1)S(1)} %add_convert_fusion), channel_id=1, source_target_pairs={{0,16},{16,0},{1,17},{17,1},{2,18},{18,2},{3,19},{19,3},{4,20},{20... | collective-permute-start | bytes 1327112 | tf_op jit(solution)/shard_map/ppermute | solution.py:73
  491.5 103.4 %collective-permute-start.75 = (bf16[3,192,1024]{2,1,0:T(8,128)(2,1)S(1)}, bf16[3,192,1024]{2,1,0:T(8,128)(2,1)S(1)}, u32[]{:S(2)}, u32[]{:S(2)}) collective-permute-start(bf16[3,192,1024]{2,1,0:T(8,128)(2,1)S(1)} %fusion.3.refs_0_), channel_id=1, source_target_pairs={{0,8},{4,12},{8,0},{12,4},{1,9},{5,13},{9,1},{13,5},{2,10},{6,14},... | collective-permute-start | bytes 3538952 | tf_op jit(solution)/shard_map/ppermute | solution.py:73
  492.9 102.1 %collective-permute-start.80 = (bf16[3,192,1024]{2,1,0:T(8,128)(2,1)S(1)}, bf16[3,192,1024]{2,1,0:T(8,128)(2,1)}, u32[]{:S(2)}, u32[]{:S(2)}) collective-permute-start(bf16[3,192,1024]{2,1,0:T(8,128)(2,1)S(1)} %fusion.2.refs_4_), channel_id=1, source_target_pairs={{0,8},{4,12},{8,0},{12,4},{1,9},{5,13},{9,1},{13,5},{2,10},{6,14},... | collective-permute-start | bytes 3538952 | tf_op jit(solution)/shard_map/ppermute | solution.py:73
  494.2 47.4 %collective-permute-start.52 = (f32[31,768]{1,0:T(8,128)S(1)}, f32[31,768]{1,0:T(8,128)S(1)}, u32[]{:S(2)}, u32[]{:S(2)}) collective-permute-start(f32[31,768]{1,0:T(8,128)S(1)} %add.130), channel_id=1, source_target_pairs={{0,16},{16,0},{1,17},{17,1},{2,18},{18,2},{3,19},{19,3},{4,20},{20... | collective-permute-start | bytes 285704 | tf_op jit(solution)/shard_map/ppermute | solution.py:73
  506.9 34.6 %collective-permute-start.46 = (f32[1,768]{1,0:T(1,128)S(1)}, f32[1,768]{1,0:T(1,128)S(1)}, u32[]{:S(2)}, u32[]{:S(2)}) collective-permute-start(f32[1,768]{1,0:T(1,128)S(1)} %add.124), channel_id=1, source_target_pairs={{0,8},{4,12},{8,0},{12,4},{1,9},{5,13},{9,1},{13,5},{2,10},{6,14},... | collective-permute-start | bytes 9224 | tf_op jit(solution)/shard_map/ppermute | solution.py:73
  507.9 62.9 %collective-permute-start.69 = (bf16[192,768]{1,0:T(8,128)(2,1)S(1)}, bf16[192,768]{1,0:T(8,128)(2,1)S(1)}, u32[]{:S(2)}, u32[]{:S(2)}) collective-permute-start(bf16[192,768]{1,0:T(8,128)(2,1)S(1)} %pad_maximum_fusion.1.refs_0_), channel_id=1, source_target_pairs={{0,4},{4,0},{8,12},{12,8},{1,5},{5,1},{9,13},{13,9},{2,6},{6,2},{1... | collective-permute-start | bytes 884744 | tf_op jit(solution)/shard_map/ppermute | solution.py:73
  541.6 53.0 %collective-permute-start.59 = (bf16[576,768]{1,0:T(8,128)(2,1)}, bf16[576,768]{1,0:T(8,128)(2,1)S(1)}, u32[]{:S(2)}, u32[]{:S(2)}) collective-permute-start(bf16[576,768]{1,0:T(8,128)(2,1)} %pad_maximum_fusion.refs_0_), channel_id=1, source_target_pairs={{0,4},{4,0},{8,12},{12,8},{1,5},{5,1},{9,13},{13,9},{2,6},{6,2},{1... | collective-permute-start | bytes 2654216 | tf_op jit(solution)/shard_map/ppermute | solution.py:73
  569.3 26.8 %collective-permute-start.60 = (bf16[576,768]{1,0:T(8,128)(2,1)}, bf16[576,768]{1,0:T(8,128)(2,1)}, u32[]{:S(2)}, u32[]{:S(2)}) collective-permute-start(bf16[576,768]{1,0:T(8,128)(2,1)} %pad_maximum_fusion.refs_0_), channel_id=1, source_target_pairs={{0,8},{4,12},{8,0},{12,4},{1,9},{5,13},{9,1},{13,5},{2,10},{6,14},... | collective-permute-start | bytes 2654216 | tf_op jit(solution)/shard_map/ppermute | solution.py:73
  594.4 29.7 %collective-permute-start.74 = (bf16[3,192,1024]{2,1,0:T(8,128)(2,1)S(1)}, bf16[3,192,1024]{2,1,0:T(8,128)(2,1)}, u32[]{:S(2)}, u32[]{:S(2)}) collective-permute-start(bf16[3,192,1024]{2,1,0:T(8,128)(2,1)S(1)} %fusion.3.refs_0_), channel_id=1, source_target_pairs={{0,4},{4,0},{8,12},{12,8},{1,5},{5,1},{9,13},{13,9},{2,6},{6,2},{1... | collective-permute-start | bytes 3538952 | tf_op jit(solution)/shard_map/ppermute | solution.py:73
  594.5 29.5 %collective-permute-start.79 = (bf16[3,192,1024]{2,1,0:T(8,128)(2,1)S(1)}, bf16[3,192,1024]{2,1,0:T(8,128)(2,1)}, u32[]{:S(2)}, u32[]{:S(2)}) collective-permute-start(bf16[3,192,1024]{2,1,0:T(8,128)(2,1)S(1)} %fusion.2.refs_4_), channel_id=1, source_target_pairs={{0,4},{4,0},{8,12},{12,8},{1,5},{5,1},{9,13},{13,9},{2,6},{6,2},{1... | collective-permute-start | bytes 3538952 | tf_op jit(solution)/shard_map/ppermute | solution.py:73
  594.9 29.2 %collective-permute-start.76 = (bf16[3,192,1024]{2,1,0:T(8,128)(2,1)S(1)}, bf16[3,192,1024]{2,1,0:T(8,128)(2,1)}, u32[]{:S(2)}, u32[]{:S(2)}) collective-permute-start(bf16[3,192,1024]{2,1,0:T(8,128)(2,1)S(1)} %collective-permute-done.75.refs_2_), channel_id=1, source_target_pairs={{0,4},{4,0},{8,12},{12,8},{1,5},{5,1},{9,13},{13,9},{2,6},{6,2},{1... | collective-permute-start | bytes 3538952 | tf_op jit(solution)/shard_map/ppermute | solution.py:73
  595.4 28.6 %collective-permute-start.81 = (bf16[3,192,1024]{2,1,0:T(8,128)(2,1)}, bf16[3,192,1024]{2,1,0:T(8,128)(2,1)}, u32[]{:S(2)}, u32[]{:S(2)}) collective-permute-start(bf16[3,192,1024]{2,1,0:T(8,128)(2,1)} %collective-permute-done.80.refs_6_), channel_id=1, source_target_pairs={{0,4},{4,0},{8,12},{12,8},{1,5},{5,1},{9,13},{13,9},{2,6},{6,2},{1... | collective-permute-start | bytes 3538952 | tf_op jit(solution)/shard_map/ppermute | solution.py:73
  (107 other events, 1911.4 us)

commit v3 on v1

v3 whole, which is shorter than its diff:
```python
import functools

import jax
import jax.numpy as jnp
from jax import lax
from jax.experimental import pallas as pl
from jax.experimental.pallas import tpu as pltpu
from jax.sharding import PartitionSpec as P

HEADS = 12
CAP = 128

norm_eps = 1e-05
clip_limit = 3.0
low_start = -1e30
mask_fill = -3e38
highest = lax.Precision.HIGHEST
NN = (((1,), (0,)), ((), ()))
NT = (((1,), (1,)), ((), ()))
TN = (((0,), (0,)), ((), ()))
f32 = jnp.float32
bf16 = jnp.bfloat16
MESH = pl.DeviceIdType.MESH


def mm(left, right, dims=NN):
    return lax.dot_general(left, right, dims, preferred_element_type=f32)


def mm_full(left, right, dims=NN):
    return lax.dot_general(left, right, dims, precision=highest, preferred_element_type=f32)


def shape_of(shape, dtype):
    return jax.ShapeDtypeStruct(shape, dtype)


def whole(array):
    rank = len(array.shape)
    return pl.BlockSpec(array.shape, lambda *_: (0,) * rank)


def cost(flops, moved, exps=0):
    return pl.CostEstimate(flops=int(flops), bytes_accessed=int(moved), transcendentals=int(exps))


def run(body, grid, inputs, outputs, scratch=(), meta=None, flops=0, moved=0, exps=0, aliases=None, talks=None):
    prefetch = 0 if meta is None else 1
    args = ([] if meta is None else [meta]) + [a for a, _ in inputs]
    return pl.pallas_call(
        body,
        out_shape=[o for o, _ in outputs],
        grid_spec=pltpu.PrefetchScalarGridSpec(
            num_scalar_prefetch=prefetch,
            grid=grid,
            in_specs=[s for _, s in inputs],
            out_specs=[s for _, s in outputs],
            scratch_shapes=list(scratch),
        ),
        compiler_params=pltpu.CompilerParams(
            dimension_semantics=("arbitrary",) * len(grid),
            vmem_limit_bytes=60 * 1024 * 1024,
            collective_id=talks,
            has_side_effects=talks is not None,
        ),
        cost_estimate=cost(flops, moved, exps),
        input_output_aliases={} if aliases is None else aliases,
    )(*args)


def swap(value, axis, distance):
    count = lax.axis_size(axis)
    return lax.ppermute(value, axis, [(i, i ^ distance) for i in range(count)])


def flip(value, bits):
    bit = 1
    while bit <= bits:
        if bits & bit:
            value = value + bit - 2 * bit * lax.rem(lax.div(value, bit), 2)
        bit *= 2
    return value


def powers(axis):
    found, bit = [], 1
    while bit < lax.axis_size(axis):
        found.append(bit)
        bit *= 2
    return found


def slot_peer(r, count, exp_now, me):
    return {"exp": flip(exp_now, r // count), "ctx": flip(me, 2 * (r % count))}


def slot_swap(value, r, count):
    groups = lax.axis_size("exp")
    total = groups * lax.axis_size("ctx")
    apart = 2 * (r % count) * groups + r // count
    return lax.ppermute(value, ("ctx", "exp"), [(i, i ^ apart) for i in range(total)])


def remote(src, dst, sent, arrived, peer):
    return pltpu.make_async_remote_copy(
        src_ref=src, dst_ref=dst, send_sem=sent, recv_sem=arrived,
        device_id=peer, device_id_type=MESH,
    )


def greet(peers):
    barrier = pltpu.get_barrier_semaphore()
    for peer in peers:
        pl.semaphore_signal(barrier, inc=1, device_id=peer, device_id_type=MESH)
    return lambda: pl.semaphore_wait(barrier, len(peers))


anywhere = pl.BlockSpec(memory_space=pl.ANY)
scalars = pl.BlockSpec(memory_space=pltpu.SMEM)
vector = pl.BlockSpec(memory_space=pltpu.VMEM)
dma = pltpu.SemaphoreType.DMA


def gather_near(value, axis):
    count = lax.axis_size(axis)
    found = {0: value}
    bit = count // 2
    while bit:
        for have in list(found):
            found[have | bit] = swap(found[have], axis, bit)
        bit //= 2
    return [found[j] for j in range(count)]


def add_low(*terms):
    total = terms[0].astype(f32)
    for term in terms[1:]:
        total = total + term.astype(f32)
    return total.astype(bf16)


def project(turn, rows_low, gain, weights_t, meta, earlier, group_rows, tile, layout):
    row_count, width = rows_low.shape
    per_group = weights_t.shape[2]
    head_width = width // HEADS
    heads = per_group // head_width
    steps = row_count // tile
    scale = head_width**-0.5

    def body(meta_ref, x_ref, gain_ref, w_ref, *refs):
        q_ref, k_ref, v_ref, kt_ref, vt_ref, h_ref = refs[-6:]
        x = x_ref[...].astype(f32)
        inverse = lax.rsqrt(jnp.mean(x * x, axis=1, keepdims=True) + norm_eps)
        low = (x * inverse * gain_ref[...]).astype(bf16)
        h_ref[...] = low
        q = mm(low, w_ref[0, 0], NT).astype(bf16) * jnp.asarray(scale, bf16)
        k = mm(low, w_ref[1, 0], NT).astype(bf16)
        v = mm(low, w_ref[2, 0], NT).astype(bf16)
        for h in range(heads):
            part = slice(h * head_width, (h + 1) * head_width)
            q_ref[h] = q[:, part]
            k_ref[h] = k[:, part]
            v_ref[h] = v[:, part]
        kt_ref[...] = mm(w_ref[1, 0], low, NT).astype(bf16)
        vt_ref[...] = mm(w_ref[2, 0], low, NT).astype(bf16)

    by_head = shape_of((heads, group_rows, head_width), bf16)
    by_column = shape_of((per_group, group_rows), bf16)
    hidden = shape_of((group_rows, width), bf16)
    head_spec = pl.BlockSpec((heads, tile, head_width), lambda i, m: (0, block_place(m, turn * steps + i, steps, layout), 0))
    column_spec = pl.BlockSpec((per_group, tile), lambda i, m: (0, block_place(m, turn * steps + i, steps, layout)))
    hidden_spec = pl.BlockSpec((tile, width), lambda i, m: (turn * steps + i, 0))
    inputs = [
        (rows_low, pl.BlockSpec((tile, width), lambda i, m: (i, 0))),
        (gain, pl.BlockSpec((1, width), lambda i, m: (0, 0))),
        (weights_t, pl.BlockSpec((3, 1, per_group, width), lambda i, m: (0, m[0], 0, 0))),
    ]
    aliases = None
    if earlier is not None:
        inputs += [(a, pl.BlockSpec(memory_space=pl.ANY)) for a in earlier]
        aliases = {4 + n: n for n in range(6)}
    return run(
        body,
        (steps,),
        inputs,
        [(by_head, head_spec)] * 3 + [(by_column, column_spec)] * 2 + [(hidden, hidden_spec)],
        meta=meta,
        flops=2 * row_count * width * per_group * 5,
        moved=row_count * width * 8 + weights_t.size // 2,
        aliases=aliases,
    )


def block_place(meta_ref, block, per_member, layout):
    member = meta_ref[0] ^ (block // per_member)
    return meta_ref[layout["order"] + member * per_member + block % per_member]


def document_start(meta_ref, position, layout):
    start = jnp.zeros_like(position)
    end = jnp.int32(0)
    for s in range(layout["sequences"]):
        end = end + meta_ref[layout["lengths"] + s]
        start = jnp.where(position >= end, end, start)
    return start


def block_range(meta_ref, query_block, key_block, rows, layout):
    q_first = query_block * rows
    k_first = key_block * rows
    begin = document_start(meta_ref, q_first, layout)
    begin_last = document_start(meta_ref, q_first + rows - 1, layout)
    needed = (k_first <= q_first) & (k_first + rows - 1 >= begin)
    full = (k_first < q_first) & (k_first >= begin_last)
    return q_first, k_first, needed, full


def allowed_pairs(meta_ref, q_first, k_first, rows, layout):
    q_pos = q_first + lax.broadcasted_iota(jnp.int32, (1, rows), 1)
    k_pos = k_first + lax.broadcasted_iota(jnp.int32, (rows, 1), 0)
    return (k_pos <= q_pos) & (k_pos >= document_start(meta_ref, q_pos, layout))


def attend(meta, q, k, vt, rows, layout):
    heads, group_rows, head_width = q.shape
    blocks = group_rows // rows
    width = heads * head_width

    def body(meta_ref, q_ref, k_ref, vt_ref, o_ref, ot_ref, lse_ref, top_ref, m_ref, l_ref, a_ref):
        i = pl.program_id(0)
        m_ref[...] = jnp.full_like(m_ref, low_start)
        l_ref[...] = jnp.zeros_like(l_ref)
        a_ref[...] = jnp.zeros_like(a_ref)

        def one(j, _):
            q_first, k_first, needed, full = block_range(meta_ref, i, j, rows, layout)
            at = pl.multiple_of(j * rows, rows)

            def step(masked):
                if masked:
                    allowed = allowed_pairs(meta_ref, q_first, k_first, rows, layout)
                for h in range(heads):
                    part = slice(h * head_width, (h + 1) * head_width)
                    s = mm(k_ref[h, pl.ds(at, rows), :], q_ref[h], NT)
                    if masked:
                        s = jnp.where(allowed, s, mask_fill)
                    old = m_ref[h]
                    new = jnp.maximum(old, jnp.max(s, axis=0, keepdims=True))
                    shrink = jnp.exp(old - new)
                    p = jnp.exp(s - new)
                    m_ref[h] = new
                    l_ref[h] = l_ref[h] * shrink + jnp.sum(p, axis=0, keepdims=True)
                    a_ref[part, :] = a_ref[part, :] * shrink + mm(
                        vt_ref[part, pl.ds(at, rows)], p.astype(bf16)
                    )

            @pl.when(full)
            def _():
                step(False)

            @pl.when(needed & jnp.logical_not(full))
            def _():
                step(True)

            return 0

        lax.fori_loop(0, i + 1, one, 0)
        for h in range(heads):
            part = slice(h * head_width, (h + 1) * head_width)
            ot_ref[part, :] = a_ref[part, :] / l_ref[h]
            lse_ref[pl.ds(h, 1), :] = m_ref[h] + jnp.log(l_ref[h])
            top_ref[pl.ds(h, 1), :] = m_ref[h]
        o_ref[...] = jnp.transpose(ot_ref[...]).astype(bf16)

    row = shape_of((heads, group_rows), f32)
    row_spec = pl.BlockSpec((heads, rows), lambda i, m: (0, i))
    return run(
        body,
        (blocks,),
        [
            (q, pl.BlockSpec((heads, rows, head_width), lambda i, m: (0, i, 0))),
            (k, whole(k)),
            (vt, whole(vt)),
        ],
        [
            (
                shape_of((group_rows, width), bf16),
                pl.BlockSpec((rows, width), lambda i, m: (m[layout["inverse"] + i], 0)),
            ),
            (shape_of((width, group_rows), f32), pl.BlockSpec((width, rows), lambda i, m: (0, i))),
            (row, row_spec),
            (row, row_spec),
        ],
        scratch=[
            pltpu.VMEM((heads, 1, rows), f32),
            pltpu.VMEM((heads, 1, rows), f32),
            pltpu.VMEM((width, rows), f32),
        ],
        meta=meta,
        flops=2 * 2 * group_rows * group_rows * width,
        moved=group_rows * width * 14,
        exps=group_rows * group_rows * heads // 2,
    )


def attend_back(meta, q, k, v, kt, grad, ot, lse, rows, layout):
    heads, group_rows, head_width = q.shape
    blocks = group_rows // rows
    width = heads * head_width
    scale = head_width**-0.5
    members = len(grad)
    per = grad[0].shape[0] // rows

    def body(meta_ref, q_ref, k_ref, v_ref, kt_ref, *refs):
        grads = refs[:members]
        ot_ref, lse_ref, out_ref, dk_ref, dv_ref, dq_ref, g_ref, delta_ref = refs[members:]
        i = pl.program_id(0)

        @pl.when(i == 0)
        def _():
            dk_ref[...] = jnp.zeros_like(dk_ref)
            dv_ref[...] = jnp.zeros_like(dv_ref)

        for n in range(members):

            @pl.when(meta_ref[layout["inverse"] + i] // per == n)
            def _():
                g = grads[n][...]
                for h in range(heads):
                    g_ref[h] = g[:, h * head_width : (h + 1) * head_width]
                product = jnp.transpose(g.astype(f32)) * ot_ref[...]
                for h in range(heads):
                    part = slice(h * head_width, (h + 1) * head_width)
                    delta_ref[h] = jnp.sum(product[part, :], axis=0, keepdims=True)

        dq_ref[...] = jnp.zeros_like(dq_ref)

        def one(j, _):
            q_first, k_first, needed, full = block_range(meta_ref, i, j, rows, layout)
            at = pl.multiple_of(j * rows, rows)

            def step(masked):
                if masked:
                    allowed = allowed_pairs(meta_ref, q_first, k_first, rows, layout)
                for h in range(heads):
                    part = slice(h * head_width, (h + 1) * head_width)
                    s = mm(k_ref[h, pl.ds(at, rows), :], q_ref[h], NT)
                    if masked:
                        s = jnp.where(allowed, s, mask_fill)
                    p = jnp.exp(s - lse_ref[pl.ds(h, 1), :])
                    dp = mm(v_ref[h, pl.ds(at, rows), :], g_ref[h], NT)
                    ds = (p * (dp - delta_ref[h])).astype(bf16)
                    dv_ref[h, pl.ds(at, rows), :] += mm(p.astype(bf16), g_ref[h])
                    dk_ref[h, pl.ds(at, rows), :] += mm(ds, q_ref[h])
                    dq_ref[part, :] += mm(kt_ref[part, pl.ds(at, rows)], ds)

            @pl.when(full)
            def _():
                step(False)

            @pl.when(needed & jnp.logical_not(full))
            def _():
                step(True)

            return 0

        lax.fori_loop(0, i + 1, one, 0)
        here = pl.multiple_of(meta_ref[layout["inverse"] + i] * rows, rows)
        out_ref[pl.ds(here, rows), 0:width] = (jnp.transpose(dq_ref[...]) * scale).astype(bf16)

        @pl.when(i == blocks - 1)
        def _():
            def store(b, _):
                spot = pl.multiple_of(b * rows, rows)
                there = pl.multiple_of(meta_ref[layout["inverse"] + b] * rows, rows)
                out_ref[pl.ds(there, rows), width : 3 * width] = jnp.concatenate(
                    [dk_ref[h, pl.ds(spot, rows), :] for h in range(heads)]
                    + [dv_ref[h, pl.ds(spot, rows), :] for h in range(heads)],
                    axis=1,
                ).astype(bf16)
                return 0

            lax.fori_loop(0, blocks, store, 0)

    grad_specs = [
        pl.BlockSpec((rows, width), lambda i, m, n=n: (jnp.clip(m[layout["inverse"] + i] - n * per, 0, per - 1), 0))
        for n in range(members)
    ]
    out = shape_of((group_rows, 3 * width), bf16)
    return run(
        body,
        (blocks,),
        [
            (q, pl.BlockSpec((heads, rows, head_width), lambda i, m: (0, i, 0))),
            (k, whole(k)),
            (v, whole(v)),
            (kt, whole(kt)),
        ]
        + list(zip(grad, grad_specs))
        + [
            (ot, pl.BlockSpec((width, rows), lambda i, m: (0, i))),
            (lse, pl.BlockSpec((heads, rows), lambda i, m: (0, i))),
        ],
        [(out, whole(out))],
        scratch=[
            pltpu.VMEM((heads, group_rows, head_width), f32),
            pltpu.VMEM((heads, group_rows, head_width), f32),
            pltpu.VMEM((width, rows), f32),
            pltpu.VMEM((heads, rows, head_width), bf16),
            pltpu.VMEM((heads, 1, rows), f32),
        ],
        meta=meta,
        flops=5 * 2 * group_rows * group_rows * width,
        moved=group_rows * width * 24,
        exps=group_rows * group_rows * heads // 2,
    )[0]


def slot_targets(route_ids, expert_count, local_experts, mine, side):
    rows = route_ids.shape[0]
    experts = jnp.arange(expert_count, dtype=jnp.int32)
    hits = route_ids[:, :, None] == experts[None, None, :]
    hit = jnp.any(hits, axis=1)
    order = lax.broadcasted_iota(jnp.int32, (rows, rows), 0)
    other = lax.broadcasted_iota(jnp.int32, (rows, rows), 1)
    ahead = mm((other < order).astype(bf16), hit.astype(bf16)).astype(jnp.int32)
    rank = jnp.sum(jnp.where(hits, ahead[:, None, :], 0), axis=2)
    near = ((route_ids // local_experts) ^ mine) * local_experts + (
        (route_ids % local_experts) ^ side
    )
    return jnp.where(route_ids < expert_count, near * CAP + rank, -1)


def slot_choice(first, count, target_ref):
    rows = target_ref.shape[1]
    ids = first + lax.broadcasted_iota(jnp.int32, (count, rows), 0)
    match = (ids == target_ref[0:1, :]) | (ids == target_ref[1:2, :])
    return jnp.where(match, 1.0, 0.0).astype(bf16)


def dispatch(target_rows, source, places):
    rows, width = source.shape

    def body(target_ref, source_ref, out_ref):
        choice = slot_choice(pl.program_id(0) * CAP, CAP, target_ref)
        out_ref[0] = mm(choice, source_ref[...]).astype(bf16)

    return run(
        body,
        (places,),
        [(target_rows, whole(target_rows)), (source, whole(source))],
        [
            (
                shape_of((places, CAP, width), bf16),
                pl.BlockSpec((1, CAP, width), lambda r: (r, 0, 0)),
            )
        ],
        flops=2 * rows * width * places * CAP,
        moved=(rows + places * CAP) * width * 2,
    )[0]


def token_front(
    x, o, w_out, gain, w_router, previous, w_carry, target_rows, grad, routes, logit_w, vectors, local
):
    rows, width = x.shape
    members, columns = w_out.shape[0], w_out.shape[1]
    expert_all = w_router.shape[1]
    groups = lax.axis_size("exp")
    places = groups * local
    expert_count = places
    kinds = vectors.shape[0]
    tile = 128

    def body(*refs):
        (x_ref, o_hbm, w_ref, gain_ref, router_ref, prev_ref, carry_ref, target_ref) = refs[:8]
        dy_ref, route_ref, lw_ref, vec_ref = refs[8:12]
        x1_ref, h2_ref, prob_ref, rows_out, gates_out, base_ref, dh_ref, dgate_ref, sums_ref = refs[12:21]
        o_near, low, split, packed, arrived, gate_mine, gate_near = refs[21:28]
        o_s, o_r, t_s, t_r, g_s, g_r, out_sem = refs[28:]
        me, exp_now = lax.axis_index("ctx"), lax.axis_index("exp")
        side = lax.div(me, 2)
        peers = [{"ctx": flip(me, j)} for j in range(1, members)]
        peers += [slot_peer(r, local, exp_now, me) for r in range(local, places)]
        ready = greet(peers)

        def o_copy(j):
            src = o_hbm.at[pl.ds(j * rows, rows), :]
            if j == 0:
                return pltpu.make_async_copy(src, o_near.at[0], o_r.at[0])
            return remote(src, o_near.at[j], o_s.at[j], o_r.at[j], {"ctx": flip(me, j)})

        def row_copy(r):
            return remote(
                packed.at[r], arrived.at[r], t_s.at[r], t_r.at[r], slot_peer(r, local, exp_now, me)
            )

        def gate_copy(r):
            return remote(
                gate_mine.at[r], gate_near.at[r], g_s.at[r], g_r.at[r],
                slot_peer(r, local, exp_now, me),
            )

        o_copy(0).start()
        ready()
        for j in range(1, members):
            o_copy(j).start()
        for j in range(members):
            o_copy(j).wait()

        def front_rows(t, _):
            here = pl.ds(pl.multiple_of(t * tile, tile), tile)
            total = x_ref[here, :].astype(f32)
            for j in range(members):
                total = total + mm(o_near[j, here, :], w_ref[flip(me, j)])
            x1_ref[here, :] = total
            inverse = lax.rsqrt(jnp.mean(total * total, axis=1, keepdims=True) + norm_eps)
            h2 = total * inverse * gain_ref[...]
            h2_ref[here, :] = h2
            logits = mm_full(h2, router_ref[...]) + mm_full(prev_ref[here, :], carry_ref[...])
            shifted = jnp.exp(logits - jnp.max(logits, axis=1, keepdims=True))
            prob = shifted / jnp.sum(shifted, axis=1, keepdims=True)
            prob_ref[here, :] = prob
            low[here, :] = h2.astype(bf16)
            top = prob.astype(bf16)
            rest = prob - top.astype(f32)
            middle = rest.astype(bf16)
            split[0, here, :] = top
            split[1, here, :] = middle
            split[2, here, :] = (rest - middle.astype(f32)).astype(bf16)
            return 0

        lax.fori_loop(0, rows // tile, front_rows, 0)
        diagonal = lax.broadcasted_iota(jnp.int32, (CAP, CAP), 0) == lax.broadcasted_iota(
            jnp.int32, (CAP, CAP), 1
        )
        lanes = lax.broadcasted_iota(jnp.int32, (CAP, expert_all), 1)
        for r in list(range(1, places)) + [0]:
            choice = slot_choice(r * CAP, CAP, target_ref)
            packed[r] = mm(choice, low[...]).astype(bf16)
            picked = mm(choice, split[0]) + mm(choice, split[1]) + mm(choice, split[2])
            expert = flip(exp_now, r // local) * local + flip(side, r % local)
            column = jnp.sum(jnp.where(lanes == expert, picked, 0.0), axis=1, keepdims=True)
            gate_mine[r] = jnp.sum(jnp.where(diagonal, column, 0.0), axis=0, keepdims=True)
            last = r - 1 if r else places - 1
            if last:
                row_copy(last).start()
                gate_copy(last).start()

        def own_copy(n):
            src, dst = (packed, rows_out) if n == 0 else (gate_mine, gates_out)
            return pltpu.make_async_copy(src.at[0], dst.at[0], out_sem.at[n])

        own_copy(0).start()
        own_copy(1).start()

        def zero_rows(t, _):
            here = pl.ds(pl.multiple_of(t * tile, tile), tile)
            h2 = h2_ref[here, :]
            dy = dy_ref[here, :].astype(f32)
            prob_now = prob_ref[here, :]
            classes = lax.broadcasted_iota(jnp.int32, (tile, expert_all), 1)
            chosen = route_ref[here, :]
            ids = [chosen[:, c : c + 1] for c in range(2)]
            gates = [
                jnp.sum(jnp.where(classes == r, prob_now, 0.0), axis=1, keepdims=True) for r in ids
            ]
            along = jnp.sum(dy * h2, axis=1, keepdims=True)
            copies = [(r == expert_count + 1).astype(f32) for r in ids]
            keep = copies[0] * gates[0] + copies[1] * gates[1]
            dgates = [copies[c] * along for c in range(2)]
            scores = [
                jnp.sum(h2 * lw_ref[n : n + 1, :], axis=1, keepdims=True) for n in range(2 * kinds)
            ]
            base = x1_ref[here, :]
            dh = jnp.zeros_like(h2)
            for j in range(kinds):
                top = jnp.maximum(scores[2 * j], scores[2 * j + 1])
                e0 = jnp.exp(scores[2 * j] - top)
                e1 = jnp.exp(scores[2 * j + 1] - top)
                a0 = e0 / (e0 + e1)
                a1 = e1 / (e0 + e1)
                vec = vec_ref[j : j + 1, :]
                along_vec = jnp.sum(dy * vec, axis=1, keepdims=True)
                these = [(r == expert_count + 2 + j).astype(f32) for r in ids]
                weight = these[0] * gates[0] + these[1] * gates[1]
                for c in range(2):
                    dgates[c] = dgates[c] + these[c] * (a0 * along + a1 * along_vec)
                keep = keep + weight * a0
                base = base + (weight * a1) * vec
                d0 = weight * along
                d1 = weight * along_vec
                mean = a0 * d0 + a1 * d1
                z0 = a0 * (d0 - mean)
                z1 = a1 * (d1 - mean)
                dh = dh + z0 * lw_ref[2 * j : 2 * j + 1, :] + z1 * lw_ref[2 * j + 1 : 2 * j + 2, :]
                sums_ref[j : j + 1, :] += jnp.sum((weight * a1) * dy, axis=0, keepdims=True)
                at = kinds + 2 * j
                sums_ref[at : at + 1, :] += jnp.sum(z0 * h2, axis=0, keepdims=True)
                sums_ref[at + 1 : at + 2, :] += jnp.sum(z1 * h2, axis=0, keepdims=True)
            base_ref[here, :] = base + keep * h2
            dh_ref[here, :] = dh + keep * dy
            dgate_ref[here, :] = jnp.concatenate(dgates, axis=1)
            return 0

        sums_ref[...] = jnp.zeros_like(sums_ref)
        lax.fori_loop(0, rows // tile, zero_rows, 0)

        def rows_store(r):
            return pltpu.make_async_copy(arrived.at[r], rows_out.at[r], out_sem.at[2 * r])

        def gates_store(r):
            return pltpu.make_async_copy(gate_near.at[r], gates_out.at[r], out_sem.at[2 * r + 1])

        for r in range(1, places):
            row_copy(r).wait()
            gate_copy(r).wait()
            rows_store(r).start()
            gates_store(r).start()
        own_copy(0).wait()
        own_copy(1).wait()
        for r in range(1, places):
            rows_store(r).wait()
            gates_store(r).wait()

    wide = shape_of((rows, width), f32)
    placed = shape_of((places, CAP, width), bf16)
    lines = shape_of((places, 1, CAP), f32)
    return run(
        body,
        (),
        [(x, vector), (o, anywhere), (w_out, vector), (gain, vector), (w_router, vector)]
        + [(previous, vector), (w_carry, vector), (target_rows, vector), (grad, vector)]
        + [(routes, vector), (logit_w, vector), (vectors, vector)],
        [(wide, vector), (wide, vector), (shape_of((rows, expert_all), f32), vector)]
        + [(placed, anywhere), (lines, anywhere), (wide, vector), (wide, vector)]
        + [(shape_of((rows, 2), f32), vector), (shape_of((3 * kinds, width), f32), vector)],
        scratch=[
            pltpu.VMEM((members, rows, columns), bf16),
            pltpu.VMEM((rows, width), bf16),
            pltpu.VMEM((3, rows, expert_all), bf16),
            pltpu.VMEM((places, CAP, width), bf16),
            pltpu.VMEM((places, CAP, width), bf16),
            pltpu.VMEM((places, 1, CAP), f32),
            pltpu.VMEM((places, 1, CAP), f32),
            dma((members,)), dma((members,)),
            dma((places,)), dma((places,)), dma((places,)), dma((places,)),
            dma((2 * places,)),
        ],
        flops=2 * rows * width * (width + places * CAP),
        moved=rows * width * 30,
        talks=1,
    )


def expert_layer(arrived, grads, gates, w_gate, w_up, w_down):
    places = arrived.shape[0]
    local = w_gate.shape[0]
    rows = places * CAP
    width, hidden = w_gate.shape[1], w_gate.shape[2]
    parts = lax.axis_size("dp")
    half = width // 2
    per_part = hidden // parts
    tile = min(256, per_part)
    steps = hidden // tile
    tiles = per_part // tile
    away = steps - tiles
    chunk = 256

    def body(*refs):
        x_ref, dy_ref, gates_ref, wg_hbm, wu_hbm, wd_hbm = refs[:6]
        y_out, dx_out, dots_out, sum_out = refs[6:10]
        x_all, xt_all, dy_all, dyt_all, gate_all, y_acc, dx_acc, dot_acc = refs[10:18]
        hid_t, dgt, dut, scaled_t, wg_buf, wu_buf, wd_buf = refs[18:25]
        send, total, taken, far, dx_low, dx_near, dots, dots_near = refs[25:33]
        w_sem, c_s, c_r, f_s, f_r, b_s, b_r, d_s, d_r, out_sem = refs[33:]
        me, exp_now, dp_now = lax.axis_index("ctx"), lax.axis_index("exp"), lax.axis_index("dp")
        core, side = lax.rem(me, 2), lax.div(me, 2)
        sibling = {"ctx": flip(me, 1)}
        peers = [sibling] + [{"dp": flip(dp_now, d)} for d in range(1, parts)]
        peers += [slot_peer(r, local, exp_now, me) for r in range(1, places)]
        ready = greet(peers)
        diagonal = lax.broadcasted_iota(jnp.int32, (CAP, CAP), 0) == lax.broadcasted_iota(
            jnp.int32, (CAP, CAP), 1
        )

        def dp_of(f):
            distance = parts - 1 - lax.div(f, tiles)
            found, bit = dp_now, 1
            while bit < parts:
                on = lax.rem(lax.div(distance, bit), 2)
                now = lax.rem(lax.div(found, bit), 2)
                found = found + on * bit * (1 - 2 * now)
                bit *= 2
            return found

        def weights(f, slot):
            at = pl.multiple_of(dp_of(f) * per_part + lax.rem(f, tiles) * tile, tile)
            return [
                pltpu.make_async_copy(
                    wg_hbm.at[side, :, pl.ds(at, tile)], wg_buf.at[slot], w_sem.at[0, slot]
                ),
                pltpu.make_async_copy(
                    wu_hbm.at[side, :, pl.ds(at, tile)], wu_buf.at[slot], w_sem.at[1, slot]
                ),
                pltpu.make_async_copy(
                    wd_hbm.at[side, pl.ds(at, tile), :], wd_buf.at[slot], w_sem.at[2, slot]
                ),
            ]

        def core_copy(f, slot):
            return remote(send.at[slot], taken.at[f], c_s.at[slot], c_r.at[f], sibling)

        def far_copy(f):
            return remote(total.at[f], far.at[f], f_s.at[f], f_r.at[f], {"dp": dp_of(f)})

        def back_copy(r):
            return remote(
                dx_low.at[r], dx_near.at[r], b_s.at[r], b_r.at[r],
                slot_peer(r, local, exp_now, me),
            )

        def dots_copy(r):
            return remote(
                dots.at[r], dots_near.at[r], d_s.at[r], d_r.at[r],
                slot_peer(r, local, exp_now, me),
            )

        for copy in weights(0, 0):
            copy.start()
        for r in range(places):
            here = slice(r * CAP, (r + 1) * CAP)
            x_all[here, :] = x_ref[r]
            xt_all[:, here] = jnp.transpose(x_ref[r])
            dy_all[here, :] = dy_ref[r]
            dyt_all[:, here] = jnp.transpose(dy_ref[r])
            gate_all[here, :] = jnp.sum(
                jnp.where(diagonal, gates_ref[r], 0.0), axis=1, keepdims=True
            )
        y_acc[...] = jnp.zeros_like(y_acc)
        dx_acc[...] = jnp.zeros_like(dx_acc)
        dot_acc[...] = jnp.zeros_like(dot_acc)
        ready()
        mine = pl.ds(pl.multiple_of(core * half, half), half)
        theirs = pl.ds(pl.multiple_of((1 - core) * half, half), half)

        def core_sum(f):
            core_copy(f, lax.rem(f, 2)).wait_recv()
            for n in range(3):
                total[f, n] = (total[f, n].astype(f32) + taken[f, n].astype(f32)).astype(bf16)

        def step(f, _):
            slot = lax.rem(f, 2)
            for copy in weights(f, slot):
                copy.wait()

            @pl.when(f + 1 < steps)
            def _():
                for copy in weights(f + 1, 1 - slot):
                    copy.start()

            wg, wu, wd = wg_buf.at[slot], wu_buf.at[slot], wd_buf.at[slot]

            def row_chunk(c, _):
                here = pl.ds(pl.multiple_of(c * chunk, chunk), chunk)
                g_pre = mm(x_all[here, :], wg[...])
                u_pre = mm(x_all[here, :], wu[...])
                back = mm(dy_all[here, :], wd[...], NT)
                gate = gate_all[here, :]
                sig = 1.0 / (1.0 + jnp.exp(-g_pre))
                act = g_pre * sig
                hid = act * u_pre
                hid_t[here, :] = hid.astype(bf16)
                scaled_t[here, :] = (gate * hid).astype(bf16)
                along = hid * back
                lines = along[:, 0:128]
                for n in range(1, tile // 128):
                    lines = lines + along[:, n * 128 : (n + 1) * 128]
                dot_acc[here, :] += lines
                dhid = gate * back
                dgt[here, :] = (dhid * u_pre * sig * (1.0 + g_pre * (1.0 - sig))).astype(bf16)
                dut[here, :] = (dhid * act).astype(bf16)
                return 0

            lax.fori_loop(0, rows // chunk, row_chunk, 0)

            @pl.when(f >= 1)
            def _():
                core_sum(f - 1)

            @pl.when(f >= 2)
            def _():
                core_copy(f - 2, slot).wait_send()

            send[slot, 0] = mm(xt_all[theirs, :], dgt[...]).astype(bf16)
            send[slot, 1] = mm(xt_all[theirs, :], dut[...]).astype(bf16)
            send[slot, 2] = mm(dyt_all[theirs, :], scaled_t[...]).astype(bf16)
            total[f, 0] = mm(xt_all[mine, :], dgt[...]).astype(bf16)
            core_copy(f, slot).start()

            @pl.when((f >= 1) & (f - 1 < away))
            def _():
                far_copy(f - 1).start()

            total[f, 1] = mm(xt_all[mine, :], dut[...]).astype(bf16)
            total[f, 2] = mm(dyt_all[mine, :], scaled_t[...]).astype(bf16)
            y_acc[...] += mm(hid_t[...], wd[...])
            dx_acc[...] += mm(dgt[...], wg[...], NT) + mm(dut[...], wu[...], NT)
            return 0

        lax.fori_loop(0, steps, step, 0)
        for r in range(places):
            here = slice(r * CAP, (r + 1) * CAP)
            dx_low[r] = dx_acc[here, :].astype(bf16)
            column = jnp.sum(dot_acc[here, :], axis=1, keepdims=True)
            dots[r] = jnp.sum(jnp.where(diagonal, column, 0.0), axis=0, keepdims=True)
            if r > 1:
                back_copy(r - 1).start()
                dots_copy(r - 1).start()
        core_sum(steps - 1)
        back_copy(places - 1).start()
        dots_copy(places - 1).start()
        for r in range(places):
            here = slice(r * CAP, (r + 1) * CAP)
            y_out[r] = (gate_all[here, :] * y_acc[here, :]).astype(bf16)

        def sum_store(i):
            return pltpu.make_async_copy(
                total.at[away + i], sum_out.at[:, :, pl.ds(i * tile, tile)], out_sem.at[i]
            )

        for i in range(tiles):
            for d in range(1, parts):
                far_copy((parts - 1 - d) * tiles + i).wait_recv()
            for n in range(3):
                value = total[away + i, n].astype(f32)
                for d in range(1, parts):
                    value = value + far[(parts - 1 - d) * tiles + i, n].astype(f32)
                total[away + i, n] = value.astype(bf16)
            sum_store(i).start()
        for f in range(away):
            far_copy(f).wait_send()
        for f in range(max(0, steps - 2), steps):
            core_copy(f, f % 2).wait_send()

        dx_out[0] = dx_low[0]
        dots_out[0] = dots[0]
        for r in range(1, places):
            back_copy(r).wait()
            dots_copy(r).wait()
            dx_out[r] = dx_near[r]
            dots_out[r] = dots_near[r]
        for i in range(tiles):
            sum_store(i).wait()

    placed = shape_of((places, CAP, width), bf16)
    lines = shape_of((places, 1, CAP), f32)
    return run(
        body,
        (),
        [(arrived, vector), (grads, vector), (gates, vector)]
        + [(w, anywhere) for w in (w_gate, w_up, w_down)],
        [(placed, vector), (placed, vector), (lines, vector)]
        + [(shape_of((3, half, per_part), bf16), anywhere)],
        scratch=[
            pltpu.VMEM((rows, width), bf16),
            pltpu.VMEM((width, rows), bf16),
            pltpu.VMEM((rows, width), bf16),
            pltpu.VMEM((width, rows), bf16),
            pltpu.VMEM((rows, 1), f32),
            pltpu.VMEM((rows, width), f32),
            pltpu.VMEM((rows, width), f32),
            pltpu.VMEM((rows, 128), f32),
            pltpu.VMEM((rows, tile), bf16),
            pltpu.VMEM((rows, tile), bf16),
            pltpu.VMEM((rows, tile), bf16),
            pltpu.VMEM((rows, tile), bf16),
            pltpu.VMEM((2, width, tile), bf16),
            pltpu.VMEM((2, width, tile), bf16),
            pltpu.VMEM((2, tile, width), bf16),
            pltpu.VMEM((2, 3, half, tile), bf16),
            pltpu.VMEM((steps, 3, half, tile), bf16),
            pltpu.VMEM((steps, 3, half, tile), bf16),
            pltpu.VMEM((max(1, away), 3, half, tile), bf16),
            pltpu.VMEM((places, CAP, width), bf16),
            pltpu.VMEM((places, CAP, width), bf16),
            pltpu.VMEM((places, 1, CAP), f32),
            pltpu.VMEM((places, 1, CAP), f32),
            dma((3, 2)), dma((2,)), dma((steps,)),
            dma((max(1, away),)), dma((max(1, away),)),
            dma((places,)), dma((places,)), dma((places,)), dma((places,)),
            dma((tiles,)),
        ],
        flops=9 * 2 * rows * width * hidden,
        moved=12 * width * hidden + rows * width * 8,
        exps=rows * hidden,
        talks=2,
    )


def slot_sum(targets, source_ref):
    tile = targets.shape[0]
    total = None
    for r in range(source_ref.shape[0]):
        ids = r * CAP + lax.broadcasted_iota(jnp.int32, (tile, CAP), 1)
        choice = jnp.where((ids == targets[:, 0:1]) | (ids == targets[:, 1:2]), 1.0, 0.0)
        part = mm(choice.astype(bf16), source_ref[r])
        total = part if total is None else total + part
    return total


def token_back(
    meta, x1, h2, grad, prob, previous, routes, targets, back, dots, dgate_zero, dh_zero, gain, router_t, w_out
):
    rows, width = x1.shape
    tile = 128
    places = back.shape[0]
    expert_all = prob.shape[1]
    members, head_columns = w_out.shape[0], w_out.shape[1]

    def body(meta_ref, *refs):
        (x1_ref, h2_ref, dy_ref, prob_ref, prev_ref, route_ref, target_ref) = refs[:7]
        back_ref, dots_ref, dz_ref, dh_ref, gain_ref, router_ref = refs[7:13]
        w_refs = refs[13 : 13 + members]
        dx1_ref, low_ref = refs[13 + members : 15 + members]
        out_refs = refs[15 + members : 15 + 2 * members]
        sums_ref, carry_ref = refs[15 + 2 * members :]
        i = pl.program_id(0)
        prob_now = prob_ref[...]
        lanes = lax.broadcasted_iota(jnp.int32, (tile, expert_all), 1)
        dprob = jnp.zeros_like(prob_now)
        for c in range(2):
            target = target_ref[:, c : c + 1]
            dgate = dz_ref[:, c : c + 1]
            for n in range(places):
                ids = n * CAP + lax.broadcasted_iota(jnp.int32, (tile, CAP), 1)
                dgate = dgate + jnp.sum(
                    jnp.where(ids == target, dots_ref[n], 0.0), axis=1, keepdims=True
                )
            dprob = dprob + jnp.where(lanes == route_ref[:, c : c + 1], dgate, 0.0)
        dlogit = prob_now * (dprob - jnp.sum(prob_now * dprob, axis=1, keepdims=True))
        h2 = h2_ref[...]
        dh2 = (
            slot_sum(target_ref[...], back_ref)
            + dh_ref[...]
            + mm_full(dlogit, router_ref[...])
        )
        x1 = x1_ref[...]
        inverse = lax.rsqrt(jnp.mean(x1 * x1, axis=1, keepdims=True) + norm_eps)
        normed = x1 * inverse
        router_part = mm_full(dlogit, h2, TN)
        carry_part = mm_full(dlogit, prev_ref[...], TN)
        gain_part = jnp.sum(dh2 * normed, axis=0, keepdims=True)

        @pl.when(i == 0)
        def _():
            sums_ref[0:expert_all, :] = router_part
            sums_ref[expert_all : expert_all + 1, :] = gain_part
            carry_ref[...] = carry_part

        @pl.when(i > 0)
        def _():
            sums_ref[0:expert_all, :] += router_part
            sums_ref[expert_all : expert_all + 1, :] += gain_part
            carry_ref[...] += carry_part

        dn = dh2 * gain_ref[...]
        dx1 = dy_ref[...].astype(f32) + inverse * (
            dn - normed * jnp.mean(dn * normed, axis=1, keepdims=True)
        )
        dx1_ref[...] = dx1
        low = dx1.astype(bf16)
        low_ref[...] = low
        for n in range(members):
            out_refs[n][...] = mm(low, w_refs[n][0], NT).astype(bf16)

    row_spec = pl.BlockSpec((tile, width), lambda i, m: (i, 0))
    pair_spec = pl.BlockSpec((tile, 2), lambda i, m: (i, 0))
    small_spec = pl.BlockSpec((tile, expert_all), lambda i, m: (i, 0))
    sums = shape_of((expert_all + 1, width), f32)
    carry = shape_of((expert_all, expert_all), f32)
    return run(
        body,
        (rows // tile,),
        [
            (x1, row_spec),
            (h2, row_spec),
            (grad, row_spec),
            (prob, small_spec),
            (previous, small_spec),
            (routes, pair_spec),
            (targets, pair_spec),
        ]
        + [
            (back, whole(back)),
            (dots, whole(dots)),
            (dgate_zero, pair_spec),
            (dh_zero, row_spec),
            (gain, whole(gain)),
            (router_t, whole(router_t)),
        ]
        + [
            (w_out, pl.BlockSpec((1, head_columns, width), lambda i, m, n=n: (m[0] ^ n, 0, 0)))
            for n in range(members)
        ],
        [
            (shape_of((rows, width), f32), row_spec),
            (shape_of((rows, width), bf16), row_spec),
        ]
        + [
            (
                shape_of((rows, head_columns), bf16),
                pl.BlockSpec((tile, head_columns), lambda i, m: (i, 0)),
            )
        ]
        * members
        + [(sums, whole(sums)), (carry, whole(carry))],
        meta=meta,
        flops=2 * rows * width * (places * CAP + width),
        moved=rows * width * 24,
    )


def finish(dqkv_all, h1, x, gain, dx1, weights_t, out_sum, small, tops, produced, base, targets):
    members, per_group = weights_t.shape[1], weights_t.shape[2]
    rows, width = x.shape
    group_rows = dqkv_all.shape[0]
    parts, groups = lax.axis_size("dp"), lax.axis_size("exp")
    team = parts * groups
    places = produced.shape[0]
    local = places // groups
    wide_share, out_share = 3 * per_group // team, per_group // team
    small_rows = small.shape[0]
    small_steps = [(axis, bit) for axis in ("ctx", "dp", "exp") for bit in powers(axis)]
    hops = len(small_steps)
    row_tile = min(256, rows)

    def body(*refs):
        it = iter(refs)

        def take(count=None):
            return next(it) if count is None else [next(it) for _ in range(count)]

        dqkv_hbm, h1_hbm, x_hbm, gain_ref, dx1_hbm, w_hbm, out_ref = take(7)
        small_ref, tops_ref, produced_hbm, base_hbm, target_ref = take(5)
        input_out, wide_out, flat_out, small_out, gain_out, tops_out, result_out = take(7)
        dqkv, dqkv_near, product, h1_all, x_all, dx1_all, w_all, base_all, y_near = take(9)
        wide_mine, wide_far, wide_all = take(3)
        flat_mine, flat_far, flat_all = take(3)
        small_acc, small_far, gain_acc, gain_far, tops_acc, tops_far = take(6)
        load_sem, near_s, near_r, y_s, y_r = take(5)
        dense_sems = [take(8), take(8)]
        hop_s, hop_r, gain_s, gain_r, top_s, top_r = take(6)

        me = lax.axis_index("ctx")
        dp_now, exp_now = lax.axis_index("dp"), lax.axis_index("exp")
        seat = dp_now * groups + exp_now

        def near_peer(j):
            return {"ctx": flip(me, j)}

        def team_peer(r):
            return {"dp": flip(dp_now, r // groups), "exp": flip(exp_now, r % groups)}

        peers = [near_peer(j) for j in range(1, members)]
        peers += [team_peer(r) for r in range(1, team)]
        peers += [
            slot_peer(r, local, exp_now, me) for r in range(local, places) if r % local
        ]
        ready = greet(peers)

        loads = [
            (dqkv_hbm, dqkv), (h1_hbm, h1_all), (x_hbm, x_all), (dx1_hbm, dx1_all), (w_hbm, w_all),
            (base_hbm, base_all), (produced_hbm.at[0], y_near.at[0]),
        ]

        def load(n):
            return pltpu.make_async_copy(loads[n][0], loads[n][1], load_sem.at[n])

        class Dense:
            def __init__(self, mine, far_buf, all_buf, sems, share):
                self.mine, self.far, self.all, self.share = mine, far_buf, all_buf, share
                (self.rs, self.rr, self.gs, self.gr, self.ys, self.yr, self.cs, self.cr) = sems[:8]

            def reduce_copy(self, r):
                return remote(
                    self.mine.at[flip(seat, r)], self.far.at[r - 1], self.rs.at[r - 1],
                    self.rr.at[r - 1], team_peer(r),
                )

            def gather_copy(self, r):
                return remote(
                    self.all.at[0, seat], self.all.at[0, seat], self.gs.at[r - 1],
                    self.gr.at[r - 1], team_peer(r),
                )

            def gather_arrival(self, r):
                spot = self.all.at[0, flip(seat, r)]
                return remote(spot, spot, self.gs.at[r - 1], self.gr.at[r - 1], team_peer(r))

            def y_forward(self, r):
                return remote(
                    self.all.at[0, flip(seat, r)], self.all.at[2, flip(seat, r)], self.ys.at[r],
                    self.yr.at[r], near_peer(2),
                )

            def core_forward(self, n):
                return remote(
                    self.all.at[2 * n], self.all.at[2 * n + 1], self.cs.at[n], self.cr.at[n],
                    near_peer(1),
                )

            def scatter(self):
                for r in range(1, team):
                    self.reduce_copy(r).start()

            def collect(self):
                for r in range(1, team):
                    self.reduce_copy(r).wait_recv()
                total = self.mine[seat].astype(f32)
                for r in range(1, team):
                    total = total + self.far[r - 1].astype(f32)
                self.all[0, seat] = total.astype(bf16)

            def gather(self):
                for r in range(1, team):
                    self.gather_copy(r).start()
                self.y_forward(0).start()

            def forward(self):
                for r in range(1, team):
                    self.gather_arrival(r).wait_recv()
                    self.y_forward(r).start()
                for r in range(1, team):
                    self.reduce_copy(r).wait_send()
                    self.gather_copy(r).wait_send()
                self.core_forward(0).start()

            def forward_far(self):
                for r in range(team):
                    self.y_forward(r).wait()
                self.core_forward(1).start()

            def done(self):
                for n in range(2):
                    self.core_forward(n).wait()

        wide = Dense(wide_mine, wide_far, wide_all, dense_sems[0], wide_share)
        flat = Dense(flat_mine, flat_far, flat_all, dense_sems[1], out_share)

        def hop_peer(n):
            axis, bit = small_steps[n]
            return {axis: flip(lax.axis_index(axis), bit)}

        def small_copy(n):
            return remote(small_acc.at[n], small_far.at[n], hop_s.at[n], hop_r.at[n], hop_peer(n))

        def tops_copy(n):
            return remote(tops_acc.at[n], tops_far.at[n], top_s.at[n], top_r.at[n], hop_peer(n))

        def gain_copy(n):
            return remote(gain_acc.at[n], gain_far.at[n], gain_s.at[n], gain_r.at[n], hop_peer(n))

        def small_start(n):
            small_copy(n).start()
            tops_copy(n).start()

        def small_sum(n):
            small_copy(n).wait()
            tops_copy(n).wait()
            small_acc[n + 1] = small_acc[n] + small_far[n]
            tops_acc[n + 1] = jnp.maximum(tops_acc[n], tops_far[n])

        small_hops = list(range(hops))

        def small_next():
            if small_hops:
                n = small_hops.pop(0)
                small_sum(n)
                if n + 1 < hops:
                    small_start(n + 1)

        def dqkv_copy(j):
            return remote(
                dqkv_hbm.at[pl.ds(j * rows, rows), :], dqkv_near.at[j - 1], near_s.at[j - 1],
                near_r.at[j - 1], near_peer(j),
            )

        def y_copy(r):
            return remote(
                produced_hbm.at[r], y_near.at[r], y_s.at[r], y_r.at[r],
                slot_peer(r, local, exp_now, me),
            )

        for n in range(len(loads)):
            load(n).start()
        small_acc[0] = small_ref[...]
        tops_acc[0] = tops_ref[...]
        product[0:per_group, :] = out_ref[...].astype(f32)
        for c in range(team):
            flat_mine[c] = product[c * out_share : (c + 1) * out_share, :].astype(bf16)
        ready()
        for j in reversed(range(1, members)):
            dqkv_copy(j).start()
        flat.scatter()
        small_start(0)
        load(0).wait()
        load(1).wait()
        product[...] = mm(dqkv[0:rows, :], h1_all[0:rows, :], TN)

        def weigh(j, _):
            here = pl.ds(pl.multiple_of(j * rows, rows), rows)
            product[...] += mm(dqkv[here, :], h1_all[here, :], TN)
            return 0

        lax.fori_loop(1, group_rows // rows, weigh, 0)
        for c in range(team):
            wide_mine[c] = product[c * wide_share : (c + 1) * wide_share, :].astype(bf16)
        flat.collect()
        wide.scatter()
        flat.gather()
        for r in range(1, places):
            y_copy(r).start()
        for n in range(2, len(loads)):
            load(n).wait()
        small_next()
        small_next()
        flat.forward()
        wide.collect()
        small_next()
        wide.gather()
        for j in range(1, members):
            dqkv_copy(j).wait()

        def input_rows(t, gain_part):
            here = pl.ds(pl.multiple_of(t * row_tile, row_tile), row_tile)
            dh = None
            for j in range(members):
                member = flip(me, j)
                for w in range(3):
                    at = slice(w * per_group, (w + 1) * per_group)
                    source = dqkv[here, at] if j == 0 else dqkv_near[j - 1, here, at]
                    part = mm(source, w_all[w, member])
                    dh = part if dh is None else dh + part
            x_now = x_all[here, :].astype(f32)
            inv = lax.rsqrt(jnp.mean(x_now * x_now, axis=1, keepdims=True) + norm_eps)
            normed = x_now * inv
            dn = dh * gain_ref[...]
            dx1_all[here, :] = dx1_all[here, :] + inv * (
                dn - normed * jnp.mean(dn * normed, axis=1, keepdims=True)
            )
            return gain_part + jnp.sum(dh * normed, axis=0, keepdims=True)

        gain_acc[0] = lax.fori_loop(
            0, rows // row_tile, input_rows, jnp.zeros((1, width), f32)
        )
        store = pltpu.make_async_copy(dx1_all, input_out, load_sem.at[len(loads)])
        store.start()
        small_next()
        gain_copy(0).start()
        wide.forward()
        small_next()
        flat.forward_far()
        for n in range(hops):
            gain_copy(n).wait()
            gain_acc[n + 1] = gain_acc[n] + gain_far[n]
            if n == 0:
                for r in range(1, places):
                    y_copy(r).wait()
            if n < rows // 128:
                here = slice(n * 128, (n + 1) * 128)
                result_out[here, :] = (
                    base_all[here, :] + slot_sum(target_ref[here, :], y_near)
                ).astype(bf16)
            if n + 1 < hops:
                gain_copy(n + 1).start()
        for n in range(hops, rows // 128):
            here = slice(n * 128, (n + 1) * 128)
            result_out[here, :] = (
                base_all[here, :] + slot_sum(target_ref[here, :], y_near)
            ).astype(bf16)
        while small_hops:
            small_next()
        flat.done()
        wide.forward_far()
        wide.done()
        final = [
            pltpu.make_async_copy(wide_all, wide_out, load_sem.at[len(loads) + 1]),
            pltpu.make_async_copy(flat_all, flat_out, load_sem.at[len(loads) + 2]),
        ]
        for copy in final:
            copy.start()
        small_out[...] = small_acc[hops]
        gain_out[...] = gain_acc[hops]
        tops_out[...] = tops_acc[hops]
        store.wait()
        for copy in final:
            copy.wait()

    def dense_scratch(share):
        return [
            pltpu.VMEM((team, share, width), bf16),
            pltpu.VMEM((max(1, team - 1), share, width), bf16),
            pltpu.VMEM((members, team, share, width), bf16),
        ]

    dense_sem = [dma((team,))] * 6 + [dma((2,))] * 2
    wide_rows = shape_of((rows, width), f32)
    return run(
        body,
        (),
        [(dqkv_all, anywhere), (h1, anywhere), (x, anywhere), (gain, vector), (dx1, anywhere)]
        + [(weights_t, anywhere), (out_sum, vector), (small, vector), (tops, vector)]
        + [(produced, anywhere), (base, anywhere), (targets, vector)],
        [
            (wide_rows, anywhere),
            (shape_of((members, team, wide_share, width), bf16), anywhere),
            (shape_of((members, team, out_share, width), bf16), anywhere),
            (shape_of((small_rows, width), f32), vector),
            (shape_of((1, width), f32), vector),
            (shape_of(tops.shape, f32), vector),
            (shape_of((rows, width), bf16), vector),
        ],
        scratch=[
            pltpu.VMEM((group_rows, 3 * per_group), bf16),
            pltpu.VMEM((members - 1, rows, 3 * per_group), bf16),
            pltpu.VMEM((3 * per_group, width), f32),
            pltpu.VMEM((group_rows, width), bf16),
            pltpu.VMEM((rows, width), bf16),
            pltpu.VMEM((rows, width), f32),
            pltpu.VMEM(weights_t.shape, bf16),
            pltpu.VMEM((rows, width), f32),
            pltpu.VMEM((places, CAP, width), bf16),
        ]
        + dense_scratch(wide_share)
        + dense_scratch(out_share)
        + [pltpu.VMEM((hops + 1, small_rows, width), f32), pltpu.VMEM((hops, small_rows, width), f32)]
        + [pltpu.VMEM((hops + 1, 1, width), f32), pltpu.VMEM((hops, 1, width), f32)]
        + [pltpu.VMEM((hops + 1,) + tops.shape, f32), pltpu.VMEM((hops,) + tops.shape, f32)]
        + [dma((10,)), dma((members,)), dma((members,))]
        + [dma((places,)), dma((places,))]
        + dense_sem
        + dense_sem
        + [dma((hops,))] * 6,
        flops=4 * 2 * rows * width * width * 3,
        moved=20 * 1024 * 1024,
        talks=3,
    )


def place_experts(meta, near, which, turned):
    _, half, columns = near[0].shape
    members = len(near)
    local = members // 2
    tile = min(256, columns)

    def body(meta_ref, *refs):
        out_ref, hold = refs[members:]
        n = pl.program_id(0)
        for away in range(local):

            @pl.when(n == away)
            def _():
                for j in range(2):
                    at = pl.multiple_of((meta_ref[2] ^ j) * half, half)
                    piece = refs[2 * away + j][0].astype(f32)
                    if turned:
                        hold[pl.ds(at, half), :] = piece
                    else:
                        out_ref[0, pl.ds(at, half), :] = piece

        if turned:
            out_ref[0] = jnp.transpose(hold[...])

    def spec(j):
        last = columns // tile - 1
        if j < 2:
            return pl.BlockSpec(
                (1, half, tile), lambda n, f, m: (which, 0, jnp.where(n == 0, f, last))
            )
        return pl.BlockSpec((1, half, tile), lambda n, f, m: (which, 0, jnp.where(n == 0, 0, f)))

    if turned:
        out = shape_of((local, columns, 2 * half), f32)
        out_spec = pl.BlockSpec((1, tile, 2 * half), lambda n, f, m: (m[3] ^ n, f, 0))
    else:
        out = shape_of((local, 2 * half, columns), f32)
        out_spec = pl.BlockSpec((1, 2 * half, tile), lambda n, f, m: (m[3] ^ n, 0, f))
    return run(
        body,
        (local, columns // tile),
        [(p, spec(j)) for j, p in enumerate(near)],
        [(out, out_spec)],
        scratch=[pltpu.VMEM((2 * half, tile) if turned else (8, 128), f32)],
        meta=meta,
        moved=out.size * 6,
    )[0]


def place_columns(meta, near, per_group):
    members, team, share, width = near.shape

    def body(meta_ref, near_ref, out_ref, rows_ref, hold):
        w = pl.program_id(0)

        @pl.when(w == 0)
        def _():
            for n in range(members):
                for c in range(team):
                    rows_ref[n, c * share : (c + 1) * share, :] = near_ref[n, c].astype(f32)

        for n in range(members):
            at = pl.multiple_of((meta_ref[0] ^ n) * per_group, per_group)
            source = pl.multiple_of(w * per_group, per_group)
            hold[pl.ds(at, per_group), :] = rows_ref[n, pl.ds(source, per_group), :]
        out_ref[0] = jnp.transpose(hold[...])

    out = shape_of((3, width, width), f32)
    return run(
        body,
        (3,),
        [(near, whole(near))],
        [(out, pl.BlockSpec((1, width, width), lambda w, m: (w, 0, 0)))],
        scratch=[
            pltpu.VMEM((members, team * share, width), f32),
            pltpu.VMEM((width, width), f32),
        ],
        meta=meta,
        moved=3 * width * width * 6,
    )[0]


def place_rows(meta, near):
    members, team, share, width = near.shape

    def body(meta_ref, near_ref, out_ref):
        for c in range(team):
            out_ref[0, c * share : (c + 1) * share, :] = near_ref[0, c].astype(f32)

    out = shape_of((members, team * share, width), f32)
    return run(
        body,
        (members,),
        [(near, pl.BlockSpec((1, team, share, width), lambda j, m: (j, 0, 0, 0)))],
        [(out, pl.BlockSpec((1, team * share, width), lambda j, m: (m[0] ^ j, 0, 0)))],
        meta=meta,
        moved=out.size * 6,
    )[0]


def shards(
    inputs,
    lengths,
    block_order,
    routes,
    prev_logits,
    norm1_gain,
    norm2_gain,
    w_qkv,
    w_out,
    w_router,
    w_carry,
    const_logit_w,
    const_vec,
    w_gate,
    w_up,
    w_down,
    cotangent,
):
    members = lax.axis_size("ctx")
    groups = lax.axis_size("exp")
    parts = lax.axis_size("dp")
    me = lax.axis_index("ctx")
    mine = lax.axis_index("exp")
    x, grad = inputs[0], cotangent[0]
    rows, width = x.shape
    group_rows = rows * members
    deal_block = group_rows // block_order.shape[1]
    per_member = rows // deal_block
    local = w_gate.shape[0]
    expert_count = local * groups
    head_width = width // HEADS
    heads = HEADS // members
    per_group = heads * head_width
    blocks = block_order.shape[1]
    layout = {
        "order": 4, "lengths": 4 + blocks, "sequences": lengths.shape[1],
        "inverse": 4 + blocks + lengths.shape[1],
    }
    numbers = jnp.arange(blocks, dtype=jnp.int32)
    given = jnp.sum(jnp.where(block_order[0][None, :] == numbers[:, None], numbers[None, :], 0), axis=1)
    inverse = (((given // per_member) ^ me) * per_member + given % per_member).astype(jnp.int32)
    meta = jnp.concatenate(
        [
            jnp.stack([me, mine, me % 2, me // 2]).astype(jnp.int32),
            block_order[0],
            lengths[0],
            inverse,
        ]
    )
    gain1 = norm1_gain.reshape(1, width)
    gain2 = norm2_gain.reshape(1, width)
    weights_t = jnp.swapaxes(w_qkv, 1, 2).reshape(3, members, per_group, width)
    w_out_parts = w_out.reshape(members, per_group, width)
    route_ids = routes[0]
    previous = prev_logits[0]

    near = gather_near(x, "ctx")
    held = None
    for j in range(members):
        held = project(
            j, near[j], gain1, weights_t, meta, held, group_rows, deal_block, layout
        )
    q, k, v, kt, vt, h1 = held
    o, ot, lse, tops = attend(meta, q, k, vt, deal_block, layout)
    targets = slot_targets(route_ids, expert_count, local, mine, me // 2)
    target_rows = jnp.transpose(targets)
    places = groups * local
    grad_slots = dispatch(target_rows, grad, places)
    grad_near = jnp.stack(
        [slot_swap(grad_slots[r], r, local) if r else grad_slots[0] for r in range(places)]
    )
    logit_rows = jnp.swapaxes(const_logit_w, 1, 2).reshape(-1, width)
    x1, h2, prob, token_near, gate_near, base, dh_zero, dgate_zero, zero_sums = token_front(
        x, o, w_out_parts, gain2, w_router, previous, w_carry, target_rows, grad, route_ids,
        logit_rows, const_vec, local,
    )
    produced, token_back_rows, dots, expert_sum = expert_layer(
        token_near, grad_near, gate_near, w_gate, w_up, w_down
    )
    back = token_back(
        meta, x1, h2, grad, prob, previous, route_ids, targets, token_back_rows, dots, dgate_zero,
        dh_zero, gain2, jnp.transpose(w_router), w_out_parts,
    )
    dx1, da = back[:2]
    do_near = [back[2 + j] if j == 0 else swap(back[2 + j], "ctx", j) for j in range(members)]
    token_sums, carry_sum = back[2 + members :]

    o_near = [swap(o[j * rows : (j + 1) * rows], "ctx", j) if j else o[:rows] for j in range(members)]
    out_parts = [mm(o_near[j], da, TN).astype(bf16) for j in range(members)]
    out_sum = add_low(*[swap(out_parts[j], "ctx", j) if j else out_parts[0] for j in range(members)])
    dqkv = attend_back(meta, q, k, v, kt, do_near, ot, lse, deal_block, layout)

    expert_all = w_router.shape[1]
    small = jnp.concatenate(
        [token_sums, zero_sums, jnp.pad(carry_sum, ((0, 0), (0, width - expert_all)))], axis=0
    )
    top_rows = jnp.full((members, heads), low_start, f32).at[me].set(jnp.max(tops, axis=1))
    tops_line = jnp.pad(top_rows.reshape(1, HEADS), ((0, 0), (0, 128 - HEADS)), constant_values=low_start)
    input_grad, qkv_near, out_near, small, norm1_grad, top_all, result = finish(
        dqkv, h1, x, gain1, dx1, weights_t, out_sum, small, tops_line, produced, base, targets
    )
    across = swap(expert_sum, "ctx", 2)
    expert_near = [expert_sum, swap(expert_sum, "ctx", 1), across, swap(across, "ctx", 1)]
    out_grad = place_rows(meta, out_near).reshape(width, width)
    qkv_grad = place_columns(meta, qkv_near, per_group)
    kinds = const_vec.shape[0]
    router_grad = jnp.transpose(small[:expert_all])
    norm2_grad = small[expert_all]
    start = expert_all + 1
    vec_grad = small[start : start + kinds]
    logit_grad = jnp.swapaxes(small[start + kinds : start + 3 * kinds].reshape(kinds, 2, width), 1, 2)
    carry_grad = jnp.transpose(small[start + 3 * kinds :, :expert_all])
    head_max = top_all[0, :HEADS]
    clip_ratio = jnp.sqrt(jnp.minimum(1.0, clip_limit / head_max))
    head_scale = jnp.repeat(clip_ratio, head_width)
    clipped = w_qkv[:2].astype(f32) * head_scale[None, None, :]
    gate_grad = place_experts(meta, expert_near, 0, False)
    up_grad = place_experts(meta, expert_near, 1, False)
    down_grad = place_experts(meta, expert_near, 2, True)
    return (
        result[None],
        input_grad[None],
        norm1_grad[0],
        norm2_grad,
        qkv_grad,
        out_grad,
        router_grad,
        carry_grad,
        logit_grad,
        vec_grad,
        gate_grad,
        up_grad,
        down_grad,
        clipped,
    )


def solution(mesh):
    tokens = P(("dp", "exp"), "ctx", None)
    packs = P(("dp", "exp"), None)
    experts = P("exp", None, None)
    in_specs = (
        tokens, packs, packs, tokens, tokens, P(), P(), P(), P(), P(), P(), P(), P(),
        experts, experts, experts, tokens,
    )
    out_specs = (
        tokens, tokens, P(), P(), P(), P(), P(), P(), P(), P(),
        P("exp", None, "dp"), P("exp", None, "dp"), P("exp", "dp", None), P(),
    )
    return jax.shard_map(shards, mesh=mesh, in_specs=in_specs, out_specs=out_specs, check_vma=False)
```

time: 722 us -> 551 us (0.76)
  waiting for transfers between devices: 314 us -> 71.6 us
  Pallas kernels: 212 us -> 409 us
  starting transfers between devices: 112 us -> 23.1 us
  local copies, waits for them, and re-layouts: 42.5 us -> 28.7 us
  other arithmetic: 21.4 us -> 8.67 us
    ppermute x113 -> x15, waiting for transfers between devices: 314 us -> 53.9 us  [swap(): return lax.ppermute(value, axis, [(i, i ^ distance) for i in range(count)])]
    pallas_call x19 -> x16, Pallas kernels: 212 us -> 409 us  [run(): pl.pallas_call(body, out_shape=[o for o, _ in outputs], grid_spec=pltpu.P...]
    ppermute x113 -> x15, starting transfers between devices: 112 us -> 10.6 us  [swap(): return lax.ppermute(value, axis, [(i, i ^ distance) for i in range(count)])]
    ppermute x0 -> x7, waiting for transfers between devices: none -> 17.7 us  [slot_swap(): lax.ppermute(value, ('ctx', 'exp'), [(i, i ^ apart) for i in range(total)])]
    convert_element_type x24 -> x0, other arithmetic: 13.3 us -> none  [add_low(): return total.astype(bf16)]
    ppermute x0 -> x7, starting transfers between devices: none -> 12.5 us  [slot_swap(): lax.ppermute(value, ('ctx', 'exp'), [(i, i ^ apart) for i in range(total)])]
    slice x21 -> x2, local copies, waits for them, and re-layouts: 13.7 us -> 2.14 us  [the longest x1 1.33 us: shards(): vec_grad = small[start:start + kinds]]
  transfers between devices with their start and end apart: 113 -> 22, of which waited for: 42 -> 7; matrix products, arithmetic and copies ran while one was open for 10% -> 7% of each run, Pallas kernels for 29% -> 37%
where the time goes in v3:
time: 551 us; the launch traced here: 548 us
  Pallas kernels  409 us (74%)
  waiting for transfers between devices  71.6 us (13%)
  local copies, waits for them, and re-layouts  28.7 us (5%)
  starting transfers between devices  23.1 us (4%)
  other arithmetic  8.67 us (2%)
  matrix products  6.5 us (1%)
    pallas_call x16, Pallas kernels, run(): pl.pallas_call(body, out_shape=[o for o, _ in outputs], grid_spec=pltpu.P...  409 us
    ppermute x15, waiting for transfers between devices, swap(): return lax.ppermute(value, axis, [(i, i ^ distance) for i in range(count)])  53.9 us
    ppermute x7, waiting for transfers between devices, slot_swap(): lax.ppermute(value, ('ctx', 'exp'), [(i, i ^ apart) for i in range(total)])  17.7 us
    ppermute x7, starting transfers between devices, slot_swap(): lax.ppermute(value, ('ctx', 'exp'), [(i, i ^ apart) for i in range(total)])  12.5 us
    unnamed x68, local copies, waits for them, and re-layouts  11.5 us
  transfers between devices with their start and end apart: 22, of which 7 were waited for; matrix products, arithmetic and copies ran while one was open for 7% of the time, Pallas kernels for 37%

profile of v3, /device:TPU:0, one launch (start us, length us, event | category | flops | bytes accessed | tf_op | source)
XLA Modules:
  0.0 548.2 jit_solution(6036070088233413627)
XLA Ops:
  0.6 3.0 collective-permute-start
  6.3 5.4 shard_map.278
  11.7 2.6 slice_bitcast_fusion
  14.4 2.0 collective-permute-start.4
  16.4 1.4 collective-permute-start.5
  19.0 3.7 copy.68
  23.3 1.7 copy.75.refs_4_
  25.0 1.6 copy.69
  27.9 1.3 concatenate.10.meta_ref
  29.2 4.9 shard_map.272
  34.2 2.6 collective-permute-start.6
  36.8 0.9 bitcast_dynamic-update-slice_fusion.6
  37.9 0.9 bitcast_dynamic-update-slice_fusion.5
  38.8 3.9 collective-permute-start.8
  42.8 0.9 bitcast_dynamic-update-slice_fusion.4
  43.7 11.7 %collective-permute-done.6 = bf16[128,768]{1,0:T(8,128)(2,1)S(1)} collective-permute-done((bf16[128,768]{1,0:T(8,128)(2,1)S(1)}, bf16[128,768]{1,0:T(8,128)(2,1)S(1)}, u32[]{:S(2)}, u32[]{:S(2)}) %collective-permute-start.6) | collective-permute-done | bytes 196640 | tf_op jit(solution)/shard_map/ppermute | solution.py:101
  55.4 2.4 collective-permute-start.9
  57.9 3.6 collective-permute-done.7
  61.5 2.4 collective-permute-done.9
  63.9 4.8 shard_map.273
  68.7 4.8 shard_map.274
  73.5 0.9 copy-done.6
  74.4 4.8 shard_map.275
  79.2 29.5 %shard_map.276 = (bf16[2048,192]{1,0:T(8,128)(2,1)}, f32[192,2048]{1,0:T(8,128)}, f32[3,2048]{1,0:T(4,128)}, f32[3,2048]{1,0:T(4,128)}) custom-call(s32[22]{0:T(128)} %concatenate.10.meta_ref, bf16[3,2048,64]{2,1,0:T(8,128)(2,1)} %get-tuple-element.100.q_ref, bf16[3,2048,64]{2,1,0:T(8,128)(2,1)} %get-tuple-element.101.k_ref, ...), custom_call_target="tpu_custom_call" | custom-call | flops 3221225472 | bytes 5505024 | tf_op jit(solution)/shard_map/pallas_call | solution.py:50
  108.6 61.5 %shard_map.277 = (f32[512,768]{1,0:T(8,128)}, f32[512,768]{1,0:T(8,128)}, f32[512,12]{1,0:T(8,128)}, bf16[8,128,768]{2,1,0:T(8,128)(2,1)}, f32[8,1,128]{2,1,0:T(...) custom-call(bf16[512,768]{1,0:T(8,128)(2,1)} %bitcast.89, ...), custom_call_target="tpu_custom_call" | custom-call | flops 1409286144 | bytes 11796480 | tf_op jit(solution)/shard_map/pallas_call | solution.py:50
  170.2 83.8 %shard_map.279 = (bf16[8,128,768]{2,1,0:T(8,128)(2,1)}, bf16[8,128,768]{2,1,0:T(8,128)(2,1)}, f32[8,1,128]{2,1,0:T(1,128)}, bf16[3,384,1024]{2,1,0:T(8,128)(2,1)}) custom-call(bf16[8,128,768]{2,1,0:T(8,128)(2,1)} %get-tuple-element.109.refs_0_, bf16[8,128,768]{2,1,0:T(8,128)(2,1)} %copy-done.16, f32[8,1,128]{2,1,0:T(1,128)} %get-tuple-element.110.refs_2_, ...), custom_call_target="tpu_custom_call" | custom-call | flops 28991029248 | bytes 25165824 | tf_op jit(solution)/shard_map/pallas_call | solution.py:50
  254.0 1.4 collective-permute-start.20
  256.1 12.0 %shard_map.280 = (f32[512,768]{1,0:T(8,128)}, bf16[512,768]{1,0:T(8,128)(2,1)}, bf16[512,192]{1,0:T(8,128)(2,1)}, bf16[512,192]{1,0:T(8,128)(2,1)}, bf16[512,192...) custom-call(s32[22]{0:T(128)} %concatenate.10.meta_ref, ...), custom_call_target="tpu_custom_call" | custom-call | flops 1409286144 | bytes 9437184 | tf_op jit(solution)/shard_map/pallas_call | solution.py:50
  269.3 2.0 fusion.15
  274.2 41.5 %collective-permute-done.17 = bf16[512,192]{1,0:T(8,128)(2,1)} collective-permute-done((bf16[512,192]{1,0:T(8,128)(2,1)}, bf16[512,192]{1,0:T(8,128)(2,1)}, u32[]{:S(2)}, u32[]{:S(2)}) %collective-permute-start.17) | collective-permute-done | bytes 196640 | tf_op jit(solution)/shard_map/ppermute | solution.py:73
  316.3 2.0 convolution_convert_fusion
  318.3 6.7 %collective-permute-done.15 = bf16[512,192]{1,0:T(8,128)(2,1)S(1)} collective-permute-done((bf16[512,192]{1,0:T(8,128)(2,1)}, bf16[512,192]{1,0:T(8,128)(2,1)S(1)}, u32[]{:S(2)}, u32[]{:S(2)}) %collective-permute-start.15) | collective-permute-done | bytes 196640 | tf_op jit(solution)/shard_map/ppermute | solution.py:73
  325.1 1.1 convolution_convert_fusion.1
  326.7 1.1 convolution_convert_fusion.2
  327.8 1.6 collective-permute-start.18
  329.6 5.3 collective-permute-done.12.refs_3_
  336.3 34.7 %shard_map.281.refs_0_ = bf16[2048,576]{1,0:T(8,128)(2,1)} custom-call(s32[22]{0:T(128)} %concatenate.10.meta_ref, bf16[3,2048,64]{2,1,0:T(8,128)(2,1)} %get-tuple-element.100.q_ref, bf16[3,2048,64]{2,1,0:T(8,128)(2,1)} %get-tuple-element.101.k_ref, bf16[3,2048,64]{2,1,0:T(8,128)(2,1)} %get-tuple-element.102.v_ref, ...), custom_call_target="tpu_custom_call" | custom-call | flops 8053063680 | bytes 9437184 | tf_op jit(solution)/shard_map/pallas_call | solution.py:50
  371.0 2.1 add_convert_fusion.refs_6_
  373.2 124.9 %shard_map.282 = (f32[512,768]{1,0:T(8,128)}, bf16[4,8,72,768]{3,2,1,0:T(8,128)(2,1)}, bf16[4,8,24,768]{3,2,1,0:T(8,128)(2,1)}, f32[31,768]{1,0:T(8,128)}, f32[1...) custom-call(bf16[2048,576]{1,0:T(8,128)(2,1)} %shard_map.281.refs_0_, ...), custom_call_target="tpu_custom_call" | custom-call | flops 7247757312 | bytes 20971520 | tf_op jit(solution)/shard_map/pallas_call | solution.py:50
  498.9 1.3 slice.87
  500.2 7.6 %shard_map.283 = f32[3,768,768]{2,1,0:T(8,128)} custom-call(s32[22]{0:T(128)} %concatenate.10.meta_ref, bf16[4,8,72,768]{3,2,1,0:T(8,128)(2,1)} %get-tuple-element.134.near_ref), custom_call_target="tpu_custom_call" | custom-call | bytes 10616832 | tf_op jit(solution)/shard_map/pallas_call | solution.py:50
  507.8 4.5 shard_map.284
  515.6 4.2 convert_multiply_fusion
  519.8 8.2 %shard_map.285 = f32[2,768,1024]{2,1,0:T(8,128)} custom-call(s32[22]{0:T(128)} %concatenate.10.meta_ref, bf16[3,384,1024]{2,1,0:T(8,128)(2,1)} %get-tuple-element.136.refs_0_, bf16[3,384,1024]{2,1,0:T(8,128)(2,1)} %collective-permute-done.19.refs_1_, bf16[3,384,1024]{2,1,0:T(8,128)(2,1)} %copy-done, bf16[3,384,1024]{2,1,0:T(8,128)(2,1)} %collective-permute-done.21.refs_3_), custom_call_target="tpu_custom_call" | custom-call | bytes 9437184 | tf_op jit(solution)/shard_map/pallas_call | solution.py:50
  528.1 8.2 %shard_map.286 = f32[2,768,1024]{2,1,0:T(8,128)} custom-call(s32[22]{0:T(128)} %concatenate.10.meta_ref, bf16[3,384,1024]{2,1,0:T(8,128)(2,1)} %get-tuple-element.136.refs_0_, bf16[3,384,1024]{2,1,0:T(8,128)(2,1)} %collective-permute-done.19.refs_1_, bf16[3,384,1024]{2,1,0:T(8,128)(2,1)} %copy-done, bf16[3,384,1024]{2,1,0:T(8,128)(2,1)} %collective-permute-done.21.refs_3_), custom_call_target="tpu_custom_call" | custom-call | bytes 9437184 | tf_op jit(solution)/shard_map/pallas_call | solution.py:50
  536.3 9.0 %shard_map.287 = f32[2,1024,768]{2,1,0:T(8,128)} custom-call(s32[22]{0:T(128)} %concatenate.10.meta_ref, bf16[3,384,1024]{2,1,0:T(8,128)(2,1)} %get-tuple-element.136.refs_0_, bf16[3,384,1024]{2,1,0:T(8,128)(2,1)} %collective-permute-done.19.refs_1_, bf16[3,384,1024]{2,1,0:T(8,128)(2,1)} %copy-done, bf16[3,384,1024]{2,1,0:T(8,128)(2,1)} %collective-permute-done.21.refs_3_), custom_call_target="tpu_custom_call" | custom-call | bytes 9437184 | tf_op jit(solution)/shard_map/pallas_call | solution.py:50
  545.4 0.9 copy.108
  547.1 1.1 copy.109
  (123 shorter events, 18.6 us)
Async XLA Ops:
  0.6 57.1 %collective-permute-start = (bf16[512,768]{1,0:T(8,128)(2,1)}, bf16[512,768]{1,0:T(8,128)(2,1)}, u32[]{:S(2)}, u32[]{:S(2)}) collective-permute-start(bf16[512,768]{1,0:T(8,128)(2,1)} %bitcast.86), channel_id=1, source_target_pairs={{0,8},{4,12},{8,0},{12,4},{1,9},{5,13},{9,1},{13,5},{2,10},{6,14},... | collective-permute-start | bytes 2359304 | tf_op jit(solution)/shard_map/ppermute | solution.py:73
  3.7 60.2 %collective-permute-start.2 = (bf16[512,768]{1,0:T(8,128)(2,1)}, bf16[512,768]{1,0:T(8,128)(2,1)}, u32[]{:S(2)}, u32[]{:S(2)}) collective-permute-start(bf16[512,768]{1,0:T(8,128)(2,1)} %bitcast.87), channel_id=1, source_target_pairs={{0,4},{4,0},{8,12},{12,8},{1,5},{5,1},{9,13},{13,9},{2,6},{6,2},{1... | collective-permute-start | bytes 2359304 | tf_op jit(solution)/shard_map/ppermute | solution.py:73
  4.5 1.7 copy-start.3
  6.3 12.8 %copy-start.2 = (bf16[3,768,768]{2,1,0:T(8,128)(2,1)S(1)}, bf16[3,768,768]{2,1,0:T(8,128)(2,1)}, u32[]{:S(2)}) copy-start(bf16[3,768,768]{2,1,0:T(8,128)(2,1)} %param.26) | copy-start | bytes 10616836
  11.7 6.1 %copy-start.24 = (s32[1,8]{1,0:T(1,128)S(1)}, s32[1,8]{1,0:T(1,128)}, u32[]{:S(2)}) copy-start(s32[1,8]{1,0:T(1,128)} %param.21) | copy-start | bytes 100
  11.7 6.7 %copy-start.20 = (f32[768]{0:T(1024)S(1)}, f32[768]{0:T(1024)}, u32[]{:S(2)}) copy-start(f32[768]{0:T(1024)} %param.24) | copy-start | bytes 9220
  14.3 19.8 %collective-permute-start.3 = (bf16[128,768]{1,0:T(8,128)(2,1)}, bf16[128,768]{1,0:T(8,128)(2,1)}, u32[]{:S(2)}, u32[]{:S(2)}) collective-permute-start(bf16[128,768]{1,0:T(8,128)(2,1)} %get-tuple-element.186), channel_id=1, source_target_pairs={{0,8},{1,9},{2,10},{3,11},{4,12},{5,13},{6,14},{7,15},{8,0},{9,1},... | collective-permute-start | bytes 589832 | tf_op jit(solution)/shard_map/ppermute | solution.py:101
  14.4 23.3 %collective-permute-start.4 = (bf16[128,768]{1,0:T(8,128)(2,1)}, bf16[128,768]{1,0:T(8,128)(2,1)}, u32[]{:S(2)}, u32[]{:S(2)}) collective-permute-start(bf16[128,768]{1,0:T(8,128)(2,1)} %get-tuple-element.185), channel_id=1, source_target_pairs={{0,1},{1,0},{2,3},{3,2},{4,5},{5,4},{6,7},{7,6},{8,9},{9,8},{10,11... | collective-permute-start | bytes 589832 | tf_op jit(solution)/shard_map/ppermute | solution.py:101
  16.4 22.4 %collective-permute-start.5 = (bf16[128,768]{1,0:T(8,128)(2,1)}, bf16[128,768]{1,0:T(8,128)(2,1)}, u32[]{:S(2)}, u32[]{:S(2)}) collective-permute-start(bf16[128,768]{1,0:T(8,128)(2,1)} %get-tuple-element.184), channel_id=1, source_target_pairs={{0,9},{1,8},{2,11},{3,10},{4,13},{5,12},{6,15},{7,14},{8,1},{9,0},... | collective-permute-start | bytes 589832 | tf_op jit(solution)/shard_map/ppermute | solution.py:101
  19.0 3.7 copy-start.21
  19.0 7.6 %copy-start.18 = (f32[2,768,2]{1,2,0:T(2,128)S(1)}, f32[2,768,2]{1,2,0:T(2,128)}, u32[]{:S(2)}) copy-start(f32[2,768,2]{1,2,0:T(2,128)} %param.30) | copy-start | bytes 36868
  29.2 4.9 copy-start.11
  29.2 7.6 %copy-start.15 = (bf16[8,128,768]{2,1,0:T(8,128)(2,1)S(1)}, bf16[8,128,768]{2,1,0:T(8,128)(2,1)}, u32[]{:S(2)}) copy-start(bf16[8,128,768]{2,1,0:T(8,128)(2,1)} %get-tuple-element.187) | copy-start | bytes 4718596
  29.2 8.5 %copy-start.10 = (bf16[128,768]{1,0:T(8,128)(2,1)S(1)}, bf16[128,768]{1,0:T(8,128)(2,1)}, u32[]{:S(2)}) copy-start(bf16[128,768]{1,0:T(8,128)(2,1)} %get-tuple-element.182) | copy-start | bytes 589828
  29.2 9.6 %copy-start.9 = (bf16[128,768]{1,0:T(8,128)(2,1)S(1)}, bf16[128,768]{1,0:T(8,128)(2,1)}, u32[]{:S(2)}) copy-start(bf16[128,768]{1,0:T(8,128)(2,1)} %get-tuple-element.181) | copy-start | bytes 589828
  29.2 26.2 %copy-start.8 = (bf16[128,768]{1,0:T(8,128)(2,1)S(1)}, bf16[128,768]{1,0:T(8,128)(2,1)}, u32[]{:S(2)}) copy-start(bf16[128,768]{1,0:T(8,128)(2,1)} %get-tuple-element.180) | copy-start | bytes 589828
  34.2 21.2 %collective-permute-start.6 = (bf16[128,768]{1,0:T(8,128)(2,1)S(1)}, bf16[128,768]{1,0:T(8,128)(2,1)S(1)}, u32[]{:S(2)}, u32[]{:S(2)}) collective-permute-start(bf16[128,768]{1,0:T(8,128)(2,1)S(1)} %copy-done.11), channel_id=1, source_target_pairs={{0,2},{1,3},{2,0},{3,1},{4,6},{5,7},{6,4},{7,5},{8,10},{9,11},{10,... | collective-permute-start | bytes 589832 | tf_op jit(solution)/shard_map/ppermute | solution.py:101
  37.8 23.7 %collective-permute-start.7 = (bf16[128,768]{1,0:T(8,128)(2,1)S(1)}, bf16[128,768]{1,0:T(8,128)(2,1)S(1)}, u32[]{:S(2)}, u32[]{:S(2)}) collective-permute-start(bf16[128,768]{1,0:T(8,128)(2,1)S(1)} %copy-done.10), channel_id=1, source_target_pairs={{0,10},{1,11},{2,8},{3,9},{4,14},{5,15},{6,12},{7,13},{8,2},{9,3},... | collective-permute-start | bytes 589832 | tf_op jit(solution)/shard_map/ppermute | solution.py:101
  38.8 22.7 %collective-permute-start.8 = (bf16[128,768]{1,0:T(8,128)(2,1)S(1)}, bf16[128,768]{1,0:T(8,128)(2,1)S(1)}, u32[]{:S(2)}, u32[]{:S(2)}) collective-permute-start(bf16[128,768]{1,0:T(8,128)(2,1)S(1)} %copy-done.9), channel_id=1, source_target_pairs={{0,3},{1,2},{2,1},{3,0},{4,7},{5,6},{6,5},{7,4},{8,11},{9,10},{10,... | collective-permute-start | bytes 589832 | tf_op jit(solution)/shard_map/ppermute | solution.py:101
  55.4 8.5 %collective-permute-start.9 = (bf16[128,768]{1,0:T(8,128)(2,1)S(1)}, bf16[128,768]{1,0:T(8,128)(2,1)S(1)}, u32[]{:S(2)}, u32[]{:S(2)}) collective-permute-start(bf16[128,768]{1,0:T(8,128)(2,1)S(1)} %copy-done.8), channel_id=1, source_target_pairs={{0,11},{1,10},{2,9},{3,8},{4,15},{5,14},{6,13},{7,12},{8,3},{9,2},... | collective-permute-start | bytes 589832 | tf_op jit(solution)/shard_map/ppermute | solution.py:101
  57.8 15.7 %collective-permute-start.1 = (bf16[512,768]{1,0:T(8,128)(2,1)}, bf16[512,768]{1,0:T(8,128)(2,1)S(1)}, u32[]{:S(2)}, u32[]{:S(2)}) collective-permute-start(bf16[512,768]{1,0:T(8,128)(2,1)} %collective-permute-done.x_ref), channel_id=1, source_target_pairs={{0,4},{4,0},{8,12},{12,8},{1,5},{5,1},{9,13},{13,9},{2,6},{6,2},{1... | collective-permute-start | bytes 2359304 | tf_op jit(solution)/shard_map/ppermute | solution.py:73
  63.9 4.8 copy-start.16
  73.5 0.9 copy-start.6
  170.1 85.2 %copy-start.23 = (s32[2]{0:T(128)S(1)}, s32[2]{0:T(128)}, u32[]{:S(2)}) copy-start(s32[2]{0:T(128)} %constant.107.clone.1) | copy-start | bytes 28
  254.0 81.6 %collective-permute-start.20 = (bf16[3,384,1024]{2,1,0:T(8,128)(2,1)}, bf16[3,384,1024]{2,1,0:T(8,128)(2,1)S(1)}, u32[]{:S(2)}, u32[]{:S(2)}) collective-permute-start(bf16[3,384,1024]{2,1,0:T(8,128)(2,1)} %get-tuple-element.136.refs_0_), channel_id=1, source_target_pairs={{0,8},{4,12},{8,0},{12,4},{1,9},{5,13},{9,1},{13,5},{2,10},{6,14},... | collective-permute-start | bytes 7077896 | tf_op jit(solution)/shard_map/ppermute | solution.py:73
  256.1 263.7 %collective-permute-start.19 = (bf16[3,384,1024]{2,1,0:T(8,128)(2,1)}, bf16[3,384,1024]{2,1,0:T(8,128)(2,1)}, u32[]{:S(2)}, u32[]{:S(2)}) collective-permute-start(bf16[3,384,1024]{2,1,0:T(8,128)(2,1)} %get-tuple-element.136.refs_0_), channel_id=1, source_target_pairs={{0,4},{4,0},{8,12},{12,8},{1,5},{5,1},{9,13},{13,9},{2,6},{6,2},{1... | collective-permute-start | bytes 7077896 | tf_op jit(solution)/shard_map/ppermute | solution.py:73
  268.1 4.0 copy-start.14
  268.1 5.4 copy-start.13
  268.1 5.4 copy-start.17
  268.1 5.4 copy-start.19
  268.1 48.2 %copy-start.1 = (bf16[512,768]{1,0:T(8,128)(2,1)S(1)}, bf16[512,768]{1,0:T(8,128)(2,1)}, u32[]{:S(2)}) copy-start(bf16[512,768]{1,0:T(8,128)(2,1)} %get-tuple-element.123) | copy-start | bytes 2359300
  268.1 59.6 %collective-permute-start.10 = (bf16[512,192]{1,0:T(8,128)(2,1)}, bf16[512,192]{1,0:T(8,128)(2,1)}, u32[]{:S(2)}, u32[]{:S(2)}) collective-permute-start(bf16[512,192]{1,0:T(8,128)(2,1)} %get-tuple-element.116), channel_id=1, source_target_pairs={{0,4},{4,0},{8,12},{12,8},{1,5},{5,1},{9,13},{13,9},{2,6},{6,2},{1... | collective-permute-start | bytes 589832 | tf_op jit(solution)/shard_map/ppermute | solution.py:73
  268.7 60.7 %collective-permute-start.11 = (bf16[512,192]{1,0:T(8,128)(2,1)}, bf16[512,192]{1,0:T(8,128)(2,1)}, u32[]{:S(2)}, u32[]{:S(2)}) collective-permute-start(bf16[512,192]{1,0:T(8,128)(2,1)} %get-tuple-element.117), channel_id=1, source_target_pairs={{0,8},{4,12},{8,0},{12,4},{1,9},{5,13},{9,1},{13,5},{2,10},{6,14},... | collective-permute-start | bytes 589832 | tf_op jit(solution)/shard_map/ppermute | solution.py:73
  271.3 44.4 %collective-permute-start.17 = (bf16[512,192]{1,0:T(8,128)(2,1)}, bf16[512,192]{1,0:T(8,128)(2,1)}, u32[]{:S(2)}, u32[]{:S(2)}) collective-permute-start(bf16[512,192]{1,0:T(8,128)(2,1)} %get-tuple-element.189), channel_id=1, source_target_pairs={{0,12},{4,8},{8,4},{12,0},{1,13},{5,9},{9,5},{13,1},{2,14},{6,10},... | collective-permute-start | bytes 589832 | tf_op jit(solution)/shard_map/ppermute | solution.py:73
  273.0 53.6 %copy-start.25 = (bf16[512,192]{1,0:T(8,128)(2,1)S(1)}, bf16[512,192]{1,0:T(8,128)(2,1)}, u32[]{:S(2)}) copy-start(bf16[512,192]{1,0:T(8,128)(2,1)} %get-tuple-element.118) | copy-start | bytes 589828
  315.7 9.3 %collective-permute-start.15 = (bf16[512,192]{1,0:T(8,128)(2,1)}, bf16[512,192]{1,0:T(8,128)(2,1)S(1)}, u32[]{:S(2)}, u32[]{:S(2)}) collective-permute-start(bf16[512,192]{1,0:T(8,128)(2,1)} %get-tuple-element.190), channel_id=1, source_target_pairs={{0,8},{4,12},{8,0},{12,4},{1,9},{5,13},{9,1},{13,5},{2,10},{6,14},... | collective-permute-start | bytes 589832 | tf_op jit(solution)/shard_map/ppermute | solution.py:73
  325.0 1.5 collective-permute-start.13
  326.6 8.3 %collective-permute-start.12 = (bf16[512,192]{1,0:T(8,128)(2,1)S(1)}, bf16[512,192]{1,0:T(8,128)(2,1)S(1)}, u32[]{:S(2)}, u32[]{:S(2)}) collective-permute-start(bf16[512,192]{1,0:T(8,128)(2,1)S(1)} %copy-done.25), channel_id=1, source_target_pairs={{0,12},{4,8},{8,4},{12,0},{1,13},{5,9},{9,5},{13,1},{2,14},{6,10},... | collective-permute-start | bytes 589832 | tf_op jit(solution)/shard_map/ppermute | solution.py:73
  327.8 43.2 %collective-permute-start.18 = (bf16[192,768]{1,0:T(8,128)(2,1)}, bf16[192,768]{1,0:T(8,128)(2,1)S(1)}, u32[]{:S(2)}, u32[]{:S(2)}) collective-permute-start(bf16[192,768]{1,0:T(8,128)(2,1)} %convolution_convert_fusion), channel_id=1, source_target_pairs={{0,12},{4,8},{8,4},{12,0},{1,13},{5,9},{9,5},{13,1},{2,14},{6,10},... | collective-permute-start | bytes 884744 | tf_op jit(solution)/shard_map/ppermute | solution.py:73
  329.4 41.6 %collective-permute-start.16 = (bf16[192,768]{1,0:T(8,128)(2,1)}, bf16[192,768]{1,0:T(8,128)(2,1)S(1)}, u32[]{:S(2)}, u32[]{:S(2)}) collective-permute-start(bf16[192,768]{1,0:T(8,128)(2,1)} %convolution_convert_fusion.1), channel_id=1, source_target_pairs={{0,8},{4,12},{8,0},{12,4},{1,9},{5,13},{9,1},{13,5},{2,10},{6,14},... | collective-permute-start | bytes 884744 | tf_op jit(solution)/shard_map/ppermute | solution.py:73
  334.9 36.1 %collective-permute-start.14 = (bf16[192,768]{1,0:T(8,128)(2,1)}, bf16[192,768]{1,0:T(8,128)(2,1)}, u32[]{:S(2)}, u32[]{:S(2)}) collective-permute-start(bf16[192,768]{1,0:T(8,128)(2,1)} %convolution_convert_fusion.2), channel_id=1, source_target_pairs={{0,4},{4,0},{8,12},{12,8},{1,5},{5,1},{9,13},{13,9},{2,6},{6,2},{1... | collective-permute-start | bytes 884744 | tf_op jit(solution)/shard_map/ppermute | solution.py:73
  335.6 35.4 %copy-start = (bf16[3,384,1024]{2,1,0:T(8,128)(2,1)}, bf16[3,384,1024]{2,1,0:T(8,128)(2,1)S(1)}, u32[]{:S(2)}) copy-start(bf16[3,384,1024]{2,1,0:T(8,128)(2,1)S(1)} %collective-permute-done.20.refs_2_) | copy-start | bytes 7077892
  335.6 184.2 %collective-permute-start.21 = (bf16[3,384,1024]{2,1,0:T(8,128)(2,1)S(1)}, bf16[3,384,1024]{2,1,0:T(8,128)(2,1)}, u32[]{:S(2)}, u32[]{:S(2)}) collective-permute-start(bf16[3,384,1024]{2,1,0:T(8,128)(2,1)S(1)} %collective-permute-done.20.refs_2_), channel_id=1, source_target_pairs={{0,4},{4,0},{8,12},{12,8},{1,5},{5,1},{9,13},{13,9},{2,6},{6,2},{1... | collective-permute-start | bytes 7077896 | tf_op jit(solution)/shard_map/ppermute | solution.py:73
  507.8 4.5 copy-start.12
  507.8 5.8 %copy-start.27 = (f32[1,128]{1,0:T(1,128)S(1)}, f32[1,128]{1,0:T(1,128)}, u32[]{:S(2)}) copy-start(f32[1,128]{1,0:T(1,128)} %get-tuple-element.137) | copy-start | bytes 1540
  507.8 5.9 %copy-start.22 = (f32[1,768]{1,0:T(1,128)S(1)}, f32[1,768]{1,0:T(1,128)}, u32[]{:S(2)}) copy-start(f32[1,768]{1,0:T(1,128)} %get-tuple-element.132) | copy-start | bytes 9220
  536.3 9.1 %copy-start.7 = (bf16[512,768]{1,0:T(8,128)(2,1)S(1)}, bf16[512,768]{1,0:T(8,128)(2,1)}, u32[]{:S(2)}) copy-start(bf16[512,768]{1,0:T(8,128)(2,1)} %get-tuple-element.130) | copy-start | bytes 2359300
  545.4 1.7 copy-start.5
  (2 other events, 1.5 us)

commit v4 on v3

--- a/solution.py
+++ b/solution.py
@@ -1,4 +1,4 @@
-import functools
+import math
 
 import jax
 import jax.numpy as jnp
@@ -121,17 +121,6 @@
 dma = pltpu.SemaphoreType.DMA
 
 
-def gather_near(value, axis):
-    count = lax.axis_size(axis)
-    found = {0: value}
-    bit = count // 2
-    while bit:
-        for have in list(found):
-            found[have | bit] = swap(found[have], axis, bit)
-        bit //= 2
-    return [found[j] for j in range(count)]
-
-
 def add_low(*terms):
     total = terms[0].astype(f32)
     for term in terms[1:]:
@@ -139,61 +128,187 @@
     return total.astype(bf16)
 
 
-def project(turn, rows_low, gain, weights_t, meta, earlier, group_rows, tile, layout):
-    row_count, width = rows_low.shape
-    per_group = weights_t.shape[2]
+def begin(x, grad, routes, gain, w_qkv, local):
+    rows, width = x.shape
+    members, groups = lax.axis_size("ctx"), lax.axis_size("exp")
+    group_rows = rows * members
+    heads = HEADS // members
     head_width = width // HEADS
-    heads = per_group // head_width
-    steps = row_count // tile
+    columns = heads * head_width
+    places = groups * local
     scale = head_width**-0.5
-
-    def body(meta_ref, x_ref, gain_ref, w_ref, *refs):
-        q_ref, k_ref, v_ref, kt_ref, vt_ref, h_ref = refs[-6:]
-        x = x_ref[...].astype(f32)
-        inverse = lax.rsqrt(jnp.mean(x * x, axis=1, keepdims=True) + norm_eps)
-        low = (x * inverse * gain_ref[...]).astype(bf16)
-        h_ref[...] = low
-        q = mm(low, w_ref[0, 0], NT).astype(bf16) * jnp.asarray(scale, bf16)
-        k = mm(low, w_ref[1, 0], NT).astype(bf16)
-        v = mm(low, w_ref[2, 0], NT).astype(bf16)
-        for h in range(heads):
-            part = slice(h * head_width, (h + 1) * head_width)
-            q_ref[h] = q[:, part]
-            k_ref[h] = k[:, part]
-            v_ref[h] = v[:, part]
-        kt_ref[...] = mm(w_ref[1, 0], low, NT).astype(bf16)
-        vt_ref[...] = mm(w_ref[2, 0], low, NT).astype(bf16)
-
-    by_head = shape_of((heads, group_rows, head_width), bf16)
-    by_column = shape_of((per_group, group_rows), bf16)
-    hidden = shape_of((group_rows, width), bf16)
-    head_spec = pl.BlockSpec((heads, tile, head_width), lambda i, m: (0, block_place(m, turn * steps + i, steps, layout), 0))
-    column_spec = pl.BlockSpec((per_group, tile), lambda i, m: (0, block_place(m, turn * steps + i, steps, layout)))
-    hidden_spec = pl.BlockSpec((tile, width), lambda i, m: (turn * steps + i, 0))
-    inputs = [
-        (rows_low, pl.BlockSpec((tile, width), lambda i, m: (i, 0))),
-        (gain, pl.BlockSpec((1, width), lambda i, m: (0, 0))),
-        (weights_t, pl.BlockSpec((3, 1, per_group, width), lambda i, m: (0, m[0], 0, 0))),
-    ]
-    aliases = None
-    if earlier is not None:
-        inputs += [(a, pl.BlockSpec(memory_space=pl.ANY)) for a in earlier]
-        aliases = {4 + n: n for n in range(6)}
+    tile = min(256, rows)
+    per_member = rows // tile
+
+    def body(*refs):
+        x_hbm, dy_ref, route_ref, gain_ref, w_hbm = refs[:5]
+        q_out, k_out, v_out, kt_out, vt_out, h_out, wt_out = refs[5:12]
+        target_out, target_rows, near_out, rest_out = refs[12:16]
+        x_near, w_in, w_t, q_all, k_all, v_all, kt_all, vt_all, h_all, packed, near = refs[16:27]
+        load_sem, x_s, x_r, r_s, r_r, out_sem, near_sem = refs[27:]
+        me, exp_now = lax.axis_index("ctx"), lax.axis_index("exp")
+        side = lax.div(me, 2)
+        peers = [{"ctx": flip(me, 1)}, {"ctx": flip(me, 2)}]
+        peers += [slot_peer(local * g, local, exp_now, me) for g in range(1, groups)]
+        ready = greet(peers)
+        own = pltpu.make_async_copy(x_hbm, x_near.at[0], load_sem.at[0])
+        weights = pltpu.make_async_copy(w_hbm, w_in, load_sem.at[1])
+        own.start()
+        weights.start()
+
+        def across():
+            return remote(x_hbm, x_near.at[2], x_s.at[2], x_r.at[2], {"ctx": flip(me, 2)})
+
+        def beside():
+            return remote(x_hbm, x_near.at[1], x_s.at[1], x_r.at[1], {"ctx": flip(me, 1)})
+
+        def passed():
+            return remote(x_near.at[2], x_near.at[3], x_s.at[3], x_r.at[3], {"ctx": flip(me, 1)})
+
+        def row_copy(g):
+            return remote(
+                packed.at[g], near.at[g], r_s.at[g], r_r.at[g],
+                slot_peer(local * g, local, exp_now, me),
+            )
+
+        ready()
+        across().start()
+        beside().start()
+
+        chosen = route_ref[...]
+        expert_count = places
+        lanes = lax.broadcasted_iota(jnp.int32, (rows, 128), 1)
+        hits = [lanes == chosen[:, c : c + 1] for c in range(2)]
+        hit = jnp.where((hits[0] | hits[1]) & (lanes < expert_count), 1.0, 0.0)
+        later = lax.broadcasted_iota(jnp.int32, (rows, rows), 0)
+        sooner = lax.broadcasted_iota(jnp.int32, (rows, rows), 1)
+        ahead = mm(jnp.where(sooner < later, 1.0, 0.0).astype(bf16), hit.astype(bf16))
+        spots = []
+        for c in range(2):
+            ids = chosen[:, c : c + 1]
+            rank = jnp.sum(jnp.where(hits[c], ahead, 0.0), axis=1, keepdims=True).astype(jnp.int32)
+            far_z = lax.div(ids, local)
+            far_y = lax.rem(ids, local)
+            z = jnp.zeros_like(ids)
+            bit = 1
+            while bit < groups:
+                z = z + bit * jnp.where(
+                    lax.rem(lax.div(far_z, bit), 2) == lax.rem(lax.div(exp_now, bit), 2), 0, 1
+                )
+                bit *= 2
+            y = jnp.where(far_y == side, 0, 1)
+            spots.append(jnp.where(ids < expert_count, (z * local + y) * CAP + rank, -1))
+        target_out[...] = jnp.concatenate(spots, axis=1)
+        wide = jnp.where(lanes == 0, spots[0], spots[1]).astype(f32)
+        target_rows[...] = jnp.transpose(wide)[0:2, :].astype(jnp.int32)
+
+        def pack(n, r):
+            packed[n] = mm(slot_choice(r * CAP, CAP, target_rows), dy_ref[...]).astype(bf16)
+
+        for g in range(groups - 1, -1, -1):
+            pack(g, local * g)
+            if g < groups - 1:
+                row_copy(g + 1).start()
+        odd = [r for r in range(places) if r % local]
+        for n, r in enumerate(odd):
+            pack(groups + n, r)
+        stores = [
+            pltpu.make_async_copy(packed.at[0], near_out.at[0], near_sem.at[0]),
+            pltpu.make_async_copy(packed.at[pl.ds(groups, len(odd))], rest_out, near_sem.at[groups]),
+        ]
+        for copy in stores:
+            copy.start()
+        weights.wait()
+        for w in range(3):
+            w_t[w] = jnp.transpose(w_in[w])
+        w_store = pltpu.make_async_copy(w_t, wt_out, load_sem.at[2])
+        w_store.start()
+        here = pl.ds(pl.multiple_of(me * columns, columns), columns)
+
+        def chunk(j):
+            def project(t, _):
+                at = pl.multiple_of(t * tile, tile)
+                to = pl.ds(pl.multiple_of(j * rows + t * tile, tile), tile)
+                value = x_near[j, pl.ds(at, tile), :].astype(f32)
+                inverse = lax.rsqrt(jnp.mean(value * value, axis=1, keepdims=True) + norm_eps)
+                low = (value * inverse * gain_ref[...]).astype(bf16)
+                h_all[to, :] = low
+                q = mm(low, w_t[0, here, :], NT).astype(bf16) * jnp.asarray(scale, bf16)
+                k = mm(low, w_t[1, here, :], NT).astype(bf16)
+                v = mm(low, w_t[2, here, :], NT).astype(bf16)
+                for h in range(heads):
+                    part = slice(h * head_width, (h + 1) * head_width)
+                    q_all[h, to, :] = q[:, part]
+                    k_all[h, to, :] = k[:, part]
+                    v_all[h, to, :] = v[:, part]
+                kt_all[:, to] = mm(w_t[1, here, :], low, NT).astype(bf16)
+                vt_all[:, to] = mm(w_t[2, here, :], low, NT).astype(bf16)
+                return 0
+
+            lax.fori_loop(0, per_member, project, 0)
+            for copy in chunk_stores(j):
+                copy.start()
+
+        def chunk_stores(j):
+            to = pl.ds(j * rows, rows)
+            pairs = [(q_all, q_out), (k_all, k_out), (v_all, v_out)]
+            found = [(a.at[:, to, :], b.at[:, to, :]) for a, b in pairs]
+            found += [(a.at[:, to], b.at[:, to]) for a, b in ((kt_all, kt_out), (vt_all, vt_out))]
+            found += [(h_all.at[to, :], h_out.at[to, :])]
+            return [
+                pltpu.make_async_copy(a, b, out_sem.at[6 * j + n]) for n, (a, b) in enumerate(found)
+            ]
+
+        own.wait()
+        chunk(0)
+        beside().wait()
+        chunk(1)
+        across().wait()
+        passed().start()
+        chunk(2)
+        passed().wait()
+        chunk(3)
+        for g in range(1, groups):
+            row_copy(g).wait()
+            pltpu.make_async_copy(near.at[g], near_out.at[g], near_sem.at[g]).start()
+        for copy in stores:
+            copy.wait()
+        w_store.wait()
+        for j in range(members):
+            for copy in chunk_stores(j):
+                copy.wait()
+        for g in range(1, groups):
+            pltpu.make_async_copy(near.at[g], near_out.at[g], near_sem.at[g]).wait()
+
+    by_head = (heads, group_rows, head_width)
+    by_column = (columns, group_rows)
+    slots = (places, CAP, width)
     return run(
         body,
-        (steps,),
-        inputs,
-        [(by_head, head_spec)] * 3 + [(by_column, column_spec)] * 2 + [(hidden, hidden_spec)],
-        meta=meta,
-        flops=2 * row_count * width * per_group * 5,
-        moved=row_count * width * 8 + weights_t.size // 2,
-        aliases=aliases,
-    )
-
-
-def block_place(meta_ref, block, per_member, layout):
-    member = meta_ref[0] ^ (block // per_member)
-    return meta_ref[layout["order"] + member * per_member + block % per_member]
+        (),
+        [(x, anywhere), (grad, vector), (routes, vector), (gain, vector), (w_qkv, anywhere)],
+        [(shape_of(by_head, bf16), anywhere)] * 3
+        + [(shape_of(by_column, bf16), anywhere)] * 2
+        + [(shape_of((group_rows, width), bf16), anywhere)]
+        + [(shape_of((3, width, width), bf16), anywhere)]
+        + [(shape_of((rows, 2), jnp.int32), vector), (shape_of((2, rows), jnp.int32), vector)]
+        + [(shape_of((groups, CAP, width), bf16), anywhere)]
+        + [(shape_of((places - groups, CAP, width), bf16), anywhere)],
+        scratch=[
+            pltpu.VMEM((members, rows, width), bf16),
+            pltpu.VMEM((3, width, width), bf16),
+            pltpu.VMEM((3, width, width), bf16),
+            pltpu.VMEM(by_head, bf16), pltpu.VMEM(by_head, bf16), pltpu.VMEM(by_head, bf16),
+            pltpu.VMEM(by_column, bf16), pltpu.VMEM(by_column, bf16),
+            pltpu.VMEM((group_rows, width), bf16),
+            pltpu.VMEM(slots, bf16), pltpu.VMEM(slots, bf16),
+            dma((3,)), dma((members,)), dma((members,)), dma((places,)), dma((places,)),
+            dma((6 * members,)), dma((places + 1,)),
+        ],
+        flops=2 * group_rows * width * columns * 5,
+        moved=20 * 1024 * 1024,
+        talks=4,
+    )
 
 
 def document_start(meta_ref, position, layout):
@@ -234,7 +349,7 @@
 
         def one(j, _):
             q_first, k_first, needed, full = block_range(meta_ref, i, j, rows, layout)
-            at = pl.multiple_of(j * rows, rows)
+            at = pl.multiple_of(meta_ref[layout["inverse"] + j] * rows, rows)
 
             def step(masked):
                 if masked:
@@ -269,7 +384,16 @@
             part = slice(h * head_width, (h + 1) * head_width)
             ot_ref[part, :] = a_ref[part, :] / l_ref[h]
             lse_ref[pl.ds(h, 1), :] = m_ref[h] + jnp.log(l_ref[h])
-            top_ref[pl.ds(h, 1), :] = m_ref[h]
+            top = m_ref[h]
+
+            @pl.when(i == 0)
+            def _():
+                top_ref[pl.ds(h, 1), :] = top
+
+            @pl.when(i > 0)
+            def _():
+                top_ref[pl.ds(h, 1), :] = jnp.maximum(top_ref[pl.ds(h, 1), :], top)
+
         o_ref[...] = jnp.transpose(ot_ref[...]).astype(bf16)
 
     row = shape_of((heads, group_rows), f32)
@@ -278,7 +402,12 @@
         body,
         (blocks,),
         [
-            (q, pl.BlockSpec((heads, rows, head_width), lambda i, m: (0, i, 0))),
+            (
+                q,
+                pl.BlockSpec(
+                    (heads, rows, head_width), lambda i, m: (0, m[layout["inverse"] + i], 0)
+                ),
+            ),
             (k, whole(k)),
             (vt, whole(vt)),
         ],
@@ -289,7 +418,7 @@
             ),
             (shape_of((width, group_rows), f32), pl.BlockSpec((width, rows), lambda i, m: (0, i))),
             (row, row_spec),
-            (row, row_spec),
+            (shape_of((heads, rows), f32), pl.BlockSpec((heads, rows), lambda i, m: (0, 0))),
         ],
         scratch=[
             pltpu.VMEM((heads, 1, rows), f32),
@@ -303,17 +432,15 @@
     )
 
 
-def attend_back(meta, q, k, v, kt, grad, ot, lse, rows, layout):
+def attend_back(meta, q, k, v, kt, grad, w_out, ot, lse, rows, layout):
     heads, group_rows, head_width = q.shape
     blocks = group_rows // rows
     width = heads * head_width
     scale = head_width**-0.5
-    members = len(grad)
-    per = grad[0].shape[0] // rows
-
-    def body(meta_ref, q_ref, k_ref, v_ref, kt_ref, *refs):
-        grads = refs[:members]
-        ot_ref, lse_ref, out_ref, dk_ref, dv_ref, dq_ref, g_ref, delta_ref = refs[members:]
+    per = grad.shape[1] // rows
+
+    def body(meta_ref, q_ref, k_ref, v_ref, kt_ref, grad_ref, w_ref, *refs):
+        ot_ref, lse_ref, out_ref, rows_ref, dk_ref, dv_ref, dq_ref, g_ref, delta_ref, sum_ref = refs
         i = pl.program_id(0)
 
         @pl.when(i == 0)
@@ -321,23 +448,31 @@
             dk_ref[...] = jnp.zeros_like(dk_ref)
             dv_ref[...] = jnp.zeros_like(dv_ref)
 
-        for n in range(members):
-
-            @pl.when(meta_ref[layout["inverse"] + i] // per == n)
-            def _():
-                g = grads[n][...]
-                for h in range(heads):
-                    g_ref[h] = g[:, h * head_width : (h + 1) * head_width]
-                product = jnp.transpose(g.astype(f32)) * ot_ref[...]
-                for h in range(heads):
-                    part = slice(h * head_width, (h + 1) * head_width)
-                    delta_ref[h] = jnp.sum(product[part, :], axis=0, keepdims=True)
+        da = grad_ref[0]
+        g = mm(da, w_ref[0], NT).astype(bf16)
+        part_sum = mm(ot_ref[...].astype(bf16), da)
+
+        @pl.when(i == 0)
+        def _():
+            sum_ref[...] = part_sum
+
+        @pl.when(i > 0)
+        def _():
+            sum_ref[...] += part_sum
+
+        for h in range(heads):
+            g_ref[h] = g[:, h * head_width : (h + 1) * head_width]
+        product = jnp.transpose(g.astype(f32)) * ot_ref[...]
+        for h in range(heads):
+            part = slice(h * head_width, (h + 1) * head_width)
+            delta_ref[h] = jnp.sum(product[part, :], axis=0, keepdims=True)
 
         dq_ref[...] = jnp.zeros_like(dq_ref)
 
         def one(j, _):
             q_first, k_first, needed, full = block_range(meta_ref, i, j, rows, layout)
-            at = pl.multiple_of(j * rows, rows)
+            at = pl.multiple_of(meta_ref[layout["inverse"] + j] * rows, rows)
+            to = pl.multiple_of(j * rows, rows)
 
             def step(masked):
                 if masked:
@@ -350,8 +485,8 @@
                     p = jnp.exp(s - lse_ref[pl.ds(h, 1), :])
                     dp = mm(v_ref[h, pl.ds(at, rows), :], g_ref[h], NT)
                     ds = (p * (dp - delta_ref[h])).astype(bf16)
-                    dv_ref[h, pl.ds(at, rows), :] += mm(p.astype(bf16), g_ref[h])
-                    dk_ref[h, pl.ds(at, rows), :] += mm(ds, q_ref[h])
+                    dv_ref[h, pl.ds(to, rows), :] += mm(p.astype(bf16), g_ref[h])
+                    dk_ref[h, pl.ds(to, rows), :] += mm(ds, q_ref[h])
                     dq_ref[part, :] += mm(kt_ref[part, pl.ds(at, rows)], ds)
 
             @pl.when(full)
@@ -370,6 +505,8 @@
 
         @pl.when(i == blocks - 1)
         def _():
+            rows_ref[...] = sum_ref[...].astype(bf16)
+
             def store(b, _):
                 spot = pl.multiple_of(b * rows, rows)
                 there = pl.multiple_of(meta_ref[layout["inverse"] + b] * rows, rows)
@@ -382,53 +519,50 @@
 
             lax.fori_loop(0, blocks, store, 0)
 
-    grad_specs = [
-        pl.BlockSpec((rows, width), lambda i, m, n=n: (jnp.clip(m[layout["inverse"] + i] - n * per, 0, per - 1), 0))
-        for n in range(members)
-    ]
     out = shape_of((group_rows, 3 * width), bf16)
+    out_rows = shape_of((width, grad.shape[2]), bf16)
     return run(
         body,
         (blocks,),
         [
-            (q, pl.BlockSpec((heads, rows, head_width), lambda i, m: (0, i, 0))),
+            (
+                q,
+                pl.BlockSpec(
+                    (heads, rows, head_width), lambda i, m: (0, m[layout["inverse"] + i], 0)
+                ),
+            ),
             (k, whole(k)),
             (v, whole(v)),
             (kt, whole(kt)),
         ]
-        + list(zip(grad, grad_specs))
         + [
+            (
+                grad,
+                pl.BlockSpec(
+                    (1, rows, grad.shape[2]),
+                    lambda i, m: (
+                        m[layout["inverse"] + i] // per, m[layout["inverse"] + i] % per, 0
+                    ),
+                ),
+            ),
+            (w_out, pl.BlockSpec((1, width, grad.shape[2]), lambda i, m: (m[0], 0, 0))),
             (ot, pl.BlockSpec((width, rows), lambda i, m: (0, i))),
             (lse, pl.BlockSpec((heads, rows), lambda i, m: (0, i))),
         ],
-        [(out, whole(out))],
+        [(out, whole(out)), (out_rows, whole(out_rows))],
         scratch=[
             pltpu.VMEM((heads, group_rows, head_width), f32),
             pltpu.VMEM((heads, group_rows, head_width), f32),
             pltpu.VMEM((width, rows), f32),
             pltpu.VMEM((heads, rows, head_width), bf16),
             pltpu.VMEM((heads, 1, rows), f32),
+            pltpu.VMEM((width, grad.shape[2]), f32),
         ],
         meta=meta,
         flops=5 * 2 * group_rows * group_rows * width,
         moved=group_rows * width * 24,
         exps=group_rows * group_rows * heads // 2,
-    )[0]
-
-
-def slot_targets(route_ids, expert_count, local_experts, mine, side):
-    rows = route_ids.shape[0]
-    experts = jnp.arange(expert_count, dtype=jnp.int32)
-    hits = route_ids[:, :, None] == experts[None, None, :]
-    hit = jnp.any(hits, axis=1)
-    order = lax.broadcasted_iota(jnp.int32, (rows, rows), 0)
-    other = lax.broadcasted_iota(jnp.int32, (rows, rows), 1)
-    ahead = mm((other < order).astype(bf16), hit.astype(bf16)).astype(jnp.int32)
-    rank = jnp.sum(jnp.where(hits, ahead[:, None, :], 0), axis=2)
-    near = ((route_ids // local_experts) ^ mine) * local_experts + (
-        (route_ids % local_experts) ^ side
-    )
-    return jnp.where(route_ids < expert_count, near * CAP + rank, -1)
+    )
 
 
 def slot_choice(first, count, target_ref):
@@ -436,28 +570,6 @@
     ids = first + lax.broadcasted_iota(jnp.int32, (count, rows), 0)
     match = (ids == target_ref[0:1, :]) | (ids == target_ref[1:2, :])
     return jnp.where(match, 1.0, 0.0).astype(bf16)
-
-
-def dispatch(target_rows, source, places):
-    rows, width = source.shape
-
-    def body(target_ref, source_ref, out_ref):
-        choice = slot_choice(pl.program_id(0) * CAP, CAP, target_ref)
-        out_ref[0] = mm(choice, source_ref[...]).astype(bf16)
-
-    return run(
-        body,
-        (places,),
-        [(target_rows, whole(target_rows)), (source, whole(source))],
-        [
-            (
-                shape_of((places, CAP, width), bf16),
-                pl.BlockSpec((1, CAP, width), lambda r: (r, 0, 0)),
-            )
-        ],
-        flops=2 * rows * width * places * CAP,
-        moved=(rows + places * CAP) * width * 2,
-    )[0]
 
 
 def token_front(
@@ -653,12 +765,13 @@
     )
 
 
-def expert_layer(arrived, grads, gates, w_gate, w_up, w_down):
+def expert_layer(arrived, grads, late, gates, w_gate, w_up, w_down):
     places = arrived.shape[0]
     local = w_gate.shape[0]
     rows = places * CAP
     width, hidden = w_gate.shape[1], w_gate.shape[2]
     parts = lax.axis_size("dp")
+    groups = places // local
     half = width // 2
     per_part = hidden // parts
     tile = min(256, per_part)
@@ -669,11 +782,18 @@
 
     def body(*refs):
         x_ref, dy_ref, gates_ref, wg_hbm, wu_hbm, wd_hbm = refs[:6]
-        y_out, dx_out, dots_out, sum_out = refs[6:10]
-        x_all, xt_all, dy_all, dyt_all, gate_all, y_acc, dx_acc, dot_acc = refs[10:18]
-        hid_t, dgt, dut, scaled_t, wg_buf, wu_buf, wd_buf = refs[18:25]
-        send, total, taken, far, dx_low, dx_near, dots, dots_near = refs[25:33]
-        w_sem, c_s, c_r, f_s, f_r, b_s, b_r, d_s, d_r, out_sem = refs[33:]
+        dy_late, refs = refs[6 : 6 + len(late)], refs[:6] + refs[6 + len(late) :]
+        dy_parts = [
+            dy_late[r // local] if r % local else dy_ref.at[r // local] for r in range(places)
+        ]
+        y_out, dx_out, dots_out, sum_out, beside_out = refs[6:11]
+        x_all, xt_all, dy_all, dyt_all, gate_all, y_acc, dx_acc, dot_acc = refs[11:19]
+        hid_t, dgt, dut, scaled_t, wg_buf, wu_buf, wd_buf = refs[19:26]
+        hid_own, dg_own, du_own, scaled_own, wg_own, wu_own, wd_own = refs[26:33]
+        send, total, taken, far, dx_low, dx_near, dots, dots_near = refs[33:41]
+        beside, y_odd, relay = refs[41:44]
+        w_sem, own_sem, c_s, c_r, f_s, f_r, b_s, b_r, d_s, d_r, out_sem = refs[44:55]
+        e_s, e_r, beside_sem, y_s, y_r = refs[55:]
         me, exp_now, dp_now = lax.axis_index("ctx"), lax.axis_index("exp"), lax.axis_index("dp")
         core, side = lax.rem(me, 2), lax.div(me, 2)
         sibling = {"ctx": flip(me, 1)}
@@ -726,14 +846,31 @@
                 slot_peer(r, local, exp_now, me),
             )
 
-        for copy in weights(0, 0):
+        def own_weights():
+            at = pl.ds(pl.multiple_of(dp_now * per_part, per_part), per_part)
+            return [
+                pltpu.make_async_copy(wg_hbm.at[side, :, at], wg_own, own_sem.at[0]),
+                pltpu.make_async_copy(wu_hbm.at[side, :, at], wu_own, own_sem.at[1]),
+                pltpu.make_async_copy(wd_hbm.at[side, at, :], wd_own, own_sem.at[2]),
+            ]
+
+        if away:
+            for copy in weights(0, 0):
+                copy.start()
+        for copy in own_weights():
             copy.start()
+        first_half = pl.ds(pl.multiple_of((1 - core) * half, half), half)
+        second_half = pl.ds(pl.multiple_of(core * half, half), half)
         for r in range(places):
             here = slice(r * CAP, (r + 1) * CAP)
             x_all[here, :] = x_ref[r]
-            xt_all[:, here] = jnp.transpose(x_ref[r])
-            dy_all[here, :] = dy_ref[r]
-            dyt_all[:, here] = jnp.transpose(dy_ref[r])
+            turned = jnp.transpose(x_ref[r])
+            xt_all[first_half, here] = turned[:half, :]
+            xt_all[second_half, here] = turned[half:, :]
+            dy_all[here, :] = dy_parts[r][...]
+            turned = jnp.transpose(dy_parts[r][...])
+            dyt_all[first_half, here] = turned[:half, :]
+            dyt_all[second_half, here] = turned[half:, :]
             gate_all[here, :] = jnp.sum(
                 jnp.where(diagonal, gates_ref[r], 0.0), axis=1, keepdims=True
             )
@@ -741,88 +878,178 @@
         dx_acc[...] = jnp.zeros_like(dx_acc)
         dot_acc[...] = jnp.zeros_like(dot_acc)
         ready()
-        mine = pl.ds(pl.multiple_of(core * half, half), half)
-        theirs = pl.ds(pl.multiple_of((1 - core) * half, half), half)
 
         def core_sum(f):
             core_copy(f, lax.rem(f, 2)).wait_recv()
             for n in range(3):
                 total[f, n] = (total[f, n].astype(f32) + taken[f, n].astype(f32)).astype(bf16)
 
-        def step(f, _):
+        def forward_back(here, wg, wu, wd, hid_ref, dg_ref, du_ref, scaled_ref):
+            g_pre = mm(x_all[here, :], wg)
+            u_pre = mm(x_all[here, :], wu)
+            back = mm(dy_all[here, :], wd, NT)
+            gate = gate_all[here, :]
+            sig = 1.0 / (1.0 + jnp.exp(-g_pre))
+            act = g_pre * sig
+            hid = act * u_pre
+            hid_ref[here, :] = hid.astype(bf16)
+            scaled_ref[here, :] = (gate * hid).astype(bf16)
+            along = hid * back
+            lines = along[:, 0:128]
+            for n in range(1, tile // 128):
+                lines = lines + along[:, n * 128 : (n + 1) * 128]
+            dot_acc[here, :] += lines
+            dhid = gate * back
+            dg = (dhid * u_pre * sig * (1.0 + g_pre * (1.0 - sig))).astype(bf16)
+            du = (dhid * act).astype(bf16)
+            dg_ref[here, :] = dg
+            du_ref[here, :] = du
+
+        def rows_back(here, wg, wu, dg_ref, du_ref):
+            dx_acc[here, :] += mm(dg_ref[here, :], wg, NT) + mm(du_ref[here, :], wu, NT)
+
+        def weight_sums(f, slot, hid_ref, dg_ref, du_ref, scaled_ref, wd):
+            @pl.when(f >= 1)
+            def _():
+                core_sum(f - 1)
+
+            @pl.when(f >= 2)
+            def _():
+                core_copy(f - 2, slot).wait_send()
+
+            for n, (left, right) in enumerate(((xt_all, dg_ref), (xt_all, du_ref), (dyt_all, scaled_ref))):
+                found = mm(left[...], right[...]).astype(bf16)
+                send[slot, n] = found[:half, :]
+                total[f, n] = found[half:, :]
+            core_copy(f, slot).start()
+
+            @pl.when((f >= 1) & (f - 1 < away))
+            def _():
+                far_copy(f - 1).start()
+
+            y_acc[...] += mm(hid_ref[...], wd)
+
+        def away_step(f, _):
             slot = lax.rem(f, 2)
             for copy in weights(f, slot):
                 copy.wait()
 
-            @pl.when(f + 1 < steps)
+            @pl.when(f + 1 < away)
             def _():
                 for copy in weights(f + 1, 1 - slot):
                     copy.start()
 
-            wg, wu, wd = wg_buf.at[slot], wu_buf.at[slot], wd_buf.at[slot]
-
             def row_chunk(c, _):
                 here = pl.ds(pl.multiple_of(c * chunk, chunk), chunk)
-                g_pre = mm(x_all[here, :], wg[...])
-                u_pre = mm(x_all[here, :], wu[...])
-                back = mm(dy_all[here, :], wd[...], NT)
-                gate = gate_all[here, :]
-                sig = 1.0 / (1.0 + jnp.exp(-g_pre))
-                act = g_pre * sig
-                hid = act * u_pre
-                hid_t[here, :] = hid.astype(bf16)
-                scaled_t[here, :] = (gate * hid).astype(bf16)
-                along = hid * back
-                lines = along[:, 0:128]
-                for n in range(1, tile // 128):
-                    lines = lines + along[:, n * 128 : (n + 1) * 128]
-                dot_acc[here, :] += lines
-                dhid = gate * back
-                dgt[here, :] = (dhid * u_pre * sig * (1.0 + g_pre * (1.0 - sig))).astype(bf16)
-                dut[here, :] = (dhid * act).astype(bf16)
+                forward_back(
+                    here, wg_buf[slot], wu_buf[slot], wd_buf[slot], hid_t, dgt, dut, scaled_t
+                )
                 return 0
 
             lax.fori_loop(0, rows // chunk, row_chunk, 0)
-
-            @pl.when(f >= 1)
+            weight_sums(f, slot, hid_t, dgt, dut, scaled_t, wd_buf[slot])
+            rows_back(slice(0, rows), wg_buf[slot], wu_buf[slot], dgt, dut)
+            return 0
+
+        lax.fori_loop(0, away, away_step, 0)
+        for copy in own_weights():
+            copy.wait()
+        if away:
+            core_sum(away - 1)
+            far_copy(away - 1).start()
+
+        def own_rows(first, count):
+            size = min(chunk, count)
+
+            def own_tile(i, _):
+                at = pl.ds(pl.multiple_of(i * tile, tile), tile)
+                for c in range(count // size):
+                    forward_back(
+                        slice(first + c * size, first + (c + 1) * size),
+                        wg_own[:, at], wu_own[:, at], wd_own[at, :],
+                        hid_own.at[i], dg_own.at[i], du_own.at[i], scaled_own.at[i],
+                    )
+                rows_back(
+                    slice(first, first + count), wg_own[:, at], wu_own[:, at], dg_own.at[i], du_own.at[i]
+                )
+                return 0
+
+            lax.fori_loop(0, tiles, own_tile, 0)
+
+        def send_back(first, last):
+            for r in range(first, last):
+                here = slice(r * CAP, (r + 1) * CAP)
+                dx_low[r] = dx_acc[here, :].astype(bf16)
+                column = jnp.sum(dot_acc[here, :], axis=1, keepdims=True)
+                dots[r] = jnp.sum(jnp.where(diagonal, column, 0.0), axis=0, keepdims=True)
+                if r - 1 >= max(1, first):
+                    back_copy(r - 1).start()
+                    dots_copy(r - 1).start()
+
+        def send_last(r):
+            back_copy(r).start()
+            dots_copy(r).start()
+
+        middle = places // 2
+        own_rows(middle * CAP, rows - middle * CAP)
+        send_back(middle, places)
+        own_rows(0, middle * CAP)
+        send_last(places - 1)
+        send_back(0, middle)
+
+        def own_step(i, _):
+            f = away + i
+            at = pl.ds(pl.multiple_of(i * tile, tile), tile)
+
+            @pl.when(i == 1)
+            def _():
+                send_last(middle - 1)
+
+            @pl.when(i >= 1)
             def _():
                 core_sum(f - 1)
+
+            slot = lax.rem(f, 2)
 
             @pl.when(f >= 2)
             def _():
                 core_copy(f - 2, slot).wait_send()
 
-            send[slot, 0] = mm(xt_all[theirs, :], dgt[...]).astype(bf16)
-            send[slot, 1] = mm(xt_all[theirs, :], dut[...]).astype(bf16)
-            send[slot, 2] = mm(dyt_all[theirs, :], scaled_t[...]).astype(bf16)
-            total[f, 0] = mm(xt_all[mine, :], dgt[...]).astype(bf16)
+            dg, du, scaled = dg_own.at[i], du_own.at[i], scaled_own.at[i]
+            for n, (left, right) in enumerate(((xt_all, dg), (xt_all, du), (dyt_all, scaled))):
+                found = mm(left[...], right[...]).astype(bf16)
+                send[slot, n] = found[:half, :]
+                total[f, n] = found[half:, :]
             core_copy(f, slot).start()
-
-            @pl.when((f >= 1) & (f - 1 < away))
-            def _():
-                far_copy(f - 1).start()
-
-            total[f, 1] = mm(xt_all[mine, :], dut[...]).astype(bf16)
-            total[f, 2] = mm(dyt_all[mine, :], scaled_t[...]).astype(bf16)
-            y_acc[...] += mm(hid_t[...], wd[...])
-            dx_acc[...] += mm(dgt[...], wg[...], NT) + mm(dut[...], wu[...], NT)
+            y_acc[...] += mm(hid_own[i], wd_own[at, :])
             return 0
 
-        lax.fori_loop(0, steps, step, 0)
-        for r in range(places):
+        lax.fori_loop(0, tiles, own_step, 0)
+        if tiles == 1:
+            send_last(middle - 1)
+        core_sum(steps - 1)
+        def relay_copy(g):
+            return remote(y_odd.at[g], relay.at[g], y_s.at[g], y_r.at[g], {"ctx": flip(me, 2)})
+
+        def result(r):
             here = slice(r * CAP, (r + 1) * CAP)
-            dx_low[r] = dx_acc[here, :].astype(bf16)
-            column = jnp.sum(dot_acc[here, :], axis=1, keepdims=True)
-            dots[r] = jnp.sum(jnp.where(diagonal, column, 0.0), axis=0, keepdims=True)
-            if r > 1:
-                back_copy(r - 1).start()
-                dots_copy(r - 1).start()
-        core_sum(steps - 1)
-        back_copy(places - 1).start()
-        dots_copy(places - 1).start()
-        for r in range(places):
-            here = slice(r * CAP, (r + 1) * CAP)
-            y_out[r] = (gate_all[here, :] * y_acc[here, :]).astype(bf16)
+            return (gate_all[here, :] * y_acc[here, :]).astype(bf16)
+
+        for g in range(groups):
+            y_odd[g] = result(local * g + 1)
+            if g:
+                relay_copy(g - 1).start()
+        for g in range(groups):
+            y_out[g, 0] = result(local * g)
+        relay_copy(groups - 1).start()
+
+        def beside_copy(i):
+            return remote(total.at[away + i], beside.at[i], e_s.at[i], e_r.at[i], sibling)
+
+        def beside_store(i):
+            return pltpu.make_async_copy(
+                beside.at[i], beside_out.at[:, :, pl.ds(i * tile, tile)], beside_sem.at[i]
+            )
 
         def sum_store(i):
             return pltpu.make_async_copy(
@@ -837,7 +1064,10 @@
                 for d in range(1, parts):
                     value = value + far[(parts - 1 - d) * tiles + i, n].astype(f32)
                 total[away + i, n] = value.astype(bf16)
+            if i:
+                beside_copy(i - 1).start()
             sum_store(i).start()
+        beside_copy(tiles - 1).start()
         for f in range(away):
             far_copy(f).wait_send()
         for f in range(max(0, steps - 2), steps):
@@ -850,18 +1080,27 @@
             dots_copy(r).wait()
             dx_out[r] = dx_near[r]
             dots_out[r] = dots_near[r]
+        for g in range(groups):
+            relay_copy(g).wait()
+            y_out[g, 1] = relay[g]
+        for i in range(tiles):
+            beside_copy(i).wait()
+            beside_store(i).start()
         for i in range(tiles):
             sum_store(i).wait()
+            beside_store(i).wait()
 
     placed = shape_of((places, CAP, width), bf16)
+    pairs = shape_of((groups, local, CAP, width), bf16)
     lines = shape_of((places, 1, CAP), f32)
     return run(
         body,
         (),
         [(arrived, vector), (grads, vector), (gates, vector)]
-        + [(w, anywhere) for w in (w_gate, w_up, w_down)],
-        [(placed, vector), (placed, vector), (lines, vector)]
-        + [(shape_of((3, half, per_part), bf16), anywhere)],
+        + [(w, anywhere) for w in (w_gate, w_up, w_down)]
+        + [(g, vector) for g in late],
+        [(pairs, vector), (placed, vector), (lines, vector)]
+        + [(shape_of((3, half, per_part), bf16), anywhere)] * 2,
         scratch=[
             pltpu.VMEM((rows, width), bf16),
             pltpu.VMEM((width, rows), bf16),
@@ -878,6 +1117,13 @@
             pltpu.VMEM((2, width, tile), bf16),
             pltpu.VMEM((2, width, tile), bf16),
             pltpu.VMEM((2, tile, width), bf16),
+            pltpu.VMEM((tiles, rows, tile), bf16),
+            pltpu.VMEM((tiles, rows, tile), bf16),
+            pltpu.VMEM((tiles, rows, tile), bf16),
+            pltpu.VMEM((tiles, rows, tile), bf16),
+            pltpu.VMEM((width, per_part), bf16),
+            pltpu.VMEM((width, per_part), bf16),
+            pltpu.VMEM((per_part, width), bf16),
             pltpu.VMEM((2, 3, half, tile), bf16),
             pltpu.VMEM((steps, 3, half, tile), bf16),
             pltpu.VMEM((steps, 3, half, tile), bf16),
@@ -886,10 +1132,14 @@
             pltpu.VMEM((places, CAP, width), bf16),
             pltpu.VMEM((places, 1, CAP), f32),
             pltpu.VMEM((places, 1, CAP), f32),
-            dma((3, 2)), dma((2,)), dma((steps,)),
+            pltpu.VMEM((tiles, 3, half, tile), bf16),
+            pltpu.VMEM((groups, CAP, width), bf16),
+            pltpu.VMEM((groups, CAP, width), bf16),
+            dma((3, 2)), dma((3,)), dma((2,)), dma((steps,)),
             dma((max(1, away),)), dma((max(1, away),)),
             dma((places,)), dma((places,)), dma((places,)), dma((places,)),
-            dma((tiles,)),
+            dma((tiles,)), dma((tiles,)), dma((tiles,)), dma((tiles,)),
+            dma((groups,)), dma((groups,)),
         ],
         flops=9 * 2 * rows * width * hidden,
         moved=12 * width * hidden + rows * width * 8,
@@ -910,114 +1160,110 @@
 
 
 def token_back(
-    meta, x1, h2, grad, prob, previous, routes, targets, back, dots, dgate_zero, dh_zero, gain, router_t, w_out
+    x1, h2, grad, prob, previous, routes, targets, back, dots, dgate_zero, dh_zero, gain, router_t,
 ):
     rows, width = x1.shape
     tile = 128
+    tiles = rows // tile
     places = back.shape[0]
     expert_all = prob.shape[1]
-    members, head_columns = w_out.shape[0], w_out.shape[1]
-
-    def body(meta_ref, *refs):
+    members = lax.axis_size("ctx")
+
+    def body(*refs):
         (x1_ref, h2_ref, dy_ref, prob_ref, prev_ref, route_ref, target_ref) = refs[:7]
         back_ref, dots_ref, dz_ref, dh_ref, gain_ref, router_ref = refs[7:13]
-        w_refs = refs[13 : 13 + members]
-        dx1_ref, low_ref = refs[13 + members : 15 + members]
-        out_refs = refs[15 + members : 15 + 2 * members]
-        sums_ref, carry_ref = refs[15 + 2 * members :]
-        i = pl.program_id(0)
-        prob_now = prob_ref[...]
-        lanes = lax.broadcasted_iota(jnp.int32, (tile, expert_all), 1)
-        dprob = jnp.zeros_like(prob_now)
-        for c in range(2):
-            target = target_ref[:, c : c + 1]
-            dgate = dz_ref[:, c : c + 1]
-            for n in range(places):
-                ids = n * CAP + lax.broadcasted_iota(jnp.int32, (tile, CAP), 1)
-                dgate = dgate + jnp.sum(
-                    jnp.where(ids == target, dots_ref[n], 0.0), axis=1, keepdims=True
-                )
-            dprob = dprob + jnp.where(lanes == route_ref[:, c : c + 1], dgate, 0.0)
-        dlogit = prob_now * (dprob - jnp.sum(prob_now * dprob, axis=1, keepdims=True))
-        h2 = h2_ref[...]
-        dh2 = (
-            slot_sum(target_ref[...], back_ref)
-            + dh_ref[...]
-            + mm_full(dlogit, router_ref[...])
+        dx1_ref, sums_ref, carry_ref, da_out, da_near, a_s, a_r, out_sem = refs[13:]
+        me = lax.axis_index("ctx")
+        peers = [{"ctx": flip(me, 1)}, {"ctx": flip(me, 2)}]
+        ready = greet(peers)
+
+        def da_copy(kind, t):
+            here = pl.ds(pl.multiple_of(t * tile, tile), tile)
+            n = kind * tiles + t
+            src, dst = ((0, 1), (0, 2), (2, 3))[kind]
+            return remote(
+                da_near.at[src, here, :], da_near.at[dst, here, :], a_s.at[n], a_r.at[n],
+                {"ctx": flip(me, 2 if kind == 1 else 1)},
+            )
+
+        sums_ref[...] = jnp.zeros_like(sums_ref)
+        carry_ref[...] = jnp.zeros_like(carry_ref)
+        ready()
+
+        def token_rows(t, _):
+            here = pl.ds(pl.multiple_of(t * tile, tile), tile)
+            prob_now = prob_ref[here, :]
+            chosen, target, zero = route_ref[here, :], target_ref[here, :], dz_ref[here, :]
+            lanes = lax.broadcasted_iota(jnp.int32, (tile, expert_all), 1)
+            dprob = jnp.zeros_like(prob_now)
+            for c in range(2):
+                dgate = zero[:, c : c + 1]
+                for n in range(places):
+                    ids = n * CAP + lax.broadcasted_iota(jnp.int32, (tile, CAP), 1)
+                    dgate = dgate + jnp.sum(
+                        jnp.where(ids == target[:, c : c + 1], dots_ref[n], 0.0),
+                        axis=1,
+                        keepdims=True,
+                    )
+                dprob = dprob + jnp.where(lanes == chosen[:, c : c + 1], dgate, 0.0)
+            dlogit = prob_now * (dprob - jnp.sum(prob_now * dprob, axis=1, keepdims=True))
+            h2 = h2_ref[here, :]
+            dh2 = slot_sum(target, back_ref) + dh_ref[here, :] + mm_full(dlogit, router_ref[...])
+            x1 = x1_ref[here, :]
+            inverse = lax.rsqrt(jnp.mean(x1 * x1, axis=1, keepdims=True) + norm_eps)
+            normed = x1 * inverse
+            dn = dh2 * gain_ref[...]
+            dx1 = dy_ref[here, :].astype(f32) + inverse * (
+                dn - normed * jnp.mean(dn * normed, axis=1, keepdims=True)
+            )
+            dx1_ref[here, :] = dx1
+            da_near[0, here, :] = dx1.astype(bf16)
+            sums_ref[0:expert_all, :] += mm_full(dlogit, h2, TN)
+            sums_ref[expert_all : expert_all + 1, :] += jnp.sum(dh2 * normed, axis=0, keepdims=True)
+            carry_ref[...] += mm_full(dlogit, prev_ref[here, :], TN)
+            da_copy(1, t).start()
+            da_copy(0, t).start()
+
+            @pl.when(t >= 2)
+            def _():
+                da_copy(1, t - 2).wait_recv()
+                da_copy(2, t - 2).start()
+
+            return 0
+
+        lax.fori_loop(0, tiles, token_rows, 0)
+        for t in range(max(0, tiles - 2), tiles):
+            da_copy(1, t).wait_recv()
+            da_copy(2, t).start()
+        mine = pltpu.make_async_copy(da_near.at[0], da_out.at[0], out_sem.at[0])
+        mine.start()
+        for t in range(tiles):
+            da_copy(0, t).wait()
+            da_copy(1, t).wait_send()
+            da_copy(2, t).wait()
+        rest = pltpu.make_async_copy(
+            da_near.at[pl.ds(1, members - 1)], da_out.at[pl.ds(1, members - 1)], out_sem.at[1]
         )
-        x1 = x1_ref[...]
-        inverse = lax.rsqrt(jnp.mean(x1 * x1, axis=1, keepdims=True) + norm_eps)
-        normed = x1 * inverse
-        router_part = mm_full(dlogit, h2, TN)
-        carry_part = mm_full(dlogit, prev_ref[...], TN)
-        gain_part = jnp.sum(dh2 * normed, axis=0, keepdims=True)
-
-        @pl.when(i == 0)
-        def _():
-            sums_ref[0:expert_all, :] = router_part
-            sums_ref[expert_all : expert_all + 1, :] = gain_part
-            carry_ref[...] = carry_part
-
-        @pl.when(i > 0)
-        def _():
-            sums_ref[0:expert_all, :] += router_part
-            sums_ref[expert_all : expert_all + 1, :] += gain_part
-            carry_ref[...] += carry_part
-
-        dn = dh2 * gain_ref[...]
-        dx1 = dy_ref[...].astype(f32) + inverse * (
-            dn - normed * jnp.mean(dn * normed, axis=1, keepdims=True)
-        )
-        dx1_ref[...] = dx1
-        low = dx1.astype(bf16)
-        low_ref[...] = low
-        for n in range(members):
-            out_refs[n][...] = mm(low, w_refs[n][0], NT).astype(bf16)
-
-    row_spec = pl.BlockSpec((tile, width), lambda i, m: (i, 0))
-    pair_spec = pl.BlockSpec((tile, 2), lambda i, m: (i, 0))
-    small_spec = pl.BlockSpec((tile, expert_all), lambda i, m: (i, 0))
-    sums = shape_of((expert_all + 1, width), f32)
-    carry = shape_of((expert_all, expert_all), f32)
+        rest.start()
+        mine.wait()
+        rest.wait()
+
     return run(
         body,
-        (rows // tile,),
-        [
-            (x1, row_spec),
-            (h2, row_spec),
-            (grad, row_spec),
-            (prob, small_spec),
-            (previous, small_spec),
-            (routes, pair_spec),
-            (targets, pair_spec),
-        ]
-        + [
-            (back, whole(back)),
-            (dots, whole(dots)),
-            (dgate_zero, pair_spec),
-            (dh_zero, row_spec),
-            (gain, whole(gain)),
-            (router_t, whole(router_t)),
-        ]
-        + [
-            (w_out, pl.BlockSpec((1, head_columns, width), lambda i, m, n=n: (m[0] ^ n, 0, 0)))
-            for n in range(members)
+        (),
+        [(a, vector) for a in (x1, h2, grad, prob, previous, routes, targets, back, dots)]
+        + [(a, vector) for a in (dgate_zero, dh_zero, gain, router_t)],
+        [(shape_of((rows, width), f32), vector)]
+        + [(shape_of((expert_all + 1, width), f32), vector)]
+        + [(shape_of((expert_all, expert_all), f32), vector)]
+        + [(shape_of((members, rows, width), bf16), anywhere)],
+        scratch=[
+            pltpu.VMEM((members, rows, width), bf16),
+            dma((3 * tiles,)), dma((3 * tiles,)), dma((2,)),
         ],
-        [
-            (shape_of((rows, width), f32), row_spec),
-            (shape_of((rows, width), bf16), row_spec),
-        ]
-        + [
-            (
-                shape_of((rows, head_columns), bf16),
-                pl.BlockSpec((tile, head_columns), lambda i, m: (i, 0)),
-            )
-        ]
-        * members
-        + [(sums, whole(sums)), (carry, whole(carry))],
-        meta=meta,
         flops=2 * rows * width * (places * CAP + width),
         moved=rows * width * 24,
+        talks=5,
     )
 
 
@@ -1027,9 +1273,9 @@
     group_rows = dqkv_all.shape[0]
     parts, groups = lax.axis_size("dp"), lax.axis_size("exp")
     team = parts * groups
-    places = produced.shape[0]
-    local = places // groups
-    wide_share, out_share = 3 * per_group // team, per_group // team
+    local = produced[0].shape[0]
+    places = groups * local
+    wide_share, out_share = width // team, per_group // team
     small_rows = small.shape[0]
     small_steps = [(axis, bit) for axis in ("ctx", "dp", "exp") for bit in powers(axis)]
     hops = len(small_steps)
@@ -1042,13 +1288,15 @@
             return next(it) if count is None else [next(it) for _ in range(count)]
 
         dqkv_hbm, h1_hbm, x_hbm, gain_ref, dx1_hbm, w_hbm, out_ref = take(7)
-        small_ref, tops_ref, produced_hbm, base_hbm, target_ref = take(5)
+        small_ref, tops_ref, base_hbm, target_ref = take(4)
+        produced_hbm = take(groups)
         input_out, wide_out, flat_out, small_out, gain_out, tops_out, result_out = take(7)
-        dqkv, dqkv_near, product, h1_all, x_all, dx1_all, w_all, base_all, y_near = take(9)
+        dqkv, product, h1_all, x_all, dx1_all, w_all, base_all, y_near = take(8)
+        part_send, part_core, part_y, y_got, part_own = take(5)
         wide_mine, wide_far, wide_all = take(3)
         flat_mine, flat_far, flat_all = take(3)
         small_acc, small_far, gain_acc, gain_far, tops_acc, tops_far = take(6)
-        load_sem, near_s, near_r, y_s, y_r = take(5)
+        load_sem, near_s, near_r = take(3)
         dense_sems = [take(8), take(8)]
         hop_s, hop_r, gain_s, gain_r, top_s, top_r = take(6)
 
@@ -1064,14 +1312,14 @@
 
         peers = [near_peer(j) for j in range(1, members)]
         peers += [team_peer(r) for r in range(1, team)]
-        peers += [
-            slot_peer(r, local, exp_now, me) for r in range(local, places) if r % local
+        ready = greet(peers)
+
+        loads = [
+            (dqkv_hbm, dqkv), (h1_hbm, h1_all), (x_hbm, x_all), (dx1_hbm, dx1_all),
+            (w_hbm.at[:, me], w_all), (base_hbm, base_all),
         ]
-        ready = greet(peers)
-
-        loads = [
-            (dqkv_hbm, dqkv), (h1_hbm, h1_all), (x_hbm, x_all), (dx1_hbm, dx1_all), (w_hbm, w_all),
-            (base_hbm, base_all), (produced_hbm.at[0], y_near.at[0]),
+        loads += [
+            (produced_hbm[g], y_near.at[pl.ds(g * local, local)]) for g in range(groups)
         ]
 
         def load(n):
@@ -1180,68 +1428,108 @@
                 if n + 1 < hops:
                     small_start(n + 1)
 
-        def dqkv_copy(j):
+        row_tiles = rows // row_tile
+
+        def tile_rows(t, first=0):
+            return pl.ds(first + t * row_tile, row_tile)
+
+        def core_part(j, t):
+            n = j // 2
             return remote(
-                dqkv_hbm.at[pl.ds(j * rows, rows), :], dqkv_near.at[j - 1], near_s.at[j - 1],
-                near_r.at[j - 1], near_peer(j),
+                part_send.at[n, tile_rows(t), :], part_core.at[n, tile_rows(t), :],
+                near_s.at[n * row_tiles + t], near_r.at[n * row_tiles + t], near_peer(1),
             )
 
-        def y_copy(r):
+        def y_part(t):
+            n = 2 * row_tiles + t
             return remote(
-                produced_hbm.at[r], y_near.at[r], y_s.at[r], y_r.at[r],
-                slot_peer(r, local, exp_now, me),
+                part_y.at[tile_rows(t), :], y_got.at[tile_rows(t), :], near_s.at[n], near_r.at[n],
+                near_peer(2),
             )
+
+        def part(j, t):
+            here = pl.ds(j * rows + t * row_tile, row_tile)
+            found = None
+            for w in range(3):
+                add = mm(dqkv[here, w * per_group : (w + 1) * per_group], w_all[w])
+                found = add if found is None else found + add
+            return found
 
         for n in range(len(loads)):
             load(n).start()
         small_acc[0] = small_ref[...]
-        tops_acc[0] = tops_ref[...]
-        product[0:per_group, :] = out_ref[...].astype(f32)
+        lanes = lax.broadcasted_iota(jnp.int32, tops_acc.shape[1:], 1)
+        tops_acc[0] = jnp.where(
+            lanes == me, jnp.max(tops_ref[...], axis=1, keepdims=True), low_start
+        )
+        flat_rows = out_ref[...].astype(f32)
         for c in range(team):
-            flat_mine[c] = product[c * out_share : (c + 1) * out_share, :].astype(bf16)
+            flat_mine[c] = flat_rows[c * out_share : (c + 1) * out_share, :].astype(bf16)
         ready()
-        for j in reversed(range(1, members)):
-            dqkv_copy(j).start()
         flat.scatter()
         small_start(0)
         load(0).wait()
         load(1).wait()
-        product[...] = mm(dqkv[0:rows, :], h1_all[0:rows, :], TN)
+        product[...] = mm(h1_all[0:rows, :], dqkv[0:rows, :], TN)
 
         def weigh(j, _):
             here = pl.ds(pl.multiple_of(j * rows, rows), rows)
-            product[...] += mm(dqkv[here, :], h1_all[here, :], TN)
+            product[...] += mm(h1_all[here, :], dqkv[here, :], TN)
             return 0
 
         lax.fori_loop(1, group_rows // rows, weigh, 0)
         for c in range(team):
             wide_mine[c] = product[c * wide_share : (c + 1) * wide_share, :].astype(bf16)
-        flat.collect()
         wide.scatter()
-        flat.gather()
-        for r in range(1, places):
-            y_copy(r).start()
         for n in range(2, len(loads)):
             load(n).wait()
+        queue = [(j, t) for j in (3, 1) for t in range(row_tiles)]
+        for n, (j, t) in enumerate(queue):
+            part_send[j // 2, tile_rows(t), :] = part(j, t).astype(bf16)
+            if n:
+                core_part(*queue[n - 1]).start()
+        own_part = [part(2, t) for t in range(1)]
+        core_part(*queue[-1]).start()
+        for t in range(row_tiles):
+            value = own_part[0] if t == 0 else part(2, t)
+            core_part(3, t).wait_recv()
+            part_y[tile_rows(t), :] = (
+                value + part_core[1, tile_rows(t), :].astype(f32)
+            ).astype(bf16)
+            if t:
+                y_part(t - 1).start()
+        part_own[tile_rows(0), :] = part(0, 0)
+        y_part(row_tiles - 1).start()
+        for t in range(1, row_tiles):
+            part_own[tile_rows(t), :] = part(0, t)
+        flat.collect()
+        flat.gather()
         small_next()
         small_next()
+
+        def token_rows(t, _):
+            here = pl.ds(pl.multiple_of(t * 128, 128), 128)
+            result_out[here, :] = (
+                base_all[here, :] + slot_sum(target_ref[here, :], y_near)
+            ).astype(bf16)
+            return 0
+
+        lax.fori_loop(0, rows // 128, token_rows, 0)
         flat.forward()
+        small_next()
         wide.collect()
         small_next()
         wide.gather()
-        for j in range(1, members):
-            dqkv_copy(j).wait()
+        for t in range(row_tiles):
+            core_part(1, t).wait()
+            core_part(3, t).wait_send()
+            y_part(t).wait()
 
         def input_rows(t, gain_part):
             here = pl.ds(pl.multiple_of(t * row_tile, row_tile), row_tile)
-            dh = None
-            for j in range(members):
-                member = flip(me, j)
-                for w in range(3):
-                    at = slice(w * per_group, (w + 1) * per_group)
-                    source = dqkv[here, at] if j == 0 else dqkv_near[j - 1, here, at]
-                    part = mm(source, w_all[w, member])
-                    dh = part if dh is None else dh + part
+            dh = (
+                part_own[here, :] + part_core[0, here, :].astype(f32) + y_got[here, :].astype(f32)
+            )
             x_now = x_all[here, :].astype(f32)
             inv = lax.rsqrt(jnp.mean(x_now * x_now, axis=1, keepdims=True) + norm_eps)
             normed = x_now * inv
@@ -1264,21 +1552,8 @@
         for n in range(hops):
             gain_copy(n).wait()
             gain_acc[n + 1] = gain_acc[n] + gain_far[n]
-            if n == 0:
-                for r in range(1, places):
-                    y_copy(r).wait()
-            if n < rows // 128:
-                here = slice(n * 128, (n + 1) * 128)
-                result_out[here, :] = (
-                    base_all[here, :] + slot_sum(target_ref[here, :], y_near)
-                ).astype(bf16)
             if n + 1 < hops:
                 gain_copy(n + 1).start()
-        for n in range(hops, rows // 128):
-            here = slice(n * 128, (n + 1) * 128)
-            result_out[here, :] = (
-                base_all[here, :] + slot_sum(target_ref[here, :], y_near)
-            ).astype(bf16)
         while small_hops:
             small_next()
         flat.done()
@@ -1297,11 +1572,11 @@
         for copy in final:
             copy.wait()
 
-    def dense_scratch(share):
+    def dense_scratch(share, across):
         return [
-            pltpu.VMEM((team, share, width), bf16),
-            pltpu.VMEM((max(1, team - 1), share, width), bf16),
-            pltpu.VMEM((members, team, share, width), bf16),
+            pltpu.VMEM((team, share, across), bf16),
+            pltpu.VMEM((max(1, team - 1), share, across), bf16),
+            pltpu.VMEM((members, team, share, across), bf16),
         ]
 
     dense_sem = [dma((team,))] * 6 + [dma((2,))] * 2
@@ -1311,34 +1586,38 @@
         (),
         [(dqkv_all, anywhere), (h1, anywhere), (x, anywhere), (gain, vector), (dx1, anywhere)]
         + [(weights_t, anywhere), (out_sum, vector), (small, vector), (tops, vector)]
-        + [(produced, anywhere), (base, anywhere), (targets, vector)],
+        + [(base, anywhere), (targets, vector)]
+        + [(a, anywhere) for a in produced],
         [
             (wide_rows, anywhere),
-            (shape_of((members, team, wide_share, width), bf16), anywhere),
+            (shape_of((members, team, wide_share, 3 * per_group), bf16), anywhere),
             (shape_of((members, team, out_share, width), bf16), anywhere),
             (shape_of((small_rows, width), f32), vector),
             (shape_of((1, width), f32), vector),
-            (shape_of(tops.shape, f32), vector),
+            (shape_of((tops.shape[0], 128), f32), vector),
             (shape_of((rows, width), bf16), vector),
         ],
         scratch=[
             pltpu.VMEM((group_rows, 3 * per_group), bf16),
-            pltpu.VMEM((members - 1, rows, 3 * per_group), bf16),
-            pltpu.VMEM((3 * per_group, width), f32),
+            pltpu.VMEM((width, 3 * per_group), f32),
             pltpu.VMEM((group_rows, width), bf16),
             pltpu.VMEM((rows, width), bf16),
             pltpu.VMEM((rows, width), f32),
-            pltpu.VMEM(weights_t.shape, bf16),
+            pltpu.VMEM((3, per_group, width), bf16),
             pltpu.VMEM((rows, width), f32),
             pltpu.VMEM((places, CAP, width), bf16),
+            pltpu.VMEM((2, rows, width), bf16),
+            pltpu.VMEM((2, rows, width), bf16),
+            pltpu.VMEM((rows, width), bf16),
+            pltpu.VMEM((rows, width), bf16),
+            pltpu.VMEM((rows, width), f32),
         ]
-        + dense_scratch(wide_share)
-        + dense_scratch(out_share)
+        + dense_scratch(wide_share, 3 * per_group)
+        + dense_scratch(out_share, width)
         + [pltpu.VMEM((hops + 1, small_rows, width), f32), pltpu.VMEM((hops, small_rows, width), f32)]
         + [pltpu.VMEM((hops + 1, 1, width), f32), pltpu.VMEM((hops, 1, width), f32)]
-        + [pltpu.VMEM((hops + 1,) + tops.shape, f32), pltpu.VMEM((hops,) + tops.shape, f32)]
-        + [dma((10,)), dma((members,)), dma((members,))]
-        + [dma((places,)), dma((places,))]
+        + [pltpu.VMEM((hops + 1, tops.shape[0], 128), f32), pltpu.VMEM((hops, tops.shape[0], 128), f32)]
+        + [dma((10 + places,))] + [dma((3 * (rows // row_tile),))] * 2
         + dense_sem
         + dense_sem
         + [dma((hops,))] * 6,
@@ -1348,85 +1627,86 @@
     )
 
 
-def place_experts(meta, near, which, turned):
-    _, half, columns = near[0].shape
-    members = len(near)
+def place_experts(meta, near, turned):
+    _, half, columns = near[0][0][0].shape
+    members = len(near[0])
     local = members // 2
-    tile = min(256, columns)
+    count = len(near)
+    tile = 128
+    tiles = half // tile
 
     def body(meta_ref, *refs):
-        out_ref, hold = refs[members:]
-        n = pl.program_id(0)
-        for away in range(local):
-
-            @pl.when(n == away)
+        outs = refs[count * members :]
+        step = pl.program_id(0) * 2 + pl.program_id(1)
+        for j in range(members):
+
+            @pl.when(step == j)
             def _():
-                for j in range(2):
-                    at = pl.multiple_of((meta_ref[2] ^ j) * half, half)
-                    piece = refs[2 * away + j][0].astype(f32)
-                    if turned:
-                        hold[pl.ds(at, half), :] = piece
-                    else:
-                        out_ref[0, pl.ds(at, half), :] = piece
-
-        if turned:
-            out_ref[0] = jnp.transpose(hold[...])
-
-    def spec(j):
-        last = columns // tile - 1
-        if j < 2:
-            return pl.BlockSpec(
-                (1, half, tile), lambda n, f, m: (which, 0, jnp.where(n == 0, f, last))
+                for n in range(count):
+                    piece = refs[n * members + j][0].astype(f32)
+                    outs[n][0] = jnp.transpose(piece) if turned[n] else piece
+
+    def in_spec(which, j):
+        def index(n, c, t, m):
+            step = n * 2 + c
+            return (which, jnp.where(step == j, t, jnp.where(step < j, 0, tiles - 1)), 0)
+
+        return pl.BlockSpec((1, tile, columns), index)
+
+    outputs = []
+    for flag in turned:
+        if flag:
+            outputs.append(
+                (
+                    shape_of((local, columns, 2 * half), f32),
+                    pl.BlockSpec(
+                        (1, columns, tile),
+                        lambda n, c, t, m: (m[3] ^ n, 0, (m[2] ^ c) * tiles + t),
+                    ),
+                )
             )
-        return pl.BlockSpec((1, half, tile), lambda n, f, m: (which, 0, jnp.where(n == 0, 0, f)))
-
-    if turned:
-        out = shape_of((local, columns, 2 * half), f32)
-        out_spec = pl.BlockSpec((1, tile, 2 * half), lambda n, f, m: (m[3] ^ n, f, 0))
-    else:
-        out = shape_of((local, 2 * half, columns), f32)
-        out_spec = pl.BlockSpec((1, 2 * half, tile), lambda n, f, m: (m[3] ^ n, 0, f))
+        else:
+            outputs.append(
+                (
+                    shape_of((local, 2 * half, columns), f32),
+                    pl.BlockSpec(
+                        (1, tile, columns),
+                        lambda n, c, t, m: (m[3] ^ n, (m[2] ^ c) * tiles + t, 0),
+                    ),
+                )
+            )
     return run(
         body,
-        (local, columns // tile),
-        [(p, spec(j)) for j, p in enumerate(near)],
-        [(out, out_spec)],
-        scratch=[pltpu.VMEM((2 * half, tile) if turned else (8, 128), f32)],
+        (local, 2, tiles),
+        [(a, in_spec(which, j)) for listed in near for j, (a, which) in enumerate(listed)],
+        outputs,
+        meta=meta,
+        moved=count * local * 2 * half * columns * 6,
+    )
+
+
+def place_columns(meta, near, per_group):
+    members, team, share, _ = near.shape
+    width = team * share
+    step = 8 // math.gcd(share, 8)
+
+    def body(meta_ref, near_ref, out_ref):
+        for c in range(step):
+            pieces = [near_ref[meta_ref[0] ^ g, c] for g in range(members)]
+            for w in range(3):
+                at = slice(w * per_group, (w + 1) * per_group)
+                out_ref[w, c * share : (c + 1) * share, :] = jnp.concatenate(
+                    [piece[:, at] for piece in pieces], axis=1
+                ).astype(f32)
+
+    out = shape_of((3, width, members * per_group), f32)
+    return run(
+        body,
+        (team // step,),
+        [(near, pl.BlockSpec((members, step, share, 3 * per_group), lambda c, m: (0, c, 0, 0)))],
+        [(out, pl.BlockSpec((3, step * share, members * per_group), lambda c, m: (0, c, 0)))],
         meta=meta,
         moved=out.size * 6,
-    )[0]
-
-
-def place_columns(meta, near, per_group):
-    members, team, share, width = near.shape
-
-    def body(meta_ref, near_ref, out_ref, rows_ref, hold):
-        w = pl.program_id(0)
-
-        @pl.when(w == 0)
-        def _():
-            for n in range(members):
-                for c in range(team):
-                    rows_ref[n, c * share : (c + 1) * share, :] = near_ref[n, c].astype(f32)
-
-        for n in range(members):
-            at = pl.multiple_of((meta_ref[0] ^ n) * per_group, per_group)
-            source = pl.multiple_of(w * per_group, per_group)
-            hold[pl.ds(at, per_group), :] = rows_ref[n, pl.ds(source, per_group), :]
-        out_ref[0] = jnp.transpose(hold[...])
-
-    out = shape_of((3, width, width), f32)
-    return run(
-        body,
-        (3,),
-        [(near, whole(near))],
-        [(out, pl.BlockSpec((1, width, width), lambda w, m: (w, 0, 0)))],
-        scratch=[
-            pltpu.VMEM((members, team * share, width), f32),
-            pltpu.VMEM((width, width), f32),
-        ],
-        meta=meta,
-        moved=3 * width * width * 6,
     )[0]
 
 
@@ -1500,58 +1780,48 @@
     )
     gain1 = norm1_gain.reshape(1, width)
     gain2 = norm2_gain.reshape(1, width)
-    weights_t = jnp.swapaxes(w_qkv, 1, 2).reshape(3, members, per_group, width)
     w_out_parts = w_out.reshape(members, per_group, width)
     route_ids = routes[0]
     previous = prev_logits[0]
-
-    near = gather_near(x, "ctx")
-    held = None
-    for j in range(members):
-        held = project(
-            j, near[j], gain1, weights_t, meta, held, group_rows, deal_block, layout
-        )
-    q, k, v, kt, vt, h1 = held
+    odd = [r for r in range(groups * local) if r % local]
+
+    q, k, v, kt, vt, h1, weights_t, targets, target_rows, grad_near, grad_rest = begin(
+        x, grad, route_ids, gain1, w_qkv, local
+    )
+    weights_t = weights_t.reshape(3, members, per_group, width)
+    grad_late = [slot_swap(grad_rest[n], r, local) for n, r in enumerate(odd)]
     o, ot, lse, tops = attend(meta, q, k, vt, deal_block, layout)
-    targets = slot_targets(route_ids, expert_count, local, mine, me // 2)
-    target_rows = jnp.transpose(targets)
-    places = groups * local
-    grad_slots = dispatch(target_rows, grad, places)
-    grad_near = jnp.stack(
-        [slot_swap(grad_slots[r], r, local) if r else grad_slots[0] for r in range(places)]
-    )
     logit_rows = jnp.swapaxes(const_logit_w, 1, 2).reshape(-1, width)
     x1, h2, prob, token_near, gate_near, base, dh_zero, dgate_zero, zero_sums = token_front(
         x, o, w_out_parts, gain2, w_router, previous, w_carry, target_rows, grad, route_ids,
         logit_rows, const_vec, local,
     )
-    produced, token_back_rows, dots, expert_sum = expert_layer(
-        token_near, grad_near, gate_near, w_gate, w_up, w_down
-    )
-    back = token_back(
-        meta, x1, h2, grad, prob, previous, route_ids, targets, token_back_rows, dots, dgate_zero,
-        dh_zero, gain2, jnp.transpose(w_router), w_out_parts,
-    )
-    dx1, da = back[:2]
-    do_near = [back[2 + j] if j == 0 else swap(back[2 + j], "ctx", j) for j in range(members)]
-    token_sums, carry_sum = back[2 + members :]
-
-    o_near = [swap(o[j * rows : (j + 1) * rows], "ctx", j) if j else o[:rows] for j in range(members)]
-    out_parts = [mm(o_near[j], da, TN).astype(bf16) for j in range(members)]
-    out_sum = add_low(*[swap(out_parts[j], "ctx", j) if j else out_parts[0] for j in range(members)])
-    dqkv = attend_back(meta, q, k, v, kt, do_near, ot, lse, deal_block, layout)
+    produced, token_back_rows, dots, expert_sum, beside = expert_layer(
+        token_near, grad_near, grad_late, gate_near, w_gate, w_up, w_down
+    )
+    dx1, token_sums, carry_sum, da_near = token_back(
+        x1, h2, grad, prob, previous, route_ids, targets, token_back_rows, dots, dgate_zero,
+        dh_zero, gain2, jnp.transpose(w_router),
+    )
+    expert_now, da_near = lax.optimization_barrier((expert_sum, da_near))
+    over_first, over_last = swap(expert_now[:2], "ctx", 2), swap(expert_now[2:], "ctx", 2)
+    y_near = [swap(produced[g], "exp", g) if g else produced[0] for g in range(groups)]
+    dqkv, out_sum = attend_back(
+        meta, q, k, v, kt, da_near, w_out_parts, ot, lse, deal_block, layout
+    )
 
     expert_all = w_router.shape[1]
     small = jnp.concatenate(
         [token_sums, zero_sums, jnp.pad(carry_sum, ((0, 0), (0, width - expert_all)))], axis=0
     )
-    top_rows = jnp.full((members, heads), low_start, f32).at[me].set(jnp.max(tops, axis=1))
-    tops_line = jnp.pad(top_rows.reshape(1, HEADS), ((0, 0), (0, 128 - HEADS)), constant_values=low_start)
     input_grad, qkv_near, out_near, small, norm1_grad, top_all, result = finish(
-        dqkv, h1, x, gain1, dx1, weights_t, out_sum, small, tops_line, produced, base, targets
-    )
-    across = swap(expert_sum, "ctx", 2)
-    expert_near = [expert_sum, swap(expert_sum, "ctx", 1), across, swap(across, "ctx", 1)]
+        dqkv, h1, x, gain1, dx1, weights_t, out_sum, small, tops, y_near, base, targets
+    )
+    corner_first, corner_last = swap(over_first, "ctx", 1), swap(over_last, "ctx", 1)
+    near = [
+        [(expert_sum, n), (beside, n), (over_first, n), (corner_first, n)] for n in range(2)
+    ] + [[(expert_sum, 2), (beside, 2), (over_last, 0), (corner_last, 0)]]
+    gate_grad, up_grad, down_grad = place_experts(meta, near, (False, False, True))
     out_grad = place_rows(meta, out_near).reshape(width, width)
     qkv_grad = place_columns(meta, qkv_near, per_group)
     kinds = const_vec.shape[0]
@@ -1561,13 +1831,10 @@
     vec_grad = small[start : start + kinds]
     logit_grad = jnp.swapaxes(small[start + kinds : start + 3 * kinds].reshape(kinds, 2, width), 1, 2)
     carry_grad = jnp.transpose(small[start + 3 * kinds :, :expert_all])
-    head_max = top_all[0, :HEADS]
+    head_max = jnp.transpose(top_all[:, :members]).reshape(HEADS)
     clip_ratio = jnp.sqrt(jnp.minimum(1.0, clip_limit / head_max))
     head_scale = jnp.repeat(clip_ratio, head_width)
     clipped = w_qkv[:2].astype(f32) * head_scale[None, None, :]
-    gate_grad = place_experts(meta, expert_near, 0, False)
-    up_grad = place_experts(meta, expert_near, 1, False)
-    down_grad = place_experts(meta, expert_near, 2, True)
     return (
         result[None],
         input_grad[None],

time: 551 us -> 435 us (0.79)
  waiting for transfers between devices: 71.6 us -> 0.03 us
  Pallas kernels: 409 us -> 390 us
  starting transfers between devices: 23.1 us -> 13.7 us
  local copies, waits for them, and re-layouts: 28.7 us -> 20.5 us
  matrix products: 6.5 us -> 0 us
    ppermute x15 -> x7, waiting for transfers between devices: 53.9 us -> 0.02 us  [swap(): return lax.ppermute(value, axis, [(i, i ^ distance) for i in range(count)])]
    pallas_call x16 -> x10, Pallas kernels: 409 us -> 390 us  [run(): pl.pallas_call(body, out_shape=[o for o, _ in outputs], grid_spec=pltpu.P...]
    ppermute x7 -> x4, waiting for transfers between devices: 17.7 us -> 0.01 us  [slot_swap(): lax.ppermute(value, ('ctx', 'exp'), [(i, i ^ apart) for i in range(total)])]
    dot_general x5 -> x0, matrix products: 6.5 us -> none  [mm(): return lax.dot_general(left, right, dims, preferred_element_type=f32)]
    ppermute x7 -> x4, starting transfers between devices: 12.5 us -> 6.83 us  [slot_swap(): lax.ppermute(value, ('ctx', 'exp'), [(i, i ^ apart) for i in range(total)])]
    unnamed x68 -> x48, local copies, waits for them, and re-layouts: 11.5 us -> 9.07 us
  transfers between devices with their start and end apart: 22 -> 11, of which waited for: 7 -> 0; matrix products, arithmetic and copies ran while one was open for 7% -> 4% of each run, Pallas kernels for 37% -> 52%
where the time goes in v4:
time: 435 us; the launch traced here: 431 us
  Pallas kernels  390 us (90%)
  local copies, waits for them, and re-layouts  20.5 us (5%)
  starting transfers between devices  13.7 us (3%)
  other arithmetic  6.29 us (1%)
    pallas_call x10, Pallas kernels, run(): pl.pallas_call(body, out_shape=[o for o, _ in outputs], grid_spec=pltpu.P...  390 us
    unnamed x48, local copies, waits for them, and re-layouts  9.07 us
  transfers between devices with their start and end apart: 11, of which 0 were waited for; matrix products, arithmetic and copies ran while one was open for 4% of the time, Pallas kernels for 52%

profile of v4, /device:TPU:0, one launch (start us, length us, event | category | flops | bytes accessed | tf_op | source)
XLA Modules:
  0.0 431.4 jit_solution(14467301697906547203)
XLA Ops:
  0.6 1.5 copy.36
  2.2 1.3 reshape.56.refs_3_
  3.5 31.3 %shard_map.272 = (bf16[3,2048,64]{2,1,0:T(8,128)(2,1)}, bf16[3,2048,64]{2,1,0:T(8,128)(2,1)}, bf16[3,2048,64]{2,1,0:T(8,128)(2,1)}, bf16[192,2048]{1,0:T(8,128)(...) custom-call(bf16[512,768]{1,0:T(8,128)(2,1)} %bitcast.59, ...), custom_call_target="tpu_custom_call" | custom-call | flops 3019898880 | bytes 20971520 | tf_op jit(solution)/shard_map/pallas_call | solution.py:50
  34.8 1.3 slice_bitcast_fusion.4
  36.0 0.6 collective-permute-start
  36.6 1.5 collective-permute-start.1
  38.1 1.5 collective-permute-start.2
  39.6 3.3 collective-permute-start.3
  43.0 0.6 concatenate.6.meta_ref
  43.7 29.8 %shard_map.273 = (bf16[2048,192]{1,0:T(8,128)(2,1)}, f32[192,2048]{1,0:T(8,128)}, f32[3,2048]{1,0:T(4,128)}, f32[3,256]{1,0:T(4,128)}) custom-call(s32[22]{0:T(128)} %concatenate.6.meta_ref, bf16[3,2048,64]{2,1,0:T(8,128)(2,1)} %get-tuple-element.61.q_ref, bf16[3,2048,64]{2,1,0:T(8,128)(2,1)} %get-tuple-element.62.k_ref, ...), custom_call_target="tpu_custom_call" | custom-call | flops 3221225472 | bytes 5505024 | tf_op jit(solution)/shard_map/pallas_call | solution.py:50
  73.4 0.6 reshape.58.refs_3_.refs_11_
  74.0 0.9 copy.38.refs_4_
  75.0 0.9 copy.37
  75.8 0.6 reshape.59.refs_10_
  76.4 54.4 %shard_map.274 = (f32[512,768]{1,0:T(8,128)}, f32[512,768]{1,0:T(8,128)}, f32[512,12]{1,0:T(8,128)}, bf16[8,128,768]{2,1,0:T(8,128)(2,1)}, f32[8,1,128]{2,1,0:T(...) custom-call(bf16[512,768]{1,0:T(8,128)(2,1)} %bitcast.60, ...), custom_call_target="tpu_custom_call" | custom-call | flops 1409286144 | bytes 11796480 | tf_op jit(solution)/shard_map/pallas_call | solution.py:50
  130.9 0.6 copy-done.17
  131.7 92.5 %shard_map.275 = (bf16[4,2,128,768]{3,2,1,0:T(8,128)(2,1)}, bf16[8,128,768]{2,1,0:T(8,128)(2,1)}, f32[8,1,128]{2,1,0:T(1,128)}, bf16[3,384,1024]{2,1,0:T(8,128)(2,1)}, bf16[3,384,1024]{2,1,0:T(8,128)(2,1)}) custom-call(bf16[8,128,768]{2,1,0:T(8,128)(2,1)} %get-tuple-element.68.refs_0_, bf16[4,128,768]{2,1,0:T(8,128)(2,1)} %get-tuple-element.69.refs_1_, ...), custom_call_target="tpu_custom_call" | custom-call | flops 28991029248 | bytes 25165824 | tf_op jit(solution)/shard_map/pallas_call | solution.py:50
  224.2 28.1 %shard_map.276 = (f32[512,768]{1,0:T(8,128)}, f32[13,768]{1,0:T(8,128)}, f32[12,12]{1,0:T(8,128)}, bf16[4,512,768]{2,1,0:T(8,128)(2,1)}) custom-call(f32[512,768]{1,0:T(8,128)} %get-tuple-element.73.refs_0_, f32[512,768]{1,0:T(8,128)} %get-tuple-element.74.refs_1_, bf16[512,768]{1,0:T(8,128)(2,1)} %bitcast.49, f32[512,12]{1,0:T(8,128)} %get-tuple-element.75.refs_3_, ...), custom_call_target="tpu_custom_call" | custom-call | flops 1409286144 | bytes 9437184 | tf_op jit(solution)/shard_map/pallas_call | solution.py:50
  252.3 0.1 slice.64
  252.4 1.1 collective-permute-start.7
  253.6 0.9 slice.65
  254.5 1.0 slice_bitcast_fusion
  255.6 1.6 collective-permute-start.4
  257.2 1.3 collective-permute-start.5
  258.5 1.5 collective-permute-start.6
  259.9 1.0 collective-permute-start.9
  260.9 37.2 %shard_map.277 = (bf16[2048,576]{1,0:T(8,128)(2,1)}, bf16[192,768]{1,0:T(8,128)(2,1)}) custom-call(s32[22]{0:T(128)} %concatenate.6.meta_ref, bf16[3,2048,64]{2,1,0:T(8,128)(2,1)} %get-tuple-element.61.q_ref, bf16[3,2048,64]{2,1,0:T(8,128)(2,1)} %get-tuple-element.62.k_ref, bf16[3,2048,64]{2,1,0:T(8,128)(2,1)} %get-tuple-element.63.v_ref, ...), custom_call_target="tpu_custom_call" | custom-call | flops 8053063680 | bytes 9437184 | tf_op jit(solution)/shard_map/pallas_call | solution.py:50
  298.1 0.7 select_maximum_fusion.refs_7_
  298.8 89.7 %shard_map.278 = (f32[512,768]{1,0:T(8,128)}, bf16[4,8,96,576]{3,2,1,0:T(8,128)(2,1)}, bf16[4,8,24,768]{3,2,1,0:T(8,128)(2,1)}, f32[31,768]{1,0:T(8,128)}, f32[1...) custom-call(bf16[2048,576]{1,0:T(8,128)(2,1)} %get-tuple-element.85.refs_0_, ...), custom_call_target="tpu_custom_call" | custom-call | flops 7247757312 | bytes 20971520 | tf_op jit(solution)/shard_map/pallas_call | solution.py:50
  388.5 0.7 slice_bitcast_fusion.9
  389.2 0.4 collective-permute-start.10
  389.6 0.7 sqrt_bitcast_fusion
  390.3 0.8 slice.62
  391.1 1.3 slice.63
  392.4 8.0 %shard_map.279 = f32[3,768,768]{2,1,0:T(8,128)} custom-call(s32[22]{0:T(128)} %concatenate.6.meta_ref, bf16[4,8,96,576]{3,2,1,0:T(8,128)(2,1)} %get-tuple-element.100.near_ref), custom_call_target="tpu_custom_call" | custom-call | bytes 10616832 | tf_op jit(solution)/shard_map/pallas_call | solution.py:50
  400.4 4.5 %shard_map.280 = f32[4,192,768]{2,1,0:T(8,128)} custom-call(s32[22]{0:T(128)} %concatenate.6.meta_ref, bf16[4,8,24,768]{3,2,1,0:T(8,128)(2,1)} %get-tuple-element.101.near_ref), custom_call_target="tpu_custom_call" | custom-call | bytes 3538944 | tf_op jit(solution)/shard_map/pallas_call | solution.py:50
  404.9 0.7 copy.40
  405.6 0.6 reshape.62
  406.5 0.6 reduce
  407.1 0.6 slice_reduce_fusion
  407.7 0.6 slice_bitcast_fusion.8
  408.4 4.2 convert_multiply_fusion
  412.6 0.9 copy-done.4
  413.5 0.5 copy-done.1
  414.0 14.1 %shard_map.281 = (f32[2,768,1024]{2,1,0:T(8,128)}, f32[2,768,1024]{2,1,0:T(8,128)}, f32[2,1024,768]{2,1,0:T(8,128)}) custom-call(s32[22]{0:T(128)} %concatenate.6.meta_ref, bf16[3,384,1024]{2,1,0:T(8,128)(2,1)} %get-tuple-element.103.refs_0_.refs_4_.refs_8_, bf16[3,384,1024]{2,1,0:T(8,128)(2,1)} %get-tuple-element.102.refs_1_.refs_5_.refs_9_, ...), custom_call_target="tpu_custom_call" | custom-call | bytes 28311552 | tf_op jit(solution)/shard_map/pallas_call | solution.py:50
  428.1 0.9 copy.43
  429.0 0.8 copy-done.2
  429.8 1.1 copy.44
  (56 shorter events, 0.8 us)
Async XLA Ops:
  3.5 39.4 %copy-start.15 = (s32[1,8]{1,0:T(1,128)S(1)}, s32[1,8]{1,0:T(1,128)}, u32[]{:S(2)}) copy-start(s32[1,8]{1,0:T(1,128)} %param.19) | copy-start | bytes 100
  3.5 39.6 %copy-start.16 = (s32[1,2]{1,0:T(1,128)S(1)}, s32[1,2]{1,0:T(1,128)}, u32[]{:S(2)}) copy-start(s32[1,2]{1,0:T(1,128)} %param.18) | copy-start | bytes 28
  36.0 94.8 %collective-permute-start = (bf16[128,768]{1,0:T(8,128)(2,1)S(1)}, bf16[128,768]{1,0:T(8,128)(2,1)S(1)}, u32[]{:S(2)}, u32[]{:S(2)}) collective-permute-start(bf16[128,768]{1,0:T(8,128)(2,1)S(1)} %get-tuple-element.143), channel_id=1, source_target_pairs={{0,8},{1,9},{2,10},{3,11},{4,12},{5,13},{6,14},{7,15},{8,0},{9,1},... | collective-permute-start | bytes 589832 | tf_op jit(solution)/shard_map/ppermute | solution.py:101
  36.6 94.3 %collective-permute-start.1 = (bf16[128,768]{1,0:T(8,128)(2,1)S(1)}, bf16[128,768]{1,0:T(8,128)(2,1)S(1)}, u32[]{:S(2)}, u32[]{:S(2)}) collective-permute-start(bf16[128,768]{1,0:T(8,128)(2,1)S(1)} %get-tuple-element.142), channel_id=1, source_target_pairs={{0,9},{1,8},{2,11},{3,10},{4,13},{5,12},{6,15},{7,14},{8,1},{9,0},... | collective-permute-start | bytes 589832 | tf_op jit(solution)/shard_map/ppermute | solution.py:101
  38.1 92.8 %collective-permute-start.2 = (bf16[128,768]{1,0:T(8,128)(2,1)S(1)}, bf16[128,768]{1,0:T(8,128)(2,1)S(1)}, u32[]{:S(2)}, u32[]{:S(2)}) collective-permute-start(bf16[128,768]{1,0:T(8,128)(2,1)S(1)} %get-tuple-element.141), channel_id=1, source_target_pairs={{0,10},{1,11},{2,8},{3,9},{4,14},{5,15},{6,12},{7,13},{8,2},{9,3},... | collective-permute-start | bytes 589832 | tf_op jit(solution)/shard_map/ppermute | solution.py:101
  39.6 91.3 %collective-permute-start.3 = (bf16[128,768]{1,0:T(8,128)(2,1)S(1)}, bf16[128,768]{1,0:T(8,128)(2,1)S(1)}, u32[]{:S(2)}, u32[]{:S(2)}) collective-permute-start(bf16[128,768]{1,0:T(8,128)(2,1)S(1)} %get-tuple-element.140), channel_id=1, source_target_pairs={{0,11},{1,10},{2,9},{3,8},{4,15},{5,14},{6,13},{7,12},{8,3},{9,2},... | collective-permute-start | bytes 589832 | tf_op jit(solution)/shard_map/ppermute | solution.py:101
  43.7 29.8 %copy-start.13 = (f32[768]{0:T(1024)S(1)}, f32[768]{0:T(1024)}, u32[]{:S(2)}) copy-start(f32[768]{0:T(1024)} %param.23) | copy-start | bytes 9220
  43.7 30.4 %copy-start.6 = (f32[768,12]{0,1:T(8,128)S(1)}, f32[768,12]{0,1:T(8,128)}, u32[]{:S(2)}) copy-start(f32[768,12]{0,1:T(8,128)} %param.26) | copy-start | bytes 110596
  43.7 31.3 %copy-start.9 = (f32[1,512,12]{1,0,2:T(1,128)S(1)}, f32[1,512,12]{1,0,2:T(1,128)}, u32[]{:S(2)}) copy-start(f32[1,512,12]{1,0,2:T(1,128)} %param.21) | copy-start | bytes 73732
  43.7 32.1 %copy-start.11 = (f32[2,768,2]{1,2,0:T(2,128)S(1)}, f32[2,768,2]{1,2,0:T(2,128)}, u32[]{:S(2)}) copy-start(f32[2,768,2]{1,2,0:T(2,128)} %param.28) | copy-start | bytes 36868
  130.9 0.7 copy-start.17
  130.9 0.7 copy-start.18
  130.9 0.8 copy-start.19
  130.9 0.8 copy-start.20
  224.2 28.1 %copy-start = (bf16[3,384,1024]{2,1,0:T(8,128)(2,1)S(1)}, bf16[3,384,1024]{2,1,0:T(8,128)(2,1)}, u32[]{:S(2)}) copy-start(bf16[3,384,1024]{2,1,0:T(8,128)(2,1)} %get-tuple-element.103.refs_0_.refs_4_.refs_8_) | copy-start | bytes 7077892
  252.3 2.2 copy-start.3
  252.4 46.3 %collective-permute-start.7 = (bf16[2,384,1024]{2,1,0:T(8,128)(2,1)S(1)}, bf16[2,384,1024]{2,1,0:T(8,128)(2,1)}, u32[]{:S(2)}, u32[]{:S(2)}) collective-permute-start(bf16[2,384,1024]{2,1,0:T(8,128)(2,1)S(1)} %slice.64), channel_id=1, source_target_pairs={{0,8},{4,12},{8,0},{12,4},{1,9},{5,13},{9,1},{13,5},{2,10},{6,14},... | collective-permute-start | bytes 4718600 | tf_op jit(solution)/shard_map/ppermute | solution.py:73
  255.6 43.2 %collective-permute-start.4 = (bf16[2,128,768]{2,1,0:T(8,128)(2,1)}, bf16[2,128,768]{2,1,0:T(8,128)(2,1)}, u32[]{:S(2)}, u32[]{:S(2)}) collective-permute-start(bf16[2,128,768]{2,1,0:T(8,128)(2,1)} %get-tuple-element.138), channel_id=1, source_target_pairs={{0,1},{1,0},{2,3},{3,2},{4,5},{5,4},{6,7},{7,6},{8,9},{9,8},{10,11... | collective-permute-start | bytes 1179656 | tf_op jit(solution)/shard_map/ppermute | solution.py:73
  257.2 41.6 %collective-permute-start.5 = (bf16[2,128,768]{2,1,0:T(8,128)(2,1)}, bf16[2,128,768]{2,1,0:T(8,128)(2,1)}, u32[]{:S(2)}, u32[]{:S(2)}) collective-permute-start(bf16[2,128,768]{2,1,0:T(8,128)(2,1)} %get-tuple-element.137), channel_id=1, source_target_pairs={{0,2},{1,3},{2,0},{3,1},{4,6},{5,7},{6,4},{7,5},{8,10},{9,11},{10,... | collective-permute-start | bytes 1179656 | tf_op jit(solution)/shard_map/ppermute | solution.py:73
  258.5 40.3 %collective-permute-start.6 = (bf16[2,128,768]{2,1,0:T(8,128)(2,1)S(1)}, bf16[2,128,768]{2,1,0:T(8,128)(2,1)}, u32[]{:S(2)}, u32[]{:S(2)}) collective-permute-start(bf16[2,128,768]{2,1,0:T(8,128)(2,1)S(1)} %get-tuple-element.136), channel_id=1, source_target_pairs={{0,3},{1,2},{2,1},{3,0},{4,7},{5,6},{6,5},{7,4},{8,11},{9,10},{10,... | collective-permute-start | bytes 1179656 | tf_op jit(solution)/shard_map/ppermute | solution.py:73
  259.9 129.3 %collective-permute-start.9 = (bf16[1,384,1024]{2,1,0:T(8,128)(2,1)}, bf16[1,384,1024]{2,1,0:T(8,128)(2,1)}, u32[]{:S(2)}, u32[]{:S(2)}) collective-permute-start(bf16[1,384,1024]{2,1,0:T(8,128)(2,1)} %slice.65), channel_id=1, source_target_pairs={{0,8},{4,12},{8,0},{12,4},{1,9},{5,13},{9,1},{13,5},{2,10},{6,14},... | collective-permute-start | bytes 2359304 | tf_op jit(solution)/shard_map/ppermute | solution.py:73
  260.9 37.2 %copy-start.8 = (f32[13,768]{1,0:T(8,128)S(1)}, f32[13,768]{1,0:T(8,128)}, u32[]{:S(2)}) copy-start(f32[13,768]{1,0:T(8,128)} %get-tuple-element.90) | copy-start | bytes 119812
  260.9 37.2 %copy-start.10 = (f32[6,768]{1,0:T(8,128)S(1)}, f32[6,768]{1,0:T(8,128)}, u32[]{:S(2)}) copy-start(f32[6,768]{1,0:T(8,128)} %get-tuple-element.91) | copy-start | bytes 55300
  260.9 37.2 %copy-start.12 = (f32[12,12]{1,0:T(8,128)S(1)}, f32[12,12]{1,0:T(8,128)}, u32[]{:S(2)}) copy-start(f32[12,12]{1,0:T(8,128)} %get-tuple-element.92) | copy-start | bytes 1732
  298.8 113.8 %collective-permute-start.8 = (bf16[2,384,1024]{2,1,0:T(8,128)(2,1)}, bf16[2,384,1024]{2,1,0:T(8,128)(2,1)S(1)}, u32[]{:S(2)}, u32[]{:S(2)}) collective-permute-start(bf16[2,384,1024]{2,1,0:T(8,128)(2,1)} %collective-permute-done.7.refs_2_.refs_6_), channel_id=1, source_target_pairs={{0,4},{4,0},{8,12},{12,8},{1,5},{5,1},{9,13},{13,9},{2,6},{6,2},{1... | collective-permute-start | bytes 4718600 | tf_op jit(solution)/shard_map/ppermute | solution.py:73
  389.2 23.4 %collective-permute-start.10 = (bf16[1,384,1024]{2,1,0:T(8,128)(2,1)}, bf16[1,384,1024]{2,1,0:T(8,128)(2,1)S(1)}, u32[]{:S(2)}, u32[]{:S(2)}) collective-permute-start(bf16[1,384,1024]{2,1,0:T(8,128)(2,1)} %collective-permute-done.9.refs_10_), channel_id=1, source_target_pairs={{0,4},{4,0},{8,12},{12,8},{1,5},{5,1},{9,13},{13,9},{2,6},{6,2},{1... | collective-permute-start | bytes 2359304 | tf_op jit(solution)/shard_map/ppermute | solution.py:73
  400.4 6.1 %copy-start.14 = (f32[1,768]{1,0:T(1,128)S(1)}, f32[1,768]{1,0:T(1,128)}, u32[]{:S(2)}) copy-start(f32[1,768]{1,0:T(1,128)} %get-tuple-element.98) | copy-start | bytes 9220
  400.4 6.7 %copy-start.7 = (f32[31,768]{1,0:T(8,128)S(1)}, f32[31,768]{1,0:T(8,128)}, u32[]{:S(2)}) copy-start(f32[31,768]{1,0:T(8,128)} %get-tuple-element.99) | copy-start | bytes 285700
  412.6 0.9 copy-start.4
  412.6 1.4 copy-start.1
  414.0 14.1 %copy-start.5 = (bf16[512,768]{1,0:T(8,128)(2,1)S(1)}, bf16[512,768]{1,0:T(8,128)(2,1)}, u32[]{:S(2)}) copy-start(bf16[512,768]{1,0:T(8,128)(2,1)} %get-tuple-element.96) | copy-start | bytes 2359300
  428.1 1.7 copy-start.2

commit v5 on v4

--- a/solution.py
+++ b/solution.py
@@ -136,6 +136,7 @@
     head_width = width // HEADS
     columns = heads * head_width
     places = groups * local
+    odd = [r for r in range(places) if r % local]
     scale = head_width**-0.5
     tile = min(256, rows)
     per_member = rows // tile
@@ -143,7 +144,8 @@
     def body(*refs):
         x_hbm, dy_ref, route_ref, gain_ref, w_hbm = refs[:5]
         q_out, k_out, v_out, kt_out, vt_out, h_out, wt_out = refs[5:12]
-        target_out, target_rows, near_out, rest_out = refs[12:16]
+        target_out, target_rows, chosen_out, near_out = refs[12:16]
+        rest_out, refs = refs[16 : 16 + len(odd)], refs[:16] + refs[16 + len(odd) :]
         x_near, w_in, w_t, q_all, k_all, v_all, kt_all, vt_all, h_all, packed, near = refs[16:27]
         load_sem, x_s, x_r, r_s, r_r, out_sem, near_sem = refs[27:]
         me, exp_now = lax.axis_index("ctx"), lax.axis_index("exp")
@@ -175,7 +177,9 @@
         across().start()
         beside().start()
 
-        chosen = route_ref[...]
+        lines = jnp.concatenate([route_ref[...].astype(f32), jnp.zeros((6, rows), f32)], axis=0)
+        chosen = jnp.transpose(lines)[:, 0:2].astype(jnp.int32)
+        chosen_out[...] = chosen
         expert_count = places
         lanes = lax.broadcasted_iota(jnp.int32, (rows, 128), 1)
         hits = [lanes == chosen[:, c : c + 1] for c in range(2)]
@@ -209,12 +213,13 @@
             pack(g, local * g)
             if g < groups - 1:
                 row_copy(g + 1).start()
-        odd = [r for r in range(places) if r % local]
         for n, r in enumerate(odd):
             pack(groups + n, r)
         stores = [
             pltpu.make_async_copy(packed.at[0], near_out.at[0], near_sem.at[0]),
-            pltpu.make_async_copy(packed.at[pl.ds(groups, len(odd))], rest_out, near_sem.at[groups]),
+        ] + [
+            pltpu.make_async_copy(packed.at[groups + n], rest_out[n], near_sem.at[groups + n])
+            for n in range(len(odd))
         ]
         for copy in stores:
             copy.start()
@@ -292,8 +297,9 @@
         + [(shape_of((group_rows, width), bf16), anywhere)]
         + [(shape_of((3, width, width), bf16), anywhere)]
         + [(shape_of((rows, 2), jnp.int32), vector), (shape_of((2, rows), jnp.int32), vector)]
+        + [(shape_of((rows, 2), jnp.int32), vector)]
         + [(shape_of((groups, CAP, width), bf16), anywhere)]
-        + [(shape_of((places - groups, CAP, width), bf16), anywhere)],
+        + [(shape_of((CAP, width), bf16), anywhere)] * len(odd),
         scratch=[
             pltpu.VMEM((members, rows, width), bf16),
             pltpu.VMEM((3, width, width), bf16),
@@ -341,11 +347,13 @@
     blocks = group_rows // rows
     width = heads * head_width
 
-    def body(meta_ref, q_ref, k_ref, vt_ref, o_ref, ot_ref, lse_ref, top_ref, m_ref, l_ref, a_ref):
+    def body(meta_ref, q_ref, k_ref, vt_ref, o_ref, ot_ref, lse_ref, top_ref, m_ref, l_ref, a_ref, qt_ref):
         i = pl.program_id(0)
         m_ref[...] = jnp.full_like(m_ref, low_start)
         l_ref[...] = jnp.zeros_like(l_ref)
         a_ref[...] = jnp.zeros_like(a_ref)
+        for h in range(heads):
+            qt_ref[h] = jnp.transpose(q_ref[h])
 
         def one(j, _):
             q_first, k_first, needed, full = block_range(meta_ref, i, j, rows, layout)
@@ -356,7 +364,7 @@
                     allowed = allowed_pairs(meta_ref, q_first, k_first, rows, layout)
                 for h in range(heads):
                     part = slice(h * head_width, (h + 1) * head_width)
-                    s = mm(k_ref[h, pl.ds(at, rows), :], q_ref[h], NT)
+                    s = mm(k_ref[h, pl.ds(at, rows), :], qt_ref[h])
                     if masked:
                         s = jnp.where(allowed, s, mask_fill)
                     old = m_ref[h]
@@ -424,6 +432,7 @@
             pltpu.VMEM((heads, 1, rows), f32),
             pltpu.VMEM((heads, 1, rows), f32),
             pltpu.VMEM((width, rows), f32),
+            pltpu.VMEM((heads, head_width, rows), bf16),
         ],
         meta=meta,
         flops=2 * 2 * group_rows * group_rows * width,
@@ -440,7 +449,7 @@
     per = grad.shape[1] // rows
 
     def body(meta_ref, q_ref, k_ref, v_ref, kt_ref, grad_ref, w_ref, *refs):
-        ot_ref, lse_ref, out_ref, rows_ref, dk_ref, dv_ref, dq_ref, g_ref, delta_ref, sum_ref = refs
+        ot_ref, lse_ref, out_ref, rows_ref, dk_ref, dv_ref, dq_ref, g_ref, delta_ref, sum_ref, qt_ref, gt_ref = refs
         i = pl.program_id(0)
 
         @pl.when(i == 0)
@@ -462,7 +471,11 @@
 
         for h in range(heads):
             g_ref[h] = g[:, h * head_width : (h + 1) * head_width]
-        product = jnp.transpose(g.astype(f32)) * ot_ref[...]
+        turned = jnp.transpose(g.astype(f32))
+        gt_ref[...] = turned.astype(bf16)
+        for h in range(heads):
+            qt_ref[h] = jnp.transpose(q_ref[h])
+        product = turned * ot_ref[...]
         for h in range(heads):
             part = slice(h * head_width, (h + 1) * head_width)
             delta_ref[h] = jnp.sum(product[part, :], axis=0, keepdims=True)
@@ -479,11 +492,11 @@
                     allowed = allowed_pairs(meta_ref, q_first, k_first, rows, layout)
                 for h in range(heads):
                     part = slice(h * head_width, (h + 1) * head_width)
-                    s = mm(k_ref[h, pl.ds(at, rows), :], q_ref[h], NT)
+                    s = mm(k_ref[h, pl.ds(at, rows), :], qt_ref[h])
                     if masked:
                         s = jnp.where(allowed, s, mask_fill)
                     p = jnp.exp(s - lse_ref[pl.ds(h, 1), :])
-                    dp = mm(v_ref[h, pl.ds(at, rows), :], g_ref[h], NT)
+                    dp = mm(v_ref[h, pl.ds(at, rows), :], gt_ref[part, :])
                     ds = (p * (dp - delta_ref[h])).astype(bf16)
                     dv_ref[h, pl.ds(to, rows), :] += mm(p.astype(bf16), g_ref[h])
                     dk_ref[h, pl.ds(to, rows), :] += mm(ds, q_ref[h])
@@ -557,6 +570,8 @@
             pltpu.VMEM((heads, rows, head_width), bf16),
             pltpu.VMEM((heads, 1, rows), f32),
             pltpu.VMEM((width, grad.shape[2]), f32),
+            pltpu.VMEM((heads, head_width, rows), bf16),
+            pltpu.VMEM((width, rows), bf16),
         ],
         meta=meta,
         flops=5 * 2 * group_rows * group_rows * width,
@@ -573,11 +588,11 @@
 
 
 def token_front(
-    x, o, w_out, gain, w_router, previous, w_carry, target_rows, grad, routes, logit_w, vectors, local
+    x, o, w_out, gain, router_t, previous_t, w_carry, target_rows, grad, routes, logit_w, vectors, local
 ):
     rows, width = x.shape
     members, columns = w_out.shape[0], w_out.shape[1]
-    expert_all = w_router.shape[1]
+    expert_all = router_t.shape[0]
     groups = lax.axis_size("exp")
     places = groups * local
     expert_count = places
@@ -629,7 +644,9 @@
             inverse = lax.rsqrt(jnp.mean(total * total, axis=1, keepdims=True) + norm_eps)
             h2 = total * inverse * gain_ref[...]
             h2_ref[here, :] = h2
-            logits = mm_full(h2, router_ref[...]) + mm_full(prev_ref[here, :], carry_ref[...])
+            logits = mm_full(h2, router_ref[...], NT) + mm_full(
+                prev_ref[:, here], carry_ref[...], TN
+            )
             shifted = jnp.exp(logits - jnp.max(logits, axis=1, keepdims=True))
             prob = shifted / jnp.sum(shifted, axis=1, keepdims=True)
             prob_ref[here, :] = prob
@@ -741,8 +758,8 @@
     return run(
         body,
         (),
-        [(x, vector), (o, anywhere), (w_out, vector), (gain, vector), (w_router, vector)]
-        + [(previous, vector), (w_carry, vector), (target_rows, vector), (grad, vector)]
+        [(x, vector), (o, anywhere), (w_out, vector), (gain, vector), (router_t, vector)]
+        + [(previous_t, vector), (w_carry, vector), (target_rows, vector), (grad, vector)]
         + [(routes, vector), (logit_w, vector), (vectors, vector)],
         [(wide, vector), (wide, vector), (shape_of((rows, expert_all), f32), vector)]
         + [(placed, anywhere), (lines, anywhere), (wide, vector), (wide, vector)]
@@ -786,7 +803,9 @@
         dy_parts = [
             dy_late[r // local] if r % local else dy_ref.at[r // local] for r in range(places)
         ]
-        y_out, dx_out, dots_out, sum_out, beside_out = refs[6:11]
+        y_out, refs = refs[6 : 6 + groups], refs[:6] + refs[6 + groups :]
+        dx_out, dots_out, sum_out, beside_out = refs[6:10]
+        refs = refs[:6] + (None,) + refs[6:]
         x_all, xt_all, dy_all, dyt_all, gate_all, y_acc, dx_acc, dot_acc = refs[11:19]
         hid_t, dgt, dut, scaled_t, wg_buf, wu_buf, wd_buf = refs[19:26]
         hid_own, dg_own, du_own, scaled_own, wg_own, wu_own, wd_own = refs[26:33]
@@ -997,13 +1016,31 @@
         send_last(places - 1)
         send_back(0, middle)
 
+        def own_result(i, _):
+            at = pl.ds(pl.multiple_of(i * tile, tile), tile)
+            y_acc[...] += mm(hid_own[i], wd_own[at, :])
+            return 0
+
+        lax.fori_loop(0, tiles, own_result, 0)
+        send_last(middle - 1)
+
+        def relay_copy(g):
+            return remote(y_odd.at[g], relay.at[g], y_s.at[g], y_r.at[g], {"ctx": flip(me, 2)})
+
+        def result(r):
+            here = slice(r * CAP, (r + 1) * CAP)
+            return (gate_all[here, :] * y_acc[here, :]).astype(bf16)
+
+        for g in range(groups):
+            y_odd[g] = result(local * g + 1)
+            if g:
+                relay_copy(g - 1).start()
+        for g in range(groups):
+            y_out[g][0] = result(local * g)
+        relay_copy(groups - 1).start()
+
         def own_step(i, _):
             f = away + i
-            at = pl.ds(pl.multiple_of(i * tile, tile), tile)
-
-            @pl.when(i == 1)
-            def _():
-                send_last(middle - 1)
 
             @pl.when(i >= 1)
             def _():
@@ -1021,28 +1058,10 @@
                 send[slot, n] = found[:half, :]
                 total[f, n] = found[half:, :]
             core_copy(f, slot).start()
-            y_acc[...] += mm(hid_own[i], wd_own[at, :])
             return 0
 
         lax.fori_loop(0, tiles, own_step, 0)
-        if tiles == 1:
-            send_last(middle - 1)
         core_sum(steps - 1)
-        def relay_copy(g):
-            return remote(y_odd.at[g], relay.at[g], y_s.at[g], y_r.at[g], {"ctx": flip(me, 2)})
-
-        def result(r):
-            here = slice(r * CAP, (r + 1) * CAP)
-            return (gate_all[here, :] * y_acc[here, :]).astype(bf16)
-
-        for g in range(groups):
-            y_odd[g] = result(local * g + 1)
-            if g:
-                relay_copy(g - 1).start()
-        for g in range(groups):
-            y_out[g, 0] = result(local * g)
-        relay_copy(groups - 1).start()
-
         def beside_copy(i):
             return remote(total.at[away + i], beside.at[i], e_s.at[i], e_r.at[i], sibling)
 
@@ -1082,7 +1101,7 @@
             dots_out[r] = dots_near[r]
         for g in range(groups):
             relay_copy(g).wait()
-            y_out[g, 1] = relay[g]
+            y_out[g][1] = relay[g]
         for i in range(tiles):
             beside_copy(i).wait()
             beside_store(i).start()
@@ -1091,7 +1110,7 @@
             beside_store(i).wait()
 
     placed = shape_of((places, CAP, width), bf16)
-    pairs = shape_of((groups, local, CAP, width), bf16)
+    pair = shape_of((local, CAP, width), bf16)
     lines = shape_of((places, 1, CAP), f32)
     return run(
         body,
@@ -1099,7 +1118,8 @@
         [(arrived, vector), (grads, vector), (gates, vector)]
         + [(w, anywhere) for w in (w_gate, w_up, w_down)]
         + [(g, vector) for g in late],
-        [(pairs, vector), (placed, vector), (lines, vector)]
+        [(pair, vector)] * groups
+        + [(placed, vector), (lines, vector)]
         + [(shape_of((3, half, per_part), bf16), anywhere)] * 2,
         scratch=[
             pltpu.VMEM((rows, width), bf16),
@@ -1160,7 +1180,8 @@
 
 
 def token_back(
-    x1, h2, grad, prob, previous, routes, targets, back, dots, dgate_zero, dh_zero, gain, router_t,
+    x1, h2, grad, prob, previous_t, routes, targets, back, dots, dgate_zero, dh_zero, gain, router_t,
+    zero_sums,
 ):
     rows, width = x1.shape
     tile = 128
@@ -1168,11 +1189,12 @@
     places = back.shape[0]
     expert_all = prob.shape[1]
     members = lax.axis_size("ctx")
+    last = expert_all + 1 + zero_sums.shape[0]
 
     def body(*refs):
         (x1_ref, h2_ref, dy_ref, prob_ref, prev_ref, route_ref, target_ref) = refs[:7]
-        back_ref, dots_ref, dz_ref, dh_ref, gain_ref, router_ref = refs[7:13]
-        dx1_ref, sums_ref, carry_ref, da_out, da_near, a_s, a_r, out_sem = refs[13:]
+        back_ref, dots_ref, dz_ref, dh_ref, gain_ref, router_ref, zero_ref = refs[7:14]
+        dx1_ref, sums_ref, da_out, da_near, a_s, a_r, out_sem = refs[14:]
         me = lax.axis_index("ctx")
         peers = [{"ctx": flip(me, 1)}, {"ctx": flip(me, 2)}]
         ready = greet(peers)
@@ -1187,7 +1209,7 @@
             )
 
         sums_ref[...] = jnp.zeros_like(sums_ref)
-        carry_ref[...] = jnp.zeros_like(carry_ref)
+        sums_ref[expert_all + 1 : last, :] = zero_ref[...]
         ready()
 
         def token_rows(t, _):
@@ -1220,7 +1242,7 @@
             da_near[0, here, :] = dx1.astype(bf16)
             sums_ref[0:expert_all, :] += mm_full(dlogit, h2, TN)
             sums_ref[expert_all : expert_all + 1, :] += jnp.sum(dh2 * normed, axis=0, keepdims=True)
-            carry_ref[...] += mm_full(dlogit, prev_ref[here, :], TN)
+            sums_ref[last:, 0:expert_all] += mm_full(prev_ref[:, here], dlogit)
             da_copy(1, t).start()
             da_copy(0, t).start()
 
@@ -1251,11 +1273,10 @@
     return run(
         body,
         (),
-        [(a, vector) for a in (x1, h2, grad, prob, previous, routes, targets, back, dots)]
-        + [(a, vector) for a in (dgate_zero, dh_zero, gain, router_t)],
+        [(a, vector) for a in (x1, h2, grad, prob, previous_t, routes, targets, back, dots)]
+        + [(a, vector) for a in (dgate_zero, dh_zero, gain, router_t, zero_sums)],
         [(shape_of((rows, width), f32), vector)]
-        + [(shape_of((expert_all + 1, width), f32), vector)]
-        + [(shape_of((expert_all, expert_all), f32), vector)]
+        + [(shape_of((last + expert_all, width), f32), vector)]
         + [(shape_of((members, rows, width), bf16), anywhere)],
         scratch=[
             pltpu.VMEM((members, rows, width), bf16),
@@ -1275,7 +1296,7 @@
     team = parts * groups
     local = produced[0].shape[0]
     places = groups * local
-    wide_share, out_share = width // team, per_group // team
+    wide_share, out_share = width // (2 * team), per_group // team
     small_rows = small.shape[0]
     small_steps = [(axis, bit) for axis in ("ctx", "dp", "exp") for bit in powers(axis)]
     hops = len(small_steps)
@@ -1293,11 +1314,11 @@
         input_out, wide_out, flat_out, small_out, gain_out, tops_out, result_out = take(7)
         dqkv, product, h1_all, x_all, dx1_all, w_all, base_all, y_near = take(8)
         part_send, part_core, part_y, y_got, part_own = take(5)
-        wide_mine, wide_far, wide_all = take(3)
-        flat_mine, flat_far, flat_all = take(3)
+        wide_mine, wide_far_x, wide_far_z, wide_all = take(4)
+        flat_mine, flat_far_x, flat_far_z, flat_all = take(4)
         small_acc, small_far, gain_acc, gain_far, tops_acc, tops_far = take(6)
         load_sem, near_s, near_r = take(3)
-        dense_sems = [take(8), take(8)]
+        wide_sems, flat_sems = [take(12), take(12)], take(12)
         hop_s, hop_r, gain_s, gain_r, top_s, top_r = take(6)
 
         me = lax.axis_index("ctx")
@@ -1326,75 +1347,106 @@
             return pltpu.make_async_copy(loads[n][0], loads[n][1], load_sem.at[n])
 
         class Dense:
-            def __init__(self, mine, far_buf, all_buf, sems, share):
-                self.mine, self.far, self.all, self.share = mine, far_buf, all_buf, share
-                (self.rs, self.rr, self.gs, self.gr, self.ys, self.yr, self.cs, self.cr) = sems[:8]
-
-            def reduce_copy(self, r):
+            def __init__(self, mine, far_x, far_z, all_buf, sems):
+                self.mine, self.far_x, self.far_z, self.all = mine, far_x, far_z, all_buf
+                self.sems = sems
+
+            def own_block(self, d=0):
+                return pl.ds(flip(dp_now, d) * groups, groups)
+
+            def x_copy(self, d):
                 return remote(
-                    self.mine.at[flip(seat, r)], self.far.at[r - 1], self.rs.at[r - 1],
-                    self.rr.at[r - 1], team_peer(r),
+                    self.mine.at[self.own_block(d)], self.far_x.at[d - 1], self.sems[0].at[d],
+                    self.sems[1].at[d], {"dp": flip(dp_now, d)},
                 )
 
-            def gather_copy(self, r):
+            def z_copy(self, g):
                 return remote(
-                    self.all.at[0, seat], self.all.at[0, seat], self.gs.at[r - 1],
-                    self.gr.at[r - 1], team_peer(r),
+                    self.mine.at[dp_now * groups + flip(exp_now, g)], self.far_z.at[g - 1],
+                    self.sems[2].at[g], self.sems[3].at[g], {"exp": flip(exp_now, g)},
                 )
 
-            def gather_arrival(self, r):
-                spot = self.all.at[0, flip(seat, r)]
-                return remote(spot, spot, self.gs.at[r - 1], self.gr.at[r - 1], team_peer(r))
-
-            def y_forward(self, r):
+            def gz_copy(self, g, theirs=False):
+                spot = self.all.at[0, dp_now * groups + flip(exp_now, g) if theirs else seat]
                 return remote(
-                    self.all.at[0, flip(seat, r)], self.all.at[2, flip(seat, r)], self.ys.at[r],
-                    self.yr.at[r], near_peer(2),
+                    spot, spot, self.sems[4].at[g], self.sems[5].at[g], {"exp": flip(exp_now, g)}
                 )
 
-            def core_forward(self, n):
+            def gx_copy(self, d, theirs=False):
+                spot = self.all.at[0, self.own_block(d if theirs else 0)]
                 return remote(
-                    self.all.at[2 * n], self.all.at[2 * n + 1], self.cs.at[n], self.cr.at[n],
-                    near_peer(1),
+                    spot, spot, self.sems[6].at[d], self.sems[7].at[d], {"dp": flip(dp_now, d)}
                 )
 
-            def scatter(self):
-                for r in range(1, team):
-                    self.reduce_copy(r).start()
-
-            def collect(self):
-                for r in range(1, team):
-                    self.reduce_copy(r).wait_recv()
-                total = self.mine[seat].astype(f32)
-                for r in range(1, team):
-                    total = total + self.far[r - 1].astype(f32)
-                self.all[0, seat] = total.astype(bf16)
+            def y_copy(self, d):
+                return remote(
+                    self.all.at[0, self.own_block(d)], self.all.at[2, self.own_block(d)],
+                    self.sems[8].at[d], self.sems[9].at[d], near_peer(2),
+                )
+
+            def core_copy(self, n):
+                return remote(
+                    self.all.at[2 * n], self.all.at[2 * n + 1], self.sems[10].at[n],
+                    self.sems[11].at[n], near_peer(1),
+                )
+
+            def start(self):
+                for d in range(1, parts):
+                    self.x_copy(d).start()
+
+            def to_z(self):
+                for d in range(1, parts):
+                    self.x_copy(d).wait()
+                for g in list(range(1, groups)) + [0]:
+                    c = dp_now * groups + flip(exp_now, g)
+                    value = self.mine[c].astype(f32)
+                    for d in range(1, parts):
+                        value = value + self.far_x[d - 1, flip(exp_now, g)].astype(f32)
+                    self.mine[c] = value.astype(bf16)
+                for g in range(1, groups):
+                    self.z_copy(g).start()
+
+            def to_gather(self):
+                for g in range(1, groups):
+                    self.z_copy(g).wait()
+                value = self.mine[seat].astype(f32)
+                for g in range(1, groups):
+                    value = value + self.far_z[g - 1].astype(f32)
+                self.all[0, seat] = value.astype(bf16)
 
             def gather(self):
-                for r in range(1, team):
-                    self.gather_copy(r).start()
-                self.y_forward(0).start()
-
-            def forward(self):
-                for r in range(1, team):
-                    self.gather_arrival(r).wait_recv()
-                    self.y_forward(r).start()
-                for r in range(1, team):
-                    self.reduce_copy(r).wait_send()
-                    self.gather_copy(r).wait_send()
-                self.core_forward(0).start()
-
-            def forward_far(self):
-                for r in range(team):
-                    self.y_forward(r).wait()
-                self.core_forward(1).start()
+                for g in range(1, groups):
+                    self.gz_copy(g).start()
+
+            def to_x(self):
+                for g in range(1, groups):
+                    self.gz_copy(g).wait_send()
+                    self.gz_copy(g, True).wait_recv()
+                for d in range(1, parts):
+                    self.gx_copy(d).start()
+                self.y_copy(0).start()
+
+            def to_y(self):
+                for d in range(1, parts):
+                    self.gx_copy(d).wait_send()
+                    self.gx_copy(d, True).wait_recv()
+                    self.y_copy(d).start()
+                self.core_copy(0).start()
+
+            def to_core(self):
+                for d in range(parts):
+                    self.y_copy(d).wait()
+                self.core_copy(1).start()
 
             def done(self):
                 for n in range(2):
-                    self.core_forward(n).wait()
-
-        wide = Dense(wide_mine, wide_far, wide_all, dense_sems[0], wide_share)
-        flat = Dense(flat_mine, flat_far, flat_all, dense_sems[1], out_share)
+                    self.core_copy(n).wait()
+
+        wides = [
+            Dense(wide_mine.at[n], wide_far_x.at[n], wide_far_z.at[n], wide_all.at[n], wide_sems[n])
+            for n in range(2)
+        ]
+        flat = Dense(flat_mine, flat_far_x, flat_far_z, flat_all, flat_sems)
 
         def hop_peer(n):
             axis, bit = small_steps[n]
@@ -1466,21 +1518,26 @@
         for c in range(team):
             flat_mine[c] = flat_rows[c * out_share : (c + 1) * out_share, :].astype(bf16)
         ready()
-        flat.scatter()
+        flat.start()
         small_start(0)
         load(0).wait()
         load(1).wait()
-        product[...] = mm(h1_all[0:rows, :], dqkv[0:rows, :], TN)
-
-        def weigh(j, _):
-            here = pl.ds(pl.multiple_of(j * rows, rows), rows)
+
+        def weigh(n, _):
+            here = pl.ds(pl.multiple_of(n * rows, rows), rows)
             product[...] += mm(h1_all[here, :], dqkv[here, :], TN)
             return 0
 
+        product[...] = mm(h1_all[0:rows, :], dqkv[0:rows, :], TN)
         lax.fori_loop(1, group_rows // rows, weigh, 0)
-        for c in range(team):
-            wide_mine[c] = product[c * wide_share : (c + 1) * wide_share, :].astype(bf16)
-        wide.scatter()
+        for n in range(2):
+            for c in range(team):
+                at = (n * team + c) * wide_share
+                wide_mine[n, c] = product[at : at + wide_share, :].astype(bf16)
+            if n:
+                wides[0].start()
+        flat.to_z()
+        wides[1].start()
         for n in range(2, len(loads)):
             load(n).wait()
         queue = [(j, t) for j in (3, 1) for t in range(row_tiles)]
@@ -1502,10 +1559,12 @@
         y_part(row_tiles - 1).start()
         for t in range(1, row_tiles):
             part_own[tile_rows(t), :] = part(0, t)
-        flat.collect()
+        wides[0].to_z()
+        flat.to_gather()
+        small_next()
+        wides[1].to_z()
         flat.gather()
-        small_next()
-        small_next()
+        wides[0].to_gather()
 
         def token_rows(t, _):
             here = pl.ds(pl.multiple_of(t * 128, 128), 128)
@@ -1514,12 +1573,15 @@
             ).astype(bf16)
             return 0
 
-        lax.fori_loop(0, rows // 128, token_rows, 0)
-        flat.forward()
+        lax.fori_loop(0, rows // 256, token_rows, 0)
+        wides[0].gather()
         small_next()
-        wide.collect()
+        flat.to_x()
+        wides[1].to_gather()
+        lax.fori_loop(rows // 256, rows // 128, token_rows, 0)
+        wides[1].gather()
+        wides[0].to_x()
         small_next()
-        wide.gather()
         for t in range(row_tiles):
             core_part(1, t).wait()
             core_part(3, t).wait_send()
@@ -1544,42 +1606,53 @@
         )
         store = pltpu.make_async_copy(dx1_all, input_out, load_sem.at[len(loads)])
         store.start()
+        flat.to_y()
+        gain_copy(0).start()
+        wides[1].to_x()
+        wides[0].to_y()
         small_next()
-        gain_copy(0).start()
-        wide.forward()
-        small_next()
-        flat.forward_far()
+        events = [
+            flat.to_core, wides[1].to_y, wides[0].to_core, flat.done, wides[1].to_core,
+        ]
         for n in range(hops):
             gain_copy(n).wait()
             gain_acc[n + 1] = gain_acc[n] + gain_far[n]
+            if events:
+                events.pop(0)()
             if n + 1 < hops:
                 gain_copy(n + 1).start()
         while small_hops:
             small_next()
-        flat.done()
-        wide.forward_far()
-        wide.done()
-        final = [
-            pltpu.make_async_copy(wide_all, wide_out, load_sem.at[len(loads) + 1]),
-            pltpu.make_async_copy(flat_all, flat_out, load_sem.at[len(loads) + 2]),
-        ]
+        while events:
+            events.pop(0)()
+        final = [pltpu.make_async_copy(flat_all, flat_out, load_sem.at[len(loads) + 1])]
+        for n in range(2):
+            wides[n].done()
+            final.append(
+                pltpu.make_async_copy(
+                    wide_all.at[n], wide_out.at[n], load_sem.at[len(loads) + 2 + n]
+                )
+            )
         for copy in final:
             copy.start()
         small_out[...] = small_acc[hops]
-        gain_out[...] = gain_acc[hops]
+        gain_out[...] = gain_acc[hops, 0, :]
         tops_out[...] = tops_acc[hops]
         store.wait()
         for copy in final:
             copy.wait()
 
-    def dense_scratch(share, across):
+    def dense_scratch(share, across, lead=()):
         return [
-            pltpu.VMEM((team, share, across), bf16),
-            pltpu.VMEM((max(1, team - 1), share, across), bf16),
-            pltpu.VMEM((members, team, share, across), bf16),
+            pltpu.VMEM(lead + (team, share, across), bf16),
+            pltpu.VMEM(lead + (max(1, parts - 1), groups, share, across), bf16),
+            pltpu.VMEM(lead + (max(1, groups - 1), share, across), bf16),
+            pltpu.VMEM(lead + (members, team, share, across), bf16),
         ]
 
-    dense_sem = [dma((team,))] * 6 + [dma((2,))] * 2
+    dense_sem = (
+        [dma((parts,))] * 2 + [dma((groups,))] * 4 + [dma((parts,))] * 4 + [dma((2,))] * 2
+    )
     wide_rows = shape_of((rows, width), f32)
     return run(
         body,
@@ -1590,10 +1663,10 @@
         + [(a, anywhere) for a in produced],
         [
             (wide_rows, anywhere),
-            (shape_of((members, team, wide_share, 3 * per_group), bf16), anywhere),
+            (shape_of((2, members, team, wide_share, 3 * per_group), bf16), anywhere),
             (shape_of((members, team, out_share, width), bf16), anywhere),
             (shape_of((small_rows, width), f32), vector),
-            (shape_of((1, width), f32), vector),
+            (shape_of((width,), f32), vector),
             (shape_of((tops.shape[0], 128), f32), vector),
             (shape_of((rows, width), bf16), vector),
         ],
@@ -1612,14 +1685,13 @@
             pltpu.VMEM((rows, width), bf16),
             pltpu.VMEM((rows, width), f32),
         ]
-        + dense_scratch(wide_share, 3 * per_group)
+        + dense_scratch(wide_share, 3 * per_group, (2,))
         + dense_scratch(out_share, width)
         + [pltpu.VMEM((hops + 1, small_rows, width), f32), pltpu.VMEM((hops, small_rows, width), f32)]
         + [pltpu.VMEM((hops + 1, 1, width), f32), pltpu.VMEM((hops, 1, width), f32)]
         + [pltpu.VMEM((hops + 1, tops.shape[0], 128), f32), pltpu.VMEM((hops, tops.shape[0], 128), f32)]
-        + [dma((10 + places,))] + [dma((3 * (rows // row_tile),))] * 2
-        + dense_sem
-        + dense_sem
+        + [dma((12 + places,))] + [dma((3 * (rows // row_tile),))] * 2
+        + dense_sem * 3
         + [dma((hops,))] * 6,
         flops=4 * 2 * rows * width * width * 3,
         moved=20 * 1024 * 1024,
@@ -1685,47 +1757,102 @@
     )
 
 
-def place_columns(meta, near, per_group):
-    members, team, share, _ = near.shape
-    width = team * share
+def place_dense(meta, near, flat, tops, small, w_qkv, kinds):
+    _, members, team, share, lanes = near.shape
+    per_group = lanes // 3
+    half = team * share
+    width = 2 * half
+    rows_all = flat.shape[1] * flat.shape[2]
     step = 8 // math.gcd(share, 8)
-
-    def body(meta_ref, near_ref, out_ref):
+    while team // step > 4:
+        step *= 2
+    per_half = team // step
+    tall = step * share
+
+    heads = HEADS // members
+    head_width = width // HEADS
+    expert_all = (small.shape[0] - 1 - 3 * kinds) // 2
+    at_vec = expert_all + 1
+    at_logit = at_vec + kinds
+    at_carry = at_logit + 2 * kinds
+
+    def body(meta_ref, near_ref, flat_ref, tops_ref, small_ref, w_ref, *outs):
+        out_ref, flat_out, clip_ref, router_out, norm_out, vec_out, logit_out, carry_out = outs[:8]
+        scale_ref = outs[8]
+
+        @pl.when((pl.program_id(0) == 0) & (pl.program_id(1) == 0))
+        def _():
+            lanes = lax.broadcasted_iota(jnp.int32, (1, width), 1)
+            scale = jnp.zeros((1, width), f32)
+            for n in range(HEADS):
+                top = tops_ref[n % heads : n % heads + 1, n // heads : n // heads + 1]
+                ratio = jnp.sqrt(jnp.minimum(1.0, clip_limit / top))
+                inside = (lanes >= n * head_width) & (lanes < (n + 1) * head_width)
+                scale = jnp.where(inside, ratio, scale)
+            scale_ref[...] = scale
+            router_out[...] = small_ref[0:expert_all, :]
+            norm_out[...] = small_ref[expert_all, :]
+            vec_out[...] = small_ref[at_vec : at_vec + kinds, :]
+            for n in range(kinds):
+                logit_out[n] = small_ref[at_logit + 2 * n : at_logit + 2 * n + 2, :]
+            carry_out[...] = small_ref[at_carry:, 0:expert_all]
+
         for c in range(step):
-            pieces = [near_ref[meta_ref[0] ^ g, c] for g in range(members)]
+            pieces = [near_ref[0, meta_ref[0] ^ g, c] for g in range(members)]
             for w in range(3):
                 at = slice(w * per_group, (w + 1) * per_group)
                 out_ref[w, c * share : (c + 1) * share, :] = jnp.concatenate(
                     [piece[:, at] for piece in pieces], axis=1
                 ).astype(f32)
-
-    out = shape_of((3, width, members * per_group), f32)
+        clip_ref[...] = w_ref[...].astype(f32) * scale_ref[...]
+
+        @pl.when(pl.program_id(1) == 0)
+        def _():
+            for c in range(team):
+                at = slice(c * flat.shape[2], (c + 1) * flat.shape[2])
+                for j in range(2):
+                    member = pl.program_id(0) * 2 + j
+                    flat_out[j, at, :] = flat_ref[meta_ref[0] ^ member, c].astype(f32)
+
+    square = shape_of((3, width, width), f32)
     return run(
         body,
-        (team // step,),
-        [(near, pl.BlockSpec((members, step, share, 3 * per_group), lambda c, m: (0, c, 0, 0)))],
-        [(out, pl.BlockSpec((3, step * share, members * per_group), lambda c, m: (0, c, 0)))],
+        (2, per_half),
+        [
+            (
+                near,
+                pl.BlockSpec((1, members, step, share, lanes), lambda n, c, m: (n, 0, c, 0, 0)),
+            ),
+            (flat, whole(flat)),
+            (tops, whole(tops)),
+            (small, whole(small)),
+            (w_qkv, pl.BlockSpec((2, tall, width), lambda n, c, m: (0, n * per_half + c, 0))),
+        ],
+        [
+            (square, pl.BlockSpec((3, tall, width), lambda n, c, m: (0, n * per_half + c, 0))),
+            (
+                shape_of((members, rows_all, width), f32),
+                pl.BlockSpec((2, rows_all, width), lambda n, c, m: (n, 0, 0)),
+            ),
+            (
+                shape_of((2, width, width), f32),
+                pl.BlockSpec((2, tall, width), lambda n, c, m: (0, n * per_half + c, 0)),
+            ),
+        ]
+        + [
+            (o, whole(o))
+            for o in (
+                shape_of((expert_all, width), f32),
+                shape_of((width,), f32),
+                shape_of((kinds, width), f32),
+                shape_of((kinds, 2, width), f32),
+                shape_of((expert_all, expert_all), f32),
+            )
+        ],
+        scratch=[pltpu.VMEM((1, width), f32)],
         meta=meta,
-        moved=out.size * 6,
-    )[0]
-
-
-def place_rows(meta, near):
-    members, team, share, width = near.shape
-
-    def body(meta_ref, near_ref, out_ref):
-        for c in range(team):
-            out_ref[0, c * share : (c + 1) * share, :] = near_ref[0, c].astype(f32)
-
-    out = shape_of((members, team * share, width), f32)
-    return run(
-        body,
-        (members,),
-        [(near, pl.BlockSpec((1, team, share, width), lambda j, m: (j, 0, 0, 0)))],
-        [(out, pl.BlockSpec((1, team * share, width), lambda j, m: (m[0] ^ j, 0, 0)))],
-        meta=meta,
-        moved=out.size * 6,
-    )[0]
+        moved=square.size * 12,
+    )
 
 
 def shards(
@@ -1778,67 +1905,52 @@
             inverse,
         ]
     )
-    gain1 = norm1_gain.reshape(1, width)
-    gain2 = norm2_gain.reshape(1, width)
+    gain1, gain2 = norm1_gain, norm2_gain
     w_out_parts = w_out.reshape(members, per_group, width)
-    route_ids = routes[0]
-    previous = prev_logits[0]
+    previous_t = jnp.transpose(prev_logits[0])
+    router_t = jnp.transpose(w_router)
     odd = [r for r in range(groups * local) if r % local]
 
-    q, k, v, kt, vt, h1, weights_t, targets, target_rows, grad_near, grad_rest = begin(
-        x, grad, route_ids, gain1, w_qkv, local
-    )
+    begun = begin(x, grad, jnp.transpose(routes[0]), gain1, w_qkv, local)
+    q, k, v, kt, vt, h1, weights_t, targets, target_rows, route_ids, grad_near = begun[:11]
+    grad_rest = begun[11:]
     weights_t = weights_t.reshape(3, members, per_group, width)
     grad_late = [slot_swap(grad_rest[n], r, local) for n, r in enumerate(odd)]
     o, ot, lse, tops = attend(meta, q, k, vt, deal_block, layout)
     logit_rows = jnp.swapaxes(const_logit_w, 1, 2).reshape(-1, width)
     x1, h2, prob, token_near, gate_near, base, dh_zero, dgate_zero, zero_sums = token_front(
-        x, o, w_out_parts, gain2, w_router, previous, w_carry, target_rows, grad, route_ids,
+        x, o, w_out_parts, gain2, router_t, previous_t, w_carry, target_rows, grad, route_ids,
         logit_rows, const_vec, local,
     )
-    produced, token_back_rows, dots, expert_sum, beside = expert_layer(
-        token_near, grad_near, grad_late, gate_near, w_gate, w_up, w_down
-    )
-    dx1, token_sums, carry_sum, da_near = token_back(
-        x1, h2, grad, prob, previous, route_ids, targets, token_back_rows, dots, dgate_zero,
-        dh_zero, gain2, jnp.transpose(w_router),
+    worked = expert_layer(token_near, grad_near, grad_late, gate_near, w_gate, w_up, w_down)
+    produced = worked[:groups]
+    token_back_rows, dots, expert_sum, beside = worked[groups:]
+    dx1, small, da_near = token_back(
+        x1, h2, grad, prob, previous_t, route_ids, targets, token_back_rows, dots, dgate_zero,
+        dh_zero, gain2, router_t, zero_sums,
     )
     expert_now, da_near = lax.optimization_barrier((expert_sum, da_near))
-    over_first, over_last = swap(expert_now[:2], "ctx", 2), swap(expert_now[2:], "ctx", 2)
+    over = swap(expert_now, "ctx", 2)
     y_near = [swap(produced[g], "exp", g) if g else produced[0] for g in range(groups)]
     dqkv, out_sum = attend_back(
         meta, q, k, v, kt, da_near, w_out_parts, ot, lse, deal_block, layout
     )
 
-    expert_all = w_router.shape[1]
-    small = jnp.concatenate(
-        [token_sums, zero_sums, jnp.pad(carry_sum, ((0, 0), (0, width - expert_all)))], axis=0
-    )
     input_grad, qkv_near, out_near, small, norm1_grad, top_all, result = finish(
         dqkv, h1, x, gain1, dx1, weights_t, out_sum, small, tops, y_near, base, targets
     )
-    corner_first, corner_last = swap(over_first, "ctx", 1), swap(over_last, "ctx", 1)
-    near = [
-        [(expert_sum, n), (beside, n), (over_first, n), (corner_first, n)] for n in range(2)
-    ] + [[(expert_sum, 2), (beside, 2), (over_last, 0), (corner_last, 0)]]
+    over, qkv_near = lax.optimization_barrier((over, qkv_near))
+    corner = swap(over, "ctx", 1)
+    near = [[(a, n) for a in (expert_sum, beside, over, corner)] for n in range(3)]
+    dense = place_dense(meta, qkv_near, out_near, top_all, small, w_qkv, const_vec.shape[0])
+    qkv_grad, out_grad, clipped, router_grad, norm2_grad, vec_grad, logit_grad, carry_grad = dense
+    router_grad, logit_grad = jnp.transpose(router_grad), jnp.swapaxes(logit_grad, 1, 2)
+    out_grad = out_grad.reshape(width, width)
     gate_grad, up_grad, down_grad = place_experts(meta, near, (False, False, True))
-    out_grad = place_rows(meta, out_near).reshape(width, width)
-    qkv_grad = place_columns(meta, qkv_near, per_group)
-    kinds = const_vec.shape[0]
-    router_grad = jnp.transpose(small[:expert_all])
-    norm2_grad = small[expert_all]
-    start = expert_all + 1
-    vec_grad = small[start : start + kinds]
-    logit_grad = jnp.swapaxes(small[start + kinds : start + 3 * kinds].reshape(kinds, 2, width), 1, 2)
-    carry_grad = jnp.transpose(small[start + 3 * kinds :, :expert_all])
-    head_max = jnp.transpose(top_all[:, :members]).reshape(HEADS)
-    clip_ratio = jnp.sqrt(jnp.minimum(1.0, clip_limit / head_max))
-    head_scale = jnp.repeat(clip_ratio, head_width)
-    clipped = w_qkv[:2].astype(f32) * head_scale[None, None, :]
     return (
         result[None],
         input_grad[None],
-        norm1_grad[0],
+        norm1_grad,
         norm2_grad,
         qkv_grad,
         out_grad,

time: 435 us -> 386 us (0.89)
  Pallas kernels: 390 us -> 359 us
  local copies, waits for them, and re-layouts: 20.5 us -> 8.29 us
  other arithmetic: 6.29 us -> 0.13 us
    pallas_call x10 -> x9, Pallas kernels: 390 us -> 359 us  [run(): pl.pallas_call(body, out_shape=[o for o, _ in outputs], grid_spec=pltpu.P...]
    unnamed x48 -> x38, local copies, waits for them, and re-layouts: 9.07 us -> 6.99 us
  transfers between devices with their start and end apart: 11 -> 9, of which waited for: 0 -> 0; matrix products, arithmetic and copies ran while one was open for 4% -> 1% of each run, Pallas kernels for 52% -> 52%
where the time goes in v5:
time: 386 us; the launch traced here: 382 us
  Pallas kernels  359 us (93%)
  starting transfers between devices  12.7 us (3%)
  local copies, waits for them, and re-layouts  8.29 us (2%)
    pallas_call x9, Pallas kernels, run(): pl.pallas_call(body, out_shape=[o for o, _ in outputs], grid_spec=pltpu.P...  359 us
  transfers between devices with their start and end apart: 9, of which 0 were waited for; matrix products, arithmetic and copies ran while one was open for 1% of the time, Pallas kernels for 52%

profile of v5, /device:TPU:0, one launch (start us, length us, event | category | flops | bytes accessed | tf_op | source)
XLA Modules:
  0.0 381.7 jit_solution(9397593308667762133)
XLA Ops:
  0.6 0.0 copy-start.7
  0.7 31.4 %shard_map.272 = (bf16[3,2048,64]{2,1,0:T(8,128)(2,1)}, bf16[3,2048,64]{2,1,0:T(8,128)(2,1)}, bf16[3,2048,64]{2,1,0:T(8,128)(2,1)}, bf16[192,2048]{1,0:T(8,128)(...) custom-call(bf16[512,768]{1,0:T(8,128)(2,1)} %bitcast.41, ...), custom_call_target="tpu_custom_call" | custom-call | flops 3019898880 | bytes 20971520 | tf_op jit(solution)/shard_map/pallas_call | solution.py:50
  32.0 0.6 collective-permute-start
  32.6 1.5 collective-permute-start.1
  34.1 1.5 collective-permute-start.2
  35.6 3.3 collective-permute-start.3
  38.9 0.1 select_reduce_fusion
  39.0 0.7 concatenate.3.meta_ref
  39.7 26.8 %shard_map.273 = (bf16[2048,192]{1,0:T(8,128)(2,1)}, f32[192,2048]{1,0:T(8,128)}, f32[3,2048]{1,0:T(4,128)}, f32[3,256]{1,0:T(4,128)}) custom-call(s32[22]{0:T(128)} %concatenate.3.meta_ref, bf16[3,2048,64]{2,1,0:T(8,128)(2,1)} %get-tuple-element.77.q_ref, bf16[3,2048,64]{2,1,0:T(8,128)(2,1)} %get-tuple-element.78.k_ref, ...), custom_call_target="tpu_custom_call" | custom-call | flops 3221225472 | bytes 5505024 | tf_op jit(solution)/shard_map/pallas_call | solution.py:50
  66.5 0.6 copy.33
  67.1 0.6 reshape.41.refs_10_
  67.7 56.6 %shard_map.274 = (f32[512,768]{1,0:T(8,128)}, f32[512,768]{1,0:T(8,128)}, f32[512,12]{1,0:T(8,128)}, bf16[8,128,768]{2,1,0:T(8,128)(2,1)}, f32[8,1,128]{2,1,0:T(...) custom-call(bf16[512,768]{1,0:T(8,128)(2,1)} %bitcast.42, ...), custom_call_target="tpu_custom_call" | custom-call | flops 1409286144 | bytes 11796480 | tf_op jit(solution)/shard_map/pallas_call | solution.py:50
  124.3 0.0 collective-permute-done.refs_6_
  124.3 0.0 copy-start.13
  124.4 0.0 collective-permute-done.1.refs_7_
  124.4 0.0 copy-start.14
  124.4 0.0 collective-permute-done.2.refs_8_
  124.4 0.0 copy-start.15
  124.4 0.0 collective-permute-done.3.refs_9_
  124.4 0.0 copy-start.16
  124.4 0.6 copy-done.13
  125.0 0.1 copy-done.14
  125.1 0.1 copy-done.15
  125.2 0.1 copy-done.16
  125.2 85.6 %shard_map.275 = (bf16[2,128,768]{2,1,0:T(8,128)(2,1)}, bf16[2,128,768]{2,1,0:T(8,128)(2,1)}, bf16[2,128,768]{2,1,0:T(8,128)(2,1)}, bf16[2,128,768]{2,1,0:T(8,12...) custom-call(bf16[8,128,768]{2,1,0:T(8,128)(2,1)} %get-tuple-element., ...), custom_call_target="tpu_custom_call" | custom-call | flops 28991029248 | bytes 25165824 | tf_op jit(solution)/shard_map/pallas_call | solution.py:50
  210.9 28.3 %shard_map.276 = (f32[512,768]{1,0:T(8,128)}, f32[31,768]{1,0:T(8,128)}, bf16[4,512,768]{2,1,0:T(8,128)(2,1)}) custom-call(f32[512,768]{1,0:T(8,128)} %get-tuple-element.93.refs_0_, f32[512,768]{1,0:T(8,128)} %get-tuple-element.94.refs_1_, bf16[512,768]{1,0:T(8,128)(2,1)} %bitcast.29, f32[512,12]{1,0:T(8,128)} %get-tuple-element.95.refs_3_, ...), custom_call_target="tpu_custom_call" | custom-call | flops 1409286144 | bytes 9437184 | tf_op jit(solution)/shard_map/pallas_call | solution.py:50
  239.2 1.0 collective-permute-start.7
  240.3 0.2 collective-permute-start.4
  240.4 1.8 collective-permute-start.5
  242.3 2.4 collective-permute-start.6
  244.7 34.7 %shard_map.277 = (bf16[2048,576]{1,0:T(8,128)(2,1)}, bf16[192,768]{1,0:T(8,128)(2,1)}) custom-call(s32[22]{0:T(128)} %concatenate.3.meta_ref, bf16[3,2048,64]{2,1,0:T(8,128)(2,1)} %get-tuple-element.77.q_ref, bf16[3,2048,64]{2,1,0:T(8,128)(2,1)} %get-tuple-element.78.k_ref, bf16[3,2048,64]{2,1,0:T(8,128)(2,1)} %get-tuple-element.79.v_ref, ...), custom_call_target="tpu_custom_call" | custom-call | flops 8053063680 | bytes 9437184 | tf_op jit(solution)/shard_map/pallas_call | solution.py:50
  279.3 0.0 collective-permute-done.4.refs_12_
  279.3 0.0 copy-start.12
  279.4 0.0 collective-permute-done.5.refs_13_
  279.4 0.0 collective-permute-done.6.refs_14_
  279.4 0.7 copy-done.12
  280.1 70.8 %shard_map.278 = (f32[512,768]{1,0:T(8,128)}, bf16[2,4,8,48,576]{4,3,2,1,0:T(8,128)(2,1)}, bf16[4,8,24,768]{3,2,1,0:T(8,128)(2,1)}, f32[31,768]{1,0:T(8,128)}, f...) custom-call(bf16[2048,576]{1,0:T(8,128)(2,1)} %get-tuple-element.106.refs_0_, ...), custom_call_target="tpu_custom_call" | custom-call | flops 7247757312 | bytes 20971520 | tf_op jit(solution)/shard_map/pallas_call | solution.py:50
  350.9 0.0 collective-permute-done.7.refs_2_.refs_6_.refs_10_
  350.9 0.4 collective-permute-start.8
  351.3 10.9 %shard_map.279 = (f32[3,768,768]{2,1,0:T(8,128)}, f32[4,192,768]{2,1,0:T(8,128)}, f32[2,768,768]{2,1,0:T(8,128)}, f32[12,768]{1,0:T(8,128)}, f32[768]{0:T(1024)}...) custom-call(s32[22]{0:T(128)} %concatenate.3.meta_ref, ...), custom_call_target="tpu_custom_call" | custom-call | bytes 21233664 | tf_op jit(solution)/shard_map/pallas_call | solution.py:50
  362.2 0.0 collective-permute-done.8.refs_3_.refs_7_.refs_11_
  362.2 0.0 copy-start.1
  362.3 1.4 copy-done.1
  363.7 14.1 %shard_map.280 = (f32[2,768,1024]{2,1,0:T(8,128)}, f32[2,768,1024]{2,1,0:T(8,128)}, f32[2,1024,768]{2,1,0:T(8,128)}) custom-call(s32[22]{0:T(128)} %concatenate.3.meta_ref, bf16[3,384,1024]{2,1,0:T(8,128)(2,1)} %get-tuple-element.121.refs_0_.refs_4_.refs_8_, bf16[3,384,1024]{2,1,0:T(8,128)(2,1)} %get-tuple-element.134.refs_1_.refs_5_.refs_9_, ...), custom_call_target="tpu_custom_call" | custom-call | bytes 28311552 | tf_op jit(solution)/shard_map/pallas_call | solution.py:50
  377.8 0.9 copy.37
  378.7 0.8 copy-done.2
  379.5 1.1 copy.38
  380.6 0.6 copy.39
  (21 shorter events, 0.1 us)
Async XLA Ops:
  0.6 38.2 %copy-start.7 = (s32[1,8]{1,0:T(1,128)S(1)}, s32[1,8]{1,0:T(1,128)}, u32[]{:S(2)}) copy-start(s32[1,8]{1,0:T(1,128)} %param.19) | copy-start | bytes 100
  0.7 38.4 %copy-start.8 = (s32[1,2]{1,0:T(1,128)S(1)}, s32[1,2]{1,0:T(1,128)}, u32[]{:S(2)}) copy-start(s32[1,2]{1,0:T(1,128)} %param.18) | copy-start | bytes 28
  32.0 92.3 %collective-permute-start = (bf16[128,768]{1,0:T(8,128)(2,1)}, bf16[128,768]{1,0:T(8,128)(2,1)S(1)}, u32[]{:S(2)}, u32[]{:S(2)}) collective-permute-start(bf16[128,768]{1,0:T(8,128)(2,1)} %get-tuple-element.88), channel_id=1, source_target_pairs={{0,8},{1,9},{2,10},{3,11},{4,12},{5,13},{6,14},{7,15},{8,0},{9,1},... | collective-permute-start | bytes 589832 | tf_op jit(solution)/shard_map/ppermute | solution.py:101
  32.6 91.7 %collective-permute-start.1 = (bf16[128,768]{1,0:T(8,128)(2,1)}, bf16[128,768]{1,0:T(8,128)(2,1)S(1)}, u32[]{:S(2)}, u32[]{:S(2)}) collective-permute-start(bf16[128,768]{1,0:T(8,128)(2,1)} %get-tuple-element.89), channel_id=1, source_target_pairs={{0,9},{1,8},{2,11},{3,10},{4,13},{5,12},{6,15},{7,14},{8,1},{9,0},... | collective-permute-start | bytes 589832 | tf_op jit(solution)/shard_map/ppermute | solution.py:101
  34.1 90.2 %collective-permute-start.2 = (bf16[128,768]{1,0:T(8,128)(2,1)}, bf16[128,768]{1,0:T(8,128)(2,1)S(1)}, u32[]{:S(2)}, u32[]{:S(2)}) collective-permute-start(bf16[128,768]{1,0:T(8,128)(2,1)} %get-tuple-element.90), channel_id=1, source_target_pairs={{0,10},{1,11},{2,8},{3,9},{4,14},{5,15},{6,12},{7,13},{8,2},{9,3},... | collective-permute-start | bytes 589832 | tf_op jit(solution)/shard_map/ppermute | solution.py:101
  35.6 88.8 %collective-permute-start.3 = (bf16[128,768]{1,0:T(8,128)(2,1)}, bf16[128,768]{1,0:T(8,128)(2,1)S(1)}, u32[]{:S(2)}, u32[]{:S(2)}) collective-permute-start(bf16[128,768]{1,0:T(8,128)(2,1)} %get-tuple-element.91), channel_id=1, source_target_pairs={{0,11},{1,10},{2,9},{3,8},{4,15},{5,14},{6,13},{7,12},{8,3},{9,2},... | collective-permute-start | bytes 589832 | tf_op jit(solution)/shard_map/ppermute | solution.py:101
  39.7 26.8 %copy-start.4 = (f32[1,512,12]{1,0,2:T(1,128)S(1)}, f32[1,512,12]{1,0,2:T(1,128)}, u32[]{:S(2)}) copy-start(f32[1,512,12]{1,0,2:T(1,128)} %param.21) | copy-start | bytes 73732
  39.7 27.4 %copy-start.5 = (f32[2,768,2]{1,2,0:T(2,128)S(1)}, f32[2,768,2]{1,2,0:T(2,128)}, u32[]{:S(2)}) copy-start(f32[2,768,2]{1,2,0:T(2,128)} %param.28) | copy-start | bytes 36868
  124.3 0.7 copy-start.13
  124.4 0.7 copy-start.14
  124.4 0.8 copy-start.15
  124.4 0.8 copy-start.16
  210.9 28.4 %copy-start = (bf16[3,384,1024]{2,1,0:T(8,128)(2,1)S(1)}, bf16[3,384,1024]{2,1,0:T(8,128)(2,1)}, u32[]{:S(2)}) copy-start(bf16[3,384,1024]{2,1,0:T(8,128)(2,1)} %get-tuple-element.121.refs_0_.refs_4_.refs_8_) | copy-start | bytes 7077892
  210.9 29.4 %copy-start.11 = (bf16[2,128,768]{2,1,0:T(8,128)(2,1)S(1)}, bf16[2,128,768]{2,1,0:T(8,128)(2,1)}, u32[]{:S(2)}) copy-start(bf16[2,128,768]{2,1,0:T(8,128)(2,1)} %get-tuple-element.115) | copy-start | bytes 1179652
  210.9 29.6 %copy-start.10 = (bf16[2,128,768]{2,1,0:T(8,128)(2,1)S(1)}, bf16[2,128,768]{2,1,0:T(8,128)(2,1)}, u32[]{:S(2)}) copy-start(bf16[2,128,768]{2,1,0:T(8,128)(2,1)} %get-tuple-element.116) | copy-start | bytes 1179652
  210.9 31.4 %copy-start.9 = (bf16[2,128,768]{2,1,0:T(8,128)(2,1)S(1)}, bf16[2,128,768]{2,1,0:T(8,128)(2,1)}, u32[]{:S(2)}) copy-start(bf16[2,128,768]{2,1,0:T(8,128)(2,1)} %get-tuple-element.117) | copy-start | bytes 1179652
  239.2 111.6 %collective-permute-start.7 = (bf16[3,384,1024]{2,1,0:T(8,128)(2,1)S(1)}, bf16[3,384,1024]{2,1,0:T(8,128)(2,1)}, u32[]{:S(2)}, u32[]{:S(2)}) collective-permute-start(bf16[3,384,1024]{2,1,0:T(8,128)(2,1)S(1)} %copy-done), channel_id=1, source_target_pairs={{0,8},{4,12},{8,0},{12,4},{1,9},{5,13},{9,1},{13,5},{2,10},{6,14},... | collective-permute-start | bytes 7077896 | tf_op jit(solution)/shard_map/ppermute | solution.py:73
  240.3 39.1 %collective-permute-start.4 = (bf16[2,128,768]{2,1,0:T(8,128)(2,1)S(1)}, bf16[2,128,768]{2,1,0:T(8,128)(2,1)S(1)}, u32[]{:S(2)}, u32[]{:S(2)}) collective-permute-start(bf16[2,128,768]{2,1,0:T(8,128)(2,1)S(1)} %copy-done.11), channel_id=1, source_target_pairs={{0,1},{1,0},{2,3},{3,2},{4,5},{5,4},{6,7},{7,6},{8,9},{9,8},{10,11... | collective-permute-start | bytes 1179656 | tf_op jit(solution)/shard_map/ppermute | solution.py:73
  240.4 38.9 %collective-permute-start.5 = (bf16[2,128,768]{2,1,0:T(8,128)(2,1)S(1)}, bf16[2,128,768]{2,1,0:T(8,128)(2,1)}, u32[]{:S(2)}, u32[]{:S(2)}) collective-permute-start(bf16[2,128,768]{2,1,0:T(8,128)(2,1)S(1)} %copy-done.10), channel_id=1, source_target_pairs={{0,2},{1,3},{2,0},{3,1},{4,6},{5,7},{6,4},{7,5},{8,10},{9,11},{10,... | collective-permute-start | bytes 1179656 | tf_op jit(solution)/shard_map/ppermute | solution.py:73
  242.3 37.1 %collective-permute-start.6 = (bf16[2,128,768]{2,1,0:T(8,128)(2,1)S(1)}, bf16[2,128,768]{2,1,0:T(8,128)(2,1)}, u32[]{:S(2)}, u32[]{:S(2)}) collective-permute-start(bf16[2,128,768]{2,1,0:T(8,128)(2,1)S(1)} %copy-done.9), channel_id=1, source_target_pairs={{0,3},{1,2},{2,1},{3,0},{4,7},{5,6},{6,5},{7,4},{8,11},{9,10},{10,... | collective-permute-start | bytes 1179656 | tf_op jit(solution)/shard_map/ppermute | solution.py:73
  279.3 0.7 copy-start.12
  350.9 11.4 %collective-permute-start.8 = (bf16[3,384,1024]{2,1,0:T(8,128)(2,1)}, bf16[3,384,1024]{2,1,0:T(8,128)(2,1)S(1)}, u32[]{:S(2)}, u32[]{:S(2)}) collective-permute-start(bf16[3,384,1024]{2,1,0:T(8,128)(2,1)} %collective-permute-done.7.refs_2_.refs_6_.refs_10_), channel_id=1, source_target_pairs={{0,4},{4,0},{8,12},{12,8},{1,5},{5,1},{9,13},{13,9},{2,6},{6,2},{1... | collective-permute-start | bytes 7077896 | tf_op jit(solution)/shard_map/ppermute | solution.py:73
  362.2 1.4 copy-start.1
  363.7 14.1 %copy-start.3 = (bf16[512,768]{1,0:T(8,128)(2,1)S(1)}, bf16[512,768]{1,0:T(8,128)(2,1)}, u32[]{:S(2)}) copy-start(bf16[512,768]{1,0:T(8,128)(2,1)} %get-tuple-element.118) | copy-start | bytes 2359300
  377.8 1.7 copy-start.2
  377.8 2.8 copy-start.6

commit v6 on v5

--- a/solution.py
+++ b/solution.py
@@ -59,7 +59,7 @@
         ),
         compiler_params=pltpu.CompilerParams(
             dimension_semantics=("arbitrary",) * len(grid),
-            vmem_limit_bytes=60 * 1024 * 1024,
+            vmem_limit_bytes=63 * 1024 * 1024,
             collective_id=talks,
             has_side_effects=talks is not None,
         ),
@@ -158,14 +158,25 @@
         own.start()
         weights.start()
 
-        def across():
-            return remote(x_hbm, x_near.at[2], x_s.at[2], x_r.at[2], {"ctx": flip(me, 2)})
+        def some(t):
+            return pl.ds(pl.multiple_of(t * tile, tile), tile)
+
+        def across(t):
+            n = 2 + t
+            return remote(
+                x_hbm.at[some(t), :], x_near.at[2, some(t), :], x_s.at[n], x_r.at[n],
+                {"ctx": flip(me, 2)},
+            )
 
         def beside():
             return remote(x_hbm, x_near.at[1], x_s.at[1], x_r.at[1], {"ctx": flip(me, 1)})
 
-        def passed():
-            return remote(x_near.at[2], x_near.at[3], x_s.at[3], x_r.at[3], {"ctx": flip(me, 1)})
+        def passed(t):
+            n = 2 + per_member + t
+            return remote(
+                x_near.at[2, some(t), :], x_near.at[3, some(t), :], x_s.at[n], x_r.at[n],
+                {"ctx": flip(me, 1)},
+            )
 
         def row_copy(g):
             return remote(
@@ -174,7 +185,8 @@
             )
 
         ready()
-        across().start()
+        for t in range(per_member):
+            across(t).start()
         beside().start()
 
         lines = jnp.concatenate([route_ref[...].astype(f32), jnp.zeros((6, rows), f32)], axis=0)
@@ -232,6 +244,11 @@
 
         def chunk(j):
             def project(t, _):
+                if j == 2:
+                    across(t).wait()
+                    passed(t).start()
+                if j == 3:
+                    passed(t).wait()
                 at = pl.multiple_of(t * tile, tile)
                 to = pl.ds(pl.multiple_of(j * rows + t * tile, tile), tile)
                 value = x_near[j, pl.ds(at, tile), :].astype(f32)
@@ -268,10 +285,7 @@
         chunk(0)
         beside().wait()
         chunk(1)
-        across().wait()
-        passed().start()
         chunk(2)
-        passed().wait()
         chunk(3)
         for g in range(1, groups):
             row_copy(g).wait()
@@ -308,8 +322,8 @@
             pltpu.VMEM(by_column, bf16), pltpu.VMEM(by_column, bf16),
             pltpu.VMEM((group_rows, width), bf16),
             pltpu.VMEM(slots, bf16), pltpu.VMEM(slots, bf16),
-            dma((3,)), dma((members,)), dma((members,)), dma((places,)), dma((places,)),
-            dma((6 * members,)), dma((places + 1,)),
+            dma((3,)), dma((2 + 2 * per_member,)), dma((2 + 2 * per_member,)),
+            dma((places,)), dma((places,)), dma((6 * members,)), dma((places + 1,)),
         ],
         flops=2 * group_rows * width * columns * 5,
         moved=20 * 1024 * 1024,
@@ -611,11 +625,13 @@
         peers += [slot_peer(r, local, exp_now, me) for r in range(local, places)]
         ready = greet(peers)
 
-        def o_copy(j):
-            src = o_hbm.at[pl.ds(j * rows, rows), :]
-            if j == 0:
-                return pltpu.make_async_copy(src, o_near.at[0], o_r.at[0])
-            return remote(src, o_near.at[j], o_s.at[j], o_r.at[j], {"ctx": flip(me, j)})
+        own_o = pltpu.make_async_copy(o_hbm.at[pl.ds(0, rows), :], o_near.at[0], o_r.at[0])
+
+        def o_copy(j, t):
+            src = o_hbm.at[pl.ds(pl.multiple_of(j * rows + t * tile, tile), tile), :]
+            dst = o_near.at[j, pl.ds(pl.multiple_of(t * tile, tile), tile), :]
+            n = j * (rows // tile) + t
+            return remote(src, dst, o_s.at[n], o_r.at[n], {"ctx": flip(me, j)})
 
         def row_copy(r):
             return remote(
@@ -628,17 +644,19 @@
                 slot_peer(r, local, exp_now, me),
             )
 
-        o_copy(0).start()
+        own_o.start()
         ready()
-        for j in range(1, members):
-            o_copy(j).start()
-        for j in range(members):
-            o_copy(j).wait()
+        for t in range(rows // tile):
+            for j in range(members - 1, 0, -1):
+                o_copy(j, t).start()
+        own_o.wait()
 
         def front_rows(t, _):
             here = pl.ds(pl.multiple_of(t * tile, tile), tile)
-            total = x_ref[here, :].astype(f32)
-            for j in range(members):
+            total = x_ref[here, :].astype(f32) + mm(o_near[0, here, :], w_ref[me])
+            for j in range(1, members):
+                o_copy(j, t).wait()
+            for j in range(1, members):
                 total = total + mm(o_near[j, here, :], w_ref[flip(me, j)])
             x1_ref[here, :] = total
             inverse = lax.rsqrt(jnp.mean(total * total, axis=1, keepdims=True) + norm_eps)
@@ -772,7 +790,7 @@
             pltpu.VMEM((places, CAP, width), bf16),
             pltpu.VMEM((places, 1, CAP), f32),
             pltpu.VMEM((places, 1, CAP), f32),
-            dma((members,)), dma((members,)),
+            dma((members * (rows // tile),)), dma((members * (rows // tile),)),
             dma((places,)), dma((places,)), dma((places,)), dma((places,)),
             dma((2 * places,)),
         ],
@@ -795,6 +813,8 @@
     steps = hidden // tile
     tiles = per_part // tile
     away = steps - tiles
+    lead = away // 2
+    kept = steps - lead
     chunk = 256
 
     def body(*refs):
@@ -803,16 +823,20 @@
         dy_parts = [
             dy_late[r // local] if r % local else dy_ref.at[r // local] for r in range(places)
         ]
-        y_out, refs = refs[6 : 6 + groups], refs[:6] + refs[6 + groups :]
-        dx_out, dots_out, sum_out, beside_out = refs[6:10]
-        refs = refs[:6] + (None,) + refs[6:]
-        x_all, xt_all, dy_all, dyt_all, gate_all, y_acc, dx_acc, dot_acc = refs[11:19]
-        hid_t, dgt, dut, scaled_t, wg_buf, wu_buf, wd_buf = refs[19:26]
-        hid_own, dg_own, du_own, scaled_own, wg_own, wu_own, wd_own = refs[26:33]
-        send, total, taken, far, dx_low, dx_near, dots, dots_near = refs[33:41]
-        beside, y_odd, relay = refs[41:44]
-        w_sem, own_sem, c_s, c_r, f_s, f_r, b_s, b_r, d_s, d_r, out_sem = refs[44:55]
-        e_s, e_r, beside_sem, y_s, y_r = refs[55:]
+        y_out, refs = refs[6 : 6 + groups], refs[6 + groups :]
+        it = iter(refs)
+
+        def take(count):
+            return [next(it) for _ in range(count)]
+
+        dx_out, dots_out, sum_out, beside_out = take(4)
+        x_all, xt_all, dy_all, dyt_all, gate_all, y_acc, dx_acc, dot_acc = take(8)
+        wg_buf, wu_buf, wd_buf, wg_keep, wu_keep, wd_keep = take(6)
+        hid_keep, dg_keep, du_keep, scaled_keep = take(4)
+        send, total, taken, far, dx_low, dx_near, dots, dots_near = take(8)
+        beside, y_odd, relay = take(3)
+        in_sem, w_sem, keep_sem, c_s, c_r, f_s, f_r, b_s, b_r, d_s, d_r, out_sem = take(12)
+        e_s, e_r, beside_sem, y_s, y_r, dx_sem = take(6)
         me, exp_now, dp_now = lax.axis_index("ctx"), lax.axis_index("exp"), lax.axis_index("dp")
         core, side = lax.rem(me, 2), lax.div(me, 2)
         sibling = {"ctx": flip(me, 1)}
@@ -865,29 +889,47 @@
                 slot_peer(r, local, exp_now, me),
             )
 
-        def own_weights():
-            at = pl.ds(pl.multiple_of(dp_now * per_part, per_part), per_part)
+        def keep_weights(k):
+            f = lead + k
+            at = pl.multiple_of(dp_of(f) * per_part + (f % tiles) * tile, tile)
             return [
-                pltpu.make_async_copy(wg_hbm.at[side, :, at], wg_own, own_sem.at[0]),
-                pltpu.make_async_copy(wu_hbm.at[side, :, at], wu_own, own_sem.at[1]),
-                pltpu.make_async_copy(wd_hbm.at[side, at, :], wd_own, own_sem.at[2]),
+                pltpu.make_async_copy(
+                    wg_hbm.at[side, :, pl.ds(at, tile)], wg_keep.at[k], keep_sem.at[0, k]
+                ),
+                pltpu.make_async_copy(
+                    wu_hbm.at[side, :, pl.ds(at, tile)], wu_keep.at[k], keep_sem.at[1, k]
+                ),
+                pltpu.make_async_copy(
+                    wd_hbm.at[side, pl.ds(at, tile), :], wd_keep.at[k], keep_sem.at[2, k]
+                ),
             ]
 
-        if away:
+        def rows_in(r):
+            here = pl.ds(r * CAP, CAP)
+            return [
+                pltpu.make_async_copy(x_ref.at[r], x_all.at[here, :], in_sem.at[r]),
+                pltpu.make_async_copy(dy_parts[r], dy_all.at[here, :], in_sem.at[places + r]),
+            ]
+
+        for r in range(places):
+            for copy in rows_in(r):
+                copy.start()
+        if lead:
             for copy in weights(0, 0):
                 copy.start()
-        for copy in own_weights():
-            copy.start()
+        for k in range(kept):
+            for copy in keep_weights(k):
+                copy.start()
         first_half = pl.ds(pl.multiple_of((1 - core) * half, half), half)
         second_half = pl.ds(pl.multiple_of(core * half, half), half)
         for r in range(places):
             here = slice(r * CAP, (r + 1) * CAP)
-            x_all[here, :] = x_ref[r]
-            turned = jnp.transpose(x_ref[r])
+            for copy in rows_in(r):
+                copy.wait()
+            turned = jnp.transpose(x_all[here, :])
             xt_all[first_half, here] = turned[:half, :]
             xt_all[second_half, here] = turned[half:, :]
-            dy_all[here, :] = dy_parts[r][...]
-            turned = jnp.transpose(dy_parts[r][...])
+            turned = jnp.transpose(dy_all[here, :])
             dyt_all[first_half, here] = turned[:half, :]
             dyt_all[second_half, here] = turned[half:, :]
             gate_all[here, :] = jnp.sum(
@@ -927,8 +969,8 @@
         def rows_back(here, wg, wu, dg_ref, du_ref):
             dx_acc[here, :] += mm(dg_ref[here, :], wg, NT) + mm(du_ref[here, :], wu, NT)
 
-        def weight_sums(f, slot, hid_ref, dg_ref, du_ref, scaled_ref, wd):
-            @pl.when(f >= 1)
+        def weight_sums(f, slot, dg_ref, du_ref, scaled_ref, first):
+            @pl.when(f > first)
             def _():
                 core_sum(f - 1)
 
@@ -936,64 +978,60 @@
             def _():
                 core_copy(f - 2, slot).wait_send()
 
-            for n, (left, right) in enumerate(((xt_all, dg_ref), (xt_all, du_ref), (dyt_all, scaled_ref))):
+            for n, (left, right) in enumerate(
+                ((xt_all, dg_ref), (xt_all, du_ref), (dyt_all, scaled_ref))
+            ):
                 found = mm(left[...], right[...]).astype(bf16)
                 send[slot, n] = found[:half, :]
                 total[f, n] = found[half:, :]
             core_copy(f, slot).start()
 
-            @pl.when((f >= 1) & (f - 1 < away))
+            @pl.when((f > first) & (f - 1 < away))
             def _():
                 far_copy(f - 1).start()
 
-            y_acc[...] += mm(hid_ref[...], wd)
-
-        def away_step(f, _):
+        def lead_step(f, _):
             slot = lax.rem(f, 2)
             for copy in weights(f, slot):
                 copy.wait()
 
-            @pl.when(f + 1 < away)
+            @pl.when(f + 1 < lead)
             def _():
                 for copy in weights(f + 1, 1 - slot):
                     copy.start()
 
+            hid, dg, du, scaled = (a.at[0] for a in (hid_keep, dg_keep, du_keep, scaled_keep))
+
             def row_chunk(c, _):
                 here = pl.ds(pl.multiple_of(c * chunk, chunk), chunk)
+                forward_back(here, wg_buf[slot], wu_buf[slot], wd_buf[slot], hid, dg, du, scaled)
+                return 0
+
+            lax.fori_loop(0, rows // chunk, row_chunk, 0)
+            weight_sums(f, slot, dg, du, scaled, 0)
+            y_acc[...] += mm(hid[...], wd_buf[slot])
+            rows_back(slice(0, rows), wg_buf[slot], wu_buf[slot], dg, du)
+            return 0
+
+        lax.fori_loop(0, lead, lead_step, 0)
+        if lead:
+            core_sum(lead - 1)
+            far_copy(lead - 1).start()
+        for k in range(kept):
+            for copy in keep_weights(k):
+                copy.wait()
+
+        def keep_rows(k, first, count):
+            size = min(chunk, count)
+            for c in range(count // size):
                 forward_back(
-                    here, wg_buf[slot], wu_buf[slot], wd_buf[slot], hid_t, dgt, dut, scaled_t
+                    slice(first + c * size, first + (c + 1) * size),
+                    wg_keep[k], wu_keep[k], wd_keep[k],
+                    hid_keep.at[k], dg_keep.at[k], du_keep.at[k], scaled_keep.at[k],
                 )
-                return 0
-
-            lax.fori_loop(0, rows // chunk, row_chunk, 0)
-            weight_sums(f, slot, hid_t, dgt, dut, scaled_t, wd_buf[slot])
-            rows_back(slice(0, rows), wg_buf[slot], wu_buf[slot], dgt, dut)
-            return 0
-
-        lax.fori_loop(0, away, away_step, 0)
-        for copy in own_weights():
-            copy.wait()
-        if away:
-            core_sum(away - 1)
-            far_copy(away - 1).start()
-
-        def own_rows(first, count):
-            size = min(chunk, count)
-
-            def own_tile(i, _):
-                at = pl.ds(pl.multiple_of(i * tile, tile), tile)
-                for c in range(count // size):
-                    forward_back(
-                        slice(first + c * size, first + (c + 1) * size),
-                        wg_own[:, at], wu_own[:, at], wd_own[at, :],
-                        hid_own.at[i], dg_own.at[i], du_own.at[i], scaled_own.at[i],
-                    )
-                rows_back(
-                    slice(first, first + count), wg_own[:, at], wu_own[:, at], dg_own.at[i], du_own.at[i]
-                )
-                return 0
-
-            lax.fori_loop(0, tiles, own_tile, 0)
+            rows_back(
+                slice(first, first + count), wg_keep[k], wu_keep[k], dg_keep.at[k], du_keep.at[k]
+            )
 
         def send_back(first, last):
             for r in range(first, last):
@@ -1010,18 +1048,48 @@
             dots_copy(r).start()
 
         middle = places // 2
-        own_rows(middle * CAP, rows - middle * CAP)
+        near_rows = middle * CAP
+
+        def far_step(k, _):
+            keep_rows(k, near_rows, rows - near_rows)
+            return 0
+
+        lax.fori_loop(0, kept, far_step, 0)
         send_back(middle, places)
-        own_rows(0, middle * CAP)
-        send_last(places - 1)
+
+        def away_step(f, _):
+            k = f - lead
+
+            keep_rows(k, 0, near_rows)
+
+            @pl.when(k == 0)
+            def _():
+                send_last(places - 1)
+
+            weight_sums(
+                f, lax.rem(f, 2), dg_keep.at[k], du_keep.at[k], scaled_keep.at[k], lead
+            )
+            return 0
+
+        lax.fori_loop(lead, away, away_step, 0)
+        if away == lead:
+            send_last(places - 1)
+        else:
+            core_sum(away - 1)
+            far_copy(away - 1).start()
+
+        def near_step(k, _):
+            keep_rows(k, 0, near_rows)
+            return 0
+
+        lax.fori_loop(away - lead, kept, near_step, 0)
         send_back(0, middle)
 
-        def own_result(i, _):
-            at = pl.ds(pl.multiple_of(i * tile, tile), tile)
-            y_acc[...] += mm(hid_own[i], wd_own[at, :])
+        def own_result(k, _):
+            y_acc[...] += mm(hid_keep[k], wd_keep[k])
             return 0
 
-        lax.fori_loop(0, tiles, own_result, 0)
+        lax.fori_loop(0, kept, own_result, 0)
         send_last(middle - 1)
 
         def relay_copy(g):
@@ -1039,29 +1107,16 @@
             y_out[g][0] = result(local * g)
         relay_copy(groups - 1).start()
 
-        def own_step(i, _):
-            f = away + i
-
-            @pl.when(i >= 1)
-            def _():
-                core_sum(f - 1)
-
-            slot = lax.rem(f, 2)
-
-            @pl.when(f >= 2)
-            def _():
-                core_copy(f - 2, slot).wait_send()
-
-            dg, du, scaled = dg_own.at[i], du_own.at[i], scaled_own.at[i]
-            for n, (left, right) in enumerate(((xt_all, dg), (xt_all, du), (dyt_all, scaled))):
-                found = mm(left[...], right[...]).astype(bf16)
-                send[slot, n] = found[:half, :]
-                total[f, n] = found[half:, :]
-            core_copy(f, slot).start()
+        def own_step(f, _):
+            k = f - lead
+            weight_sums(
+                f, lax.rem(f, 2), dg_keep.at[k], du_keep.at[k], scaled_keep.at[k], away
+            )
             return 0
 
-        lax.fori_loop(0, tiles, own_step, 0)
+        lax.fori_loop(away, steps, own_step, 0)
         core_sum(steps - 1)
+
         def beside_copy(i):
             return remote(total.at[away + i], beside.at[i], e_s.at[i], e_r.at[i], sibling)
 
@@ -1092,12 +1147,16 @@
         for f in range(max(0, steps - 2), steps):
             core_copy(f, f % 2).wait_send()
 
-        dx_out[0] = dx_low[0]
+        def dx_store(r):
+            src = dx_near.at[r] if r else dx_low.at[0]
+            return pltpu.make_async_copy(src, dx_out.at[r], dx_sem.at[r])
+
         dots_out[0] = dots[0]
+        dx_store(0).start()
         for r in range(1, places):
             back_copy(r).wait()
             dots_copy(r).wait()
-            dx_out[r] = dx_near[r]
+            dx_store(r).start()
             dots_out[r] = dots_near[r]
         for g in range(groups):
             relay_copy(g).wait()
@@ -1108,6 +1167,8 @@
         for i in range(tiles):
             sum_store(i).wait()
             beside_store(i).wait()
+        for r in range(places):
+            dx_store(r).wait()
 
     placed = shape_of((places, CAP, width), bf16)
     pair = shape_of((local, CAP, width), bf16)
@@ -1115,11 +1176,11 @@
     return run(
         body,
         (),
-        [(arrived, vector), (grads, vector), (gates, vector)]
+        [(arrived, anywhere), (grads, anywhere), (gates, vector)]
         + [(w, anywhere) for w in (w_gate, w_up, w_down)]
-        + [(g, vector) for g in late],
+        + [(g, anywhere) for g in late],
         [(pair, vector)] * groups
-        + [(placed, vector), (lines, vector)]
+        + [(placed, anywhere), (lines, vector)]
         + [(shape_of((3, half, per_part), bf16), anywhere)] * 2,
         scratch=[
             pltpu.VMEM((rows, width), bf16),
@@ -1130,20 +1191,16 @@
             pltpu.VMEM((rows, width), f32),
             pltpu.VMEM((rows, width), f32),
             pltpu.VMEM((rows, 128), f32),
-            pltpu.VMEM((rows, tile), bf16),
-            pltpu.VMEM((rows, tile), bf16),
-            pltpu.VMEM((rows, tile), bf16),
-            pltpu.VMEM((rows, tile), bf16),
             pltpu.VMEM((2, width, tile), bf16),
             pltpu.VMEM((2, width, tile), bf16),
             pltpu.VMEM((2, tile, width), bf16),
-            pltpu.VMEM((tiles, rows, tile), bf16),
-            pltpu.VMEM((tiles, rows, tile), bf16),
-            pltpu.VMEM((tiles, rows, tile), bf16),
-            pltpu.VMEM((tiles, rows, tile), bf16),
-            pltpu.VMEM((width, per_part), bf16),
-            pltpu.VMEM((width, per_part), bf16),
-            pltpu.VMEM((per_part, width), bf16),
+            pltpu.VMEM((kept, width, tile), bf16),
+            pltpu.VMEM((kept, width, tile), bf16),
+            pltpu.VMEM((kept, tile, width), bf16),
+            pltpu.VMEM((kept, rows, tile), bf16),
+            pltpu.VMEM((kept, rows, tile), bf16),
+            pltpu.VMEM((kept, rows, tile), bf16),
+            pltpu.VMEM((kept, rows, tile), bf16),
             pltpu.VMEM((2, 3, half, tile), bf16),
             pltpu.VMEM((steps, 3, half, tile), bf16),
             pltpu.VMEM((steps, 3, half, tile), bf16),
@@ -1155,11 +1212,11 @@
             pltpu.VMEM((tiles, 3, half, tile), bf16),
             pltpu.VMEM((groups, CAP, width), bf16),
             pltpu.VMEM((groups, CAP, width), bf16),
-            dma((3, 2)), dma((3,)), dma((2,)), dma((steps,)),
+            dma((2 * places,)), dma((3, 2)), dma((3, kept)), dma((2,)), dma((steps,)),
             dma((max(1, away),)), dma((max(1, away),)),
             dma((places,)), dma((places,)), dma((places,)), dma((places,)),
             dma((tiles,)), dma((tiles,)), dma((tiles,)), dma((tiles,)),
-            dma((groups,)), dma((groups,)),
+            dma((groups,)), dma((groups,)), dma((places,)),
         ],
         flops=9 * 2 * rows * width * hidden,
         moved=12 * width * hidden + rows * width * 8,

time: 386 us -> 375 us (0.972)
  Pallas kernels: 359 us -> 351 us
    pallas_call x9, Pallas kernels: 359 us -> 351 us  [run(): pl.pallas_call(body, out_shape=[o for o, _ in outputs], grid_spec=pltpu.P...]
  transfers between devices with their start and end apart: 9 -> 9, of which waited for: 0 -> 0; matrix products, arithmetic and copies ran while one was open for 1% -> 1% of each run, Pallas kernels for 52% -> 53%
where the time goes in v6:
time: 375 us; the launch traced here: 371 us
  Pallas kernels  351 us (94%)
  starting transfers between devices  12.9 us (3%)
  local copies, waits for them, and re-layouts  6.07 us (2%)
    pallas_call x9, Pallas kernels, run(): pl.pallas_call(body, out_shape=[o for o, _ in outputs], grid_spec=pltpu.P...  351 us
  transfers between devices with their start and end apart: 9, of which 0 were waited for; matrix products, arithmetic and copies ran while one was open for 1% of the time, Pallas kernels for 53%

profile of v6, /device:TPU:0, one launch (start us, length us, event | category | flops | bytes accessed | tf_op | source)
XLA Modules:
  0.0 371.5 jit_solution(4693511214673263689)
XLA Ops:
  0.6 0.0 copy-start.5
  0.7 30.3 %shard_map.272 = (bf16[3,2048,64]{2,1,0:T(8,128)(2,1)}, bf16[3,2048,64]{2,1,0:T(8,128)(2,1)}, bf16[3,2048,64]{2,1,0:T(8,128)(2,1)}, bf16[192,2048]{1,0:T(8,128)(...) custom-call(bf16[512,768]{1,0:T(8,128)(2,1)} %bitcast.41, ...), custom_call_target="tpu_custom_call" | custom-call | flops 3019898880 | bytes 20971520 | tf_op jit(solution)/shard_map/pallas_call | solution.py:50
  31.0 0.6 collective-permute-start
  31.6 1.5 collective-permute-start.1
  33.1 1.5 collective-permute-start.2
  34.5 3.3 collective-permute-start.3
  37.8 0.1 select_reduce_fusion
  38.0 0.6 concatenate.3.meta_ref
  38.6 26.8 %shard_map.273 = (bf16[2048,192]{1,0:T(8,128)(2,1)}, f32[192,2048]{1,0:T(8,128)}, f32[3,2048]{1,0:T(4,128)}, f32[3,256]{1,0:T(4,128)}) custom-call(s32[22]{0:T(128)} %concatenate.3.meta_ref, bf16[3,2048,64]{2,1,0:T(8,128)(2,1)} %get-tuple-element.77.q_ref, bf16[3,2048,64]{2,1,0:T(8,128)(2,1)} %get-tuple-element.78.k_ref, ...), custom_call_target="tpu_custom_call" | custom-call | flops 3221225472 | bytes 5505024 | tf_op jit(solution)/shard_map/pallas_call | solution.py:50
  65.3 0.6 copy.33
  65.9 0.6 reshape.41.refs_10_
  66.6 52.5 %shard_map.274 = (f32[512,768]{1,0:T(8,128)}, f32[512,768]{1,0:T(8,128)}, f32[512,12]{1,0:T(8,128)}, bf16[8,128,768]{2,1,0:T(8,128)(2,1)}, f32[8,1,128]{2,1,0:T(...) custom-call(bf16[512,768]{1,0:T(8,128)(2,1)} %bitcast.42, ...), custom_call_target="tpu_custom_call" | custom-call | flops 1409286144 | bytes 11796480 | tf_op jit(solution)/shard_map/pallas_call | solution.py:50
  119.1 0.0 collective-permute-done.refs_6_
  119.1 0.0 copy-start.9
  119.1 0.0 collective-permute-done.1.refs_7_
  119.1 0.0 copy-start.10
  119.1 0.0 collective-permute-done.2.refs_8_
  119.2 0.0 copy-start.11
  119.2 0.0 collective-permute-done.3.refs_9_
  119.2 0.0 copy-start.12
  119.2 0.6 copy-done.9
  119.8 0.1 copy-done.10
  119.9 0.1 copy-done.11
  119.9 0.1 copy-done.12
  120.0 82.2 %shard_map.275 = (bf16[2,128,768]{2,1,0:T(8,128)(2,1)}, bf16[2,128,768]{2,1,0:T(8,128)(2,1)}, bf16[2,128,768]{2,1,0:T(8,128)(2,1)}, bf16[2,128,768]{2,1,0:T(8,12...) custom-call(bf16[8,128,768]{2,1,0:T(8,128)(2,1)} %get-tuple-element., ...), custom_call_target="tpu_custom_call" | custom-call | flops 28991029248 | bytes 25165824 | tf_op jit(solution)/shard_map/pallas_call | solution.py:50
  202.2 28.5 %shard_map.276 = (f32[512,768]{1,0:T(8,128)}, f32[31,768]{1,0:T(8,128)}, bf16[4,512,768]{2,1,0:T(8,128)(2,1)}) custom-call(f32[512,768]{1,0:T(8,128)} %get-tuple-element.93.refs_0_, f32[512,768]{1,0:T(8,128)} %get-tuple-element.94.refs_1_, bf16[512,768]{1,0:T(8,128)(2,1)} %bitcast.29, f32[512,12]{1,0:T(8,128)} %get-tuple-element.95.refs_3_, ...), custom_call_target="tpu_custom_call" | custom-call | flops 1409286144 | bytes 9437184 | tf_op jit(solution)/shard_map/pallas_call | solution.py:50
  230.7 1.2 collective-permute-start.7
  231.9 0.0 collective-permute-start.4
  232.0 0.0 copy-done.8
  232.0 2.2 collective-permute-start.5
  234.1 2.2 collective-permute-start.6
  236.3 34.5 %shard_map.277 = (bf16[2048,576]{1,0:T(8,128)(2,1)}, bf16[192,768]{1,0:T(8,128)(2,1)}) custom-call(s32[22]{0:T(128)} %concatenate.3.meta_ref, bf16[3,2048,64]{2,1,0:T(8,128)(2,1)} %get-tuple-element.77.q_ref, bf16[3,2048,64]{2,1,0:T(8,128)(2,1)} %get-tuple-element.78.k_ref, bf16[3,2048,64]{2,1,0:T(8,128)(2,1)} %get-tuple-element.79.v_ref, ...), custom_call_target="tpu_custom_call" | custom-call | flops 8053063680 | bytes 9437184 | tf_op jit(solution)/shard_map/pallas_call | solution.py:50
  270.8 0.0 collective-permute-done.4.refs_12_
  270.8 0.0 collective-permute-done.5.refs_13_
  270.8 0.0 collective-permute-done.6.refs_14_
  270.8 71.5 %shard_map.278 = (f32[512,768]{1,0:T(8,128)}, bf16[2,4,8,48,576]{4,3,2,1,0:T(8,128)(2,1)}, bf16[4,8,24,768]{3,2,1,0:T(8,128)(2,1)}, f32[31,768]{1,0:T(8,128)}, f...) custom-call(bf16[2048,576]{1,0:T(8,128)(2,1)} %get-tuple-element.106.refs_0_, ...), custom_call_target="tpu_custom_call" | custom-call | flops 7247757312 | bytes 20971520 | tf_op jit(solution)/shard_map/pallas_call | solution.py:50
  342.3 0.0 collective-permute-done.7.refs_2_.refs_6_.refs_10_
  342.4 0.4 collective-permute-start.8
  342.8 10.9 %shard_map.279 = (f32[3,768,768]{2,1,0:T(8,128)}, f32[4,192,768]{2,1,0:T(8,128)}, f32[2,768,768]{2,1,0:T(8,128)}, f32[12,768]{1,0:T(8,128)}, f32[768]{0:T(1024)}...) custom-call(s32[22]{0:T(128)} %concatenate.3.meta_ref, ...), custom_call_target="tpu_custom_call" | custom-call | bytes 21233664 | tf_op jit(solution)/shard_map/pallas_call | solution.py:50
  353.7 0.0 collective-permute-done.8.refs_3_.refs_7_.refs_11_
  353.7 14.1 %shard_map.280 = (f32[2,768,1024]{2,1,0:T(8,128)}, f32[2,768,1024]{2,1,0:T(8,128)}, f32[2,1024,768]{2,1,0:T(8,128)}) custom-call(s32[22]{0:T(128)} %concatenate.3.meta_ref, bf16[3,384,1024]{2,1,0:T(8,128)(2,1)} %get-tuple-element.121.refs_0_.refs_4_.refs_8_, bf16[3,384,1024]{2,1,0:T(8,128)(2,1)} %get-tuple-element.134.refs_1_.refs_5_.refs_9_, ...), custom_call_target="tpu_custom_call" | custom-call | bytes 28311552 | tf_op jit(solution)/shard_map/pallas_call | solution.py:50
  367.9 0.0 copy-start
  367.9 0.0 copy-done.1
  367.9 0.0 copy-start.4
  367.9 0.9 copy.37
  368.8 0.8 copy-done
  369.6 1.1 copy.38
  370.7 0.6 copy.39
  (13 shorter events, 0.0 us)
Async XLA Ops:
  0.6 37.2 %copy-start.5 = (s32[1,8]{1,0:T(1,128)S(1)}, s32[1,8]{1,0:T(1,128)}, u32[]{:S(2)}) copy-start(s32[1,8]{1,0:T(1,128)} %param.19) | copy-start | bytes 100
  0.7 37.3 %copy-start.6 = (s32[1,2]{1,0:T(1,128)S(1)}, s32[1,2]{1,0:T(1,128)}, u32[]{:S(2)}) copy-start(s32[1,2]{1,0:T(1,128)} %param.18) | copy-start | bytes 28
  31.0 88.1 %collective-permute-start = (bf16[128,768]{1,0:T(8,128)(2,1)}, bf16[128,768]{1,0:T(8,128)(2,1)S(1)}, u32[]{:S(2)}, u32[]{:S(2)}) collective-permute-start(bf16[128,768]{1,0:T(8,128)(2,1)} %get-tuple-element.88), channel_id=1, source_target_pairs={{0,8},{1,9},{2,10},{3,11},{4,12},{5,13},{6,14},{7,15},{8,0},{9,1},... | collective-permute-start | bytes 589832 | tf_op jit(solution)/shard_map/ppermute | solution.py:101
  31.6 87.6 %collective-permute-start.1 = (bf16[128,768]{1,0:T(8,128)(2,1)}, bf16[128,768]{1,0:T(8,128)(2,1)S(1)}, u32[]{:S(2)}, u32[]{:S(2)}) collective-permute-start(bf16[128,768]{1,0:T(8,128)(2,1)} %get-tuple-element.89), channel_id=1, source_target_pairs={{0,9},{1,8},{2,11},{3,10},{4,13},{5,12},{6,15},{7,14},{8,1},{9,0},... | collective-permute-start | bytes 589832 | tf_op jit(solution)/shard_map/ppermute | solution.py:101
  33.1 86.1 %collective-permute-start.2 = (bf16[128,768]{1,0:T(8,128)(2,1)}, bf16[128,768]{1,0:T(8,128)(2,1)S(1)}, u32[]{:S(2)}, u32[]{:S(2)}) collective-permute-start(bf16[128,768]{1,0:T(8,128)(2,1)} %get-tuple-element.90), channel_id=1, source_target_pairs={{0,10},{1,11},{2,8},{3,9},{4,14},{5,15},{6,12},{7,13},{8,2},{9,3},... | collective-permute-start | bytes 589832 | tf_op jit(solution)/shard_map/ppermute | solution.py:101
  34.5 84.6 %collective-permute-start.3 = (bf16[128,768]{1,0:T(8,128)(2,1)}, bf16[128,768]{1,0:T(8,128)(2,1)S(1)}, u32[]{:S(2)}, u32[]{:S(2)}) collective-permute-start(bf16[128,768]{1,0:T(8,128)(2,1)} %get-tuple-element.91), channel_id=1, source_target_pairs={{0,11},{1,10},{2,9},{3,8},{4,15},{5,14},{6,13},{7,12},{8,3},{9,2},... | collective-permute-start | bytes 589832 | tf_op jit(solution)/shard_map/ppermute | solution.py:101
  38.5 26.8 %copy-start.2 = (f32[1,512,12]{1,0,2:T(1,128)S(1)}, f32[1,512,12]{1,0,2:T(1,128)}, u32[]{:S(2)}) copy-start(f32[1,512,12]{1,0,2:T(1,128)} %param.21) | copy-start | bytes 73732
  38.6 27.4 %copy-start.3 = (f32[2,768,2]{1,2,0:T(2,128)S(1)}, f32[2,768,2]{1,2,0:T(2,128)}, u32[]{:S(2)}) copy-start(f32[2,768,2]{1,2,0:T(2,128)} %param.28) | copy-start | bytes 36868
  119.1 0.7 copy-start.9
  119.1 0.7 copy-start.10
  119.2 0.8 copy-start.11
  119.2 0.8 copy-start.12
  202.2 29.8 %copy-start.8 = (bf16[2,128,768]{2,1,0:T(8,128)(2,1)S(1)}, bf16[2,128,768]{2,1,0:T(8,128)(2,1)}, u32[]{:S(2)}) copy-start(bf16[2,128,768]{2,1,0:T(8,128)(2,1)} %get-tuple-element.116) | copy-start | bytes 1179652
  202.2 32.0 %copy-start.7 = (bf16[2,128,768]{2,1,0:T(8,128)(2,1)S(1)}, bf16[2,128,768]{2,1,0:T(8,128)(2,1)}, u32[]{:S(2)}) copy-start(bf16[2,128,768]{2,1,0:T(8,128)(2,1)} %get-tuple-element.117) | copy-start | bytes 1179652
  230.7 111.6 %collective-permute-start.7 = (bf16[3,384,1024]{2,1,0:T(8,128)(2,1)}, bf16[3,384,1024]{2,1,0:T(8,128)(2,1)}, u32[]{:S(2)}, u32[]{:S(2)}) collective-permute-start(bf16[3,384,1024]{2,1,0:T(8,128)(2,1)} %get-tuple-element.121.refs_0_.refs_4_.refs_8_), channel_id=1, source_target_pairs={{0,8},{4,12},{8,0},{12,4},{1,9},{5,13},{9,1},{13,5},{2,10},{6,14},... | collective-permute-start | bytes 7077896 | tf_op jit(solution)/shard_map/ppermute | solution.py:73
  231.9 38.9 %collective-permute-start.4 = (bf16[2,128,768]{2,1,0:T(8,128)(2,1)}, bf16[2,128,768]{2,1,0:T(8,128)(2,1)}, u32[]{:S(2)}, u32[]{:S(2)}) collective-permute-start(bf16[2,128,768]{2,1,0:T(8,128)(2,1)} %get-tuple-element.115), channel_id=1, source_target_pairs={{0,1},{1,0},{2,3},{3,2},{4,5},{5,4},{6,7},{7,6},{8,9},{9,8},{10,11... | collective-permute-start | bytes 1179656 | tf_op jit(solution)/shard_map/ppermute | solution.py:73
  232.0 38.9 %collective-permute-start.5 = (bf16[2,128,768]{2,1,0:T(8,128)(2,1)S(1)}, bf16[2,128,768]{2,1,0:T(8,128)(2,1)}, u32[]{:S(2)}, u32[]{:S(2)}) collective-permute-start(bf16[2,128,768]{2,1,0:T(8,128)(2,1)S(1)} %copy-done.8), channel_id=1, source_target_pairs={{0,2},{1,3},{2,0},{3,1},{4,6},{5,7},{6,4},{7,5},{8,10},{9,11},{10,... | collective-permute-start | bytes 1179656 | tf_op jit(solution)/shard_map/ppermute | solution.py:73
  234.1 36.7 %collective-permute-start.6 = (bf16[2,128,768]{2,1,0:T(8,128)(2,1)S(1)}, bf16[2,128,768]{2,1,0:T(8,128)(2,1)}, u32[]{:S(2)}, u32[]{:S(2)}) collective-permute-start(bf16[2,128,768]{2,1,0:T(8,128)(2,1)S(1)} %copy-done.7), channel_id=1, source_target_pairs={{0,3},{1,2},{2,1},{3,0},{4,7},{5,6},{6,5},{7,4},{8,11},{9,10},{10,... | collective-permute-start | bytes 1179656 | tf_op jit(solution)/shard_map/ppermute | solution.py:73
  342.4 11.4 %collective-permute-start.8 = (bf16[3,384,1024]{2,1,0:T(8,128)(2,1)}, bf16[3,384,1024]{2,1,0:T(8,128)(2,1)}, u32[]{:S(2)}, u32[]{:S(2)}) collective-permute-start(bf16[3,384,1024]{2,1,0:T(8,128)(2,1)} %collective-permute-done.7.refs_2_.refs_6_.refs_10_), channel_id=1, source_target_pairs={{0,4},{4,0},{8,12},{12,8},{1,5},{5,1},{9,13},{13,9},{2,6},{6,2},{1... | collective-permute-start | bytes 7077896 | tf_op jit(solution)/shard_map/ppermute | solution.py:73
  353.7 14.2 %copy-start.1 = (bf16[512,768]{1,0:T(8,128)(2,1)S(1)}, bf16[512,768]{1,0:T(8,128)(2,1)}, u32[]{:S(2)}) copy-start(bf16[512,768]{1,0:T(8,128)(2,1)} %get-tuple-element.118) | copy-start | bytes 2359300
  367.9 1.7 copy-start
  367.9 2.8 copy-start.4

commit v7 on v6

--- a/solution.py
+++ b/solution.py
@@ -376,20 +376,28 @@
             def step(masked):
                 if masked:
                     allowed = allowed_pairs(meta_ref, q_first, k_first, rows, layout)
+                scores = [mm(k_ref[h, pl.ds(at, rows), :], qt_ref[h]) for h in range(heads)]
+                if masked:
+                    scores = [jnp.where(allowed, s, mask_fill) for s in scores]
+                olds = [m_ref[h] for h in range(heads)]
+                news = [
+                    jnp.maximum(old, jnp.max(s, axis=0, keepdims=True))
+                    for old, s in zip(olds, scores)
+                ]
+                chances = [jnp.exp(s - new) for s, new in zip(scores, news)]
+                mixed = [
+                    mm(
+                        vt_ref[h * head_width : (h + 1) * head_width, pl.ds(at, rows)],
+                        chances[h].astype(bf16),
+                    )
+                    for h in range(heads)
+                ]
                 for h in range(heads):
                     part = slice(h * head_width, (h + 1) * head_width)
-                    s = mm(k_ref[h, pl.ds(at, rows), :], qt_ref[h])
-                    if masked:
-                        s = jnp.where(allowed, s, mask_fill)
-                    old = m_ref[h]
-                    new = jnp.maximum(old, jnp.max(s, axis=0, keepdims=True))
-                    shrink = jnp.exp(old - new)
-                    p = jnp.exp(s - new)
-                    m_ref[h] = new
-                    l_ref[h] = l_ref[h] * shrink + jnp.sum(p, axis=0, keepdims=True)
-                    a_ref[part, :] = a_ref[part, :] * shrink + mm(
-                        vt_ref[part, pl.ds(at, rows)], p.astype(bf16)
-                    )
+                    shrink = jnp.exp(olds[h] - news[h])
+                    m_ref[h] = news[h]
+                    l_ref[h] = l_ref[h] * shrink + jnp.sum(chances[h], axis=0, keepdims=True)
+                    a_ref[part, :] = a_ref[part, :] * shrink + mixed[h]
 
             @pl.when(full)
             def _():
@@ -455,14 +463,23 @@
     )
 
 
-def attend_back(meta, q, k, v, kt, grad, w_out, ot, lse, rows, layout):
+def attend_back(meta, q, k, v, kt, grad, w_out, ot, lse, rows, layout, shares):
     heads, group_rows, head_width = q.shape
     blocks = group_rows // rows
     width = heads * head_width
     scale = head_width**-0.5
     per = grad.shape[1] // rows
 
+    _, half, lanes = shares[0].shape
+    tall = 2 * half // blocks
+    wide = lanes // blocks if lanes // blocks >= 128 else lanes
+    last = lanes // wide
+
     def body(meta_ref, q_ref, k_ref, v_ref, kt_ref, grad_ref, w_ref, *refs):
+        ot_ref, lse_ref = refs[:2]
+        flat_refs, turned_refs = refs[2:6], refs[6:8]
+        up_outs, down_out = refs[10:12], refs[12]
+        refs = refs[:2] + refs[8:10] + refs[13:]
         ot_ref, lse_ref, out_ref, rows_ref, dk_ref, dv_ref, dq_ref, g_ref, delta_ref, sum_ref, qt_ref, gt_ref = refs
         i = pl.program_id(0)
 
@@ -470,6 +487,20 @@
         def _():
             dk_ref[...] = jnp.zeros_like(dk_ref)
             dv_ref[...] = jnp.zeros_like(dv_ref)
+
+        core = lax.div(i, blocks // 2)
+        for n in range(2):
+
+            @pl.when(core == (meta_ref[2] ^ n))
+            def _():
+                for g in range(2):
+                    up_outs[g][0] = flat_refs[2 * n + g][0].astype(f32)
+
+        @pl.when(i < last)
+        def _():
+            for n in range(2):
+                to = pl.multiple_of((meta_ref[2] ^ n) * half, half)
+                down_out[0, :, pl.ds(to, half)] = jnp.transpose(turned_refs[n][0].astype(f32))
 
         da = grad_ref[0]
         g = mm(da, w_ref[0], NT).astype(bf16)
@@ -504,17 +535,21 @@
             def step(masked):
                 if masked:
                     allowed = allowed_pairs(meta_ref, q_first, k_first, rows, layout)
+                parts = [slice(h * head_width, (h + 1) * head_width) for h in range(heads)]
+                scores = [mm(k_ref[h, pl.ds(at, rows), :], qt_ref[h]) for h in range(heads)]
+                downs = [
+                    mm(v_ref[h, pl.ds(at, rows), :], gt_ref[parts[h], :]) for h in range(heads)
+                ]
+                if masked:
+                    scores = [jnp.where(allowed, s, mask_fill) for s in scores]
+                chances = [jnp.exp(scores[h] - lse_ref[pl.ds(h, 1), :]) for h in range(heads)]
+                slopes = [
+                    (chances[h] * (downs[h] - delta_ref[h])).astype(bf16) for h in range(heads)
+                ]
                 for h in range(heads):
-                    part = slice(h * head_width, (h + 1) * head_width)
-                    s = mm(k_ref[h, pl.ds(at, rows), :], qt_ref[h])
-                    if masked:
-                        s = jnp.where(allowed, s, mask_fill)
-                    p = jnp.exp(s - lse_ref[pl.ds(h, 1), :])
-                    dp = mm(v_ref[h, pl.ds(at, rows), :], gt_ref[part, :])
-                    ds = (p * (dp - delta_ref[h])).astype(bf16)
-                    dv_ref[h, pl.ds(to, rows), :] += mm(p.astype(bf16), g_ref[h])
-                    dk_ref[h, pl.ds(to, rows), :] += mm(ds, q_ref[h])
-                    dq_ref[part, :] += mm(kt_ref[part, pl.ds(at, rows)], ds)
+                    dv_ref[h, pl.ds(to, rows), :] += mm(chances[h].astype(bf16), g_ref[h])
+                    dk_ref[h, pl.ds(to, rows), :] += mm(slopes[h], q_ref[h])
+                    dq_ref[parts[h], :] += mm(kt_ref[parts[h], pl.ds(at, rows)], slopes[h])
 
             @pl.when(full)
             def _():
@@ -546,6 +581,30 @@
 
             lax.fori_loop(0, blocks, store, 0)
 
+    def flat_spec(g, n):
+        def index(i, m):
+            now = jnp.clip(i - (m[2] ^ n) * (blocks // 2), 0, blocks // 2 - 1)
+            return (g, now, 0)
+
+        return pl.BlockSpec((1, tall, lanes), index)
+
+    def turned_place(i, m):
+        return (2, 0, jnp.minimum(i, last - 1))
+
+    local = layout["sides"]
+    placed = [
+        (
+            shape_of((local, 2 * half, lanes), f32),
+            pl.BlockSpec((1, tall, lanes), lambda i, m: (m[3], i, 0)),
+        )
+    ] * 2 + [
+        (
+            shape_of((local, lanes, 2 * half), f32),
+            pl.BlockSpec(
+                (1, wide, 2 * half), lambda i, m: (m[3], jnp.minimum(i, last - 1), 0)
+            ),
+        )
+    ]
     out = shape_of((group_rows, 3 * width), bf16)
     out_rows = shape_of((width, grad.shape[2]), bf16)
     return run(
@@ -575,8 +634,10 @@
             (w_out, pl.BlockSpec((1, width, grad.shape[2]), lambda i, m: (m[0], 0, 0))),
             (ot, pl.BlockSpec((width, rows), lambda i, m: (0, i))),
             (lse, pl.BlockSpec((heads, rows), lambda i, m: (0, i))),
-        ],
-        [(out, whole(out)), (out_rows, whole(out_rows))],
+        ]
+        + [(shares[n], flat_spec(g, n)) for n in range(2) for g in range(2)]
+        + [(shares[n], pl.BlockSpec((1, half, wide), turned_place)) for n in range(2)],
+        [(out, whole(out)), (out_rows, whole(out_rows))] + placed,
         scratch=[
             pltpu.VMEM((heads, group_rows, head_width), f32),
             pltpu.VMEM((heads, group_rows, head_width), f32),
@@ -1515,8 +1576,14 @@
         def tops_copy(n):
             return remote(tops_acc.at[n], tops_far.at[n], top_s.at[n], top_r.at[n], hop_peer(n))
 
-        def gain_copy(n):
-            return remote(gain_acc.at[n], gain_far.at[n], gain_s.at[n], gain_r.at[n], hop_peer(n))
+        def gain_pack(j, theirs=False):
+            spot = gain_acc.at[flip(me, j) if theirs else me]
+            return remote(spot, spot, gain_s.at[j], gain_r.at[j], near_peer(j))
+
+        def gain_team(r, theirs=False):
+            spot = gain_far.at[flip(seat, r) if theirs else seat]
+            n = members + r
+            return remote(spot, spot, gain_s.at[n], gain_r.at[n], team_peer(r))
 
         def small_start(n):
             small_copy(n).start()
@@ -1658,30 +1725,40 @@
             )
             return gain_part + jnp.sum(dh * normed, axis=0, keepdims=True)
 
-        gain_acc[0] = lax.fori_loop(
+        gain_acc[me] = lax.fori_loop(
             0, rows // row_tile, input_rows, jnp.zeros((1, width), f32)
         )
         store = pltpu.make_async_copy(dx1_all, input_out, load_sem.at[len(loads)])
         store.start()
         flat.to_y()
-        gain_copy(0).start()
+        for j in range(1, members):
+            gain_pack(j).start()
         wides[1].to_x()
         wides[0].to_y()
+        for j in range(1, members):
+            gain_pack(j).wait_send()
+            gain_pack(j, True).wait_recv()
+        value = gain_acc[0]
+        for n in range(1, members):
+            value = value + gain_acc[n]
+        gain_far[seat] = value
         small_next()
-        events = [
-            flat.to_core, wides[1].to_y, wides[0].to_core, flat.done, wides[1].to_core,
-        ]
-        for n in range(hops):
-            gain_copy(n).wait()
-            gain_acc[n + 1] = gain_acc[n] + gain_far[n]
-            if events:
-                events.pop(0)()
-            if n + 1 < hops:
-                gain_copy(n + 1).start()
+        flat.to_core()
+        for r in range(1, team):
+            gain_team(r).start()
+        wides[1].to_y()
+        wides[0].to_core()
         while small_hops:
             small_next()
-        while events:
-            events.pop(0)()
+        flat.done()
+        wides[1].to_core()
+        for r in range(1, team):
+            gain_team(r).wait_send()
+            gain_team(r, True).wait_recv()
+        value = gain_far[0]
+        for n in range(1, team):
+            value = value + gain_far[n]
+        gain_out[...] = value[0]
         final = [pltpu.make_async_copy(flat_all, flat_out, load_sem.at[len(loads) + 1])]
         for n in range(2):
             wides[n].done()
@@ -1693,7 +1770,6 @@
         for copy in final:
             copy.start()
         small_out[...] = small_acc[hops]
-        gain_out[...] = gain_acc[hops, 0, :]
         tops_out[...] = tops_acc[hops]
         store.wait()
         for copy in final:
@@ -1745,72 +1821,55 @@
         + dense_scratch(wide_share, 3 * per_group, (2,))
         + dense_scratch(out_share, width)
         + [pltpu.VMEM((hops + 1, small_rows, width), f32), pltpu.VMEM((hops, small_rows, width), f32)]
-        + [pltpu.VMEM((hops + 1, 1, width), f32), pltpu.VMEM((hops, 1, width), f32)]
+        + [pltpu.VMEM((members, 1, width), f32), pltpu.VMEM((team, 1, width), f32)]
         + [pltpu.VMEM((hops + 1, tops.shape[0], 128), f32), pltpu.VMEM((hops, tops.shape[0], 128), f32)]
         + [dma((12 + places,))] + [dma((3 * (rows // row_tile),))] * 2
         + dense_sem * 3
-        + [dma((hops,))] * 6,
+        + [dma((hops,))] * 2
+        + [dma((members + team,))] * 2
+        + [dma((hops,))] * 2,
         flops=4 * 2 * rows * width * width * 3,
         moved=20 * 1024 * 1024,
         talks=3,
     )
 
 
-def place_experts(meta, near, turned):
-    _, half, columns = near[0][0][0].shape
-    members = len(near[0])
-    local = members // 2
-    count = len(near)
+def place_experts(meta, near, begun):
+    _, half, columns = near[0].shape
     tile = 128
     tiles = half // tile
+    count = 3
 
     def body(meta_ref, *refs):
-        outs = refs[count * members :]
-        step = pl.program_id(0) * 2 + pl.program_id(1)
-        for j in range(members):
-
-            @pl.when(step == j)
+        outs = refs[2 * count + count :]
+        for j in range(2):
+
+            @pl.when(pl.program_id(0) == j)
             def _():
                 for n in range(count):
-                    piece = refs[n * members + j][0].astype(f32)
-                    outs[n][0] = jnp.transpose(piece) if turned[n] else piece
+                    piece = refs[n * 2 + j][0].astype(f32)
+                    outs[n][0] = jnp.transpose(piece) if n == 2 else piece
 
     def in_spec(which, j):
-        def index(n, c, t, m):
-            step = n * 2 + c
-            return (which, jnp.where(step == j, t, jnp.where(step < j, 0, tiles - 1)), 0)
+        def index(c, t, m):
+            return (which, jnp.where(c == j, t, jnp.where(c < j, 0, tiles - 1)), 0)
 
         return pl.BlockSpec((1, tile, columns), index)
 
-    outputs = []
-    for flag in turned:
-        if flag:
-            outputs.append(
-                (
-                    shape_of((local, columns, 2 * half), f32),
-                    pl.BlockSpec(
-                        (1, columns, tile),
-                        lambda n, c, t, m: (m[3] ^ n, 0, (m[2] ^ c) * tiles + t),
-                    ),
-                )
-            )
-        else:
-            outputs.append(
-                (
-                    shape_of((local, 2 * half, columns), f32),
-                    pl.BlockSpec(
-                        (1, tile, columns),
-                        lambda n, c, t, m: (m[3] ^ n, (m[2] ^ c) * tiles + t, 0),
-                    ),
-                )
-            )
+    flat = pl.BlockSpec((1, tile, columns), lambda c, t, m: (m[3] ^ 1, (m[2] ^ c) * tiles + t, 0))
+    turned = pl.BlockSpec((1, columns, tile), lambda c, t, m: (m[3] ^ 1, 0, (m[2] ^ c) * tiles + t))
     return run(
         body,
-        (local, 2, tiles),
-        [(a, in_spec(which, j)) for listed in near for j, (a, which) in enumerate(listed)],
-        outputs,
+        (2, tiles),
+        [(near[j], in_spec(n, j)) for n in range(count) for j in range(2)]
+        + [(a, anywhere) for a in begun],
+        [
+            (shape_of(a.shape, f32), turned if n == 2 else flat)
+            for n, a in enumerate(begun)
+        ],
         meta=meta,
-        moved=count * local * 2 * half * columns * 6,
+        moved=count * 2 * half * columns * 6,
+        aliases={1 + 2 * count + n: n for n in range(count)},
     )
 
 
@@ -1949,7 +2008,7 @@
     blocks = block_order.shape[1]
     layout = {
         "order": 4, "lengths": 4 + blocks, "sequences": lengths.shape[1],
-        "inverse": 4 + blocks + lengths.shape[1],
+        "inverse": 4 + blocks + lengths.shape[1], "sides": local,
     }
     numbers = jnp.arange(blocks, dtype=jnp.int32)
     given = jnp.sum(jnp.where(block_order[0][None, :] == numbers[:, None], numbers[None, :], 0), axis=1)
@@ -1989,8 +2048,8 @@
     expert_now, da_near = lax.optimization_barrier((expert_sum, da_near))
     over = swap(expert_now, "ctx", 2)
     y_near = [swap(produced[g], "exp", g) if g else produced[0] for g in range(groups)]
-    dqkv, out_sum = attend_back(
-        meta, q, k, v, kt, da_near, w_out_parts, ot, lse, deal_block, layout
+    dqkv, out_sum, *begun_grads = attend_back(
+        meta, q, k, v, kt, da_near, w_out_parts, ot, lse, deal_block, layout, (expert_sum, beside)
     )
 
     input_grad, qkv_near, out_near, small, norm1_grad, top_all, result = finish(
@@ -1998,12 +2057,11 @@
     )
     over, qkv_near = lax.optimization_barrier((over, qkv_near))
     corner = swap(over, "ctx", 1)
-    near = [[(a, n) for a in (expert_sum, beside, over, corner)] for n in range(3)]
     dense = place_dense(meta, qkv_near, out_near, top_all, small, w_qkv, const_vec.shape[0])
     qkv_grad, out_grad, clipped, router_grad, norm2_grad, vec_grad, logit_grad, carry_grad = dense
     router_grad, logit_grad = jnp.transpose(router_grad), jnp.swapaxes(logit_grad, 1, 2)
     out_grad = out_grad.reshape(width, width)
-    gate_grad, up_grad, down_grad = place_experts(meta, near, (False, False, True))
+    gate_grad, up_grad, down_grad = place_experts(meta, (over, corner), begun_grads)
     return (
         result[None],
         input_grad[None],

time: 375 us -> 357 us (0.952)
  Pallas kernels: 351 us -> 334 us
    pallas_call x9, Pallas kernels: 351 us -> 334 us  [run(): pl.pallas_call(body, out_shape=[o for o, _ in outputs], grid_spec=pltpu.P...]
  transfers between devices with their start and end apart: 9 -> 9, of which waited for: 0 -> 0; matrix products, arithmetic and copies ran while one was open for 1% -> 1% of each run, Pallas kernels for 53% -> 52%
where the time goes in v7:
time: 357 us; the launch traced here: 354 us
  Pallas kernels  334 us (94%)
  starting transfers between devices  12.7 us (4%)
  local copies, waits for them, and re-layouts  6.08 us (2%)
    pallas_call x9, Pallas kernels, run(): pl.pallas_call(body, out_shape=[o for o, _ in outputs], grid_spec=pltpu.P...  334 us
  transfers between devices with their start and end apart: 9, of which 0 were waited for; matrix products, arithmetic and copies ran while one was open for 1% of the time, Pallas kernels for 52%

profile of v7, /device:TPU:0, one launch (start us, length us, event | category | flops | bytes accessed | tf_op | source)
XLA Modules:
  0.0 353.6 jit_solution(4951370920430516291)
XLA Ops:
  0.6 0.0 copy-start.5
  0.7 0.0 copy-start.6
  0.7 30.3 %shard_map.272 = (bf16[3,2048,64]{2,1,0:T(8,128)(2,1)}, bf16[3,2048,64]{2,1,0:T(8,128)(2,1)}, bf16[3,2048,64]{2,1,0:T(8,128)(2,1)}, bf16[192,2048]{1,0:T(8,128)(...) custom-call(bf16[512,768]{1,0:T(8,128)(2,1)} %bitcast.41, ...), custom_call_target="tpu_custom_call" | custom-call | flops 3019898880 | bytes 20971520 | tf_op jit(solution)/shard_map/pallas_call | solution.py:50
  30.9 0.6 collective-permute-start
  31.5 1.5 collective-permute-start.1
  33.0 1.5 collective-permute-start.2
  34.5 3.3 collective-permute-start.3
  37.8 0.1 select_reduce_fusion
  37.9 0.0 copy-done.6
  37.9 0.6 concatenate.3.meta_ref
  38.5 19.9 %shard_map.273 = (bf16[2048,192]{1,0:T(8,128)(2,1)}, f32[192,2048]{1,0:T(8,128)}, f32[3,2048]{1,0:T(4,128)}, f32[3,256]{1,0:T(4,128)}) custom-call(s32[22]{0:T(128)} %concatenate.3.meta_ref, bf16[3,2048,64]{2,1,0:T(8,128)(2,1)} %get-tuple-element.80.q_ref, bf16[3,2048,64]{2,1,0:T(8,128)(2,1)} %get-tuple-element.81.k_ref, ...), custom_call_target="tpu_custom_call" | custom-call | flops 3221225472 | bytes 5505024 | tf_op jit(solution)/shard_map/pallas_call | solution.py:50
  58.4 0.6 copy.36
  59.0 0.6 reshape.41.refs_10_
  59.6 52.3 %shard_map.274 = (f32[512,768]{1,0:T(8,128)}, f32[512,768]{1,0:T(8,128)}, f32[512,12]{1,0:T(8,128)}, bf16[8,128,768]{2,1,0:T(8,128)(2,1)}, f32[8,1,128]{2,1,0:T(...) custom-call(bf16[512,768]{1,0:T(8,128)(2,1)} %bitcast.42, ...), custom_call_target="tpu_custom_call" | custom-call | flops 1409286144 | bytes 11796480 | tf_op jit(solution)/shard_map/pallas_call | solution.py:50
  111.9 0.0 collective-permute-done.refs_6_
  111.9 0.0 copy-start.9
  111.9 0.0 collective-permute-done.1.refs_7_
  112.0 0.0 copy-start.10
  112.0 0.0 collective-permute-done.2.refs_8_
  112.0 0.0 copy-start.11
  112.0 0.0 collective-permute-done.3.refs_9_
  112.0 0.0 copy-start.12
  112.0 0.6 copy-done.9
  112.6 0.1 copy-done.10
  112.7 0.1 copy-done.11
  112.7 0.1 copy-done.12
  112.8 81.2 %shard_map.275 = (bf16[2,128,768]{2,1,0:T(8,128)(2,1)}, bf16[2,128,768]{2,1,0:T(8,128)(2,1)}, bf16[2,128,768]{2,1,0:T(8,128)(2,1)}, bf16[2,128,768]{2,1,0:T(8,12...) custom-call(bf16[8,128,768]{2,1,0:T(8,128)(2,1)} %get-tuple-element., ...), custom_call_target="tpu_custom_call" | custom-call | flops 28991029248 | bytes 25165824 | tf_op jit(solution)/shard_map/pallas_call | solution.py:50
  194.0 28.5 %shard_map.276 = (f32[512,768]{1,0:T(8,128)}, f32[31,768]{1,0:T(8,128)}, bf16[4,512,768]{2,1,0:T(8,128)(2,1)}) custom-call(f32[512,768]{1,0:T(8,128)} %get-tuple-element.96.refs_0_, f32[512,768]{1,0:T(8,128)} %get-tuple-element.97.refs_1_, bf16[512,768]{1,0:T(8,128)(2,1)} %bitcast.29, f32[512,12]{1,0:T(8,128)} %get-tuple-element.98.refs_3_, ...), custom_call_target="tpu_custom_call" | custom-call | flops 1409286144 | bytes 9437184 | tf_op jit(solution)/shard_map/pallas_call | solution.py:50
  222.5 1.1 collective-permute-start.7
  223.6 0.0 collective-permute-start.4
  223.6 2.8 collective-permute-start.5
  226.4 0.0 copy-done.7
  226.4 1.6 collective-permute-start.6
  228.0 33.3 %shard_map.277 = (bf16[2048,576]{1,0:T(8,128)(2,1)}, bf16[192,768]{1,0:T(8,128)(2,1)}, f32[2,768,1024]{2,1,0:T(8,128)}, f32[2,768,1024]{2,1,0:T(8,128)}, f32[2,1024,768]{2,1,0:T(8,128)}) custom-call(s32[22]{0:T(128)} %concatenate.3.meta_ref, bf16[3,2048,64]{2,1,0:T(8,128)(2,1)} %get-tuple-element.80.q_ref, bf16[3,2048,64]{2,1,0:T(8,128)(2,1)} %get-tuple-element.81.k_ref, ...), custom_call_target="tpu_custom_call" | custom-call | flops 8053063680 | bytes 9437184 | tf_op jit(solution)/shard_map/pallas_call | solution.py:50
  261.4 0.0 collective-permute-done.4.refs_12_
  261.4 0.0 collective-permute-done.5.refs_13_
  261.4 0.0 collective-permute-done.6.refs_14_
  261.4 69.1 %shard_map.278 = (f32[512,768]{1,0:T(8,128)}, bf16[2,4,8,48,576]{4,3,2,1,0:T(8,128)(2,1)}, bf16[4,8,24,768]{3,2,1,0:T(8,128)(2,1)}, f32[31,768]{1,0:T(8,128)}, f...) custom-call(bf16[2048,576]{1,0:T(8,128)(2,1)} %get-tuple-element.110.refs_0_, ...), custom_call_target="tpu_custom_call" | custom-call | flops 7247757312 | bytes 20971520 | tf_op jit(solution)/shard_map/pallas_call | solution.py:50
  330.5 0.0 collective-permute-done.7.refs_0_.refs_2_.refs_4_
  330.5 0.4 collective-permute-start.8
  331.0 10.9 %shard_map.279 = (f32[3,768,768]{2,1,0:T(8,128)}, f32[4,192,768]{2,1,0:T(8,128)}, f32[2,768,768]{2,1,0:T(8,128)}, f32[12,768]{1,0:T(8,128)}, f32[768]{0:T(1024)}...) custom-call(s32[22]{0:T(128)} %concatenate.3.meta_ref, ...), custom_call_target="tpu_custom_call" | custom-call | bytes 21233664 | tf_op jit(solution)/shard_map/pallas_call | solution.py:50
  341.9 0.0 collective-permute-done.8.refs_1_.refs_3_.refs_5_
  341.9 8.1 %shard_map.280 = (f32[2,768,1024]{2,1,0:T(8,128)}, f32[2,768,1024]{2,1,0:T(8,128)}, f32[2,1024,768]{2,1,0:T(8,128)}) custom-call(s32[22]{0:T(128)} %concatenate.3.meta_ref, bf16[3,384,1024]{2,1,0:T(8,128)(2,1)} %collective-permute-done.7.refs_0_.refs_2_.refs_4_, ...), custom_call_target="tpu_custom_call", output_to_operand_aliasing={{0}: (7, {}), {1}: (8, {}), {2}: (9, {})} | custom-call | bytes 14155776 | tf_op jit(solution)/shard_map/pallas_call | solution.py:50
  350.0 0.9 copy.43
  350.9 0.8 copy-done
  351.7 1.1 copy.44
  352.8 0.0 copy-done.4
  352.8 0.6 copy.45
  (13 shorter events, 0.0 us)
Async XLA Ops:
  0.6 37.1 %copy-start.5 = (s32[1,8]{1,0:T(1,128)S(1)}, s32[1,8]{1,0:T(1,128)}, u32[]{:S(2)}) copy-start(s32[1,8]{1,0:T(1,128)} %param.19) | copy-start | bytes 100
  0.7 37.3 %copy-start.6 = (s32[1,2]{1,0:T(1,128)S(1)}, s32[1,2]{1,0:T(1,128)}, u32[]{:S(2)}) copy-start(s32[1,2]{1,0:T(1,128)} %param.18) | copy-start | bytes 28
  30.9 81.0 %collective-permute-start = (bf16[128,768]{1,0:T(8,128)(2,1)}, bf16[128,768]{1,0:T(8,128)(2,1)S(1)}, u32[]{:S(2)}, u32[]{:S(2)}) collective-permute-start(bf16[128,768]{1,0:T(8,128)(2,1)} %get-tuple-element.91), channel_id=1, source_target_pairs={{0,8},{1,9},{2,10},{3,11},{4,12},{5,13},{6,14},{7,15},{8,0},{9,1},... | collective-permute-start | bytes 589832 | tf_op jit(solution)/shard_map/ppermute | solution.py:101
  31.5 80.4 %collective-permute-start.1 = (bf16[128,768]{1,0:T(8,128)(2,1)}, bf16[128,768]{1,0:T(8,128)(2,1)S(1)}, u32[]{:S(2)}, u32[]{:S(2)}) collective-permute-start(bf16[128,768]{1,0:T(8,128)(2,1)} %get-tuple-element.92), channel_id=1, source_target_pairs={{0,9},{1,8},{2,11},{3,10},{4,13},{5,12},{6,15},{7,14},{8,1},{9,0},... | collective-permute-start | bytes 589832 | tf_op jit(solution)/shard_map/ppermute | solution.py:101
  33.0 78.9 %collective-permute-start.2 = (bf16[128,768]{1,0:T(8,128)(2,1)}, bf16[128,768]{1,0:T(8,128)(2,1)S(1)}, u32[]{:S(2)}, u32[]{:S(2)}) collective-permute-start(bf16[128,768]{1,0:T(8,128)(2,1)} %get-tuple-element.93), channel_id=1, source_target_pairs={{0,10},{1,11},{2,8},{3,9},{4,14},{5,15},{6,12},{7,13},{8,2},{9,3},... | collective-permute-start | bytes 589832 | tf_op jit(solution)/shard_map/ppermute | solution.py:101
  34.5 77.5 %collective-permute-start.3 = (bf16[128,768]{1,0:T(8,128)(2,1)}, bf16[128,768]{1,0:T(8,128)(2,1)S(1)}, u32[]{:S(2)}, u32[]{:S(2)}) collective-permute-start(bf16[128,768]{1,0:T(8,128)(2,1)} %get-tuple-element.94), channel_id=1, source_target_pairs={{0,11},{1,10},{2,9},{3,8},{4,15},{5,14},{6,13},{7,12},{8,3},{9,2},... | collective-permute-start | bytes 589832 | tf_op jit(solution)/shard_map/ppermute | solution.py:101
  38.5 19.9 %copy-start.2 = (f32[1,512,12]{1,0,2:T(1,128)S(1)}, f32[1,512,12]{1,0,2:T(1,128)}, u32[]{:S(2)}) copy-start(f32[1,512,12]{1,0,2:T(1,128)} %param.21) | copy-start | bytes 73732
  38.5 20.5 %copy-start.3 = (f32[2,768,2]{1,2,0:T(2,128)S(1)}, f32[2,768,2]{1,2,0:T(2,128)}, u32[]{:S(2)}) copy-start(f32[2,768,2]{1,2,0:T(2,128)} %param.28) | copy-start | bytes 36868
  111.9 0.7 copy-start.9
  112.0 0.7 copy-start.10
  112.0 0.8 copy-start.11
  112.0 0.8 copy-start.12
  194.0 29.7 %copy-start.8 = (bf16[2,128,768]{2,1,0:T(8,128)(2,1)S(1)}, bf16[2,128,768]{2,1,0:T(8,128)(2,1)}, u32[]{:S(2)}) copy-start(bf16[2,128,768]{2,1,0:T(8,128)(2,1)} %get-tuple-element.120) | copy-start | bytes 1179652
  194.0 32.4 %copy-start.7 = (bf16[2,128,768]{2,1,0:T(8,128)(2,1)S(1)}, bf16[2,128,768]{2,1,0:T(8,128)(2,1)}, u32[]{:S(2)}) copy-start(bf16[2,128,768]{2,1,0:T(8,128)(2,1)} %get-tuple-element.121) | copy-start | bytes 1179652
  222.5 108.0 %collective-permute-start.7 = (bf16[3,384,1024]{2,1,0:T(8,128)(2,1)}, bf16[3,384,1024]{2,1,0:T(8,128)(2,1)}, u32[]{:S(2)}, u32[]{:S(2)}) collective-permute-start(bf16[3,384,1024]{2,1,0:T(8,128)(2,1)} %get-tuple-element.125.refs_2_.refs_3_.refs_6_), channel_id=1, source_target_pairs={{0,8},{4,12},{8,0},{12,4},{1,9},{5,13},{9,1},{13,5},{2,10},{6,14},... | collective-permute-start | bytes 7077896 | tf_op jit(solution)/shard_map/ppermute | solution.py:73
  223.6 37.7 %collective-permute-start.4 = (bf16[2,128,768]{2,1,0:T(8,128)(2,1)}, bf16[2,128,768]{2,1,0:T(8,128)(2,1)}, u32[]{:S(2)}, u32[]{:S(2)}) collective-permute-start(bf16[2,128,768]{2,1,0:T(8,128)(2,1)} %get-tuple-element.119), channel_id=1, source_target_pairs={{0,1},{1,0},{2,3},{3,2},{4,5},{5,4},{6,7},{7,6},{8,9},{9,8},{10,11... | collective-permute-start | bytes 1179656 | tf_op jit(solution)/shard_map/ppermute | solution.py:73
  223.6 37.7 %collective-permute-start.5 = (bf16[2,128,768]{2,1,0:T(8,128)(2,1)S(1)}, bf16[2,128,768]{2,1,0:T(8,128)(2,1)}, u32[]{:S(2)}, u32[]{:S(2)}) collective-permute-start(bf16[2,128,768]{2,1,0:T(8,128)(2,1)S(1)} %copy-done.8), channel_id=1, source_target_pairs={{0,2},{1,3},{2,0},{3,1},{4,6},{5,7},{6,4},{7,5},{8,10},{9,11},{10,... | collective-permute-start | bytes 1179656 | tf_op jit(solution)/shard_map/ppermute | solution.py:73
  226.4 35.0 %collective-permute-start.6 = (bf16[2,128,768]{2,1,0:T(8,128)(2,1)S(1)}, bf16[2,128,768]{2,1,0:T(8,128)(2,1)}, u32[]{:S(2)}, u32[]{:S(2)}) collective-permute-start(bf16[2,128,768]{2,1,0:T(8,128)(2,1)S(1)} %copy-done.7), channel_id=1, source_target_pairs={{0,3},{1,2},{2,1},{3,0},{4,7},{5,6},{6,5},{7,4},{8,11},{9,10},{10,... | collective-permute-start | bytes 1179656 | tf_op jit(solution)/shard_map/ppermute | solution.py:73
  330.5 11.4 %collective-permute-start.8 = (bf16[3,384,1024]{2,1,0:T(8,128)(2,1)}, bf16[3,384,1024]{2,1,0:T(8,128)(2,1)}, u32[]{:S(2)}, u32[]{:S(2)}) collective-permute-start(bf16[3,384,1024]{2,1,0:T(8,128)(2,1)} %collective-permute-done.7.refs_0_.refs_2_.refs_4_), channel_id=1, source_target_pairs={{0,4},{4,0},{8,12},{12,8},{1,5},{5,1},{9,13},{13,9},{2,6},{6,2},{1... | collective-permute-start | bytes 7077896 | tf_op jit(solution)/shard_map/ppermute | solution.py:73
  341.9 8.1 %copy-start.1 = (bf16[512,768]{1,0:T(8,128)(2,1)S(1)}, bf16[512,768]{1,0:T(8,128)(2,1)}, u32[]{:S(2)}) copy-start(bf16[512,768]{1,0:T(8,128)(2,1)} %get-tuple-element.122) | copy-start | bytes 2359300
  350.0 1.7 copy-start
  350.0 2.8 copy-start.4

commit v8 on v7

--- a/solution.py
+++ b/solution.py
@@ -874,7 +874,7 @@
     steps = hidden // tile
     tiles = per_part // tile
     away = steps - tiles
-    lead = away // 2
+    lead = (away + 2) // 4
     kept = steps - lead
     chunk = 256
 

time: 357 us -> 355 us (level)
  Pallas kernels: 334 us -> 327 us
    pallas_call x9, Pallas kernels: 334 us -> 327 us  [run(): pl.pallas_call(body, out_shape=[o for o, _ in outputs], grid_spec=pltpu.P...]
where the time goes in v8:
time: 355 us; the launch traced here: 350 us
  Pallas kernels  327 us (92%)
  starting transfers between devices  15.3 us (4%)
  local copies, waits for them, and re-layouts  6.08 us (2%)
    pallas_call x9, Pallas kernels, run(): pl.pallas_call(body, out_shape=[o for o, _ in outputs], grid_spec=pltpu.P...  327 us
    ppermute x5, starting transfers between devices, swap(): return lax.ppermute(value, axis, [(i, i ^ distance) for i in range(count)])  8.46 us
  transfers between devices with their start and end apart: 9, of which 0 were waited for; matrix products, arithmetic and copies ran while one was open for 1% of the time, Pallas kernels for 52%

profile of v8, /device:TPU:0, one launch (start us, length us, event | category | flops | bytes accessed | tf_op | source)
XLA Modules:
  0.0 350.1 jit_solution(12080754812385703976)
XLA Ops:
  0.6 0.0 copy-start.5
  0.7 0.0 copy-start.6
  0.7 30.3 %shard_map.272 = (bf16[3,2048,64]{2,1,0:T(8,128)(2,1)}, bf16[3,2048,64]{2,1,0:T(8,128)(2,1)}, bf16[3,2048,64]{2,1,0:T(8,128)(2,1)}, bf16[192,2048]{1,0:T(8,128)(...) custom-call(bf16[512,768]{1,0:T(8,128)(2,1)} %bitcast.41, ...), custom_call_target="tpu_custom_call" | custom-call | flops 3019898880 | bytes 20971520 | tf_op jit(solution)/shard_map/pallas_call | solution.py:50
  30.9 0.6 collective-permute-start
  31.5 1.5 collective-permute-start.1
  33.0 1.5 collective-permute-start.2
  34.5 3.3 collective-permute-start.3
  37.8 0.0 copy-done.5
  37.8 0.1 select_reduce_fusion
  37.9 0.0 copy-done.6
  37.9 0.6 concatenate.3.meta_ref
  38.5 18.8 %shard_map.273 = (bf16[2048,192]{1,0:T(8,128)(2,1)}, f32[192,2048]{1,0:T(8,128)}, f32[3,2048]{1,0:T(4,128)}, f32[3,256]{1,0:T(4,128)}) custom-call(s32[22]{0:T(128)} %concatenate.3.meta_ref, bf16[3,2048,64]{2,1,0:T(8,128)(2,1)} %get-tuple-element.80.q_ref, bf16[3,2048,64]{2,1,0:T(8,128)(2,1)} %get-tuple-element.81.k_ref, ...), custom_call_target="tpu_custom_call" | custom-call | flops 3221225472 | bytes 5505024 | tf_op jit(solution)/shard_map/pallas_call | solution.py:50
  57.4 0.6 copy.36
  58.0 0.6 reshape.41.refs_10_
  58.6 52.3 %shard_map.274 = (f32[512,768]{1,0:T(8,128)}, f32[512,768]{1,0:T(8,128)}, f32[512,12]{1,0:T(8,128)}, bf16[8,128,768]{2,1,0:T(8,128)(2,1)}, f32[8,1,128]{2,1,0:T(...) custom-call(bf16[512,768]{1,0:T(8,128)(2,1)} %bitcast.42, ...), custom_call_target="tpu_custom_call" | custom-call | flops 1409286144 | bytes 11796480 | tf_op jit(solution)/shard_map/pallas_call | solution.py:50
  110.9 0.0 collective-permute-done.refs_6_
  110.9 0.0 copy-start.9
  110.9 0.0 collective-permute-done.1.refs_7_
  111.0 0.0 copy-start.10
  111.0 0.0 collective-permute-done.2.refs_8_
  111.0 0.0 copy-start.11
  111.0 0.0 collective-permute-done.3.refs_9_
  111.0 0.0 copy-start.12
  111.0 0.6 copy-done.9
  111.6 0.1 copy-done.10
  111.7 0.1 copy-done.11
  111.7 0.1 copy-done.12
  111.8 77.8 %shard_map.275 = (bf16[2,128,768]{2,1,0:T(8,128)(2,1)}, bf16[2,128,768]{2,1,0:T(8,128)(2,1)}, bf16[2,128,768]{2,1,0:T(8,128)(2,1)}, bf16[2,128,768]{2,1,0:T(8,12...) custom-call(bf16[8,128,768]{2,1,0:T(8,128)(2,1)} %get-tuple-element., ...), custom_call_target="tpu_custom_call" | custom-call | flops 28991029248 | bytes 25165824 | tf_op jit(solution)/shard_map/pallas_call | solution.py:50
  189.6 28.9 %shard_map.276 = (f32[512,768]{1,0:T(8,128)}, f32[31,768]{1,0:T(8,128)}, bf16[4,512,768]{2,1,0:T(8,128)(2,1)}) custom-call(f32[512,768]{1,0:T(8,128)} %get-tuple-element.96.refs_0_, f32[512,768]{1,0:T(8,128)} %get-tuple-element.97.refs_1_, bf16[512,768]{1,0:T(8,128)(2,1)} %bitcast.29, f32[512,12]{1,0:T(8,128)} %get-tuple-element.98.refs_3_, ...), custom_call_target="tpu_custom_call" | custom-call | flops 1409286144 | bytes 9437184 | tf_op jit(solution)/shard_map/pallas_call | solution.py:50
  218.5 0.8 collective-permute-start.7
  219.4 4.8 %collective-permute-start.4 = (bf16[2,128,768]{2,1,0:T(8,128)(2,1)}, bf16[2,128,768]{2,1,0:T(8,128)(2,1)}, u32[]{:S(2)}, u32[]{:S(2)}) collective-permute-start(bf16[2,128,768]{2,1,0:T(8,128)(2,1)} %get-tuple-element.119), channel_id=1, source_target_pairs={{0,1},{1,0},{2,3},{3,2},{4,5},{5,4},{6,7},{7,6},{8,9},{9,8},{10,11... | collective-permute-start | bytes 1179656 | tf_op jit(solution)/shard_map/ppermute | solution.py:73
  224.2 0.0 copy-done.8
  224.2 0.0 collective-permute-start.5
  224.2 2.4 collective-permute-start.6
  226.6 32.2 %shard_map.277 = (bf16[2048,576]{1,0:T(8,128)(2,1)}, bf16[192,768]{1,0:T(8,128)(2,1)}, f32[2,768,1024]{2,1,0:T(8,128)}, f32[2,768,1024]{2,1,0:T(8,128)}, f32[2,1024,768]{2,1,0:T(8,128)}) custom-call(s32[22]{0:T(128)} %concatenate.3.meta_ref, bf16[3,2048,64]{2,1,0:T(8,128)(2,1)} %get-tuple-element.80.q_ref, bf16[3,2048,64]{2,1,0:T(8,128)(2,1)} %get-tuple-element.81.k_ref, ...), custom_call_target="tpu_custom_call" | custom-call | flops 8053063680 | bytes 9437184 | tf_op jit(solution)/shard_map/pallas_call | solution.py:50
  258.8 0.0 collective-permute-done.4.refs_12_
  258.8 0.0 collective-permute-done.5.refs_13_
  258.8 0.0 collective-permute-done.6.refs_14_
  258.8 67.9 %shard_map.278 = (f32[512,768]{1,0:T(8,128)}, bf16[2,4,8,48,576]{4,3,2,1,0:T(8,128)(2,1)}, bf16[4,8,24,768]{3,2,1,0:T(8,128)(2,1)}, f32[31,768]{1,0:T(8,128)}, f...) custom-call(bf16[2048,576]{1,0:T(8,128)(2,1)} %get-tuple-element.110.refs_0_, ...), custom_call_target="tpu_custom_call" | custom-call | flops 7247757312 | bytes 20971520 | tf_op jit(solution)/shard_map/pallas_call | solution.py:50
  326.8 0.0 collective-permute-done.7.refs_0_.refs_2_.refs_4_
  326.8 0.4 collective-permute-start.8
  327.2 10.9 %shard_map.279 = (f32[3,768,768]{2,1,0:T(8,128)}, f32[4,192,768]{2,1,0:T(8,128)}, f32[2,768,768]{2,1,0:T(8,128)}, f32[12,768]{1,0:T(8,128)}, f32[768]{0:T(1024)}...) custom-call(s32[22]{0:T(128)} %concatenate.3.meta_ref, ...), custom_call_target="tpu_custom_call" | custom-call | bytes 21233664 | tf_op jit(solution)/shard_map/pallas_call | solution.py:50
  338.1 0.0 collective-permute-done.8.refs_1_.refs_3_.refs_5_
  338.2 8.1 %shard_map.280 = (f32[2,768,1024]{2,1,0:T(8,128)}, f32[2,768,1024]{2,1,0:T(8,128)}, f32[2,1024,768]{2,1,0:T(8,128)}) custom-call(s32[22]{0:T(128)} %concatenate.3.meta_ref, bf16[3,384,1024]{2,1,0:T(8,128)(2,1)} %collective-permute-done.7.refs_0_.refs_2_.refs_4_, ...), custom_call_target="tpu_custom_call", output_to_operand_aliasing={{0}: (7, {}), {1}: (8, {}), {2}: (9, {})} | custom-call | bytes 14155776 | tf_op jit(solution)/shard_map/pallas_call | solution.py:50
  346.3 0.9 copy.43
  347.1 0.8 copy-done
  347.9 1.1 copy.44
  349.1 0.6 copy.45
  (13 shorter events, 0.0 us)
Async XLA Ops:
  0.6 37.1 %copy-start.5 = (s32[1,8]{1,0:T(1,128)S(1)}, s32[1,8]{1,0:T(1,128)}, u32[]{:S(2)}) copy-start(s32[1,8]{1,0:T(1,128)} %param.19) | copy-start | bytes 100
  0.7 37.3 %copy-start.6 = (s32[1,2]{1,0:T(1,128)S(1)}, s32[1,2]{1,0:T(1,128)}, u32[]{:S(2)}) copy-start(s32[1,2]{1,0:T(1,128)} %param.18) | copy-start | bytes 28
  30.9 80.0 %collective-permute-start = (bf16[128,768]{1,0:T(8,128)(2,1)}, bf16[128,768]{1,0:T(8,128)(2,1)S(1)}, u32[]{:S(2)}, u32[]{:S(2)}) collective-permute-start(bf16[128,768]{1,0:T(8,128)(2,1)} %get-tuple-element.91), channel_id=1, source_target_pairs={{0,8},{1,9},{2,10},{3,11},{4,12},{5,13},{6,14},{7,15},{8,0},{9,1},... | collective-permute-start | bytes 589832 | tf_op jit(solution)/shard_map/ppermute | solution.py:101
  31.5 79.4 %collective-permute-start.1 = (bf16[128,768]{1,0:T(8,128)(2,1)}, bf16[128,768]{1,0:T(8,128)(2,1)S(1)}, u32[]{:S(2)}, u32[]{:S(2)}) collective-permute-start(bf16[128,768]{1,0:T(8,128)(2,1)} %get-tuple-element.92), channel_id=1, source_target_pairs={{0,9},{1,8},{2,11},{3,10},{4,13},{5,12},{6,15},{7,14},{8,1},{9,0},... | collective-permute-start | bytes 589832 | tf_op jit(solution)/shard_map/ppermute | solution.py:101
  33.0 77.9 %collective-permute-start.2 = (bf16[128,768]{1,0:T(8,128)(2,1)}, bf16[128,768]{1,0:T(8,128)(2,1)S(1)}, u32[]{:S(2)}, u32[]{:S(2)}) collective-permute-start(bf16[128,768]{1,0:T(8,128)(2,1)} %get-tuple-element.93), channel_id=1, source_target_pairs={{0,10},{1,11},{2,8},{3,9},{4,14},{5,15},{6,12},{7,13},{8,2},{9,3},... | collective-permute-start | bytes 589832 | tf_op jit(solution)/shard_map/ppermute | solution.py:101
  34.5 76.5 %collective-permute-start.3 = (bf16[128,768]{1,0:T(8,128)(2,1)}, bf16[128,768]{1,0:T(8,128)(2,1)S(1)}, u32[]{:S(2)}, u32[]{:S(2)}) collective-permute-start(bf16[128,768]{1,0:T(8,128)(2,1)} %get-tuple-element.94), channel_id=1, source_target_pairs={{0,11},{1,10},{2,9},{3,8},{4,15},{5,14},{6,13},{7,12},{8,3},{9,2},... | collective-permute-start | bytes 589832 | tf_op jit(solution)/shard_map/ppermute | solution.py:101
  38.5 18.8 %copy-start.2 = (f32[1,512,12]{1,0,2:T(1,128)S(1)}, f32[1,512,12]{1,0,2:T(1,128)}, u32[]{:S(2)}) copy-start(f32[1,512,12]{1,0,2:T(1,128)} %param.21) | copy-start | bytes 73732
  38.5 19.5 %copy-start.3 = (f32[2,768,2]{1,2,0:T(2,128)S(1)}, f32[2,768,2]{1,2,0:T(2,128)}, u32[]{:S(2)}) copy-start(f32[2,768,2]{1,2,0:T(2,128)} %param.28) | copy-start | bytes 36868
  110.9 0.7 copy-start.9
  111.0 0.7 copy-start.10
  111.0 0.8 copy-start.11
  111.0 0.8 copy-start.12
  189.6 34.6 %copy-start.8 = (bf16[2,128,768]{2,1,0:T(8,128)(2,1)S(1)}, bf16[2,128,768]{2,1,0:T(8,128)(2,1)}, u32[]{:S(2)}) copy-start(bf16[2,128,768]{2,1,0:T(8,128)(2,1)} %get-tuple-element.120) | copy-start | bytes 1179652
  189.6 34.6 %copy-start.7 = (bf16[2,128,768]{2,1,0:T(8,128)(2,1)S(1)}, bf16[2,128,768]{2,1,0:T(8,128)(2,1)}, u32[]{:S(2)}) copy-start(bf16[2,128,768]{2,1,0:T(8,128)(2,1)} %get-tuple-element.121) | copy-start | bytes 1179652
  218.5 108.2 %collective-permute-start.7 = (bf16[3,384,1024]{2,1,0:T(8,128)(2,1)}, bf16[3,384,1024]{2,1,0:T(8,128)(2,1)}, u32[]{:S(2)}, u32[]{:S(2)}) collective-permute-start(bf16[3,384,1024]{2,1,0:T(8,128)(2,1)} %get-tuple-element.125.refs_2_.refs_3_.refs_6_), channel_id=1, source_target_pairs={{0,8},{4,12},{8,0},{12,4},{1,9},{5,13},{9,1},{13,5},{2,10},{6,14},... | collective-permute-start | bytes 7077896 | tf_op jit(solution)/shard_map/ppermute | solution.py:73
  219.4 39.4 %collective-permute-start.4 = (bf16[2,128,768]{2,1,0:T(8,128)(2,1)}, bf16[2,128,768]{2,1,0:T(8,128)(2,1)}, u32[]{:S(2)}, u32[]{:S(2)}) collective-permute-start(bf16[2,128,768]{2,1,0:T(8,128)(2,1)} %get-tuple-element.119), channel_id=1, source_target_pairs={{0,1},{1,0},{2,3},{3,2},{4,5},{5,4},{6,7},{7,6},{8,9},{9,8},{10,11... | collective-permute-start | bytes 1179656 | tf_op jit(solution)/shard_map/ppermute | solution.py:73
  224.2 34.6 %collective-permute-start.5 = (bf16[2,128,768]{2,1,0:T(8,128)(2,1)S(1)}, bf16[2,128,768]{2,1,0:T(8,128)(2,1)}, u32[]{:S(2)}, u32[]{:S(2)}) collective-permute-start(bf16[2,128,768]{2,1,0:T(8,128)(2,1)S(1)} %copy-done.8), channel_id=1, source_target_pairs={{0,2},{1,3},{2,0},{3,1},{4,6},{5,7},{6,4},{7,5},{8,10},{9,11},{10,... | collective-permute-start | bytes 1179656 | tf_op jit(solution)/shard_map/ppermute | solution.py:73
  224.2 34.6 %collective-permute-start.6 = (bf16[2,128,768]{2,1,0:T(8,128)(2,1)S(1)}, bf16[2,128,768]{2,1,0:T(8,128)(2,1)}, u32[]{:S(2)}, u32[]{:S(2)}) collective-permute-start(bf16[2,128,768]{2,1,0:T(8,128)(2,1)S(1)} %copy-done.7), channel_id=1, source_target_pairs={{0,3},{1,2},{2,1},{3,0},{4,7},{5,6},{6,5},{7,4},{8,11},{9,10},{10,... | collective-permute-start | bytes 1179656 | tf_op jit(solution)/shard_map/ppermute | solution.py:73
  326.8 11.4 %collective-permute-start.8 = (bf16[3,384,1024]{2,1,0:T(8,128)(2,1)}, bf16[3,384,1024]{2,1,0:T(8,128)(2,1)}, u32[]{:S(2)}, u32[]{:S(2)}) collective-permute-start(bf16[3,384,1024]{2,1,0:T(8,128)(2,1)} %collective-permute-done.7.refs_0_.refs_2_.refs_4_), channel_id=1, source_target_pairs={{0,4},{4,0},{8,12},{12,8},{1,5},{5,1},{9,13},{13,9},{2,6},{6,2},{1... | collective-permute-start | bytes 7077896 | tf_op jit(solution)/shard_map/ppermute | solution.py:73
  338.1 8.1 %copy-start.1 = (bf16[512,768]{1,0:T(8,128)(2,1)S(1)}, bf16[512,768]{1,0:T(8,128)(2,1)}, u32[]{:S(2)}) copy-start(bf16[512,768]{1,0:T(8,128)(2,1)} %get-tuple-element.122) | copy-start | bytes 2359300
  346.2 1.7 copy-start
  346.2 2.8 copy-start.4

commit v9 on v8

--- a/solution.py
+++ b/solution.py
@@ -1375,18 +1375,20 @@
         for t in range(max(0, tiles - 2), tiles):
             da_copy(1, t).wait_recv()
             da_copy(2, t).start()
-        mine = pltpu.make_async_copy(da_near.at[0], da_out.at[0], out_sem.at[0])
-        mine.start()
+        def da_store(n):
+            return pltpu.make_async_copy(da_near.at[n], da_out.at[n], out_sem.at[n])
+
+        da_store(0).start()
+        da_store(2).start()
         for t in range(tiles):
             da_copy(0, t).wait()
+        da_store(1).start()
+        for t in range(tiles):
             da_copy(1, t).wait_send()
             da_copy(2, t).wait()
-        rest = pltpu.make_async_copy(
-            da_near.at[pl.ds(1, members - 1)], da_out.at[pl.ds(1, members - 1)], out_sem.at[1]
-        )
-        rest.start()
-        mine.wait()
-        rest.wait()
+        da_store(3).start()
+        for n in range(members):
+            da_store(n).wait()
 
     return run(
         body,
@@ -1398,7 +1400,7 @@
         + [(shape_of((members, rows, width), bf16), anywhere)],
         scratch=[
             pltpu.VMEM((members, rows, width), bf16),
-            dma((3 * tiles,)), dma((3 * tiles,)), dma((2,)),
+            dma((3 * tiles,)), dma((3 * tiles,)), dma((members,)),
         ],
         flops=2 * rows * width * (places * CAP + width),
         moved=rows * width * 24,

time: 355 us -> 354 us (level)
  no operation moved by 1% of the time
where the time goes in v9:
time: 354 us; the launch traced here: 348 us
  Pallas kernels  326 us (92%)
  starting transfers between devices  14.8 us (4%)
  local copies, waits for them, and re-layouts  6.08 us (2%)
    pallas_call x9, Pallas kernels, run(): pl.pallas_call(body, out_shape=[o for o, _ in outputs], grid_spec=pltpu.P...  326 us
    ppermute x5, starting transfers between devices, swap(): return lax.ppermute(value, axis, [(i, i ^ distance) for i in range(count)])  7.97 us
  transfers between devices with their start and end apart: 9, of which 0 were waited for; matrix products, arithmetic and copies ran while one was open for 1% of the time, Pallas kernels for 52%

profile of v9, /device:TPU:0, one launch (start us, length us, event | category | flops | bytes accessed | tf_op | source)
XLA Modules:
  0.0 348.4 jit_solution(10214224023352458256)
XLA Ops:
  0.6 0.0 copy-start.5
  0.7 0.0 copy-start.6
  0.7 30.3 %shard_map.272 = (bf16[3,2048,64]{2,1,0:T(8,128)(2,1)}, bf16[3,2048,64]{2,1,0:T(8,128)(2,1)}, bf16[3,2048,64]{2,1,0:T(8,128)(2,1)}, bf16[192,2048]{1,0:T(8,128)(...) custom-call(bf16[512,768]{1,0:T(8,128)(2,1)} %bitcast.41, ...), custom_call_target="tpu_custom_call" | custom-call | flops 3019898880 | bytes 20971520 | tf_op jit(solution)/shard_map/pallas_call | solution.py:50
  30.9 0.6 collective-permute-start
  31.5 1.5 collective-permute-start.1
  33.0 1.5 collective-permute-start.2
  34.5 3.3 collective-permute-start.3
  37.8 0.0 copy-done.5
  37.8 0.1 select_reduce_fusion
  37.9 0.0 copy-done.6
  37.9 0.6 concatenate.3.meta_ref
  38.5 18.9 %shard_map.273 = (bf16[2048,192]{1,0:T(8,128)(2,1)}, f32[192,2048]{1,0:T(8,128)}, f32[3,2048]{1,0:T(4,128)}, f32[3,256]{1,0:T(4,128)}) custom-call(s32[22]{0:T(128)} %concatenate.3.meta_ref, bf16[3,2048,64]{2,1,0:T(8,128)(2,1)} %get-tuple-element.80.q_ref, bf16[3,2048,64]{2,1,0:T(8,128)(2,1)} %get-tuple-element.81.k_ref, ...), custom_call_target="tpu_custom_call" | custom-call | flops 3221225472 | bytes 5505024 | tf_op jit(solution)/shard_map/pallas_call | solution.py:50
  57.4 0.6 copy.36
  58.0 0.6 reshape.41.refs_10_
  58.6 52.3 %shard_map.274 = (f32[512,768]{1,0:T(8,128)}, f32[512,768]{1,0:T(8,128)}, f32[512,12]{1,0:T(8,128)}, bf16[8,128,768]{2,1,0:T(8,128)(2,1)}, f32[8,1,128]{2,1,0:T(...) custom-call(bf16[512,768]{1,0:T(8,128)(2,1)} %bitcast.42, ...), custom_call_target="tpu_custom_call" | custom-call | flops 1409286144 | bytes 11796480 | tf_op jit(solution)/shard_map/pallas_call | solution.py:50
  111.0 0.0 collective-permute-done.refs_6_
  111.0 0.0 copy-start.9
  111.0 0.0 collective-permute-done.1.refs_7_
  111.0 0.0 copy-start.10
  111.0 0.0 collective-permute-done.2.refs_8_
  111.0 0.0 copy-start.11
  111.0 0.0 collective-permute-done.3.refs_9_
  111.1 0.0 copy-start.12
  111.1 0.6 copy-done.9
  111.7 0.1 copy-done.10
  111.7 0.1 copy-done.11
  111.8 0.1 copy-done.12
  111.9 77.4 %shard_map.275 = (bf16[2,128,768]{2,1,0:T(8,128)(2,1)}, bf16[2,128,768]{2,1,0:T(8,128)(2,1)}, bf16[2,128,768]{2,1,0:T(8,128)(2,1)}, bf16[2,128,768]{2,1,0:T(8,12...) custom-call(bf16[8,128,768]{2,1,0:T(8,128)(2,1)} %get-tuple-element., ...), custom_call_target="tpu_custom_call" | custom-call | flops 28991029248 | bytes 25165824 | tf_op jit(solution)/shard_map/pallas_call | solution.py:50
  189.3 28.2 %shard_map.276 = (f32[512,768]{1,0:T(8,128)}, f32[31,768]{1,0:T(8,128)}, bf16[4,512,768]{2,1,0:T(8,128)(2,1)}) custom-call(f32[512,768]{1,0:T(8,128)} %get-tuple-element.96.refs_0_, f32[512,768]{1,0:T(8,128)} %get-tuple-element.97.refs_1_, bf16[512,768]{1,0:T(8,128)(2,1)} %bitcast.29, f32[512,12]{1,0:T(8,128)} %get-tuple-element.98.refs_3_, ...), custom_call_target="tpu_custom_call" | custom-call | flops 1409286144 | bytes 9437184 | tf_op jit(solution)/shard_map/pallas_call | solution.py:50
  217.5 1.4 collective-permute-start.7
  218.9 3.8 %collective-permute-start.4 = (bf16[2,128,768]{2,1,0:T(8,128)(2,1)}, bf16[2,128,768]{2,1,0:T(8,128)(2,1)}, u32[]{:S(2)}, u32[]{:S(2)}) collective-permute-start(bf16[2,128,768]{2,1,0:T(8,128)(2,1)} %get-tuple-element.119), channel_id=1, source_target_pairs={{0,1},{1,0},{2,3},{3,2},{4,5},{5,4},{6,7},{7,6},{8,9},{9,8},{10,11... | collective-permute-start | bytes 1179656 | tf_op jit(solution)/shard_map/ppermute | solution.py:73
  222.7 0.0 collective-permute-start.5
  222.7 2.4 collective-permute-start.6
  225.1 32.2 %shard_map.277 = (bf16[2048,576]{1,0:T(8,128)(2,1)}, bf16[192,768]{1,0:T(8,128)(2,1)}, f32[2,768,1024]{2,1,0:T(8,128)}, f32[2,768,1024]{2,1,0:T(8,128)}, f32[2,1024,768]{2,1,0:T(8,128)}) custom-call(s32[22]{0:T(128)} %concatenate.3.meta_ref, bf16[3,2048,64]{2,1,0:T(8,128)(2,1)} %get-tuple-element.80.q_ref, bf16[3,2048,64]{2,1,0:T(8,128)(2,1)} %get-tuple-element.81.k_ref, ...), custom_call_target="tpu_custom_call" | custom-call | flops 8053063680 | bytes 9437184 | tf_op jit(solution)/shard_map/pallas_call | solution.py:50
  257.2 0.0 collective-permute-done.4.refs_12_
  257.3 0.0 collective-permute-done.5.refs_13_
  257.3 0.0 collective-permute-done.6.refs_14_
  257.3 67.8 %shard_map.278 = (f32[512,768]{1,0:T(8,128)}, bf16[2,4,8,48,576]{4,3,2,1,0:T(8,128)(2,1)}, bf16[4,8,24,768]{3,2,1,0:T(8,128)(2,1)}, f32[31,768]{1,0:T(8,128)}, f...) custom-call(bf16[2048,576]{1,0:T(8,128)(2,1)} %get-tuple-element.110.refs_0_, ...), custom_call_target="tpu_custom_call" | custom-call | flops 7247757312 | bytes 20971520 | tf_op jit(solution)/shard_map/pallas_call | solution.py:50
  325.1 0.0 collective-permute-done.7.refs_0_.refs_2_.refs_4_
  325.1 0.4 collective-permute-start.8
  325.5 10.9 %shard_map.279 = (f32[3,768,768]{2,1,0:T(8,128)}, f32[4,192,768]{2,1,0:T(8,128)}, f32[2,768,768]{2,1,0:T(8,128)}, f32[12,768]{1,0:T(8,128)}, f32[768]{0:T(1024)}...) custom-call(s32[22]{0:T(128)} %concatenate.3.meta_ref, ...), custom_call_target="tpu_custom_call" | custom-call | bytes 21233664 | tf_op jit(solution)/shard_map/pallas_call | solution.py:50
  336.4 0.0 collective-permute-done.8.refs_1_.refs_3_.refs_5_
  336.5 8.1 %shard_map.280 = (f32[2,768,1024]{2,1,0:T(8,128)}, f32[2,768,1024]{2,1,0:T(8,128)}, f32[2,1024,768]{2,1,0:T(8,128)}) custom-call(s32[22]{0:T(128)} %concatenate.3.meta_ref, bf16[3,384,1024]{2,1,0:T(8,128)(2,1)} %collective-permute-done.7.refs_0_.refs_2_.refs_4_, ...), custom_call_target="tpu_custom_call", output_to_operand_aliasing={{0}: (7, {}), {1}: (8, {}), {2}: (9, {})} | custom-call | bytes 14155776 | tf_op jit(solution)/shard_map/pallas_call | solution.py:50
  344.6 0.9 copy.43
  345.5 0.8 copy-done
  346.2 1.1 copy.44
  347.4 0.0 copy-done.4
  347.4 0.6 copy.45
  (13 shorter events, 0.0 us)
Async XLA Ops:
  0.6 37.1 %copy-start.5 = (s32[1,8]{1,0:T(1,128)S(1)}, s32[1,8]{1,0:T(1,128)}, u32[]{:S(2)}) copy-start(s32[1,8]{1,0:T(1,128)} %param.19) | copy-start | bytes 100
  0.7 37.3 %copy-start.6 = (s32[1,2]{1,0:T(1,128)S(1)}, s32[1,2]{1,0:T(1,128)}, u32[]{:S(2)}) copy-start(s32[1,2]{1,0:T(1,128)} %param.18) | copy-start | bytes 28
  30.9 80.0 %collective-permute-start = (bf16[128,768]{1,0:T(8,128)(2,1)}, bf16[128,768]{1,0:T(8,128)(2,1)S(1)}, u32[]{:S(2)}, u32[]{:S(2)}) collective-permute-start(bf16[128,768]{1,0:T(8,128)(2,1)} %get-tuple-element.91), channel_id=1, source_target_pairs={{0,8},{1,9},{2,10},{3,11},{4,12},{5,13},{6,14},{7,15},{8,0},{9,1},... | collective-permute-start | bytes 589832 | tf_op jit(solution)/shard_map/ppermute | solution.py:101
  31.5 79.5 %collective-permute-start.1 = (bf16[128,768]{1,0:T(8,128)(2,1)}, bf16[128,768]{1,0:T(8,128)(2,1)S(1)}, u32[]{:S(2)}, u32[]{:S(2)}) collective-permute-start(bf16[128,768]{1,0:T(8,128)(2,1)} %get-tuple-element.92), channel_id=1, source_target_pairs={{0,9},{1,8},{2,11},{3,10},{4,13},{5,12},{6,15},{7,14},{8,1},{9,0},... | collective-permute-start | bytes 589832 | tf_op jit(solution)/shard_map/ppermute | solution.py:101
  33.0 78.0 %collective-permute-start.2 = (bf16[128,768]{1,0:T(8,128)(2,1)}, bf16[128,768]{1,0:T(8,128)(2,1)S(1)}, u32[]{:S(2)}, u32[]{:S(2)}) collective-permute-start(bf16[128,768]{1,0:T(8,128)(2,1)} %get-tuple-element.93), channel_id=1, source_target_pairs={{0,10},{1,11},{2,8},{3,9},{4,14},{5,15},{6,12},{7,13},{8,2},{9,3},... | collective-permute-start | bytes 589832 | tf_op jit(solution)/shard_map/ppermute | solution.py:101
  34.5 76.5 %collective-permute-start.3 = (bf16[128,768]{1,0:T(8,128)(2,1)}, bf16[128,768]{1,0:T(8,128)(2,1)S(1)}, u32[]{:S(2)}, u32[]{:S(2)}) collective-permute-start(bf16[128,768]{1,0:T(8,128)(2,1)} %get-tuple-element.94), channel_id=1, source_target_pairs={{0,11},{1,10},{2,9},{3,8},{4,15},{5,14},{6,13},{7,12},{8,3},{9,2},... | collective-permute-start | bytes 589832 | tf_op jit(solution)/shard_map/ppermute | solution.py:101
  38.5 18.9 %copy-start.2 = (f32[1,512,12]{1,0,2:T(1,128)S(1)}, f32[1,512,12]{1,0,2:T(1,128)}, u32[]{:S(2)}) copy-start(f32[1,512,12]{1,0,2:T(1,128)} %param.21) | copy-start | bytes 73732
  38.5 19.5 %copy-start.3 = (f32[2,768,2]{1,2,0:T(2,128)S(1)}, f32[2,768,2]{1,2,0:T(2,128)}, u32[]{:S(2)}) copy-start(f32[2,768,2]{1,2,0:T(2,128)} %param.28) | copy-start | bytes 36868
  111.0 0.7 copy-start.9
  111.0 0.7 copy-start.10
  111.0 0.8 copy-start.11
  111.1 0.8 copy-start.12
  189.3 33.4 %copy-start.8 = (bf16[2,128,768]{2,1,0:T(8,128)(2,1)S(1)}, bf16[2,128,768]{2,1,0:T(8,128)(2,1)}, u32[]{:S(2)}) copy-start(bf16[2,128,768]{2,1,0:T(8,128)(2,1)} %get-tuple-element.120) | copy-start | bytes 1179652
  189.3 33.4 %copy-start.7 = (bf16[2,128,768]{2,1,0:T(8,128)(2,1)S(1)}, bf16[2,128,768]{2,1,0:T(8,128)(2,1)}, u32[]{:S(2)}) copy-start(bf16[2,128,768]{2,1,0:T(8,128)(2,1)} %get-tuple-element.121) | copy-start | bytes 1179652
  217.5 107.6 %collective-permute-start.7 = (bf16[3,384,1024]{2,1,0:T(8,128)(2,1)}, bf16[3,384,1024]{2,1,0:T(8,128)(2,1)}, u32[]{:S(2)}, u32[]{:S(2)}) collective-permute-start(bf16[3,384,1024]{2,1,0:T(8,128)(2,1)} %get-tuple-element.125.refs_2_.refs_3_.refs_6_), channel_id=1, source_target_pairs={{0,8},{4,12},{8,0},{12,4},{1,9},{5,13},{9,1},{13,5},{2,10},{6,14},... | collective-permute-start | bytes 7077896 | tf_op jit(solution)/shard_map/ppermute | solution.py:73
  218.9 38.4 %collective-permute-start.4 = (bf16[2,128,768]{2,1,0:T(8,128)(2,1)}, bf16[2,128,768]{2,1,0:T(8,128)(2,1)}, u32[]{:S(2)}, u32[]{:S(2)}) collective-permute-start(bf16[2,128,768]{2,1,0:T(8,128)(2,1)} %get-tuple-element.119), channel_id=1, source_target_pairs={{0,1},{1,0},{2,3},{3,2},{4,5},{5,4},{6,7},{7,6},{8,9},{9,8},{10,11... | collective-permute-start | bytes 1179656 | tf_op jit(solution)/shard_map/ppermute | solution.py:73
  222.7 34.6 %collective-permute-start.5 = (bf16[2,128,768]{2,1,0:T(8,128)(2,1)S(1)}, bf16[2,128,768]{2,1,0:T(8,128)(2,1)}, u32[]{:S(2)}, u32[]{:S(2)}) collective-permute-start(bf16[2,128,768]{2,1,0:T(8,128)(2,1)S(1)} %copy-done.8), channel_id=1, source_target_pairs={{0,2},{1,3},{2,0},{3,1},{4,6},{5,7},{6,4},{7,5},{8,10},{9,11},{10,... | collective-permute-start | bytes 1179656 | tf_op jit(solution)/shard_map/ppermute | solution.py:73
  222.7 34.6 %collective-permute-start.6 = (bf16[2,128,768]{2,1,0:T(8,128)(2,1)S(1)}, bf16[2,128,768]{2,1,0:T(8,128)(2,1)}, u32[]{:S(2)}, u32[]{:S(2)}) collective-permute-start(bf16[2,128,768]{2,1,0:T(8,128)(2,1)S(1)} %copy-done.7), channel_id=1, source_target_pairs={{0,3},{1,2},{2,1},{3,0},{4,7},{5,6},{6,5},{7,4},{8,11},{9,10},{10,... | collective-permute-start | bytes 1179656 | tf_op jit(solution)/shard_map/ppermute | solution.py:73
  325.1 11.4 %collective-permute-start.8 = (bf16[3,384,1024]{2,1,0:T(8,128)(2,1)}, bf16[3,384,1024]{2,1,0:T(8,128)(2,1)}, u32[]{:S(2)}, u32[]{:S(2)}) collective-permute-start(bf16[3,384,1024]{2,1,0:T(8,128)(2,1)} %collective-permute-done.7.refs_0_.refs_2_.refs_4_), channel_id=1, source_target_pairs={{0,4},{4,0},{8,12},{12,8},{1,5},{5,1},{9,13},{13,9},{2,6},{6,2},{1... | collective-permute-start | bytes 7077896 | tf_op jit(solution)/shard_map/ppermute | solution.py:73
  336.5 8.1 %copy-start.1 = (bf16[512,768]{1,0:T(8,128)(2,1)S(1)}, bf16[512,768]{1,0:T(8,128)(2,1)}, u32[]{:S(2)}) copy-start(bf16[512,768]{1,0:T(8,128)(2,1)} %get-tuple-element.122) | copy-start | bytes 2359300
  344.6 1.7 copy-start
  344.6 2.8 copy-start.4
